TPU v7x, 32 devices: a whole 2x2x4 slice. The times are simulated.
32 devices in a mesh: dp: 16 (over z, x, core), mp: 2 (over y).
Axes of the slice: x: 2, y: 2, z: 4, core: 2. Of those that a mesh axis runs over, the one named last changes fastest.
Arguments:
- text_tokens: bfloat16 [256, 64, 768], P('dp', 'mp'), may hold values from -6 to 6
- image_tokens: bfloat16 [256, 576, 768], P('dp'), may hold values from -6 to 6
- resolution: int32 [256], P('dp'), may hold values 0 or 1
- query_self: bfloat16 [768, 768], P('dp', 'mp'), may hold values from -0.21875 to 0.21875
- key_self: bfloat16 [768, 768], P('dp', 'mp'), may hold values from -0.21875 to 0.21875
- value_self: bfloat16 [768, 768], P('dp', 'mp'), may hold values from -0.21875 to 0.21875
- mix_self: bfloat16 [768, 768], P('mp', 'dp'), may hold values from -0.875 to 0.875
- query_cross: bfloat16 [768, 768], P('dp', 'mp'), may hold values from -0.21875 to 0.21875
- key_cross: bfloat16 [768, 768], P('dp', 'mp'), may hold values from -0.21875 to 0.21875
- value_cross: bfloat16 [768, 768], P('dp', 'mp'), may hold values from -0.21875 to 0.21875
- mix_cross: bfloat16 [768, 768], P('mp', 'dp'), may hold values from -1.75 to 1.75
- expand: bfloat16 [768, 3072], P('dp', 'mp'), may hold values from -0.21875 to 0.21875
- contract: bfloat16 [3072, 768], P('mp', 'dp'), may hold values from -0.109375 to 0.109375
- first_gain: float32 [768], replicated, may hold values from 0.25 to 1.75
- first_shift: float32 [768], replicated, may hold values from -3 to 3
- second_gain: float32 [768], replicated, may hold values from 0.25 to 1.75
- second_shift: float32 [768], replicated, may hold values from -3 to 3
- third_gain: float32 [768], replicated, may hold values from 0.25 to 1.75
- third_shift: float32 [768], replicated, may hold values from -3 to 3
- cotangent: bfloat16 [256, 64, 768], P('dp', 'mp'), may hold values from -6 to 6
Outputs:
- layer_out: bfloat16 [256, 64, 768], P('dp', 'mp')
- text_grad: float32 [256, 64, 768], P('dp', 'mp')
- image_grad: float32 [256, 576, 768], P('dp', 'mp')
- grad_query_self: float32 [768, 768], P('dp', 'mp')
- grad_key_self: float32 [768, 768], P('dp', 'mp')
- grad_value_self: float32 [768, 768], P('dp', 'mp')
- grad_mix_self: float32 [768, 768], P('mp', 'dp')
- grad_query_cross: float32 [768, 768], P('dp', 'mp')
- grad_key_cross: float32 [768, 768], P('dp', 'mp')
- grad_value_cross: float32 [768, 768], P('dp', 'mp')
- grad_mix_cross: float32 [768, 768], P('mp', 'dp')
- grad_expand: float32 [768, 3072], P('dp', 'mp')
- grad_contract: float32 [3072, 768], P('mp', 'dp')
- grad_first_gain: float32 [768], replicated
- grad_first_shift: float32 [768], replicated
- grad_second_gain: float32 [768], replicated
- grad_second_shift: float32 [768], replicated
- grad_third_gain: float32 [768], replicated
- grad_third_shift: float32 [768], replicated
Inputs may be any that keep to these rules, and one draw needn't show every extreme that they name: `resolution`: 1 marks an image of 576 patches, 0 one of 196; patch slots at or past the count are padding.
All inputs are finite; a program needn't handle non-finite values. No bound on the sum of `resolution` on one device may be relied on, other than what follows from the above.
Results may differ from a plain program's by a relative error of at most 0.02.
Values may be sent and summed in bfloat16 or wider, within the bound.
A program may use at most 256 MiB of HBM per device.

v0:
```python
import jax
import jax.numpy as jnp
from jax import lax
from jax.sharding import PartitionSpec as P

HD = 64
LEN = 64
PATCH = 576
SMALLP = 196
MICRO = 2
CAPS = 8


epsilon = 1e-05
masked_score = -1000000000.0


def layer_norm(value, gain, shift):
    average = jnp.mean(value, axis=-1, keepdims=True)
    centred = value - average
    spread = jnp.mean(centred * centred, axis=-1, keepdims=True)
    return centred * lax.rsqrt(spread + epsilon) * gain + shift


def norm_back(stream, gain, shift, grad_normed):
    _, pullback = jax.vjp(layer_norm, stream, gain, shift)
    return pullback(grad_normed)


def gelu_tanh(value):
    return jax.nn.gelu(value, approximate=True)


def matmul(left, right):
    return jnp.einsum("...d,de->...e", left, right, preferred_element_type=jnp.float32)


def matmul_back(left, right):
    return jnp.einsum("...e,de->...d", left, right, preferred_element_type=jnp.float32)


def weight_grad(left, right):
    return jnp.einsum("crd,cre->de", left, right, preferred_element_type=jnp.float32)


def split_heads(rows):
    return rows.reshape(rows.shape[0], rows.shape[1], rows.shape[2] // HD, HD)


def join_heads(rows):
    return rows.reshape(rows.shape[0], rows.shape[1], rows.shape[2] * rows.shape[3])


def score_block(queries, key_rows, allowed):
    scores = jnp.einsum(
        "clhd,ckhd->chlk",
        split_heads(queries),
        split_heads(key_rows),
        preferred_element_type=jnp.float32,
    ) * HD ** (-0.5)
    return jnp.where(allowed, scores, masked_score)


def attend_forward(queries, key_rows, value_rows, allowed):
    scores = score_block(queries, key_rows, allowed)
    highest = jnp.max(scores, axis=-1, keepdims=True)
    exponent = jnp.exp(scores - highest)
    totals = jnp.sum(exponent, axis=-1, keepdims=True)
    attn_prob = (exponent / totals).astype(jnp.bfloat16)
    mixture = jnp.einsum(
        "chlk,ckhd->clhd", attn_prob, split_heads(value_rows), preferred_element_type=jnp.float32
    )
    return (join_heads(mixture).astype(jnp.bfloat16), highest + jnp.log(totals))


def attend_backward(queries, key_rows, value_rows, allowed, log_totals, grad_mix):
    score_scale = HD ** (-0.5)
    attn_prob = jnp.exp(score_block(queries, key_rows, allowed) - log_totals)
    mix_heads = split_heads(grad_mix)
    grad_prob = jnp.einsum(
        "clhd,ckhd->chlk", mix_heads, split_heads(value_rows), preferred_element_type=jnp.float32
    )
    grad_values = jnp.einsum(
        "chlk,clhd->ckhd",
        attn_prob.astype(jnp.bfloat16),
        mix_heads,
        preferred_element_type=jnp.float32,
    )
    row_inner = jnp.sum(attn_prob * grad_prob, axis=-1, keepdims=True)
    grad_score = (attn_prob * (grad_prob - row_inner)).astype(jnp.bfloat16)
    grad_queries = (
        jnp.einsum(
            "chlk,ckhd->clhd", grad_score, split_heads(key_rows), preferred_element_type=jnp.float32
        )
        * score_scale
    )
    grad_keys = (
        jnp.einsum(
            "chlk,clhd->ckhd", grad_score, split_heads(queries), preferred_element_type=jnp.float32
        )
        * score_scale
    )
    return (
        join_heads(grad_queries).astype(jnp.bfloat16),
        join_heads(grad_keys).astype(jnp.bfloat16),
        join_heads(grad_values).astype(jnp.bfloat16),
    )


def gather_rows(normed):
    return lax.all_gather(normed, "mp", axis=1, tiled=True)


def sum_rows(partial_rows):
    return lax.psum_scatter(partial_rows, "mp", scatter_dimension=1, tiled=True)


def gather_grads(grad_rows):
    return lax.all_gather(grad_rows, "mp", axis=1, tiled=True)


def sum_grads(partial_grads):
    return lax.psum_scatter(partial_grads, "mp", scatter_dimension=1, tiled=True)


def body(
    text_tokens,
    image_tokens,
    resolution,
    query_self,
    key_self,
    value_self,
    mix_self,
    query_cross,
    key_cross,
    value_cross,
    mix_cross,
    expand,
    contract,
    first_gain,
    first_shift,
    second_gain,
    second_shift,
    third_gain,
    third_shift,
    cotangent,
):
    causal = (jnp.arange(LEN)[:, None] >= jnp.arange(LEN)[None, :])[None, None]
    out_parts = []
    text_parts = []
    patch_parts = []
    grad_totals = None
    norm_totals = None
    for micro_index in range(MICRO):
        start = micro_index * CAPS
        stream = text_tokens[start : start + CAPS].astype(jnp.float32)
        patches = image_tokens[start : start + CAPS]
        valid_count = SMALLP + (PATCH - SMALLP) * resolution[start : start + CAPS]
        visible = (jnp.arange(PATCH)[None, :] < valid_count[:, None])[:, None, None, :]
        weights = (
            lax.all_gather(query_self, "dp", axis=0, tiled=True),
            lax.all_gather(key_self, "dp", axis=0, tiled=True),
            lax.all_gather(value_self, "dp", axis=0, tiled=True),
            lax.all_gather(mix_self, "dp", axis=1, tiled=True),
            lax.all_gather(query_cross, "dp", axis=0, tiled=True),
            lax.all_gather(key_cross, "dp", axis=0, tiled=True),
            lax.all_gather(value_cross, "dp", axis=0, tiled=True),
            lax.all_gather(mix_cross, "dp", axis=1, tiled=True),
            lax.all_gather(expand, "dp", axis=0, tiled=True),
            lax.all_gather(contract, "dp", axis=1, tiled=True),
        )
        (
            full_query_self,
            full_key_self,
            full_value_self,
            full_mix_self,
            full_query_cross,
            full_key_cross,
            full_value_cross,
            full_mix_cross,
            full_expand,
            full_contract,
        ) = weights
        normed_one = gather_rows(layer_norm(stream, first_gain, first_shift).astype(jnp.bfloat16))
        queries_one = matmul(normed_one, full_query_self).astype(jnp.bfloat16)
        keys_one = matmul(normed_one, full_key_self).astype(jnp.bfloat16)
        values_one = matmul(normed_one, full_value_self).astype(jnp.bfloat16)
        mixed_one, totals_one = attend_forward(queries_one, keys_one, values_one, causal)
        stream_one = stream + sum_rows(matmul(mixed_one, full_mix_self))
        normed_two = gather_rows(
            layer_norm(stream_one, second_gain, second_shift).astype(jnp.bfloat16)
        )
        queries_two = matmul(normed_two, full_query_cross).astype(jnp.bfloat16)
        keys_two = matmul(patches, full_key_cross).astype(jnp.bfloat16)
        values_two = matmul(patches, full_value_cross).astype(jnp.bfloat16)
        mixed_two, totals_two = attend_forward(queries_two, keys_two, values_two, visible)
        stream_two = stream_one + sum_rows(matmul(mixed_two, full_mix_cross))
        normed_three = gather_rows(
            layer_norm(stream_two, third_gain, third_shift).astype(jnp.bfloat16)
        )
        pre_act = matmul(normed_three, full_expand)
        hidden = gelu_tanh(pre_act).astype(jnp.bfloat16)
        out_parts.append(
            (stream_two + sum_rows(matmul(hidden, full_contract))).astype(jnp.bfloat16)
        )
        back_weights = (
            lax.all_gather(query_self, "dp", axis=0, tiled=True),
            lax.all_gather(key_self, "dp", axis=0, tiled=True),
            lax.all_gather(value_self, "dp", axis=0, tiled=True),
            lax.all_gather(mix_self, "dp", axis=1, tiled=True),
            lax.all_gather(query_cross, "dp", axis=0, tiled=True),
            lax.all_gather(key_cross, "dp", axis=0, tiled=True),
            lax.all_gather(value_cross, "dp", axis=0, tiled=True),
            lax.all_gather(mix_cross, "dp", axis=1, tiled=True),
            lax.all_gather(expand, "dp", axis=0, tiled=True),
            lax.all_gather(contract, "dp", axis=1, tiled=True),
        )
        (
            back_query_self,
            back_key_self,
            back_value_self,
            back_mix_self,
            back_query_cross,
            back_key_cross,
            back_value_cross,
            back_mix_cross,
            back_expand,
            back_contract,
        ) = back_weights
        grad_stream = cotangent[start : start + CAPS].astype(jnp.float32)
        grad_rows = gather_grads(grad_stream.astype(jnp.bfloat16))
        grad_contract = weight_grad(hidden, grad_rows)
        grad_hidden = matmul_back(grad_rows, back_contract)
        _, gelu_pull = jax.vjp(gelu_tanh, pre_act)
        grad_pre = gelu_pull(grad_hidden)[0].astype(jnp.bfloat16)
        grad_expand = weight_grad(normed_three, grad_pre)
        grad_normed = sum_grads(matmul_back(grad_pre, back_expand))
        grad_input, gain_three, shift_three = norm_back(
            stream_two, third_gain, third_shift, grad_normed
        )
        grad_stream = grad_stream + grad_input
        grad_rows = gather_grads(grad_stream.astype(jnp.bfloat16))
        grad_mix_cross = weight_grad(mixed_two, grad_rows)
        grad_mixed = matmul_back(grad_rows, back_mix_cross).astype(jnp.bfloat16)
        grad_queries, grad_keys, grad_values = attend_backward(
            queries_two, keys_two, values_two, visible, totals_two, grad_mixed
        )
        grad_query_cross = weight_grad(normed_two, grad_queries)
        grad_key_cross = weight_grad(patches, grad_keys)
        grad_value_cross = weight_grad(patches, grad_values)
        patch_term = matmul_back(grad_keys, back_key_cross) + matmul_back(
            grad_values, back_value_cross
        )
        patch_parts.append(
            lax.psum_scatter(
                patch_term.astype(jnp.bfloat16), "mp", scatter_dimension=1, tiled=True
            ).astype(jnp.float32)
        )
        grad_normed = sum_grads(matmul_back(grad_queries, back_query_cross))
        grad_input, gain_two, shift_two = norm_back(
            stream_one, second_gain, second_shift, grad_normed
        )
        grad_stream = grad_stream + grad_input
        grad_rows = gather_grads(grad_stream.astype(jnp.bfloat16))
        grad_mix_self = weight_grad(mixed_one, grad_rows)
        grad_mixed = matmul_back(grad_rows, back_mix_self).astype(jnp.bfloat16)
        grad_queries, grad_keys, grad_values = attend_backward(
            queries_one, keys_one, values_one, causal, totals_one, grad_mixed
        )
        grad_query_self = weight_grad(normed_one, grad_queries)
        grad_key_self = weight_grad(normed_one, grad_keys)
        grad_value_self = weight_grad(normed_one, grad_values)
        grad_normed = sum_grads(
            matmul_back(grad_queries, back_query_self)
            + matmul_back(grad_keys, back_key_self)
            + matmul_back(grad_values, back_value_self)
        )
        grad_input, gain_one, shift_one = norm_back(stream, first_gain, first_shift, grad_normed)
        text_parts.append(grad_stream + grad_input)
        norm_terms = (gain_one, shift_one, gain_two, shift_two, gain_three, shift_three)
        if norm_totals is None:
            norm_totals = norm_terms
        else:
            norm_totals = tuple((total + term for total, term in zip(norm_totals, norm_terms)))
        grad_terms = (
            lax.psum_scatter(grad_query_self, "dp", scatter_dimension=0, tiled=True),
            lax.psum_scatter(grad_key_self, "dp", scatter_dimension=0, tiled=True),
            lax.psum_scatter(grad_value_self, "dp", scatter_dimension=0, tiled=True),
            lax.psum_scatter(grad_mix_self, "dp", scatter_dimension=1, tiled=True),
            lax.psum_scatter(grad_query_cross, "dp", scatter_dimension=0, tiled=True),
            lax.psum_scatter(grad_key_cross, "dp", scatter_dimension=0, tiled=True),
            lax.psum_scatter(grad_value_cross, "dp", scatter_dimension=0, tiled=True),
            lax.psum_scatter(grad_mix_cross, "dp", scatter_dimension=1, tiled=True),
            lax.psum_scatter(grad_expand, "dp", scatter_dimension=0, tiled=True),
            lax.psum_scatter(grad_contract, "dp", scatter_dimension=1, tiled=True),
        )
        if grad_totals is None:
            grad_totals = grad_terms
        else:
            grad_totals = tuple((total + term for total, term in zip(grad_totals, grad_terms)))
    norm_sums = lax.psum(
        (
            norm_totals[0],
            norm_totals[1],
            norm_totals[2],
            norm_totals[3],
            norm_totals[4],
            norm_totals[5],
        ),
        ("dp", "mp"),
    )
    return (
        jnp.concatenate(out_parts, axis=0),
        jnp.concatenate(text_parts, axis=0),
        jnp.concatenate(patch_parts, axis=0),
        grad_totals[0],
        grad_totals[1],
        grad_totals[2],
        grad_totals[3],
        grad_totals[4],
        grad_totals[5],
        grad_totals[6],
        grad_totals[7],
        grad_totals[8],
        grad_totals[9],
        norm_sums[0],
        norm_sums[1],
        norm_sums[2],
        norm_sums[3],
        norm_sums[4],
        norm_sums[5],
    )


def solution(mesh):
    in_specs = (
        P("dp", "mp", None),
        P("dp", None, None),
        P("dp"),
        P("dp", "mp"),
        P("dp", "mp"),
        P("dp", "mp"),
        P("mp", "dp"),
        P("dp", "mp"),
        P("dp", "mp"),
        P("dp", "mp"),
        P("mp", "dp"),
        P("dp", "mp"),
        P("mp", "dp"),
        P(),
        P(),
        P(),
        P(),
        P(),
        P(),
        P("dp", "mp", None),
    )
    out_specs = (
        P("dp", "mp", None),
        P("dp", "mp", None),
        P("dp", "mp", None),
        P("dp", "mp"),
        P("dp", "mp"),
        P("dp", "mp"),
        P("mp", "dp"),
        P("dp", "mp"),
        P("dp", "mp"),
        P("dp", "mp"),
        P("mp", "dp"),
        P("dp", "mp"),
        P("mp", "dp"),
        P(),
        P(),
        P(),
        P(),
        P(),
        P(),
    )
    return jax.shard_map(body, mesh=mesh, in_specs=in_specs, out_specs=out_specs, check_vma=False)
```

profile of v0, /device:TPU:0, one launch (start us, length us, event | category | flops | bytes accessed | tf_op | source)
XLA Modules:
  0.0 1637.1 jit_solution(17474008075188544016)
XLA Ops:
  11.0 25.1 %all_gather.46 = bf16[768,384]{1,0:T(8,128)(2,1)S(1)} all-gather(bf16[48,384]{1,0:T(8,128)(2,1)} %param.23), channel_id=1, replica_groups=mesh['dp'=16,'mp'=2] {'dp'}, dimensions={0}, use_global_device_ids=true | all-gather | bytes 626688 | tf_op jit(solution)/shard_map/all_gather | solution.py:161
  36.1 19.3 %all_gather.47 = bf16[768,384]{1,0:T(8,128)(2,1)S(1)} all-gather(bf16[48,384]{1,0:T(8,128)(2,1)} %param.24), channel_id=1, replica_groups=mesh['dp'=16,'mp'=2] {'dp'}, dimensions={0}, use_global_device_ids=true | all-gather | bytes 626688 | tf_op jit(solution)/shard_map/all_gather | solution.py:162
  55.5 20.7 %all_gather.45 = bf16[768,384]{1,0:T(8,128)(2,1)S(1)} all-gather(bf16[48,384]{1,0:T(8,128)(2,1)} %param.25), channel_id=1, replica_groups=mesh['dp'=16,'mp'=2] {'dp'}, dimensions={0}, use_global_device_ids=true | all-gather | bytes 626688 | tf_op jit(solution)/shard_map/all_gather | solution.py:163
  76.2 20.4 %all_gather.48 = bf16[384,768]{0,1:T(8,128)(2,1)} all-gather(bf16[384,48]{0,1:T(8,128)(2,1)S(1)} %copy-done.174), channel_id=1, replica_groups=mesh['dp'=16,'mp'=2] {'dp'}, dimensions={1}, use_global_device_ids=true | all-gather | bytes 626688 | tf_op jit(solution)/shard_map/all_gather | solution.py:164
  97.7 12.0 all_gather.109
  125.6 17.5 %all_gather.44 = bf16[8,64,768]{2,1,0:T(8,128)(2,1)S(1)} all-gather(bf16[8,32,768]{2,1,0:T(8,128)(2,1)S(1)} %copy-done.82), channel_id=1, replica_groups=mesh['dp'=16,'mp'=2] {'mp'}, dimensions={1}, use_global_device_ids=true | all-gather | bytes 1179648 | tf_op jit(solution)/shard_map/all_gather | solution.py:111
  158.3 20.8 %all_gather.49 = bf16[768,384]{1,0:T(8,128)(2,1)S(1)} all-gather(bf16[48,384]{1,0:T(8,128)(2,1)S(1)} %copy-done.175), channel_id=1, replica_groups=mesh['dp'=16,'mp'=2] {'dp'}, dimensions={0}, use_global_device_ids=true | all-gather | bytes 626688 | tf_op jit(solution)/shard_map/all_gather | solution.py:167
  179.1 8.9 convolution_convert_fusion.1
  188.0 8.7 convolution_convert_fusion.3
  196.7 5.9 copy.191
  202.6 6.0 copy.182
  208.6 19.5 %all_gather.104 = bf16[768,384]{1,0:T(8,128)(2,1)S(1)} all-gather(bf16[48,384]{1,0:T(8,128)(2,1)S(1)} %copy-done.176), channel_id=1, replica_groups=mesh['dp'=16,'mp'=2] {'dp'}, dimensions={0}, use_global_device_ids=true | all-gather | bytes 626688 | tf_op jit(solution)/shard_map/all_gather | solution.py:166
  228.1 8.9 convolution_convert_fusion
  237.0 6.0 copy.192
  242.9 8.7 convolution_convert_fusion.2
  251.6 6.0 copy.183
  257.7 20.5 %all_gather.51 = bf16[768,384]{1,0:T(8,128)(2,1)S(1)} all-gather(bf16[48,384]{1,0:T(8,128)(2,1)S(1)} %copy-done.177), channel_id=1, replica_groups=mesh['dp'=16,'mp'=2] {'dp'}, dimensions={0}, use_global_device_ids=true | all-gather | bytes 626688 | tf_op jit(solution)/shard_map/all_gather | solution.py:165
  278.2 19.0 %all_gather.105 = bf16[384,768]{0,1:T(8,128)(2,1)S(1)} all-gather(bf16[384,48]{0,1:T(8,128)(2,1)S(1)} %copy-done.178), channel_id=1, replica_groups=mesh['dp'=16,'mp'=2] {'dp'}, dimensions={1}, use_global_device_ids=true | all-gather | bytes 626688 | tf_op jit(solution)/shard_map/all_gather | solution.py:168
  301.9 12.8 all_gather.50
  318.4 13.4 all_gather.110
  349.0 4.2 fusion.21
  366.2 11.0 all_gather.115
  379.1 22.8 %reduce-scatter.37.cloned.1.call-done = f32[8,32,768]{2,1,0:T(8,128)} async-done(((f32[8,64,768]{2,1,0:T(8,128)}), f32[8,32,768]{2,1,0:T(8,128)}) %reduce-scatter.37.cloned.1.call-update) | async-done | bytes 786448 | tf_op jit(solution)/shard_map/reduce_scatter | solution.py:115
  405.1 11.7 all_gather.111
  416.8 4.9 fusion.52
  421.8 28.4 %all-gather.5.cloned.1.call-done = bf16[1536,768]{0,1:T(8,128)(2,1)} async-done(((bf16[1536,48]{0,1:T(8,128)(2,1)}), bf16[1536,768]{0,1:T(8,128)(2,1)}) %all-gather.5.cloned.1.call-update) | async-done | bytes 2359312 | tf_op jit(solution)/shard_map/all_gather | solution.py:170
  450.2 5.8 fusion.35
  459.8 18.8 %all_gather.112 = bf16[8,64,768]{2,1,0:T(8,128)(2,1)S(1)} all-gather(bf16[8,32,768]{2,1,0:T(8,128)(2,1)} %get-tuple-element.135), channel_id=1, replica_groups=mesh['dp'=16,'mp'=2] {'mp'}, dimensions={1}, use_global_device_ids=true | all-gather | bytes 1179648 | tf_op jit(solution)/shard_map/all_gather | solution.py:119
  478.7 18.6 %all_gather.106 = bf16[8,64,768]{2,1,0:T(8,128)(2,1)S(1)} all-gather(bf16[8,32,768]{2,1,0:T(8,128)(2,1)S(1)} %get-tuple-element.140), channel_id=1, replica_groups=mesh['dp'=16,'mp'=2] {'mp'}, dimensions={1}, use_global_device_ids=true | all-gather | bytes 1179648 | tf_op jit(solution)/shard_map/all_gather | solution.py:111
  508.2 5.7 fusion.44
  514.1 5.7 fusion.46
  520.9 11.9 reduce-scatter.41.cloned.1.call-done
  535.5 25.8 %reduce-scatter.39.cloned.1.call-done = f32[8,32,768]{2,1,0:T(8,128)} async-done(((f32[8,64,768]{2,1,0:T(8,128)}), f32[8,32,768]{2,1,0:T(8,128)}) %reduce-scatter.39.cloned.1.call-update) | async-done | bytes 786448 | tf_op jit(solution)/shard_map/reduce_scatter | solution.py:115
  561.3 28.4 %reduce-scatter.33.cloned.1.call-done = f32[8,32,768]{2,1,0:T(8,128)} async-done(((f32[8,64,768]{2,1,0:T(8,128)}), f32[8,32,768]{2,1,0:T(8,128)}) %reduce-scatter.33.cloned.1.call-update) | async-done | bytes 786448 | tf_op jit(solution)/shard_map/reduce_scatter | solution.py:115
  594.2 11.3 all_gather.116
  609.2 7.9 multiply_reduce_fusion
  629.7 17.2 %all_gather.113 = bf16[8,64,768]{2,1,0:T(8,128)(2,1)S(1)} all-gather(bf16[8,32,768]{2,1,0:T(8,128)(2,1)} %get-tuple-element.132), channel_id=1, replica_groups=mesh['dp'=16,'mp'=2] {'mp'}, dimensions={1}, use_global_device_ids=true | all-gather | bytes 1179648 | tf_op jit(solution)/shard_map/all_gather | solution.py:119
  650.6 8.1 multiply_reduce_fusion.1
  669.2 25.6 %reduce-scatter.43.cloned.1.call-done = f32[8,32,768]{2,1,0:T(8,128)} async-done(((f32[8,64,768]{2,1,0:T(8,128)}), f32[8,32,768]{2,1,0:T(8,128)}) %reduce-scatter.43.cloned.1.call-update) | async-done | bytes 786448 | tf_op jit(solution)/shard_map/reduce_scatter | solution.py:123
  702.7 11.7 all_gather.114
  735.5 16.2 all_gather.117
  779.4 8.8 fusion.39
  788.1 3.9 fusion.134
  792.1 9.0 add_convert_fusion
  805.6 8.8 fusion.36
  814.4 3.9 fusion.136
  818.3 9.1 add_convert_fusion.1
  832.0 7.7 fusion.58
  839.7 6.0 fusion.81
  850.7 7.7 fusion.61
  858.4 6.0 fusion.75
  903.6 41.6 %all-reduce = (f32[768]{0:T(1024)}, f32[768]{0:T(1024)}, f32[768]{0:T(1024)}, f32[768]{0:T(1024)}, f32[768]{0:T(1024)}, /*index=5*/f32[768]{0:T(1024)}) all-reduce(f32[768]{0:T(1024)S(1)} %add.399, f32[768]{0:T(1024)S(1)} %add.400, f32[768]{0:T(1024)S(1)} %add.401, f32[768]{0:T(1024)S(1)} %add.402, ...), channel_id=1, replica_groups=mesh['dp'=16,'mp'=2] {'dp','mp'}, use_global_device_ids=true, to_apply=%region_72.73 | all-reduce | flops 4608 | bytes 36864 | tf_op jit(solution)/shard_map/psum | solution.py:301
  948.2 31.5 %reduce-scatter.53.cloned.1.call-done = bf16[8,288,768]{2,1,0:T(8,128)(2,1)} async-done(((bf16[8,576,768]{2,1,0:T(8,128)(2,1)}), bf16[8,288,768]{2,1,0:T(8,128)(2,1)}) %reduce-scatter.53.cloned.1.call-update) | async-done | bytes 3538960 | tf_op jit(solution)/shard_map/reduce_scatter | solution.py:255
  979.6 9.3 maximum_convert_fusion
  988.9 52.9 %reduce-scatter.67.cloned.1.call-done = f32[384,48]{0,1:T(8,128)} async-done(((f32[384,768]{0,1:T(8,128)}), f32[384,48]{0,1:T(8,128)}) %reduce-scatter.67.cloned.1.call-update) | async-done | bytes 73744 | tf_op jit(solution)/shard_map/reduce_scatter | solution.py:293
  1041.8 61.3 %reduce-scatter.75.cloned.1.call-done = f32[48,384]{1,0:T(8,128)} async-done(((f32[768,384]{1,0:T(8,128)}), f32[48,384]{1,0:T(8,128)}) %reduce-scatter.75.cloned.1.call-update) | async-done | bytes 73744
  1103.1 61.3 %reduce-scatter.65.cloned.1.call-done = f32[48,384]{1,0:T(8,128)} async-done(((f32[768,384]{1,0:T(8,128)}), f32[48,384]{1,0:T(8,128)}) %reduce-scatter.65.cloned.1.call-update) | async-done | bytes 73744 | tf_op jit(solution)/shard_map/reduce_scatter | solution.py:290
  1164.4 61.3 %reduce-scatter.73.cloned.1.call-done = f32[48,384]{1,0:T(8,128)} async-done(((f32[768,384]{1,0:T(8,128)}), f32[48,384]{1,0:T(8,128)}) %reduce-scatter.73.cloned.1.call-update) | async-done | bytes 73744
  1225.7 79.1 %reduce-scatter.71.cloned.1.call-done = f32[1536,48]{0,1:T(8,128)} async-done(((f32[1536,768]{0,1:T(8,128)}), f32[1536,48]{0,1:T(8,128)}) %reduce-scatter.71.cloned.1.call-update) | async-done | bytes 294928 | tf_op jit(solution)/shard_map/reduce_scatter | solution.py:295
  1304.8 79.0 %reduce-scatter.69.cloned.1.call-done = f32[48,1536]{1,0:T(8,128)} async-done(((f32[768,1536]{1,0:T(8,128)}), f32[48,1536]{1,0:T(8,128)}) %reduce-scatter.69.cloned.1.call-update) | async-done | bytes 294928 | tf_op jit(solution)/shard_map/reduce_scatter | solution.py:294
  1383.8 61.7 %reduce-scatter.63.cloned.1.call-done = f32[384,48]{0,1:T(8,128)} async-done(((f32[384,768]{0,1:T(8,128)}), f32[384,48]{0,1:T(8,128)}) %reduce-scatter.63.cloned.1.call-update) | async-done | bytes 73744 | tf_op jit(solution)/shard_map/reduce_scatter | solution.py:289
  1445.5 61.3 %reduce-scatter.59.cloned.1.call-done = f32[48,384]{1,0:T(8,128)} async-done(((f32[768,384]{1,0:T(8,128)}), f32[48,384]{1,0:T(8,128)}) %reduce-scatter.59.cloned.1.call-update) | async-done | bytes 73744 | tf_op jit(solution)/shard_map/reduce_scatter | solution.py:287
  1506.8 61.4 %reduce-scatter.57.cloned.1.call-done = f32[48,384]{1,0:T(8,128)} async-done(((f32[768,384]{1,0:T(8,128)}), f32[48,384]{1,0:T(8,128)}) %reduce-scatter.57.cloned.1.call-update) | async-done | bytes 73744 | tf_op jit(solution)/shard_map/reduce_scatter | solution.py:286
  1568.3 61.2 %reduce-scatter.61.cloned.1.call-done = f32[48,384]{1,0:T(8,128)} async-done(((f32[768,384]{1,0:T(8,128)}), f32[48,384]{1,0:T(8,128)}) %reduce-scatter.61.cloned.1.call-update) | async-done | bytes 73744 | tf_op jit(solution)/shard_map/reduce_scatter | solution.py:288
  (620 shorter events, 242.8 us)
Async XLA Ops:
  8.0 88.6 %copy-start.6 = (bf16[16,32,768]{2,1,0:T(8,128)(2,1)S(1)}, bf16[16,32,768]{2,1,0:T(8,128)(2,1)}, u32[]{:S(2)}) copy-start(bf16[16,32,768]{2,1,0:T(8,128)(2,1)} %param.20) | copy-start | bytes 2359300
  8.0 68.1 %copy-start.174 = (bf16[384,48]{0,1:T(8,128)(2,1)S(1)}, bf16[384,48]{0,1:T(8,128)(2,1)}, u32[]{:S(2)}) copy-start(bf16[384,48]{0,1:T(8,128)(2,1)} %param.26) | copy-start | bytes 110596
  8.0 88.5 %copy-start.145 = (f32[768]{0:T(1024)S(1)}, f32[768]{0:T(1024)}, u32[]{:S(2)}) copy-start(f32[768]{0:T(1024)} %param.33) | copy-start | bytes 9220
  8.1 88.5 %copy-start.187 = (f32[768]{0:T(1024)S(1)}, f32[768]{0:T(1024)}, u32[]{:S(2)}) copy-start(f32[768]{0:T(1024)} %param.34) | copy-start | bytes 9220
  8.1 289.2 %reduce-scatter.35.cloned.1.call-start = ((), (), s32[]{:S(2)}) async-start(), calls=%async_computation.29 | async-start | bytes 2359296 | tf_op jit(solution)/shard_map/reduce_scatter | solution.py:115
  9.5 100.2 %copy-start.128 = (f32[8,32]{1,0:T(8,128)}, f32[8,32]{1,0:T(8,128)S(1)}, u32[]{:S(2)}) copy-start(f32[8,32]{1,0:T(8,128)S(1)} %get-tuple-element.172) | copy-start | bytes 3076
  9.5 100.2 %copy-start.130 = (f32[8,32]{1,0:T(8,128)}, f32[8,32]{1,0:T(8,128)S(1)}, u32[]{:S(2)}) copy-start(f32[8,32]{1,0:T(8,128)S(1)} %get-tuple-element.173) | copy-start | bytes 3076
  11.0 25.2 %copy-start.162 = (f32[8,32]{1,0:T(8,128)}, f32[8,32]{1,0:T(8,128)S(1)}, u32[]{:S(2)}) copy-start(f32[8,32]{1,0:T(8,128)S(1)} %get-tuple-element.101) | copy-start | bytes 3076
  11.0 25.1 %copy-start.164 = (f32[8,32]{1,0:T(8,128)}, f32[8,32]{1,0:T(8,128)S(1)}, u32[]{:S(2)}) copy-start(f32[8,32]{1,0:T(8,128)S(1)} %get-tuple-element.100) | copy-start | bytes 3076
  11.0 86.7 %copy-start.147 = (f32[8,32]{1,0:T(8,128)}, f32[8,32]{1,0:T(8,128)S(1)}, u32[]{:S(2)}) copy-start(f32[8,32]{1,0:T(8,128)S(1)} %fusion.184) | copy-start | bytes 3076
  11.0 86.6 %copy-start.149 = (f32[8,32]{1,0:T(8,128)}, f32[8,32]{1,0:T(8,128)S(1)}, u32[]{:S(2)}) copy-start(f32[8,32]{1,0:T(8,128)S(1)} %fusion.187) | copy-start | bytes 3076
  36.1 108.9 %copy-start.48 = (bf16[768,384]{1,0:T(8,128)(2,1)}, bf16[768,384]{1,0:T(8,128)(2,1)S(1)}, u32[]{:S(2)}) copy-start(bf16[768,384]{1,0:T(8,128)(2,1)S(1)} %all_gather.46) | copy-start | bytes 1769476
  55.5 54.2 %copy-start.50 = (bf16[768,384]{1,0:T(8,128)(2,1)}, bf16[768,384]{1,0:T(8,128)(2,1)S(1)}, u32[]{:S(2)}) copy-start(bf16[768,384]{1,0:T(8,128)(2,1)S(1)} %all_gather.47) | copy-start | bytes 1769476
  76.2 73.0 %copy-start.44 = (bf16[768,384]{1,0:T(8,128)(2,1)}, bf16[768,384]{1,0:T(8,128)(2,1)S(1)}, u32[]{:S(2)}) copy-start(bf16[768,384]{1,0:T(8,128)(2,1)S(1)} %all_gather.45) | copy-start | bytes 1769476
  122.5 21.5 %copy-start.51 = (bf16[768,384]{1,0:T(8,128)(2,1)S(1)}, bf16[768,384]{1,0:T(8,128)(2,1)}, u32[]{:S(2)}) copy-start(bf16[768,384]{1,0:T(8,128)(2,1)} %copy-done.50) | copy-start | bytes 1769476
  125.6 171.7 %reduce-scatter.29.cloned.1.call-start = ((), (), s32[]{:S(2)}) async-start(), calls=%async_computation.24 | async-start | bytes 2359296 | tf_op jit(solution)/shard_map/reduce_scatter | solution.py:115
  158.2 219.0 %reduce-scatter.31.cloned.1.call-start = ((), (), s32[]{:S(2)}) async-start(), calls=%async_computation.25 | async-start | bytes 2359296 | tf_op jit(solution)/shard_map/reduce_scatter | solution.py:115
  251.6 26.6 %copy-start.178 = (bf16[384,48]{0,1:T(8,128)(2,1)S(1)}, bf16[384,48]{0,1:T(8,128)(2,1)}, u32[]{:S(2)}) copy-start(bf16[384,48]{0,1:T(8,128)(2,1)} %param.30) | copy-start | bytes 110596
  278.2 68.1 %copy-start.53 = (bf16[768,384]{1,0:T(8,128)(2,1)}, bf16[768,384]{1,0:T(8,128)(2,1)S(1)}, u32[]{:S(2)}) copy-start(bf16[768,384]{1,0:T(8,128)(2,1)S(1)} %all_gather.51) | copy-start | bytes 1769476
  297.3 63.9 %copy-start.60 = (bf16[384,768]{0,1:T(8,128)(2,1)}, bf16[384,768]{0,1:T(8,128)(2,1)S(1)}, u32[]{:S(2)}) copy-start(bf16[384,768]{0,1:T(8,128)(2,1)S(1)} %all_gather.105) | copy-start | bytes 1769476
  318.4 17.0 %copy-start.21 = (bf16[8,64,384]{1,2,0:T(8,128)(2,1)}, bf16[8,64,384]{1,2,0:T(8,128)(2,1)S(1)}, u32[]{:S(2)}) copy-start(bf16[8,64,384]{1,2,0:T(8,128)(2,1)S(1)} %copy.287) | copy-start | bytes 1179652
  346.3 55.6 %reduce-scatter.37.cloned.1.call-start = ((), (), s32[]{:S(2)}) async-start(), calls=%async_computation.30 | async-start | bytes 2359296 | tf_op jit(solution)/shard_map/reduce_scatter | solution.py:115
  364.2 52.7 %all-gather.3.cloned.1.call-start = ((), (), s32[]{:S(2)}) async-start(), calls=%async_computation.26 | async-start | bytes 2506752 | tf_op jit(solution)/shard_map/all_gather | solution.py:169
  364.8 85.4 %all-gather.5.cloned.1.call-start = ((), (), s32[]{:S(2)}) async-start(), calls=%async_computation.27 | async-start | bytes 2506752 | tf_op jit(solution)/shard_map/all_gather | solution.py:170
  365.4 155.6 %reduce-scatter.47.cloned.1.call-start = ((), (), s32[]{:S(2)}) async-start(), calls=%async_computation.35 | async-start | bytes 2359296 | tf_op jit(solution)/shard_map/reduce_scatter | solution.py:123
  379.1 24.3 %copy-start.170 = (f32[8,32]{1,0:T(8,128)}, f32[8,32]{1,0:T(8,128)S(1)}, u32[]{:S(2)}) copy-start(f32[8,32]{1,0:T(8,128)S(1)} %multiply_reduce_fusion.14) | copy-start | bytes 3076
  459.8 73.0 %reduce-scatter.41.cloned.1.call-start = ((), (), s32[]{:S(2)}) async-start(), calls=%async_computation.32 | async-start | bytes 2359296 | tf_op jit(solution)/shard_map/reduce_scatter | solution.py:123
  478.6 22.7 %copy-start.94 = (bf16[8,64,768]{2,1,0:T(8,128)(2,1)}, bf16[8,64,768]{2,1,0:T(8,128)(2,1)S(1)}, u32[]{:S(2)}) copy-start(bf16[8,64,768]{2,1,0:T(8,128)(2,1)S(1)} %all_gather.112) | copy-start | bytes 2359300
  508.1 53.1 %reduce-scatter.39.cloned.1.call-start = ((), (), s32[]{:S(2)}) async-start(), calls=%async_computation.31 | async-start | bytes 2359296 | tf_op jit(solution)/shard_map/reduce_scatter | solution.py:115
  514.0 18.8 %copy-start.141 = (f32[8,32]{1,0:T(8,128)S(1)}, f32[8,32]{1,0:T(8,128)}, u32[]{:S(2)}) copy-start(f32[8,32]{1,0:T(8,128)} %copy-done.139) | copy-start | bytes 3076
  514.0 18.8 %copy-start.143 = (f32[8,32]{1,0:T(8,128)S(1)}, f32[8,32]{1,0:T(8,128)}, u32[]{:S(2)}) copy-start(f32[8,32]{1,0:T(8,128)} %copy-done.142) | copy-start | bytes 3076
  514.0 18.8 %copy-start.156 = (f32[8,32]{1,0:T(8,128)S(1)}, f32[8,32]{1,0:T(8,128)}, u32[]{:S(2)}) copy-start(f32[8,32]{1,0:T(8,128)} %copy-done.155) | copy-start | bytes 3076
  514.0 18.8 %copy-start.158 = (f32[8,32]{1,0:T(8,128)S(1)}, f32[8,32]{1,0:T(8,128)}, u32[]{:S(2)}) copy-start(f32[8,32]{1,0:T(8,128)} %copy-done.157) | copy-start | bytes 3076
  514.0 18.8 %copy-start.159 = (f32[768]{0:T(1024)S(1)}, f32[768]{0:T(1024)}, u32[]{:S(2)}) copy-start(f32[768]{0:T(1024)} %param.37) | copy-start | bytes 9220
  514.0 75.7 %reduce-scatter.33.cloned.1.call-start = ((), (), s32[]{:S(2)}) async-start(), calls=%async_computation.28 | async-start | bytes 2359296 | tf_op jit(solution)/shard_map/reduce_scatter | solution.py:115
  519.8 149.4 %reduce-scatter.49.cloned.1.call-start = ((), (), s32[]{:S(2)}) async-start(), calls=%async_computation.36 | async-start | bytes 2359296 | tf_op jit(solution)/shard_map/reduce_scatter | solution.py:123
  628.3 66.6 %reduce-scatter.43.cloned.1.call-start = ((), (), s32[]{:S(2)}) async-start(), calls=%async_computation.33 | async-start | bytes 2359296 | tf_op jit(solution)/shard_map/reduce_scatter | solution.py:123
  664.8 30.1 %copy-start.125 = (f32[8,32]{1,0:T(8,128)S(1)}, f32[8,32]{1,0:T(8,128)}, u32[]{:S(2)}) copy-start(f32[8,32]{1,0:T(8,128)} %copy-done.124) | copy-start | bytes 3076
  664.8 30.1 %copy-start.127 = (f32[8,32]{1,0:T(8,128)S(1)}, f32[8,32]{1,0:T(8,128)}, u32[]{:S(2)}) copy-start(f32[8,32]{1,0:T(8,128)} %copy-done.126) | copy-start | bytes 3076
  664.8 30.1 %copy-start.144 = (f32[768]{0:T(1024)S(1)}, f32[768]{0:T(1024)}, u32[]{:S(2)}) copy-start(f32[768]{0:T(1024)} %param.35) | copy-start | bytes 9220
  666.7 30.7 %copy-start.167 = (f32[8,32]{1,0:T(8,128)S(1)}, f32[8,32]{1,0:T(8,128)}, u32[]{:S(2)}) copy-start(f32[8,32]{1,0:T(8,128)} %copy-done.166) | copy-start | bytes 3076
  666.7 30.7 %copy-start.169 = (f32[8,32]{1,0:T(8,128)S(1)}, f32[8,32]{1,0:T(8,128)}, u32[]{:S(2)}) copy-start(f32[8,32]{1,0:T(8,128)} %copy-done.168) | copy-start | bytes 3076
  666.7 30.7 %copy-start.152 = (f32[8,32]{1,0:T(8,128)S(1)}, f32[8,32]{1,0:T(8,128)}, u32[]{:S(2)}) copy-start(f32[8,32]{1,0:T(8,128)} %copy-done.151) | copy-start | bytes 3076
  666.8 30.7 %copy-start.154 = (f32[8,32]{1,0:T(8,128)S(1)}, f32[8,32]{1,0:T(8,128)}, u32[]{:S(2)}) copy-start(f32[8,32]{1,0:T(8,128)} %copy-done.153) | copy-start | bytes 3076
  668.5 230.4 %reduce-scatter.45.cloned.1.call-start = ((), (), s32[]{:S(2)}) async-start(), calls=%async_computation.34 | async-start | bytes 2359296 | tf_op jit(solution)/shard_map/reduce_scatter | solution.py:123
  669.2 30.7 %copy-start.27 = (bf16[16,32,768]{2,1,0:T(8,128)(2,1)S(1)}, bf16[16,32,768]{2,1,0:T(8,128)(2,1)}, u32[]{:S(2)}) copy-start(bf16[16,32,768]{2,1,0:T(8,128)(2,1)} %param.39) | copy-start | bytes 2359300
  732.6 19.9 %copy-start.59 = (bf16[384,768]{0,1:T(8,128)(2,1)S(1)}, bf16[384,768]{0,1:T(8,128)(2,1)}, u32[]{:S(2)}) copy-start(bf16[384,768]{0,1:T(8,128)(2,1)} %all_gather.48) | copy-start | bytes 1769476
  734.7 20.5 %copy-start.3 = (f32[8,6,64,64]{2,3,1,0:T(8,128)S(1)}, f32[8,6,64,64]{2,3,1,0:T(8,128)}, u32[]{:S(2)}) copy-start(f32[8,6,64,64]{2,3,1,0:T(8,128)} %copy-done.2) | copy-start | bytes 2359300
  734.8 164.2 %reduce-scatter.51.cloned.1.call-start = ((), (), s32[]{:S(2)}) async-start(), calls=%async_computation.37 | async-start | bytes 2359296 | tf_op jit(solution)/shard_map/reduce_scatter | solution.py:123
  775.5 172.7 %reduce-scatter.55.cloned.1.call-start = ((), (), s32[]{:S(2)}) async-start(), calls=%async_computation.39 | async-start | bytes 10616832 | tf_op jit(solution)/shard_map/reduce_scatter | solution.py:255
  801.2 178.5 %reduce-scatter.53.cloned.1.call-start = ((), (), s32[]{:S(2)}) async-start(), calls=%async_computation.38 | async-start | bytes 10616832 | tf_op jit(solution)/shard_map/reduce_scatter | solution.py:255
  827.4 214.4 %reduce-scatter.67.cloned.1.call-start = ((), (), s32[]{:S(2)}) async-start(), calls=%async_computation.45 | async-start | bytes 1253376 | tf_op jit(solution)/shard_map/reduce_scatter | solution.py:293
  832.0 271.2 %reduce-scatter.75.cloned.1.call-start = ((), (), s32[]{:S(2)}) async-start(), calls=%async_computation.49 | async-start | bytes 1253376
  847.2 317.2 %reduce-scatter.65.cloned.1.call-start = ((), (), s32[]{:S(2)}) async-start(), calls=%async_computation.44 | async-start | bytes 1253376 | tf_op jit(solution)/shard_map/reduce_scatter | solution.py:290
  850.7 375.0 %reduce-scatter.73.cloned.1.call-start = ((), (), s32[]{:S(2)}) async-start(), calls=%async_computation.48 | async-start | bytes 1253376
  865.9 438.9 %reduce-scatter.71.cloned.1.call-start = ((), (), s32[]{:S(2)}) async-start(), calls=%async_computation.47 | async-start | bytes 5013504 | tf_op jit(solution)/shard_map/reduce_scatter | solution.py:295
  874.1 509.7 %reduce-scatter.69.cloned.1.call-start = ((), (), s32[]{:S(2)}) async-start(), calls=%async_computation.46 | async-start | bytes 5013504 | tf_op jit(solution)/shard_map/reduce_scatter | solution.py:294
  881.7 563.8 %reduce-scatter.63.cloned.1.call-start = ((), (), s32[]{:S(2)}) async-start(), calls=%async_computation.43 | async-start | bytes 1253376 | tf_op jit(solution)/shard_map/reduce_scatter | solution.py:289
  887.4 619.4 %reduce-scatter.59.cloned.1.call-start = ((), (), s32[]{:S(2)}) async-start(), calls=%async_computation.41 | async-start | bytes 1253376 | tf_op jit(solution)/shard_map/reduce_scatter | solution.py:287
  890.3 677.9 %reduce-scatter.57.cloned.1.call-start = ((), (), s32[]{:S(2)}) async-start(), calls=%async_computation.40 | async-start | bytes 1253376 | tf_op jit(solution)/shard_map/reduce_scatter | solution.py:286
  894.3 735.2 %reduce-scatter.61.cloned.1.call-start = ((), (), s32[]{:S(2)}) async-start(), calls=%async_computation.42 | async-start | bytes 1253376 | tf_op jit(solution)/shard_map/reduce_scatter | solution.py:288
  898.9 46.3 %copy-start.67 = (f32[8,32,768]{2,1,0:T(8,128)S(1)}, f32[8,32,768]{2,1,0:T(8,128)}, u32[]{:S(2)}) copy-start(f32[8,32,768]{2,1,0:T(8,128)} %get-tuple-element.113) | copy-start | bytes 2359300
  898.9 46.3 %copy-start.32 = (f32[8,32,768]{2,1,0:T(8,128)S(1)}, f32[8,32,768]{2,1,0:T(8,128)}, u32[]{:S(2)}) copy-start(f32[8,32,768]{2,1,0:T(8,128)} %reduce-scatter.45.cloned.1.call-done) | copy-start | bytes 2359300
  899.0 46.2 %copy-start.33 = (f32[8,32,768]{2,1,0:T(8,128)S(1)}, f32[8,32,768]{2,1,0:T(8,128)}, u32[]{:S(2)}) copy-start(f32[8,32,768]{2,1,0:T(8,128)} %reduce-scatter.51.cloned.1.call-done) | copy-start | bytes 2359300
  (162 other events, 744.8 us)
Sparse Core Ops, SparseCore 0:
  125.7 29.2 reduce-scatter.34
  158.3 25.6 reduce-scatter.28
  346.4 23.8 reduce-scatter.30
  372.4 29.4 reduce-scatter.36
  459.9 37.5 reduce-scatter.46
  508.3 24.5 reduce-scatter.40
  535.0 26.1 reduce-scatter.38
  563.5 26.1 reduce-scatter.32
  628.4 30.3 reduce-scatter.48
  668.7 26.1 reduce-scatter.42
  734.9 29.4 reduce-scatter.44
  775.6 26.1 reduce-scatter.50
  804.1 85.6 reduce-scatter.54
  892.5 87.0 reduce-scatter.52
  983.7 58.0 reduce-scatter.66
  1045.9 57.2 reduce-scatter.74
  1107.2 57.1 reduce-scatter.64
  1168.5 57.1 reduce-scatter.72
  1230.1 74.5 reduce-scatter.70
  1309.0 74.7 reduce-scatter.68
  1388.0 57.4 reduce-scatter.62
  1449.7 57.1 reduce-scatter.58
  1511.0 57.1 reduce-scatter.56
  1572.3 57.1 reduce-scatter.60
Sparse Core Ops, SparseCore 1:
  367.0 40.0 all-gather.2
  409.2 40.9 all-gather.4
where the time goes:
time: 1650 us; the launch traced here: 1640 us
  waiting for transfers between devices  816 us (49%)
  blocking collectives  379 us (23%)
  matrix products  267 us (16%)
  local copies, waits for them, and re-layouts  94.8 us (6%)
  other arithmetic  58.6 us (4%)
  between operations  18.8 us (1%)
    unnamed x28, waiting for transfers between devices  124 us
    all_gather x6, blocking collectives, gather_grads(): return lax.all_gather(grad_rows, 'mp', axis=1, tiled=True)  86.2 us
    all_gather x6, blocking collectives, gather_rows(): return lax.all_gather(normed, 'mp', axis=1, tiled=True)  86 us
    reduce_scatter x1, waiting for transfers between devices, body(): lax.psum_scatter(grad_contract, 'dp', scatter_dimension=1, tiled=True)  79.1 us
    reduce_scatter x1, waiting for transfers between devices, body(): lax.psum_scatter(grad_expand, 'dp', scatter_dimension=0, tiled=True)  79 us
    dot_general x20, matrix products, matmul(): jnp.einsum('...d,de->...e', left, right, preferred_element_type=jnp.float32)  77 us
    reduce_scatter x6, waiting for transfers between devices, sum_rows(): return lax.psum_scatter(partial_rows, 'mp', scatter_dimension=1, tiled=True)  77 us
    reduce_scatter x1, waiting for transfers between devices, body(): lax.psum_scatter(grad_mix_self, 'dp', scatter_dimension=1, tiled=True)  61.7 us
  transfers between devices with their start and end apart: 26, of which 17 were waited for; matrix products, arithmetic and copies ran while one was open for 18% of the time, Pallas kernels for 0%

commit v1 on v0

v1 whole, which is shorter than its diff:
```python
import jax
import jax.numpy as jnp
from jax import lax
from jax.sharding import PartitionSpec as P

HD = 64
LEN = 64
PATCH = 576
SMALLP = 196
BOTH = ("dp", "mp")

epsilon = 1e-05
masked_score = -1000000000.0
bf16 = jnp.bfloat16
f32 = jnp.float32


def dot(left, right, left_dim, right_dim):
    return lax.dot_general(left, right, (((left_dim,), (right_dim,)), ((), ())), preferred_element_type=f32)


def matmul(left, right):
    return dot(left, right, 1, 0)


def matmul_t(left, right):
    return dot(left, right, 1, 1)


def weight_grad(left, right):
    return dot(left, right, 0, 0)


def norm_stats(value):
    average = jnp.mean(value, axis=-1, keepdims=True)
    centred = value - average
    spread = jnp.mean(centred * centred, axis=-1, keepdims=True)
    inverse = lax.rsqrt(spread + epsilon)
    return centred * inverse, inverse


def norm_back(normal, inverse, gain, grad):
    scaled = grad * gain
    mean_one = jnp.mean(scaled, axis=-1, keepdims=True)
    mean_two = jnp.mean(scaled * normal, axis=-1, keepdims=True)
    grad_value = (scaled - mean_one - normal * mean_two) * inverse
    return grad_value, jnp.sum(grad * normal, axis=0), jnp.sum(grad, axis=0)


def heads(rows, count):
    return rows.reshape(count, rows.shape[0] // count, rows.shape[1] // HD, HD)


def attend(queries, keys, values, allowed, count):
    scores = jnp.einsum("clhd,ckhd->chlk", heads(queries, count), heads(keys, count), preferred_element_type=f32) * HD ** (-0.5)
    scores = jnp.where(allowed, scores, masked_score)
    highest = jnp.max(scores, axis=-1, keepdims=True)
    exponent = jnp.exp(scores - highest)
    probs = exponent / jnp.sum(exponent, axis=-1, keepdims=True)
    mixed = jnp.einsum("chlk,ckhd->clhd", probs.astype(bf16), heads(values, count), preferred_element_type=f32)
    return mixed.reshape(queries.shape).astype(bf16), probs


def attend_back(queries, keys, values, probs, grad_mix, count):
    scale = HD ** (-0.5)
    mix_heads = heads(grad_mix, count)
    grad_prob = jnp.einsum("clhd,ckhd->chlk", mix_heads, heads(values, count), preferred_element_type=f32)
    grad_values = jnp.einsum("chlk,clhd->ckhd", probs.astype(bf16), mix_heads, preferred_element_type=f32)
    inner = jnp.sum(probs * grad_prob, axis=-1, keepdims=True)
    grad_score = (probs * (grad_prob - inner)).astype(bf16)
    grad_queries = jnp.einsum("chlk,ckhd->clhd", grad_score, heads(keys, count), preferred_element_type=f32) * scale
    grad_keys = jnp.einsum("chlk,clhd->ckhd", grad_score, heads(queries, count), preferred_element_type=f32) * scale
    return (
        grad_queries.reshape(queries.shape).astype(bf16),
        grad_keys.reshape(keys.shape).astype(bf16),
        grad_values.reshape(keys.shape).astype(bf16),
    )


def gelu_parts(value):
    inner = 0.7978845608028654 * (value + 0.044715 * value * value * value)
    bent = jnp.tanh(inner)
    hidden = 0.5 * value * (1.0 + bent)
    slope = 0.5 * (1.0 + bent) + 0.5 * value * (1.0 - bent * bent) * 0.7978845608028654 * (1.0 + 3 * 0.044715 * value * value)
    return hidden, slope


def layer(weights, norms, text, cotangent, patches, resolution):
    count = text.shape[0] // LEN
    query_self, key_self, value_self, mix_self, query_cross, key_cross, value_cross, mix_cross = (weights[i] for i in range(8))
    first_gain, first_shift, second_gain, second_shift, third_gain, third_shift = norms
    causal = (jnp.arange(LEN)[:, None] >= jnp.arange(LEN)[None, :])[None, None]
    valid = SMALLP + (PATCH - SMALLP) * resolution
    visible = (jnp.arange(PATCH)[None, :] < valid[:, None])[:, None, None, :]
    stream = text.astype(f32)
    normal_one, inverse_one = norm_stats(stream)
    normed_one = (normal_one * first_gain + first_shift).astype(bf16)
    queries_one = matmul(normed_one, query_self).astype(bf16)
    keys_one = matmul(normed_one, key_self).astype(bf16)
    values_one = matmul(normed_one, value_self).astype(bf16)
    mixed_one, probs_one = attend(queries_one, keys_one, values_one, causal, count)
    stream_one = stream + matmul_t(mixed_one, mix_self)
    normal_two, inverse_two = norm_stats(stream_one)
    normed_two = (normal_two * second_gain + second_shift).astype(bf16)
    queries_two = matmul(normed_two, query_cross).astype(bf16)
    keys_two = matmul(patches, key_cross).astype(bf16)
    values_two = matmul(patches, value_cross).astype(bf16)
    mixed_two, probs_two = attend(queries_two, keys_two, values_two, visible, count)
    stream_two = stream_one + matmul_t(mixed_two, mix_cross)
    normal_three, inverse_three = norm_stats(stream_two)
    normed_three = (normal_three * third_gain + third_shift).astype(bf16)
    layer_out = stream_two
    grad_normed = 0.0
    grads = [None] * 16
    chunks = (weights.shape[0] - 8) // 2
    for j in range(chunks):
        expand, contract = weights[8 + j], weights[8 + chunks + j]
        hidden, slope = gelu_parts(matmul(normed_three, expand))
        hidden = hidden.astype(bf16)
        layer_out = layer_out + matmul_t(hidden, contract)
        grads[8 + chunks + j] = weight_grad(cotangent, hidden)
        grad_pre = (slope * matmul(cotangent, contract)).astype(bf16)
        grads[8 + j] = weight_grad(normed_three, grad_pre)
        grad_normed = grad_normed + matmul_t(grad_pre, expand)
    grad_input, gain_three, shift_three = norm_back(normal_three, inverse_three, third_gain, grad_normed)
    grad_stream = cotangent.astype(f32) + grad_input
    grad_rows = grad_stream.astype(bf16)
    grads[7] = weight_grad(grad_rows, mixed_two)
    grad_mixed = matmul(grad_rows, mix_cross).astype(bf16)
    grad_queries, grad_keys, grad_values = attend_back(queries_two, keys_two, values_two, probs_two, grad_mixed, count)
    grads[4] = weight_grad(normed_two, grad_queries)
    grads[5] = weight_grad(patches, grad_keys)
    grads[6] = weight_grad(patches, grad_values)
    patch_grad = (matmul_t(grad_keys, key_cross) + matmul_t(grad_values, value_cross)).astype(bf16)
    grad_normed = matmul_t(grad_queries, query_cross)
    grad_input, gain_two, shift_two = norm_back(normal_two, inverse_two, second_gain, grad_normed)
    grad_stream = grad_stream + grad_input
    grad_rows = grad_stream.astype(bf16)
    grads[3] = weight_grad(grad_rows, mixed_one)
    grad_mixed = matmul(grad_rows, mix_self).astype(bf16)
    grad_queries, grad_keys, grad_values = attend_back(queries_one, keys_one, values_one, probs_one, grad_mixed, count)
    grads[0] = weight_grad(normed_one, grad_queries)
    grads[1] = weight_grad(normed_one, grad_keys)
    grads[2] = weight_grad(normed_one, grad_values)
    grad_normed = matmul_t(grad_queries, query_self) + matmul_t(grad_keys, key_self) + matmul_t(grad_values, value_self)
    grad_input, gain_one, shift_one = norm_back(normal_one, inverse_one, first_gain, grad_normed)
    text_grad = (grad_stream + grad_input).astype(bf16)
    grads = jnp.stack([g.astype(bf16) for g in grads])
    norm_grads = jnp.stack([gain_one, shift_one, gain_two, shift_two, gain_three, shift_three])
    return layer_out.astype(bf16), text_grad, patch_grad, grads, norm_grads


def swap(rows):
    return lax.ppermute(rows, "mp", [(0, 1), (1, 0)])


def to_captions(rows, side):
    half = rows.shape[0] // 2
    mine = lax.dynamic_slice_in_dim(rows, side * half, half, 0)
    other = swap(lax.dynamic_slice_in_dim(rows, (1 - side) * half, half, 0))
    low = jnp.where(side == 0, mine, other)
    high = jnp.where(side == 0, other, mine)
    return jnp.concatenate([low, high], axis=1)


def to_positions(rows, side):
    length = rows.shape[1] // 2
    mine = lax.dynamic_slice_in_dim(rows, side * length, length, 1)
    other = swap(lax.dynamic_slice_in_dim(rows, (1 - side) * length, length, 1))
    low = jnp.where(side == 0, mine, other)
    high = jnp.where(side == 0, other, mine)
    return jnp.concatenate([low, high], axis=0)


def pack(shards):
    narrow = shards[0].shape[1]
    parts = []
    for shard, turned in zip(shards, TURNED):
        flat = shard.T if turned else shard
        for j in range(flat.shape[1] // narrow):
            parts.append(flat[:, j * narrow : (j + 1) * narrow])
    return jnp.stack(parts)


def unpack(packed):
    chunks = (packed.shape[0] - 8) // 2
    groups = [[packed[i]] for i in range(8)]
    groups.append([packed[8 + j] for j in range(chunks)])
    groups.append([packed[8 + chunks + j] for j in range(chunks)])
    outs = []
    for group, turned in zip(groups, TURNED):
        flat = group[0] if len(group) == 1 else jnp.concatenate(group, axis=1)
        outs.append(flat.T if turned else flat)
    return tuple(outs)


TURNED = (False, False, False, True, False, False, False, True, False, True)


def gather_weights(packed):
    full = lax.all_gather(packed, "dp", axis=1, tiled=True)
    return lax.all_gather(full, "mp", axis=2, tiled=True)


def scatter_grads(grads):
    half = lax.psum_scatter(grads, "mp", scatter_dimension=2, tiled=True)
    return lax.psum_scatter(half, "dp", scatter_dimension=1, tiled=True).astype(f32)


def body(text_tokens, image_tokens, resolution, *rest):
    shards, norms, cotangent = rest[:10], rest[10:16], rest[16]
    side = lax.axis_index("mp")
    half = text_tokens.shape[0] // 2
    width = text_tokens.shape[2]
    weights = gather_weights(pack(shards))
    text = to_captions(text_tokens, side)
    grad_out = to_captions(cotangent, side)
    patches = lax.dynamic_slice_in_dim(image_tokens, side * half, half, 0)
    flags = lax.dynamic_slice_in_dim(resolution, side * half, half, 0)
    layer_out, text_grad, patch_grad, grads, norm_grads = layer(
        weights, norms, text.reshape(-1, width), grad_out.reshape(-1, width), patches.reshape(-1, width), flags
    )
    weight_outs = unpack(scatter_grads(grads))
    norm_outs = lax.psum(norm_grads, BOTH)
    return (
        to_positions(layer_out.reshape(half, LEN, width), side),
        to_positions(text_grad.reshape(half, LEN, width), side).astype(f32),
        to_positions(patch_grad.reshape(half, PATCH, width), side).astype(f32),
        *weight_outs,
        *(norm_outs[i] for i in range(6)),
    )


def solution(mesh):
    tokens = P("dp", "mp", None)
    rows, columns = P("dp", "mp"), P("mp", "dp")
    kinds = (rows, rows, rows, columns, rows, rows, rows, columns, rows, columns)
    in_specs = (tokens, P("dp", None, None), P("dp"), *kinds, *([P()] * 6), tokens)
    out_specs = (tokens, tokens, tokens, *kinds, *([P()] * 6))
    return jax.shard_map(body, mesh=mesh, in_specs=in_specs, out_specs=out_specs, check_vma=False)
```

time: 1650 us -> 1200 us (0.73)
  waiting for transfers between devices: 816 us -> 504 us
  blocking collectives: 379 us -> 108 us
  local copies, waits for them, and re-layouts: 94.8 us -> 268 us
  matrix products: 267 us -> 237 us
    reduce_scatter x22 -> x1, waiting for transfers between devices: 664 us -> 0.01 us  [scatter_grads(): lax.psum_scatter(half, 'dp', scatter_dimension=1, tiled=True).astype(f32)]
    all_gather x20 -> x0, blocking collectives: 338 us -> none  [the longest x6 86.2 us: gather_grads(): return lax.all_gather(grad_rows, 'mp', axis=1, tiled=True)]
    all_gather x2, waiting for transfers between devices: 28.4 us -> 284 us  [the longest x1 201 us: gather_weights(): return lax.all_gather(full, 'mp', axis=2, tiled=True)]
    unnamed x28 -> x5, waiting for transfers between devices: 124 us -> 212 us
    psum x1, blocking collectives: 41.6 us -> 108 us  [body(): norm_outs = lax.psum(norm_grads, BOTH)]
    unnamed x402 -> x193, local copies, waits for them, and re-layouts: 32 us -> 93.4 us
    convert_element_type x16 -> x18, local copies, waits for them, and re-layouts: 45.2 us -> 102 us  [the longest x4 31.8 us: attend_back(): grad_values.reshape(keys.shape).astype(bf16)]
    reshape x12 -> x13, local copies, waits for them, and re-layouts: 16.7 us -> 59.2 us  [heads(): return rows.reshape(count, rows.shape[0] // count, rows.shape[1] // HD, HD)]
  transfers between devices with their start and end apart: 26 -> 9, of which waited for: 17 -> 5; matrix products, arithmetic and copies ran while one was open for 18% -> 6% of each run, Pallas kernels for 0% -> 0%
where the time goes in v1:
time: 1200 us; the launch traced here: 1190 us
  waiting for transfers between devices  504 us (42%)
  local copies, waits for them, and re-layouts  268 us (22%)
  matrix products  237 us (20%)
  blocking collectives  108 us (9%)
  other arithmetic  55 us (5%)
  between operations  15.2 us (1%)
    unnamed x5, waiting for transfers between devices  212 us
    all_gather x1, waiting for transfers between devices, gather_weights(): return lax.all_gather(full, 'mp', axis=2, tiled=True)  201 us
    dot_general x48, matrix products, dot(): lax.dot_general(left, right, (((left_dim,), (right_dim,)), ((), ())), pre...  164 us
    psum x1, blocking collectives, body(): norm_outs = lax.psum(norm_grads, BOTH)  108 us
    unnamed x193, local copies, waits for them, and re-layouts  93.4 us
    all_gather x1, waiting for transfers between devices, gather_weights(): full = lax.all_gather(packed, 'dp', axis=1, tiled=True)  83.5 us
    reshape x13, local copies, waits for them, and re-layouts, heads(): return rows.reshape(count, rows.shape[0] // count, rows.shape[1] // HD, HD)  59.2 us
    convert_element_type x4, local copies, waits for them, and re-layouts, attend_back(): grad_values.reshape(keys.shape).astype(bf16)  31.8 us
  transfers between devices with their start and end apart: 9, of which 5 were waited for; matrix products, arithmetic and copies ran while one was open for 6% of the time, Pallas kernels for 0%

profile of v1, /device:TPU:0, one launch (start us, length us, event | category | flops | bytes accessed | tf_op | source)
XLA Modules:
  0.0 1191.8 jit_solution(10258114510335042485)
XLA Ops:
  20.6 83.5 %all-gather.3.cloned.1.call-done = bf16[16,768,384]{2,1,0:T(8,128)(2,1)} async-done(((bf16[16,48,384]{2,1,0:T(8,128)(2,1)}), bf16[16,768,384]{2,1,0:T(8,128)(2,1)}) %all-gather.3.cloned.1.call-update) | async-done | bytes 9437200 | tf_op jit(solution)/shard_map/all_gather | solution.py:201
  107.6 8.8 constant_dynamic-slice_fusion.4
  118.6 6.4 collective-permute-done.2
  127.6 200.9 %all-gather.5.cloned.1.call-done = bf16[16,768,768]{2,1,0:T(8,128)(2,1)} async-done(((bf16[16,768,384]{2,1,0:T(8,128)(2,1)}), bf16[16,768,768]{2,1,0:T(8,128)(2,1)}) %all-gather.5.cloned.1.call-update) | async-done | bytes 18874384 | tf_op jit(solution)/shard_map/all_gather | solution.py:202
  333.1 2.9 convolution_convert_fusion.24
  336.0 2.7 reshape.721
  338.7 2.9 copy.129
  341.6 2.9 convolution_convert_fusion.23
  344.6 2.7 reshape.722
  347.3 2.9 copy.125
  350.2 3.3 fusion.141
  360.4 10.0 convolution_convert_fusion.1
  370.4 10.4 copy.109
  380.8 13.8 %reshape.702 = bf16[8,576,12,64]{1,0,3,2:T(8,128)(2,1)} reshape(bf16[4608,768]{0,1:T(8,128)(2,1)} %copy.109) | data formatting | bytes 14155776 | tf_op jit(solution)/shard_map/reshape | solution.py:51
  402.0 3.5 copy.136
  405.5 10.5 convolution_convert_fusion
  416.1 10.4 copy.111
  426.4 13.4 %reshape.704 = bf16[8,576,12,64]{1,0,3,2:T(8,128)(2,1)} reshape(bf16[4608,768]{0,1:T(8,128)(2,1)} %copy.111) | data formatting | bytes 14155776 | tf_op jit(solution)/shard_map/reshape | solution.py:51
  439.8 10.9 fusion.12
  450.8 18.2 %fusion.143 = (f32[8,12,64]{2,1,0:T(8,128)S(1)}, f32[8,12,64,576]{3,2,1,0:T(8,128)}) fusion(f32[8,12,64,576]{3,2,1,0:T(8,128)} %fusion.12, pred[8,576]{1,0:T(8,128)(4,1)S(1)} %iota_compare_fusion.1), kind=kOutput, calls=%fused_computation.306 | output fusion | flops 21234240 | bytes 28340736 | tf_op jit(solution)/shard_map/sub | solution.py:58
  469.0 9.8 fusion.73
  481.2 2.9 convert_element_type.314
  495.3 2.6 fusion.125
  498.0 3.2 fusion.50
  501.2 2.9 fusion.45
  506.6 2.7 fusion.35
  512.3 2.7 fusion.40
  517.9 3.3 multiply_reduce_fusion.2
  526.5 2.9 copy.138
  529.5 14.0 %multiply_reduce_fusion = (f32[8,12,64]{2,1,0:T(8,128)S(1)}, f32[8,12,64,576]{3,2,1,0:T(8,128)}) fusion(f32[8,12,64,576]{3,2,1,0:T(8,128)} %get-tuple-element.68, f32[8,12,64]{2,1,0:T(8,128)S(1)} %get-tuple-element.67, bf16[8,64,12,64]{1,3,2,0:T(8,128)(2,1)} %copy.138, bf16[8,576,12,64]{1,0,3,2:T(8,128)(2,1)} %reshape.702), kind=kOutput, calls=%fused_computation.4 | convolution fusion | flops 463595520 | bytes 36225024 | tf_op jit(solution)/shard_map/clhd,ckhd->chlk/dot_general | solution.py:67
  543.5 10.9 multiply_convert_fusion.1
  554.5 3.2 copy-done.2
  557.7 7.0 fusion.51
  568.4 3.6 multiply_reduce_fusion.3
  572.6 2.9 convolution_convert_fusion.20
  575.5 4.1 reshape.725
  579.7 4.2 copy.133
  583.9 4.6 fusion.79
  595.0 4.4 fusion.14
  599.4 11.3 convert_bitcast_fusion
  610.7 3.8 copy.135
  614.5 3.4 convert_element_type.343
  618.0 2.8 copy.128
  620.8 3.6 convert_element_type.337
  624.4 2.8 copy.132
  627.1 3.4 convert_element_type.340
  630.6 11.7 copy.137
  642.3 13.0 %convert_element_type.348 = bf16[4608,768]{0,1:T(8,128)(2,1)} reshape(bf16[8,576,12,64]{1,0,3,2:T(8,128)(2,1)} %copy.137) | data formatting | bytes 14155776 | tf_op jit(solution)/shard_map/convert_element_type | solution.py:75
  655.3 11.8 copy.139
  667.1 12.8 %convert_element_type.351 = bf16[4608,768]{0,1:T(8,128)(2,1)} reshape(bf16[8,576,12,64]{1,0,3,2:T(8,128)(2,1)} %copy.139) | data formatting | bytes 14155776 | tf_op jit(solution)/shard_map/convert_element_type | solution.py:76
  679.9 3.4 fusion.87
  691.1 11.5 fusion.83
  702.7 6.7 fusion.85
  726.7 24.8 %copy.147 = bf16[16,768,768]{1,0,2:T(8,128)(2,1)} copy(bf16[16,768,768]{2,1,0:T(8,128)(2,1)} %fusion.113) | data formatting | bytes 37748736
  751.5 18.6 %copy.161 = bf16[96,8,16,768]{3,1,2,0:T(8,128)(2,1)} copy(bf16[96,8,16,768]{3,2,1,0:T(8,128)(2,1)} %bitcast.377) | data formatting | bytes 37748736
  770.2 211.8 %reduce-scatter.7.cloned.1.call-done = bf16[384,12288]{1,0:T(8,128)(2,1)} async-done(((bf16[768,12288]{1,0:T(8,128)(2,1)}), bf16[384,12288]{1,0:T(8,128)(2,1)}) %reduce-scatter.7.cloned.1.call-update) | async-done | bytes 9437200
  982.1 10.4 copy.162
  992.5 13.3 %copy.148 = bf16[16,768,384]{2,1,0:T(8,128)(2,1)} copy(bf16[16,768,384]{1,0,2:T(8,128)(2,1)} %bitcast.380) | data formatting | bytes 18874368
  1006.7 11.8 fusion.120
  1018.4 13.0 %add_convert_fusion = bf16[4608,768]{1,0:T(8,128)(2,1)S(1)} fusion(f32[4608,768]{1,0:T(8,128)} %fusion.120, bf16[4608,768]{0,1:T(8,128)(2,1)} %convert_element_type.351, bf16[16,768,768]{2,1,0:T(8,128)(2,1)} %all-gather.5.cloned.1.call-done), kind=kOutput, calls=%fused_computation.7 | convolution fusion | flops 5442895872 | bytes 29491200 | tf_op jit(solution)/shard_map/dot_general | solution.py:19
  1040.4 2.8 fusion.67
  1056.8 107.9 %psum.7 = f32[6,768]{1,0:T(8,128)S(1)} all-reduce(f32[6,768]{1,0:T(8,128)S(1)} %stack.163), channel_id=1, replica_groups=mesh['dp'=16,'mp'=2] {'dp','mp'}, use_global_device_ids=true, to_apply=%region_26.27 | all-reduce | flops 4608 | bytes 36864 | tf_op jit(solution)/shard_map/psum | solution.py:224
  1167.9 6.0 broadcast_select_fusion.1
  1173.9 8.2 maximum_convert_fusion
  (302 shorter events, 132.5 us)
Async XLA Ops:
  7.2 96.9 %all-gather.3.cloned.1.call-start = ((), (), s32[]{:S(2)}) async-start(), calls=%async_computation.2 | async-start | bytes 10027008 | tf_op jit(solution)/shard_map/all_gather | solution.py:201
  20.5 308.1 %all-gather.5.cloned.1.call-start = ((), (), s32[]{:S(2)}) async-start(), calls=%async_computation.3 | async-start | bytes 28311552 | tf_op jit(solution)/shard_map/all_gather | solution.py:202
  104.1 2.7 copy-start.37
  104.1 3.3 copy-start.65
  104.1 877.9 %reduce-scatter.7.cloned.1.call-start = ((), (), s32[]{:S(2)}) async-start(), calls=%async_computation.5 | async-start | bytes 28311552
  105.3 12.1 %collective-permute-start = (bf16[8,32,768]{2,1,0:T(8,128)(2,1)S(1)}, bf16[8,32,768]{2,1,0:T(8,128)(2,1)S(1)}, u32[]{:S(2)}, u32[]{:S(2)}) collective-permute-start(bf16[8,32,768]{2,1,0:T(8,128)(2,1)S(1)} %constant_dynamic-slice_fusion.5), channel_id=1, source_target_pairs={{0,1},{1,0},{2,3},{3,2},{4,5},{5,4},{6,7},{7,6},{8,9},{9,8},{10,11... | collective-permute-start | bytes 1179656 | tf_op jit(solution)/shard_map/ppermute | solution.py:154
  106.8 18.2 %collective-permute-start.2 = (bf16[8,32,768]{2,1,0:T(8,128)(2,1)S(1)}, bf16[8,32,768]{2,1,0:T(8,128)(2,1)S(1)}, u32[]{:S(2)}, u32[]{:S(2)}) collective-permute-start(bf16[8,32,768]{2,1,0:T(8,128)(2,1)S(1)} %constant_dynamic-slice_fusion.2), channel_id=1, source_target_pairs={{0,1},{1,0},{2,3},{3,2},{4,5},{5,4},{6,7},{7,6},{8,9},{9,8},{10,11... | collective-permute-start | bytes 1179656 | tf_op jit(solution)/shard_map/ppermute | solution.py:154
  117.4 9.1 copy-start.11
  117.4 9.1 copy-start.13
  127.6 214.0 %copy-start.33 = (bf16[8,64,768]{2,1,0:T(8,128)(2,1)}, bf16[8,64,768]{2,1,0:T(8,128)(2,1)S(1)}, u32[]{:S(2)}) copy-start(bf16[8,64,768]{2,1,0:T(8,128)(2,1)S(1)} %fusion.57) | copy-start | bytes 2359300
  353.5 4.0 copy-start.47
  380.8 13.8 %copy-start.22 = (bf16[512,768]{0,1:T(8,128)(2,1)S(1)}, bf16[512,768]{0,1:T(8,128)(2,1)}, u32[]{:S(2)}) copy-start(bf16[512,768]{0,1:T(8,128)(2,1)} %convert_element_type.306) | copy-start | bytes 2359300
  380.8 13.8 %copy-start.35 = (bf16[8,64,768]{2,1,0:T(8,128)(2,1)S(1)}, bf16[8,64,768]{2,1,0:T(8,128)(2,1)}, u32[]{:S(2)}) copy-start(bf16[8,64,768]{2,1,0:T(8,128)(2,1)} %pad_maximum_fusion) | copy-start | bytes 2359300
  396.8 87.3 %copy-start.7 = (f32[512,768]{1,0:T(8,128)}, f32[512,768]{1,0:T(8,128)S(1)}, u32[]{:S(2)}) copy-start(f32[512,768]{1,0:T(8,128)S(1)} %get-tuple-element.66) | copy-start | bytes 4718596
  405.5 34.3 %copy-start.3 = (bf16[8,64,12,64]{1,3,2,0:T(8,128)(2,1)}, bf16[8,64,12,64]{1,3,2,0:T(8,128)(2,1)S(1)}, u32[]{:S(2)}) copy-start(bf16[8,64,12,64]{1,3,2,0:T(8,128)(2,1)S(1)} %copy.136) | copy-start | bytes 2359300
  484.1 2.5 copy-start.16
  486.6 34.6 %copy-start = (f32[512,768]{1,0:T(8,128)}, f32[512,768]{1,0:T(8,128)S(1)}, u32[]{:S(2)}) copy-start(f32[512,768]{1,0:T(8,128)S(1)} %get-tuple-element.70) | copy-start | bytes 4718596
  487.7 7.6 copy-start.38
  490.0 8.0 copy-start.27
  492.7 8.6 copy-start.69
  495.3 11.2 copy-start.66
  495.3 2.7 copy-start.20
  498.0 14.3 %copy-start.72 = (f32[512,768]{1,0:T(8,128)}, f32[512,768]{1,0:T(8,128)S(1)}, u32[]{:S(2)}) copy-start(f32[512,768]{1,0:T(8,128)S(1)} %fusion.125) | copy-start | bytes 4718596
  501.2 16.6 %copy-start.31 = (bf16[512,768]{1,0:T(8,128)(2,1)}, bf16[512,768]{1,0:T(8,128)(2,1)S(1)}, u32[]{:S(2)}) copy-start(bf16[512,768]{1,0:T(8,128)(2,1)S(1)} %fusion.50) | copy-start | bytes 2359300
  504.2 2.4 copy-start.75
  554.4 3.2 copy-start.2
  568.4 3.7 copy-start.6
  568.4 3.7 copy-start.9
  579.7 4.2 copy-start.48
  583.8 4.6 copy-start.25
  583.8 4.6 copy-start.26
  583.8 4.6 copy-start.30
  589.4 3.6 copy-start.18
  589.4 5.6 slice-start
  590.8 4.2 slice-start.1
  679.9 3.4 copy-start.34
  679.9 3.4 copy-start.43
  683.3 5.7 copy-start.64
  685.2 3.8 copy-start.45
  687.1 15.5 %slice-start.4 = ((s8[7077888]{0:T(1024)(128)(4,1)}), s8[4194304]{0:T(1024)(128)(4,1)S(1)}, s32[]{:S(2)}) async-start(s8[7077888]{0:T(1024)(128)(4,1)} %bitcast.389), calls=%async_computation.10 | async-start | bytes 8388608
  689.0 13.6 %slice-start.2 = ((s8[7077888]{0:T(1024)(128)(4,1)}), s8[4194304]{0:T(1024)(128)(4,1)S(1)}, s32[]{:S(2)}) async-start(s8[7077888]{0:T(1024)(128)(4,1)} %bitcast.384), calls=%async_computation.8 | async-start | bytes 8388608
  691.1 11.5 slice-start.3
  691.1 11.5 slice-start.5
  702.6 6.7 copy-start.17
  770.2 412.0 %reduce-scatter.5.cloned.1.call-start = ((), (), s32[]{:S(2)}) async-start(), calls=%async_computation.4 | async-start | bytes 10027008 | tf_op jit(solution)/shard_map/reduce_scatter | solution.py:207
  1031.5 4.0 copy-start.15
  1031.5 4.4 copy-start.42
  1035.5 2.4 copy-start.44
  1035.5 132.4 %collective-permute-start.4 = (bf16[8,288,768]{2,1,0:T(8,128)(2,1)}, bf16[8,288,768]{2,1,0:T(8,128)(2,1)}, u32[]{:S(2)}, u32[]{:S(2)}) collective-permute-start(bf16[8,288,768]{2,1,0:T(8,128)(2,1)} %constant_dynamic-slice_fusion), channel_id=1, source_target_pairs={{0,1},{1,0},{2,3},{3,2},{4,5},{5,4},{6,7},{7,6},{8,9},{9,8},{10,11... | collective-permute-start | bytes 10616840 | tf_op jit(solution)/shard_map/ppermute | solution.py:154
  1037.9 2.5 copy-start.12
  1037.9 2.5 copy-start.14
  1037.9 2.5 copy-start.41
  1038.0 2.5 copy-start.57
  1043.3 2.5 copy-start.71
  1043.9 4.3 copy-start.74
  1043.9 121.4 %collective-permute-start.3 = (bf16[8,32,768]{2,1,0:T(8,128)(2,1)S(1)}, bf16[8,32,768]{2,1,0:T(8,128)(2,1)S(1)}, u32[]{:S(2)}, u32[]{:S(2)}) collective-permute-start(bf16[8,32,768]{2,1,0:T(8,128)(2,1)S(1)} %constant_dynamic-slice_fusion.1), channel_id=1, source_target_pairs={{0,1},{1,0},{2,3},{3,2},{4,5},{5,4},{6,7},{7,6},{8,9},{9,8},{10,11... | collective-permute-start | bytes 1179656 | tf_op jit(solution)/shard_map/ppermute | solution.py:154
  1048.2 2.5 copy-start.68
  1050.7 2.5 copy-start.1
  1050.7 2.5 copy-start.29
  1053.3 3.3 copy-start.61
  1053.3 3.3 copy-start.60
  1053.3 3.4 copy-start.55
  1053.3 3.4 copy-start.54
  1055.9 109.5 %collective-permute-start.1 = (bf16[8,32,768]{2,1,0:T(8,128)(2,1)S(1)}, bf16[8,32,768]{2,1,0:T(8,128)(2,1)S(1)}, u32[]{:S(2)}, u32[]{:S(2)}) collective-permute-start(bf16[8,32,768]{2,1,0:T(8,128)(2,1)S(1)} %constant_dynamic-slice_fusion.3), channel_id=1, source_target_pairs={{0,1},{1,0},{2,3},{3,2},{4,5},{5,4},{6,7},{7,6},{8,9},{9,8},{10,11... | collective-permute-start | bytes 1179656 | tf_op jit(solution)/shard_map/ppermute | solution.py:154
  (32 other events, 46.5 us)
Sparse Core Ops, SparseCore 0:
  20.6 83.3 all-gather.2
  105.6 222.9 all-gather.4
  770.3 211.7 reduce-scatter.6
  1006.0 111.2 reduce-scatter.4

commit v2 on v1

--- a/solution.py
+++ b/solution.py
@@ -85,7 +85,7 @@
     return hidden, slope
 
 
-def layer(weights, norms, text, cotangent, patches, resolution):
+def layer(weights, forward, norms, text, cotangent, patches, resolution):
     count = text.shape[0] // LEN
     query_self, key_self, value_self, mix_self, query_cross, key_cross, value_cross, mix_cross = (weights[i] for i in range(8))
     first_gain, first_shift, second_gain, second_shift, third_gain, third_shift = norms
@@ -112,9 +112,9 @@
     layer_out = stream_two
     grad_normed = 0.0
     grads = [None] * 16
-    chunks = (weights.shape[0] - 8) // 2
+    chunks = forward.shape[0] // 2
     for j in range(chunks):
-        expand, contract = weights[8 + j], weights[8 + chunks + j]
+        expand, contract = forward[j], forward[chunks + j]
         hidden, slope = gelu_parts(matmul(normed_three, expand))
         hidden = hidden.astype(bf16)
         layer_out = layer_out + matmul_t(hidden, contract)
@@ -145,7 +145,7 @@
     grad_normed = matmul_t(grad_queries, query_self) + matmul_t(grad_keys, key_self) + matmul_t(grad_values, value_self)
     grad_input, gain_one, shift_one = norm_back(normal_one, inverse_one, first_gain, grad_normed)
     text_grad = (grad_stream + grad_input).astype(bf16)
-    grads = jnp.stack([g.astype(bf16) for g in grads])
+    grads = [jnp.stack([g.astype(bf16) for g in part]) for part in (grads[:8], grads[8:])]
     norm_grads = jnp.stack([gain_one, shift_one, gain_two, shift_two, gain_three, shift_three])
     return layer_out.astype(bf16), text_grad, patch_grad, grads, norm_grads
 
@@ -198,13 +198,16 @@
 
 
 def gather_weights(packed):
-    full = lax.all_gather(packed, "dp", axis=1, tiled=True)
-    return lax.all_gather(full, "mp", axis=2, tiled=True)
+    full = lax.all_gather(packed, ("mp", "dp"), axis=1, tiled=True)
+    count, rows, width = full.shape
+    sides = full.reshape(count, 2, rows // 2, width)
+    return jnp.concatenate([sides[:, 0], sides[:, 1]], axis=2)
 
 
 def scatter_grads(grads):
-    half = lax.psum_scatter(grads, "mp", scatter_dimension=2, tiled=True)
-    return lax.psum_scatter(half, "dp", scatter_dimension=1, tiled=True).astype(f32)
+    width = grads.shape[2] // 2
+    sides = jnp.concatenate([grads[:, :, :width], grads[:, :, width:]], axis=1)
+    return lax.psum_scatter(sides, ("mp", "dp"), scatter_dimension=1, tiled=True).astype(f32)
 
 
 def body(text_tokens, image_tokens, resolution, *rest):
@@ -212,15 +215,17 @@
     side = lax.axis_index("mp")
     half = text_tokens.shape[0] // 2
     width = text_tokens.shape[2]
-    weights = gather_weights(pack(shards))
+    packed = pack(shards)
+    attention = gather_weights(packed[:8])
+    forward = gather_weights(packed[8:])
     text = to_captions(text_tokens, side)
     grad_out = to_captions(cotangent, side)
     patches = lax.dynamic_slice_in_dim(image_tokens, side * half, half, 0)
     flags = lax.dynamic_slice_in_dim(resolution, side * half, half, 0)
     layer_out, text_grad, patch_grad, grads, norm_grads = layer(
-        weights, norms, text.reshape(-1, width), grad_out.reshape(-1, width), patches.reshape(-1, width), flags
+        attention, forward, norms, text.reshape(-1, width), grad_out.reshape(-1, width), patches.reshape(-1, width), flags
     )
-    weight_outs = unpack(scatter_grads(grads))
+    weight_outs = unpack(jnp.concatenate([scatter_grads(part) for part in grads]))
     norm_outs = lax.psum(norm_grads, BOTH)
     return (
         to_positions(layer_out.reshape(half, LEN, width), side),

time: 1200 us -> 863 us (0.72)
  waiting for transfers between devices: 504 us -> 181 us
  local copies, waits for them, and re-layouts: 268 us -> 231 us
  matrix products: 237 us -> 207 us
  other arithmetic: 55 us -> 82.7 us
  blocking collectives: 108 us -> 132 us
    unnamed x5 -> x4, waiting for transfers between devices: 212 us -> 0.07 us
    all_gather x2, waiting for transfers between devices: 284 us -> 105 us  [gather_weights(): full = lax.all_gather(packed, ('mp', 'dp'), axis=1, tiled=True)]
    unnamed x193 -> x256, local copies, waits for them, and re-layouts: 93.4 us -> 25.4 us
    reduce_scatter x1 -> x2, waiting for transfers between devices: 0.01 us -> 62.3 us  [scatter_grads(): lax.psum_scatter(sides, ('mp', 'dp'), scatter_dimension=1, tiled=True)]
    dot_general x48, matrix products: 164 us -> 131 us  [dot(): lax.dot_general(left, right, (((left_dim,), (right_dim,)), ((), ())), pre...]
    psum x1, blocking collectives: 108 us -> 132 us  [body(): norm_outs = lax.psum(norm_grads, BOTH)]
    concatenate x0 -> x2, other arithmetic: none -> 17.2 us  [scatter_grads(): sides = jnp.concatenate([grads[:, :, :width], grads[:, :, width:]], axis=1)]
    slice x0 -> x2, local copies, waits for them, and re-layouts: none -> 14.6 us  [scatter_grads(): sides = jnp.concatenate([grads[:, :, :width], grads[:, :, width:]], axis=1)]
  transfers between devices with their start and end apart: 9 -> 9, of which waited for: 5 -> 4; matrix products, arithmetic and copies ran while one was open for 6% -> 16% of each run, Pallas kernels for 0% -> 0%
where the time goes in v2:
time: 863 us; the launch traced here: 856 us
  local copies, waits for them, and re-layouts  231 us (27%)
  matrix products  207 us (24%)
  waiting for transfers between devices  181 us (21%)
  blocking collectives  132 us (15%)
  other arithmetic  82.7 us (10%)
  between operations  15.4 us (2%)
    psum x1, blocking collectives, body(): norm_outs = lax.psum(norm_grads, BOTH)  132 us
    dot_general x48, matrix products, dot(): lax.dot_general(left, right, (((left_dim,), (right_dim,)), ((), ())), pre...  131 us
    all_gather x2, waiting for transfers between devices, gather_weights(): full = lax.all_gather(packed, ('mp', 'dp'), axis=1, tiled=True)  105 us
    reduce_scatter x2, waiting for transfers between devices, scatter_grads(): lax.psum_scatter(sides, ('mp', 'dp'), scatter_dimension=1, tiled=True)  62.3 us
    reshape x13, local copies, waits for them, and re-layouts, heads(): return rows.reshape(count, rows.shape[0] // count, rows.shape[1] // HD, HD)  59.2 us
    convert_element_type x4, local copies, waits for them, and re-layouts, attend_back(): grad_values.reshape(keys.shape).astype(bf16)  31.2 us
    convert_element_type x4, local copies, waits for them, and re-layouts, attend_back(): grad_keys.reshape(keys.shape).astype(bf16)  31.1 us
    unnamed x256, local copies, waits for them, and re-layouts  25.4 us
  transfers between devices with their start and end apart: 9, of which 4 were waited for; matrix products, arithmetic and copies ran while one was open for 16% of the time, Pallas kernels for 0%

profile of v2, /device:TPU:0, one launch (start us, length us, event | category | flops | bytes accessed | tf_op | source)
XLA Modules:
  0.0 855.8 jit_solution(7559690865699069643)
XLA Ops:
  21.5 3.1 collective-permute-start.2
  24.8 6.6 constant_dynamic-slice_fusion.4
  31.4 12.8 %collective-permute-done = bf16[8,32,768]{2,1,0:T(8,128)(2,1)S(1)} collective-permute-done((bf16[8,32,768]{2,1,0:T(8,128)(2,1)S(1)}, bf16[8,32,768]{2,1,0:T(8,128)(2,1)S(1)}, u32[]{:S(2)}, u32[]{:S(2)}) %collective-permute-start) | collective-permute-done | bytes 393248 | tf_op jit(solution)/shard_map/ppermute | solution.py:154
  48.8 51.5 %all-gather.3.cloned.1.call-done = bf16[8,1536,384]{2,1,0:T(8,128)(2,1)} async-done(((bf16[8,48,384]{2,1,0:T(8,128)(2,1)}), bf16[8,1536,384]{2,1,0:T(8,128)(2,1)}) %all-gather.3.cloned.1.call-update) | async-done | bytes 9437200 | tf_op jit(solution)/shard_map/all_gather | solution.py:201
  100.4 4.9 slice_bitcast_fusion.2
  105.3 2.6 fusion.129
  107.9 14.3 %convolution_convert_fusion = bf16[4608,768]{1,0:T(8,128)(2,1)} fusion(bf16[4608,768]{1,0:T(8,128)(2,1)} %bitcast.423, bf16[8,768,384]{2,1,0:T(8,128)(2,1)S(1)} %get-tuple-element.54, bf16[8,768,384]{2,1,0:T(8,128)(2,1)S(1)} %get-tuple-element.53), kind=kOutput, calls=%fused_computation.39 | convolution fusion | flops 5441716224 | bytes 23592960 | tf_op jit(solution)/shard_map/dot_general | solution.py:19
  122.2 7.8 convolution_convert_fusion.1
  130.1 53.9 %all-gather.5.cloned.1.call-done = bf16[8,1536,384]{2,1,0:T(8,128)(2,1)} async-done(((bf16[8,48,384]{2,1,0:T(8,128)(2,1)}), bf16[8,1536,384]{2,1,0:T(8,128)(2,1)}) %all-gather.5.cloned.1.call-update) | async-done | bytes 9437200 | tf_op jit(solution)/shard_map/all_gather | solution.py:201
  184.0 8.7 %slice_bitcast_fusion = (bf16[8,768,384]{2,1,0:T(8,128)(2,1)}, bf16[8,768,384]{2,1,0:T(8,128)(2,1)}) fusion(bf16[8,2,768,384]{3,2,1,0:T(8,128)(2,1)} %bitcast.418), kind=kLoop, calls=%fused_computation.56 | loop fusion | bytes 18874368 | tf_op jit(solution)/shard_map/squeeze | solution.py:204
  192.7 2.8 convolution_convert_fusion.25
  195.5 3.9 reshape.726
  202.4 2.7 reshape.728
  205.1 2.9 copy.90
  209.3 3.4 copy.94
  212.7 3.3 fusion.203
  229.8 3.5 copy.101
  233.4 10.9 %copy.75 = bf16[4608,768]{0,1:T(8,128)(2,1)} copy(bf16[4608,768]{1,0:T(8,128)(2,1)} %convolution_convert_fusion) | data formatting | bytes 14155776 | tf_op jit(solution)/shard_map/convert_element_type | solution.py:106
  244.3 13.4 %reshape.711 = bf16[8,576,12,64]{1,0,3,2:T(8,128)(2,1)} reshape(bf16[4608,768]{0,1:T(8,128)(2,1)} %copy.75) | data formatting | bytes 14155776 | tf_op jit(solution)/shard_map/reshape | solution.py:51
  257.7 10.3 %copy.73 = bf16[4608,768]{0,1:T(8,128)(2,1)} copy(bf16[4608,768]{1,0:T(8,128)(2,1)} %convolution_convert_fusion.1) | data formatting | bytes 14155776 | tf_op jit(solution)/shard_map/convert_element_type | solution.py:107
  268.1 13.4 %reshape.709 = bf16[8,576,12,64]{1,0,3,2:T(8,128)(2,1)} reshape(bf16[4608,768]{0,1:T(8,128)(2,1)} %copy.73) | data formatting | bytes 14155776 | tf_op jit(solution)/shard_map/reshape | solution.py:51
  281.4 11.0 %fusion.12 = f32[8,12,64,576]{3,2,1,0:T(8,128)} fusion(bf16[8,64,12,64]{1,3,2,0:T(8,128)(2,1)S(1)} %copy.101, bf16[8,576,12,64]{1,0,3,2:T(8,128)(2,1)} %reshape.711), kind=kOutput, calls=%fused_computation.53 | convolution fusion | flops 452984832 | bytes 22020096 | tf_op jit(solution)/shard_map/clhd,ckhd->chlk/dot_general | solution.py:55
  292.5 18.0 %fusion.205 = (f32[8,12,64]{2,1,0:T(8,128)S(1)}, f32[8,12,64,576]{3,2,1,0:T(8,128)}) fusion(f32[8,12,64,576]{3,2,1,0:T(8,128)} %fusion.12, pred[8,576]{1,0:T(8,128)(4,1)S(1)} %iota_compare_fusion.1), kind=kOutput, calls=%fused_computation.372 | output fusion | flops 21234240 | bytes 28340736 | tf_op jit(solution)/shard_map/sub | solution.py:58
  310.5 9.8 %fusion.73 = bf16[8,64,12,64]{1,3,2,0:T(8,128)(2,1)S(1)} fusion(bf16[8,576,12,64]{1,0,3,2:T(8,128)(2,1)} %reshape.709, f32[8,12,64,576]{3,2,1,0:T(8,128)} %get-tuple-element.84, f32[8,12,64]{2,1,0:T(8,128)S(1)} %get-tuple-element.83), kind=kOutput, calls=%fused_computation.169 | convolution fusion | flops 460455936 | bytes 22044672 | tf_op jit(solution)/shard_map/chlk,ckhd->clhd/dot_general | solution.py:60
  320.3 2.4 copy.79
  322.8 2.8 convert_element_type.317
  326.9 3.8 fusion.128
  349.5 3.2 reshape.730
  352.7 2.9 copy.103
  355.6 11.5 %convert_bitcast_fusion = bf16[8,576,12,64]{1,3,2,0:T(8,128)(2,1)} fusion(bf16[8,64,12,64]{1,3,2,0:T(8,128)(2,1)} %copy.103, f32[8,12,64,576]{3,2,1,0:T(8,128)} %get-tuple-element.84, f32[8,12,64]{2,1,0:T(8,128)S(1)} %copy-done.78), kind=kOutput, calls=%fused_computation.41 | convolution fusion | flops 463601664 | bytes 22044672 | tf_op jit(solution)/shard_map/chlk,clhd->ckhd/dot_general | solution.py:68
  367.1 13.5 %multiply_reduce_fusion = (f32[8,12,64]{2,1,0:T(8,128)S(1)}, f32[8,12,64,576]{3,2,1,0:T(8,128)}) fusion(f32[8,12,64,576]{3,2,1,0:T(8,128)} %get-tuple-element.84, f32[8,12,64]{2,1,0:T(8,128)S(1)} %copy-done.78, bf16[8,64,12,64]{1,3,2,0:T(8,128)(2,1)S(1)} %copy-done.52, bf16[8,576,12,64]{1,0,3,2:T(8,128)(2,1)} %reshape.709), kind=kOutput, calls=%fused_computation.32 | convolution fusion | flops 463595520 | bytes 36225024 | tf_op jit(solution)/shard_map/clhd,ckhd->chlk/dot_general | solution.py:67
  380.7 11.0 %multiply_convert_fusion.1 = bf16[8,12,64,576]{3,2,1,0:T(8,128)(2,1)S(1)} fusion(f32[8,12,64,576]{3,2,1,0:T(8,128)} %get-tuple-element.89, f32[8,12,64]{2,1,0:T(8,128)S(1)} %get-tuple-element.88, f32[8,12,64,576]{3,2,1,0:T(8,128)} %get-tuple-element.84, f32[8,12,64]{2,1,0:T(8,128)S(1)} %copy-done.78), kind=kLoop, calls=%fused_computation.31 | loop fusion | flops 14155776 | bytes 35438592 | tf_op jit(solution)/shard_map/convert_element_type | solution.py:70
  391.6 7.0 fusion.51
  398.7 6.8 fusion.14
  405.5 3.0 copy.86
  408.5 3.6 convert_element_type.334
  412.2 3.3 multiply_reduce_fusion.3
  421.5 4.1 copy.98
  425.7 4.1 multiply_reduce_fusion.1
  437.9 11.7 %copy.104 = bf16[8,576,12,64]{1,0,3,2:T(8,128)(2,1)} copy(bf16[8,576,12,64]{1,3,2,0:T(8,128)(2,1)} %convert_bitcast_fusion) | data formatting | bytes 14155776 | tf_op jit(solution)/shard_map/convert_element_type | solution.py:76
  449.6 13.0 %convert_element_type.354 = bf16[4608,768]{0,1:T(8,128)(2,1)} reshape(bf16[8,576,12,64]{1,0,3,2:T(8,128)(2,1)} %copy.104) | data formatting | bytes 14155776 | tf_op jit(solution)/shard_map/convert_element_type | solution.py:76
  462.6 11.7 %copy.102 = bf16[8,576,12,64]{1,0,3,2:T(8,128)(2,1)} copy(bf16[8,576,12,64]{1,3,2,0:T(8,128)(2,1)} %fusion.14) | data formatting | bytes 14155776 | tf_op jit(solution)/shard_map/convert_element_type | solution.py:75
  474.3 12.8 %convert_element_type.351 = bf16[4608,768]{0,1:T(8,128)(2,1)} reshape(bf16[8,576,12,64]{1,0,3,2:T(8,128)(2,1)} %copy.102) | data formatting | bytes 14155776 | tf_op jit(solution)/shard_map/convert_element_type | solution.py:75
  487.1 3.8 copy.100
  490.8 2.7 convert_element_type.346
  493.6 3.1 copy.93
  496.6 3.5 convert_element_type.340
  500.1 2.8 copy.97
  502.9 3.8 convert_element_type.343
  506.7 3.3 fusion.87
  517.7 11.1 %fusion.83 = bf16[8,768,768]{2,1,0:T(8,128)(2,1)} fusion(bf16[8,768,768]{2,1,0:T(8,128)(2,1)} %fusion.95, bf16[4608,768]{1,0:T(8,128)(2,1)} %bitcast.424, bf16[4608,768]{0,1:T(8,128)(2,1)} %convert_element_type.351), kind=kOutput, calls=%fused_computation.178 | convolution fusion | flops 5436407808 | bytes 15335424 | tf_op jit(solution)/shard_map/dot_general | solution.py:19
  528.9 6.7 fusion.85
  537.5 7.1 fusion.202
  544.6 8.4 pad_maximum_fusion
  554.1 3.0 fusion.99
  570.4 7.5 fusion.201
  578.0 8.8 %pad_maximum_fusion.1 = bf16[8,1536,384]{2,1,0:T(8,128)(2,1)} fusion(bf16[8,768,384]{2,1,0:T(8,128)(2,1)} %get-tuple-element.40, bf16[8,768,384]{2,1,0:T(8,128)(2,1)S(1)} %get-tuple-element.39), kind=kLoop, calls=%fused_computation.38 | loop fusion | flops 18874368 | bytes 18874368 | tf_op jit(solution)/shard_map/concatenate | solution.py:209
  587.6 11.6 %fusion.154 = f32[4608,768]{1,0:T(8,128)} fusion(bf16[4608,768]{0,1:T(8,128)(2,1)} %convert_element_type.351, bf16[8,768,384]{2,1,0:T(8,128)(2,1)} %copy-done.2, bf16[8,768,384]{2,1,0:T(8,128)(2,1)} %copy-done), kind=kOutput, calls=%fused_computation.260 | convolution fusion | flops 5438177280 | bytes 30670848 | tf_op jit(solution)/shard_map/dot_general | solution.py:19
  599.3 13.4 %add_convert_fusion = bf16[4608,768]{1,0:T(8,128)(2,1)} fusion(f32[4608,768]{1,0:T(8,128)} %fusion.154, bf16[4608,768]{0,1:T(8,128)(2,1)} %convert_element_type.354, bf16[8,768,384]{2,1,0:T(8,128)(2,1)} %copy-done.2, bf16[8,768,384]{2,1,0:T(8,128)(2,1)S(1)} %bitcast.406), kind=kOutput, calls=%fused_computation.35 | convolution fusion | flops 5445255168 | bytes 37748736 | tf_op jit(solution)/shard_map/dot_general | solution.py:19
  612.7 4.2 constant_dynamic-slice_fusion
  632.2 132.1 %psum.7 = f32[6,768]{1,0:T(8,128)S(1)} all-reduce(f32[6,768]{1,0:T(8,128)S(1)} %stack.170), channel_id=1, replica_groups=mesh['dp'=16,'mp'=2] {'dp','mp'}, use_global_device_ids=true, to_apply=%region_26.27 | all-reduce | flops 4608 | bytes 36864 | tf_op jit(solution)/shard_map/psum | solution.py:229
  768.6 6.2 broadcast_select_fusion.1
  774.7 8.2 maximum_convert_fusion
  784.8 62.3 %reduce-scatter.5.cloned.1.call-done = bf16[8,48,384]{2,1,0:T(8,128)(2,1)} async-done(((bf16[8,1536,384]{2,1,0:T(8,128)(2,1)}), bf16[8,48,384]{2,1,0:T(8,128)(2,1)}) %reduce-scatter.5.cloned.1.call-update) | async-done | bytes 294928 | tf_op jit(solution)/shard_map/reduce_scatter | solution.py:210
  (383 shorter events, 118.8 us)
Async XLA Ops:
  7.2 14.2 %copy-start.68 = (bf16[16,32,768]{2,1,0:T(8,128)(2,1)S(1)}, bf16[16,32,768]{2,1,0:T(8,128)(2,1)}, u32[]{:S(2)}) copy-start(bf16[16,32,768]{2,1,0:T(8,128)(2,1)} %param.39) | copy-start | bytes 2359300
  7.2 17.3 %copy-start.67 = (bf16[16,32,768]{2,1,0:T(8,128)(2,1)S(1)}, bf16[16,32,768]{2,1,0:T(8,128)(2,1)}, u32[]{:S(2)}) copy-start(bf16[16,32,768]{2,1,0:T(8,128)(2,1)} %param.20) | copy-start | bytes 2359300
  7.2 93.1 %all-gather.3.cloned.1.call-start = ((), (), s32[]{:S(2)}) async-start(), calls=%async_computation.2 | async-start | bytes 9732096 | tf_op jit(solution)/shard_map/all_gather | solution.py:201
  9.7 15.0 %copy-start.100 = (s32[16]{0:T(128)S(1)}, s32[16]{0:T(128)}, u32[]{:S(2)}) copy-start(s32[16]{0:T(128)} %param.22) | copy-start | bytes 196
  14.3 169.6 %all-gather.5.cloned.1.call-start = ((), (), s32[]{:S(2)}) async-start(), calls=%async_computation.3 | async-start | bytes 9732096 | tf_op jit(solution)/shard_map/all_gather | solution.py:201
  21.4 761.6 %reduce-scatter.3.cloned.1.call-start = ((), (), s32[]{:S(2)}) async-start(), calls=%async_computation.4 | async-start | bytes 9732096 | tf_op jit(solution)/shard_map/reduce_scatter | solution.py:210
  21.5 23.9 %collective-permute-start.2 = (bf16[8,32,768]{2,1,0:T(8,128)(2,1)S(1)}, bf16[8,32,768]{2,1,0:T(8,128)(2,1)S(1)}, u32[]{:S(2)}, u32[]{:S(2)}) collective-permute-start(bf16[8,32,768]{2,1,0:T(8,128)(2,1)S(1)} %constant_dynamic-slice_fusion.2), channel_id=1, source_target_pairs={{0,1},{1,0},{2,3},{3,2},{4,5},{5,4},{6,7},{7,6},{8,9},{9,8},{10,11... | collective-permute-start | bytes 1179656 | tf_op jit(solution)/shard_map/ppermute | solution.py:154
  24.6 19.6 %collective-permute-start = (bf16[8,32,768]{2,1,0:T(8,128)(2,1)S(1)}, bf16[8,32,768]{2,1,0:T(8,128)(2,1)S(1)}, u32[]{:S(2)}, u32[]{:S(2)}) collective-permute-start(bf16[8,32,768]{2,1,0:T(8,128)(2,1)S(1)} %constant_dynamic-slice_fusion.5), channel_id=1, source_target_pairs={{0,1},{1,0},{2,3},{3,2},{4,5},{5,4},{6,7},{7,6},{8,9},{9,8},{10,11... | collective-permute-start | bytes 1179656 | tf_op jit(solution)/shard_map/ppermute | solution.py:154
  105.2 17.0 %copy-start = (bf16[8,768,384]{2,1,0:T(8,128)(2,1)}, bf16[8,768,384]{2,1,0:T(8,128)(2,1)S(1)}, u32[]{:S(2)}) copy-start(bf16[8,768,384]{2,1,0:T(8,128)(2,1)S(1)} %get-tuple-element.53) | copy-start | bytes 14155780
  105.2 17.0 %copy-start.2 = (bf16[8,768,384]{2,1,0:T(8,128)(2,1)}, bf16[8,768,384]{2,1,0:T(8,128)(2,1)S(1)}, u32[]{:S(2)}) copy-start(bf16[8,768,384]{2,1,0:T(8,128)(2,1)S(1)} %get-tuple-element.54) | copy-start | bytes 14155780
  105.3 17.0 %slice-start.16 = ((s8[7077888]{0:T(1024)(128)(4,1)}), s8[4194304]{0:T(1024)(128)(4,1)S(1)}, s32[]{:S(2)}) async-start(s8[7077888]{0:T(1024)(128)(4,1)} %bitcast.425), calls=%async_computation.22 | async-start | bytes 8388608
  107.9 14.3 %slice-start.17 = ((s8[7077888]{0:T(1024)(128)(4,1)}), s8[2883584]{0:T(1024)(128)(4,1)S(1)}, s32[]{:S(2)}) async-start(s8[7077888]{0:T(1024)(128)(4,1)} %bitcast.425), calls=%async_computation.23 | async-start | bytes 5767168
  184.0 8.7 %copy-start.1 = (bf16[8,768,384]{2,1,0:T(8,128)(2,1)S(1)}, bf16[8,768,384]{2,1,0:T(8,128)(2,1)}, u32[]{:S(2)}) copy-start(bf16[8,768,384]{2,1,0:T(8,128)(2,1)} %copy-done) | copy-start | bytes 14155780
  184.0 8.7 %copy-start.3 = (bf16[8,768,384]{2,1,0:T(8,128)(2,1)S(1)}, bf16[8,768,384]{2,1,0:T(8,128)(2,1)}, u32[]{:S(2)}) copy-start(bf16[8,768,384]{2,1,0:T(8,128)(2,1)} %copy-done.2) | copy-start | bytes 14155780
  195.5 3.9 copy-start.49
  195.5 3.9 copy-start.54
  216.0 4.0 copy-start.75
  224.8 100.8 %copy-start.6 = (f32[512,768]{1,0:T(8,128)}, f32[512,768]{1,0:T(8,128)S(1)}, u32[]{:S(2)}) copy-start(f32[512,768]{1,0:T(8,128)S(1)} %get-tuple-element.82) | copy-start | bytes 4718596
  233.4 48.1 %copy-start.10 = (bf16[8,64,12,64]{1,3,2,0:T(8,128)(2,1)}, bf16[8,64,12,64]{1,3,2,0:T(8,128)(2,1)S(1)}, u32[]{:S(2)}) copy-start(bf16[8,64,12,64]{1,3,2,0:T(8,128)(2,1)S(1)} %copy.101) | copy-start | bytes 2359300
  310.5 9.8 %copy-start.77 = (f32[8,12,64]{2,1,0:T(8,128)}, f32[8,12,64]{2,1,0:T(8,128)S(1)}, u32[]{:S(2)}) copy-start(f32[8,12,64]{2,1,0:T(8,128)S(1)} %get-tuple-element.83) | copy-start | bytes 73732
  325.6 5.5 slice-start
  325.6 5.7 slice-start.4
  326.5 19.5 %copy-start.4 = (f32[512,768]{1,0:T(8,128)}, f32[512,768]{1,0:T(8,128)S(1)}, u32[]{:S(2)}) copy-start(f32[512,768]{1,0:T(8,128)S(1)} %get-tuple-element.86) | copy-start | bytes 4718596
  326.9 3.9 copy-start.85
  326.9 3.9 copy-start.93
  326.9 4.6 slice-start.1
  326.9 4.7 slice-start.5
  330.8 11.9 %copy-start.37 = (bf16[768,768]{1,0:T(8,128)(2,1)}, bf16[768,768]{1,0:T(8,128)(2,1)S(1)}, u32[]{:S(2)}) copy-start(bf16[768,768]{1,0:T(8,128)(2,1)S(1)} %get-tuple-element.43) | copy-start | bytes 3538948
  331.6 7.9 copy-start.42
  332.4 10.3 %copy-start.34 = (f32[512,768]{1,0:T(8,128)}, f32[512,768]{1,0:T(8,128)S(1)}, u32[]{:S(2)}) copy-start(f32[512,768]{1,0:T(8,128)S(1)} %fusion.131) | copy-start | bytes 4718596
  355.6 11.5 %copy-start.52 = (bf16[8,64,12,64]{1,3,2,0:T(8,128)(2,1)S(1)}, bf16[8,64,12,64]{1,3,2,0:T(8,128)(2,1)}, u32[]{:S(2)}) copy-start(bf16[8,64,12,64]{1,3,2,0:T(8,128)(2,1)} %copy.103) | copy-start | bytes 2359300
  405.5 6.6 copy-start.59
  405.5 11.9 %slice-start.8 = ((s8[4718592]{0:T(1024)(128)(4,1)}), s8[524288]{0:T(1024)(128)(4,1)S(1)}, s32[]{:S(2)}) async-start(s8[4718592]{0:T(1024)(128)(4,1)} %bitcast.403), calls=%async_computation.14 | async-start | bytes 1048576
  408.5 3.6 copy-start.7
  408.5 3.6 copy-start.87
  408.5 3.6 copy-start.91
  408.5 3.6 copy-start.97
  412.2 5.2 slice-start.9
  421.5 4.2 copy-start.76
  425.7 4.1 copy-start.47
  425.7 4.3 copy-start.53
  493.5 18.4 %copy-start.40 = (bf16[512,768]{0,1:T(8,128)(2,1)}, bf16[512,768]{0,1:T(8,128)(2,1)S(1)}, u32[]{:S(2)}) copy-start(bf16[512,768]{0,1:T(8,128)(2,1)S(1)} %convert_element_type.346) | copy-start | bytes 2359300
  510.1 5.6 copy-start.99
  511.9 3.7 copy-start.72
  513.7 15.1 %slice-start.18 = ((s8[7077888]{0:T(1024)(128)(4,1)}), s8[4194304]{0:T(1024)(128)(4,1)S(1)}, s32[]{:S(2)}) async-start(s8[7077888]{0:T(1024)(128)(4,1)} %bitcast.428), calls=%async_computation.24 | async-start | bytes 8388608
  515.6 13.3 %slice-start.14 = ((s8[7077888]{0:T(1024)(128)(4,1)}), s8[4194304]{0:T(1024)(128)(4,1)S(1)}, s32[]{:S(2)}) async-start(s8[7077888]{0:T(1024)(128)(4,1)} %bitcast.421), calls=%async_computation.20 | async-start | bytes 8388608
  517.7 11.2 %slice-start.15 = ((s8[7077888]{0:T(1024)(128)(4,1)}), s8[2883584]{0:T(1024)(128)(4,1)S(1)}, s32[]{:S(2)}) async-start(s8[7077888]{0:T(1024)(128)(4,1)} %bitcast.421), calls=%async_computation.21 | async-start | bytes 5767168
  517.7 11.2 %slice-start.19 = ((s8[7077888]{0:T(1024)(128)(4,1)}), s8[2883584]{0:T(1024)(128)(4,1)S(1)}, s32[]{:S(2)}) async-start(s8[7077888]{0:T(1024)(128)(4,1)} %bitcast.428), calls=%async_computation.25 | async-start | bytes 5767168
  528.9 6.7 copy-start.18
  528.9 6.7 copy-start.20
  553.0 294.1 %reduce-scatter.5.cloned.1.call-start = ((), (), s32[]{:S(2)}) async-start(), calls=%async_computation.5 | async-start | bytes 9732096 | tf_op jit(solution)/shard_map/reduce_scatter | solution.py:210
  586.8 12.5 %slice-start.10 = ((s8[4718592]{0:T(1024)(128)(4,1)}), s8[524288]{0:T(1024)(128)(4,1)S(1)}, s32[]{:S(2)}) async-start(s8[4718592]{0:T(1024)(128)(4,1)} %bitcast.405), calls=%async_computation.16 | async-start | bytes 1048576
  587.6 11.7 %slice-start.11 = ((s8[4718592]{0:T(1024)(128)(4,1)}), s8[4194304]{0:T(1024)(128)(4,1)S(1)}, s32[]{:S(2)}) async-start(s8[4718592]{0:T(1024)(128)(4,1)} %bitcast.405), calls=%async_computation.17 | async-start | bytes 8388608
  587.6 30.6 %slice-start.2 = ((s8[4718592]{0:T(1024)(128)(4,1)}), s8[4194304]{0:T(1024)(128)(4,1)S(1)}, s32[]{:S(2)}) async-start(s8[4718592]{0:T(1024)(128)(4,1)} %bitcast.397), calls=%async_computation.8 | async-start | bytes 8388608
  587.6 30.6 %slice-start.6 = ((s8[4718592]{0:T(1024)(128)(4,1)}), s8[4194304]{0:T(1024)(128)(4,1)S(1)}, s32[]{:S(2)}) async-start(s8[4718592]{0:T(1024)(128)(4,1)} %bitcast.401), calls=%async_computation.12 | async-start | bytes 8388608
  599.3 19.0 %slice-start.3 = ((s8[4718592]{0:T(1024)(128)(4,1)}), s8[524288]{0:T(1024)(128)(4,1)S(1)}, s32[]{:S(2)}) async-start(s8[4718592]{0:T(1024)(128)(4,1)} %bitcast.397), calls=%async_computation.9 | async-start | bytes 1048576
  599.3 19.0 %slice-start.7 = ((s8[4718592]{0:T(1024)(128)(4,1)}), s8[524288]{0:T(1024)(128)(4,1)S(1)}, s32[]{:S(2)}) async-start(s8[4718592]{0:T(1024)(128)(4,1)} %bitcast.401), calls=%async_computation.13 | async-start | bytes 1048576
  612.7 5.6 copy-start.31
  616.9 151.7 %collective-permute-start.4 = (bf16[8,288,768]{2,1,0:T(8,128)(2,1)}, bf16[8,288,768]{2,1,0:T(8,128)(2,1)}, u32[]{:S(2)}, u32[]{:S(2)}) collective-permute-start(bf16[8,288,768]{2,1,0:T(8,128)(2,1)} %constant_dynamic-slice_fusion), channel_id=1, source_target_pairs={{0,1},{1,0},{2,3},{3,2},{4,5},{5,4},{6,7},{7,6},{8,9},{9,8},{10,11... | collective-permute-start | bytes 10616840 | tf_op jit(solution)/shard_map/ppermute | solution.py:154
  620.8 6.3 slice-start.12
  623.1 4.1 slice-start.13
  624.5 140.4 %collective-permute-start.1 = (bf16[8,32,768]{2,1,0:T(8,128)(2,1)S(1)}, bf16[8,32,768]{2,1,0:T(8,128)(2,1)}, u32[]{:S(2)}, u32[]{:S(2)}) collective-permute-start(bf16[8,32,768]{2,1,0:T(8,128)(2,1)S(1)} %constant_dynamic-slice_fusion.3), channel_id=1, source_target_pairs={{0,1},{1,0},{2,3},{3,2},{4,5},{5,4},{6,7},{7,6},{8,9},{9,8},{10,11... | collective-permute-start | bytes 1179656 | tf_op jit(solution)/shard_map/ppermute | solution.py:154
  629.4 135.5 %copy-start.45 = (bf16[512,768]{1,0:T(8,128)(2,1)S(1)}, bf16[512,768]{1,0:T(8,128)(2,1)}, u32[]{:S(2)}) copy-start(bf16[512,768]{1,0:T(8,128)(2,1)} %copy-done.44) | copy-start | bytes 2359300
  630.9 134.0 %collective-permute-start.3 = (bf16[8,32,768]{2,1,0:T(8,128)(2,1)S(1)}, bf16[8,32,768]{2,1,0:T(8,128)(2,1)S(1)}, u32[]{:S(2)}, u32[]{:S(2)}) collective-permute-start(bf16[8,32,768]{2,1,0:T(8,128)(2,1)S(1)} %constant_dynamic-slice_fusion.1), channel_id=1, source_target_pairs={{0,1},{1,0},{2,3},{3,2},{4,5},{5,4},{6,7},{7,6},{8,9},{9,8},{10,11... | collective-permute-start | bytes 1179656 | tf_op jit(solution)/shard_map/ppermute | solution.py:154
  (66 other events, 116.3 us)
Sparse Core Ops, SparseCore 0:
  14.5 85.8 all-gather.2
  103.9 80.0 all-gather.4
  553.1 152.9 reduce-scatter.2
  711.9 135.2 reduce-scatter.4

commit v3 on v1

v3 whole, which is shorter than its diff:
```python
import functools

import jax
import jax.numpy as jnp
from jax import lax
from jax.experimental import pallas as pl
from jax.experimental.pallas import tpu as pltpu
from jax.sharding import PartitionSpec as P

HD = 64
D = 768
GROUP = 256
LEN = 64
PATCH = 576
SMALLP = 196
BOTH = ("dp", "mp")

epsilon = 1e-05
masked_score = -1000000000.0
bf16 = jnp.bfloat16
f32 = jnp.float32


def dot(left, right, left_dim, right_dim):
    return lax.dot_general(left, right, (((left_dim,), (right_dim,)), ((), ())), preferred_element_type=f32)


def matmul(left, right):
    return dot(left, right, 1, 0)


def matmul_t(left, right):
    return dot(left, right, 1, 1)


def weight_grad(left, right):
    return dot(left, right, 0, 0)


def norm_stats(value):
    average = jnp.mean(value, axis=-1, keepdims=True)
    centred = value - average
    spread = jnp.mean(centred * centred, axis=-1, keepdims=True)
    inverse = lax.rsqrt(spread + epsilon)
    return centred * inverse, inverse


def norm_back(normal, inverse, gain, grad):
    scaled = grad * gain
    mean_one = jnp.mean(scaled, axis=-1, keepdims=True)
    mean_two = jnp.mean(scaled * normal, axis=-1, keepdims=True)
    grad_value = (scaled - mean_one - normal * mean_two) * inverse
    return grad_value, jnp.sum(grad * normal, axis=0), jnp.sum(grad, axis=0)


def spread(rows):
    head = lax.broadcasted_iota(jnp.int32, rows.shape, 1) // HD
    zero = jnp.zeros_like(rows)
    return jnp.concatenate([jnp.where(head == h, rows, zero) for h in range(rows.shape[1] // HD)], axis=0)


def collect(blocks):
    count = blocks.shape[1] // HD
    length = blocks.shape[0] // count
    head = lax.broadcasted_iota(jnp.int32, (length, blocks.shape[1]), 1) // HD
    total = blocks[:length]
    for h in range(1, count):
        total = jnp.where(head == h, blocks[h * length : (h + 1) * length], total)
    return total


def groups(width):
    return [slice(start, start + GROUP) for start in range(0, width, GROUP)]


def attend_kernel(causal, flag_ref, query_ref, key_ref, value_ref, mix_ref, prob_ref):
    keys = key_ref.shape[0]
    shape = (keys, GROUP // HD * LEN)
    row = lax.broadcasted_iota(jnp.int32, shape, 0)
    if causal:
        allowed = row <= lax.broadcasted_iota(jnp.int32, shape, 1) % LEN
    else:
        allowed = row < SMALLP + (PATCH - SMALLP) * flag_ref[pl.program_id(0)]
    for part in groups(query_ref.shape[1]):
        queries = spread(query_ref[:, part]) * jnp.asarray(HD ** (-0.5), bf16)
        scores = jnp.where(allowed, dot(key_ref[:, part], queries, 1, 1), masked_score)
        exponent = jnp.exp(scores - jnp.max(scores, axis=0, keepdims=True))
        probs = (exponent * (1.0 / jnp.sum(exponent, axis=0, keepdims=True))).astype(bf16)
        prob_ref[:, part] = probs
        mix_ref[:, part] = collect(dot(probs, value_ref[:, part], 0, 0)).astype(bf16)


def attend_back_kernel(query_ref, key_ref, value_ref, prob_ref, grad_ref, *outs):
    width = query_ref.shape[1]
    joined = outs[-1]
    query_out, shift = (outs[0], 0) if len(outs) == 2 else (joined, width)
    for part in groups(width):
        queries = spread(query_ref[:, part]) * jnp.asarray(HD ** (-0.5), bf16)
        grads = spread(grad_ref[:, part])
        probs_low = prob_ref[:, part]
        probs = probs_low.astype(f32)
        grad_prob = dot(value_ref[:, part], grads, 1, 1)
        inner = jnp.sum(probs * grad_prob, axis=0, keepdims=True)
        grad_score = (probs * (grad_prob - inner)).astype(bf16)
        key_part = slice(shift + part.start, shift + part.stop)
        value_part = slice(shift + width + part.start, shift + width + part.stop)
        joined[:, value_part] = dot(probs_low, grads, 1, 0).astype(bf16)
        joined[:, key_part] = dot(grad_score, queries, 1, 0).astype(bf16)
        query_out[:, part] = (collect(dot(grad_score, key_ref[:, part], 0, 0)) * HD ** (-0.5)).astype(bf16)


def column(rows, width, index):
    return pl.BlockSpec((rows, width), lambda i: (i, index))


def attend_cost(queries, count, keys, products):
    flops = 2 * products * queries.shape[0] * keys * queries.shape[1] * GROUP // HD
    return pl.CostEstimate(flops=flops, bytes_accessed=products * 2 * count * keys * queries.shape[1], transcendentals=0)


def attend(queries, query_at, sources, key_at, value_at, flags, count, causal):
    keys = sources.shape[0] // count
    width = D
    grid_spec = pltpu.PrefetchScalarGridSpec(
        num_scalar_prefetch=1,
        grid=(count,),
        in_specs=[
            pl.BlockSpec((LEN, width), lambda i, flag: (i, query_at)),
            pl.BlockSpec((keys, width), lambda i, flag: (i, key_at)),
            pl.BlockSpec((keys, width), lambda i, flag: (i, value_at)),
        ],
        out_specs=[
            pl.BlockSpec((LEN, width), lambda i, flag: (i, 0)),
            pl.BlockSpec((keys, width), lambda i, flag: (i, 0)),
        ],
    )
    return pl.pallas_call(
        functools.partial(attend_kernel, causal),
        grid_spec=grid_spec,
        out_shape=(
            jax.ShapeDtypeStruct((count * LEN, width), bf16),
            jax.ShapeDtypeStruct((count * keys, width), bf16),
        ),
        cost_estimate=attend_cost(queries, count, keys, 2),
    )(flags, queries, sources, sources)


def attend_back(queries, query_at, sources, key_at, value_at, probs, grad_mix, count, whole):
    keys = sources.shape[0] // count
    width = D
    widths = [(keys, 3 * width)] if whole else [(LEN, width), (keys, 2 * width)]
    return pl.pallas_call(
        attend_back_kernel,
        grid=(count,),
        in_specs=[
            column(LEN, width, query_at),
            column(keys, width, key_at),
            column(keys, width, value_at),
            column(keys, width, 0),
            column(LEN, width, 0),
        ],
        out_specs=[column(rows, wide, 0) for rows, wide in widths],
        out_shape=[jax.ShapeDtypeStruct((count * rows, wide), bf16) for rows, wide in widths],
        cost_estimate=attend_cost(queries, count, keys, 4),
    )(queries, sources, sources, probs, grad_mix)


def gelu_parts(value):
    inner = 0.7978845608028654 * (value + 0.044715 * value * value * value)
    bent = jnp.tanh(inner)
    hidden = 0.5 * value * (1.0 + bent)
    slope = 0.5 * (1.0 + bent) + 0.5 * value * (1.0 - bent * bent) * 0.7978845608028654 * (1.0 + 3 * 0.044715 * value * value)
    return hidden, slope


def layer(weights, norms, text, cotangent, patches, resolution):
    count = text.shape[0] // LEN
    project_self, mix_self, query_cross, project_patch, mix_cross, expand, contract = weights
    first_gain, first_shift, second_gain, second_shift, third_gain, third_shift = norms
    stream = text.astype(f32)
    normal_one, inverse_one = norm_stats(stream)
    normed_one = (normal_one * first_gain + first_shift).astype(bf16)
    rows_one = matmul(normed_one, project_self).astype(bf16)
    mixed_one, probs_one = attend(rows_one, 0, rows_one, 1, 2, resolution, count, True)
    stream_one = stream + matmul_t(mixed_one, mix_self)
    normal_two, inverse_two = norm_stats(stream_one)
    normed_two = (normal_two * second_gain + second_shift).astype(bf16)
    queries_two = matmul(normed_two, query_cross).astype(bf16)
    rows_two = matmul(patches, project_patch).astype(bf16)
    mixed_two, probs_two = attend(queries_two, 0, rows_two, 0, 1, resolution, count, False)
    stream_two = stream_one + matmul_t(mixed_two, mix_cross)
    normal_three, inverse_three = norm_stats(stream_two)
    normed_three = (normal_three * third_gain + third_shift).astype(bf16)
    hidden, slope = gelu_parts(matmul(normed_three, expand))
    hidden = hidden.astype(bf16)
    layer_out = stream_two + matmul_t(hidden, contract)
    grad_pre = (slope * matmul(cotangent, contract)).astype(bf16)
    forward_grads = scatter_grads([weight_grad(normed_three, grad_pre), weight_grad(cotangent, hidden)])
    grad_normed = matmul_t(grad_pre, expand)
    grad_input, gain_three, shift_three = norm_back(normal_three, inverse_three, third_gain, grad_normed)
    grad_stream = cotangent.astype(f32) + grad_input
    grad_rows = grad_stream.astype(bf16)
    grad_mix_cross = weight_grad(grad_rows, mixed_two)
    grad_mixed = matmul(grad_rows, mix_cross).astype(bf16)
    grad_queries, grad_sources = attend_back(queries_two, 0, rows_two, 0, 1, probs_two, grad_mixed, count, False)
    patch_grad = matmul_t(grad_sources, project_patch).astype(bf16)
    grad_query_cross = weight_grad(normed_two, grad_queries)
    grad_patch = weight_grad(patches, grad_sources)
    grad_normed = matmul_t(grad_queries, query_cross)
    grad_input, gain_two, shift_two = norm_back(normal_two, inverse_two, second_gain, grad_normed)
    grad_stream = grad_stream + grad_input
    grad_rows = grad_stream.astype(bf16)
    grad_mix_self = weight_grad(grad_rows, mixed_one)
    grad_mixed = matmul(grad_rows, mix_self).astype(bf16)
    (grad_one,) = attend_back(rows_one, 0, rows_one, 1, 2, probs_one, grad_mixed, count, True)
    grad_self = weight_grad(normed_one, grad_one)
    grad_normed = matmul_t(grad_one, project_self)
    grad_input, gain_one, shift_one = norm_back(normal_one, inverse_one, first_gain, grad_normed)
    text_grad = (grad_stream + grad_input).astype(bf16)
    norm_grads = jnp.stack([gain_one, shift_one, gain_two, shift_two, gain_three, shift_three])
    attention_grads = [grad_self, grad_mix_self, grad_query_cross, grad_patch, grad_mix_cross]
    return layer_out.astype(bf16), text_grad, patch_grad, attention_grads, forward_grads, norm_grads


def swap(rows):
    return lax.ppermute(rows, "mp", [(0, 1), (1, 0)])


def to_captions(rows, side):
    half = rows.shape[0] // 2
    mine = lax.dynamic_slice_in_dim(rows, side * half, half, 0)
    other = swap(lax.dynamic_slice_in_dim(rows, (1 - side) * half, half, 0))
    low = jnp.where(side == 0, mine, other)
    high = jnp.where(side == 0, other, mine)
    return jnp.concatenate([low, high], axis=1)


def to_positions(rows, side):
    length = rows.shape[1] // 2
    mine = lax.dynamic_slice_in_dim(rows, side * length, length, 1)
    other = swap(lax.dynamic_slice_in_dim(rows, (1 - side) * length, length, 1))
    low = jnp.where(side == 0, mine, other)
    high = jnp.where(side == 0, other, mine)
    return jnp.concatenate([low, high], axis=0)


def pack(shards):
    narrow = shards[0].shape[1]
    parts = []
    for shard, turned in zip(shards, TURNED):
        flat = shard.T if turned else shard
        for j in range(flat.shape[1] // narrow):
            parts.append(flat[:, j * narrow : (j + 1) * narrow])
    return jnp.stack(parts)


def unpack(packed):
    chunks = (packed.shape[0] - 8) // 2
    groups = [[packed[i]] for i in range(8)]
    groups.append([packed[8 + j] for j in range(chunks)])
    groups.append([packed[8 + chunks + j] for j in range(chunks)])
    outs = []
    for group, turned in zip(groups, TURNED):
        flat = group[0] if len(group) == 1 else jnp.concatenate(group, axis=1)
        outs.append(flat.T if turned else flat)
    return tuple(outs)


TURNED = (False, False, False, True, False, False, False, True, False, True)


def gather_weights(packed, counts):
    full = lax.all_gather(packed, ("mp", "dp"), axis=1, tiled=True)
    outs, start = [], 0
    for count in counts:
        sides = full[start : start + count].reshape(count, 2, D, -1)
        outs.append(sides.transpose(2, 0, 1, 3).reshape(D, -1))
        start += count
    return outs


def scatter_grads(grads):
    sides = [g.astype(bf16).reshape(D, g.shape[1] // D, 2, D // 2).transpose(1, 2, 0, 3) for g in grads]
    stacked = jnp.concatenate(sides).reshape(-1, 2 * D, D // 2)
    return lax.psum_scatter(stacked, ("mp", "dp"), scatter_dimension=1, tiled=True).astype(f32)


def body(text_tokens, image_tokens, resolution, *rest):
    shards, norms, cotangent = rest[:10], rest[10:16], rest[16]
    side = lax.axis_index("mp")
    half = text_tokens.shape[0] // 2
    width = text_tokens.shape[2]
    packed = pack(shards)
    chunks = (packed.shape[0] - 8) // 2
    weights = gather_weights(packed[:8], (3, 1, 1, 2, 1)) + gather_weights(packed[8:], (chunks, chunks))
    text = to_captions(text_tokens, side)
    grad_out = to_captions(cotangent, side)
    patches = lax.dynamic_slice_in_dim(image_tokens, side * half, half, 0)
    flags = lax.dynamic_slice_in_dim(resolution, side * half, half, 0)
    layer_out, text_grad, patch_grad, attention_grads, forward_grads, norm_grads = layer(
        weights, norms, text.reshape(-1, width), grad_out.reshape(-1, width), patches.reshape(-1, width), flags
    )
    weight_outs = unpack(jnp.concatenate([scatter_grads(attention_grads), forward_grads]))
    norm_outs = lax.psum(norm_grads, BOTH)
    return (
        to_positions(layer_out.reshape(half, LEN, width), side),
        to_positions(text_grad.reshape(half, LEN, width), side).astype(f32),
        to_positions(patch_grad.reshape(half, PATCH, width), side).astype(f32),
        *weight_outs,
        *(norm_outs[i] for i in range(6)),
    )


def solution(mesh):
    tokens = P("dp", "mp", None)
    rows, columns = P("dp", "mp"), P("mp", "dp")
    kinds = (rows, rows, rows, columns, rows, rows, rows, columns, rows, columns)
    in_specs = (tokens, P("dp", None, None), P("dp"), *kinds, *([P()] * 6), tokens)
    out_specs = (tokens, tokens, tokens, *kinds, *([P()] * 6))
    return jax.shard_map(body, mesh=mesh, in_specs=in_specs, out_specs=out_specs, check_vma=False)
```

time: 1200 us -> 670 us (0.56)
  waiting for transfers between devices: 504 us -> 126 us
  local copies, waits for them, and re-layouts: 268 us -> 153 us
  matrix products: 237 us -> 124 us
  Pallas kernels: 0 us -> 56.1 us
  blocking collectives: 108 us -> 141 us
  other arithmetic: 55 us -> 40.5 us
    unnamed x5 -> x4, waiting for transfers between devices: 212 us -> 0.07 us
    all_gather x2, waiting for transfers between devices: 284 us -> 114 us  [gather_weights(): full = lax.all_gather(packed, ('mp', 'dp'), axis=1, tiled=True)]
    convert_element_type x18 -> x0, local copies, waits for them, and re-layouts: 102 us -> none  [the longest x4 31.8 us: attend_back(): grad_values.reshape(keys.shape).astype(bf16)]
    dot_general x11 -> x0, matrix products: 69.5 us -> none  [the longest x2 15.9 us: attend_back(): jnp.einsum('chlk,clhd->ckhd', probs.astype(bf16), mix_heads, preferred_el...]
    unnamed x193 -> x128, local copies, waits for them, and re-layouts: 93.4 us -> 30.7 us
    pallas_call x0 -> x4, Pallas kernels: none -> 56.1 us  [the longest x2 30.6 us: attend_back(): pl.pallas_call(attend_back_kernel, grid=(count,), in_specs=[column(LEN, w...]
    dot_general x48 -> x21, matrix products: 164 us -> 124 us  [dot(): lax.dot_general(left, right, (((left_dim,), (right_dim,)), ((), ())), pre...]
    psum x1, blocking collectives: 108 us -> 141 us  [body(): norm_outs = lax.psum(norm_grads, BOTH)]
  transfers between devices with their start and end apart: 9 -> 9, of which waited for: 5 -> 4; matrix products, arithmetic and copies ran while one was open for 6% -> 27% of each run, Pallas kernels for 0% -> 5%
where the time goes in v3:
time: 670 us; the launch traced here: 663 us
  local copies, waits for them, and re-layouts  153 us (23%)
  blocking collectives  141 us (21%)
  waiting for transfers between devices  126 us (19%)
  matrix products  124 us (19%)
  Pallas kernels  56.1 us (8%)
  other arithmetic  40.5 us (6%)
  between operations  14.7 us (2%)
  starting transfers between devices  7.02 us (1%)
    psum x1, blocking collectives, body(): norm_outs = lax.psum(norm_grads, BOTH)  141 us
    dot_general x21, matrix products, dot(): lax.dot_general(left, right, (((left_dim,), (right_dim,)), ((), ())), pre...  124 us
    all_gather x2, waiting for transfers between devices, gather_weights(): full = lax.all_gather(packed, ('mp', 'dp'), axis=1, tiled=True)  114 us
    reshape x7, local copies, waits for them, and re-layouts, scatter_grads(): g.astype(bf16).reshape(D, g.shape[1] // D, 2, D // 2).transpose(1, 2, 0, 3)  48.3 us
    unnamed x128, local copies, waits for them, and re-layouts  30.7 us
    pallas_call x2, Pallas kernels, attend_back(): pl.pallas_call(attend_back_kernel, grid=(count,), in_specs=[column(LEN, w...  30.6 us
    pallas_call x2, Pallas kernels, attend(): pl.pallas_call(functools.partial(attend_kernel, causal), grid_spec=grid_s...  25.5 us
    transpose x7, local copies, waits for them, and re-layouts, gather_weights(): outs.append(sides.transpose(2, 0, 1, 3).reshape(D, -1))  24.5 us
  transfers between devices with their start and end apart: 9, of which 4 were waited for; matrix products, arithmetic and copies ran while one was open for 27% of the time, Pallas kernels for 5%

profile of v3, /device:TPU:0, one launch (start us, length us, event | category | flops | bytes accessed | tf_op | source)
XLA Modules:
  0.0 662.5 jit_solution(12105861300240643133)
XLA Ops:
  21.5 3.1 collective-permute-start.2
  25.2 6.5 constant_dynamic-slice_fusion.4
  31.8 4.8 collective-permute-done.2
  36.6 7.6 %collective-permute-done = bf16[8,32,768]{2,1,0:T(8,128)(2,1)S(1)} collective-permute-done((bf16[8,32,768]{2,1,0:T(8,128)(2,1)S(1)}, bf16[8,32,768]{2,1,0:T(8,128)(2,1)S(1)}, u32[]{:S(2)}, u32[]{:S(2)}) %collective-permute-start) | collective-permute-done | bytes 393248 | tf_op jit(solution)/shard_map/ppermute | solution.py:226
  48.1 52.3 %all-gather.5.cloned.1.call-done = bf16[8,1536,384]{2,1,0:T(8,128)(2,1)} async-done(((bf16[8,48,384]{2,1,0:T(8,128)(2,1)}), bf16[8,1536,384]{2,1,0:T(8,128)(2,1)}) %all-gather.5.cloned.1.call-update) | async-done | bytes 9437200 | tf_op jit(solution)/shard_map/all_gather | solution.py:273
  100.4 8.5 %fusion.31 = (bf16[4,1536,384]{2,1,0:T(8,128)(2,1)}, bf16[4,1536,384]{2,1,0:T(8,128)(2,1)}) fusion(bf16[8,1536,384]{2,1,0:T(8,128)(2,1)} %all-gather.5.cloned.1.call-done), kind=kLoop, calls=%fused_computation.151 | loop fusion | bytes 18874368 | tf_op jit(solution)/shard_map/slice | solution.py:276
  108.8 6.9 %copy.54 = bf16[768,4,2,384]{0,3,2,1:T(8,128)(2,1)} copy(bf16[768,4,2,384]{3,0,2,1:T(8,128)(2,1)} %bitcast.200) | data formatting | bytes 9437184 | tf_op jit(solution)/shard_map/transpose | solution.py:277
  115.7 6.7 %copy.55 = bf16[768,4,2,384]{0,3,2,1:T(8,128)(2,1)} copy(bf16[768,4,2,384]{3,0,2,1:T(8,128)(2,1)} %bitcast.198) | data formatting | bytes 9437184 | tf_op jit(solution)/shard_map/transpose | solution.py:277
  122.4 61.6 %all-gather.3.cloned.1.call-done = bf16[8,1536,384]{2,1,0:T(8,128)(2,1)} async-done(((bf16[8,48,384]{2,1,0:T(8,128)(2,1)}), bf16[8,1536,384]{2,1,0:T(8,128)(2,1)}) %all-gather.3.cloned.1.call-update) | async-done | bytes 9437200 | tf_op jit(solution)/shard_map/all_gather | solution.py:273
  184.0 1.7 slice-done
  185.6 2.7 copy.52
  188.3 3.4 fusion.32
  191.7 1.5 copy.53
  193.1 1.4 copy.51
  194.6 2.0 slice-done.1
  196.6 3.8 copy.49
  200.4 1.6 copy.50
  202.0 5.9 convolution_convert_fusion.5.query_ref.key_ref.value_ref
  207.9 11.0 %shard_map.339 = (bf16[512,768]{1,0:T(8,128)(2,1)}, bf16[512,768]{1,0:T(8,128)(2,1)}) custom-call(s32[8]{0:T(128)} %dynamic_slice.38.flag_ref, bf16[512,2304]{1,0:T(8,128)(2,1)} %convolution_convert_fusion.5.query_ref.key_ref.value_ref, bf16[512,2304]{1,0:T(8,128)(2,1)} %convolution_convert_fusion.5.query_ref.key_ref.value_ref, ...), custom_call_target="tpu_custom_call" | custom-call | flops 1207959552 | bytes 4718592 | tf_op jit(solution)/shard_map/pallas_call | solution.py:137
  218.9 2.4 fusion.33
  221.7 17.1 %convolution_convert_fusion.key_ref.value_ref = bf16[4608,1536]{1,0:T(8,128)(2,1)} fusion(bf16[4608,768]{1,0:T(8,128)(2,1)} %bitcast.206, bf16[768,1536]{0,1:T(8,128)(2,1)S(1)} %bitcast.227), kind=kOutput, calls=%fused_computation | convolution fusion | flops 10878713856 | bytes 23592960 | tf_op jit(solution)/shard_map/dot_general | solution.py:25
  238.8 1.8 convolution_convert_fusion.12.query_ref
  240.6 14.5 %shard_map.340 = (bf16[512,768]{1,0:T(8,128)(2,1)}, bf16[4608,768]{1,0:T(8,128)(2,1)}) custom-call(s32[8]{0:T(128)} %dynamic_slice.38.flag_ref, bf16[512,768]{1,0:T(8,128)(2,1)} %convolution_convert_fusion.12.query_ref, bf16[4608,1536]{1,0:T(8,128)(2,1)} %convolution_convert_fusion.key_ref.value_ref, bf16[4608,1536]{1,0:T(8,128)(2,1)} %convolution_convert_fusion.key_ref.value_ref), custom_call_target="tpu_custom_call" | custom-call | flops 3623878656 | bytes 14155776 | tf_op jit(solution)/shard_map/pallas_call | solution.py:137
  255.1 2.4 fusion.34
  258.3 4.8 fusion.30
  263.2 4.7 convolution_convert_fusion.2
  267.9 6.7 %fusion.6 = bf16[512,3072]{1,0:T(8,128)(2,1)} fusion(f32[512,3072]{1,0:T(8,128)S(1)} %fusion.30, bf16[512,768]{1,0:T(8,128)(2,1)S(1)} %bitcast.224, bf16[768,3072]{0,1:T(8,128)(2,1)S(1)} %bitcast.216), kind=kOutput, calls=%fused_computation.12 | convolution fusion | flops 2445803520 | bytes 14942208 | tf_op jit(solution)/shard_map/dot_general | solution.py:25
  274.6 11.6 %reshape.324 = bf16[768,4,2,384]{3,2,1,0:T(2,128)(2,1)} reshape(bf16[768,3072]{1,0:T(8,128)(2,1)} %convolution_convert_fusion.2) | data formatting | bytes 9437184 | tf_op jit(solution)/shard_map/reshape | solution.py:283
  286.2 6.4 convolution_convert_fusion.3
  292.7 11.6 %reshape.323 = bf16[768,4,2,384]{3,2,1,0:T(2,128)(2,1)} reshape(bf16[768,3072]{1,0:T(8,128)(2,1)} %convolution_convert_fusion.3) | data formatting | bytes 9437184 | tf_op jit(solution)/shard_map/reshape | solution.py:283
  304.3 15.0 %pad_maximum_fusion = bf16[8,2,768,384]{3,1,0,2:T(2,128)(2,1)} fusion(bf16[4,2,768,384]{3,1,0,2:T(2,128)(2,1)} %bitcast.199, bf16[4,2,768,384]{3,1,0,2:T(2,128)(2,1)} %bitcast.201), kind=kLoop, calls=%fused_computation.3 | loop fusion | flops 4718592 | bytes 18874368 | tf_op jit(solution)/shard_map/concatenate | solution.py:284
  319.2 9.7 %copy.60 = bf16[8,2,768,384]{3,2,1,0:T(8,128)(2,1)} copy(bf16[8,2,768,384]{3,1,0,2:T(2,128)(2,1)} %pad_maximum_fusion) | data formatting | bytes 18874368 | tf_op jit(solution)/shard_map/concatenate | solution.py:284
  329.1 6.9 %multiply_reduce_fusion = (f32[768]{0:T(1024)}, f32[512]{0:T(512)S(1)}, f32[512]{0:T(512)S(1)}, f32[768]{0:T(1024)}, f32[512,768]{1,0:T(8,128)S(1)}) fusion(f32[512,768]{1,0:T(8,128)S(1)} %get-tuple-element.84, f32[512]{0:T(512)S(1)} %add_rsqrt_fusion.1, f32[512]{0:T(512)S(1)} %broadcast_multiply_fusion.7, f32[768]{0:T(1024)S(1)} %copy-done.37, ...), kind=kOutput, calls=%fused_computation.46 | convolution fusion | flops 2419455488 | bytes 11027456 | tf_op jit(solution)/shard_map/dot_general | solution.py:25
  337.4 1.8 convolution_convert_fusion.11.grad_ref
  339.1 19.7 %shard_map.341 = (bf16[512,768]{1,0:T(8,128)(2,1)}, bf16[4608,1536]{1,0:T(8,128)(2,1)}) custom-call(bf16[512,768]{1,0:T(8,128)(2,1)} %convolution_convert_fusion.12.query_ref, bf16[4608,1536]{1,0:T(8,128)(2,1)} %convolution_convert_fusion.key_ref.value_ref, bf16[4608,1536]{1,0:T(8,128)(2,1)} %convolution_convert_fusion.key_ref.value_ref, ...), custom_call_target="tpu_custom_call" | custom-call | flops 7247757312 | bytes 28311552 | tf_op jit(solution)/shard_map/pallas_call | solution.py:152
  358.8 17.4 %convolution_convert_fusion.6 = bf16[768,1536]{1,0:T(8,128)(2,1)} fusion(bf16[4608,768]{1,0:T(8,128)(2,1)} %bitcast.207, bf16[4608,1536]{1,0:T(8,128)(2,1)} %get-tuple-element.30), kind=kOutput, calls=%fused_computation.21 | convolution fusion | flops 10872815616 | bytes 23592960 | tf_op jit(solution)/shard_map/dot_general | solution.py:25
  376.3 6.0 reshape.320
  382.3 1.8 convolution_convert_fusion.7
  384.1 4.9 copy.58
  389.0 3.1 convolution_convert_fusion.8
  392.1 4.8 copy.57
  396.9 3.4 multiply_reduce_fusion.1
  402.3 2.9 copy.56
  405.2 3.0 convolution_convert_fusion.10.grad_ref
  408.2 10.9 %shard_map.342 = bf16[512,2304]{1,0:T(8,128)(2,1)} custom-call(bf16[512,2304]{1,0:T(8,128)(2,1)} %convolution_convert_fusion.5.query_ref.key_ref.value_ref, bf16[512,2304]{1,0:T(8,128)(2,1)} %convolution_convert_fusion.5.query_ref.key_ref.value_ref, bf16[512,2304]{1,0:T(8,128)(2,1)} %convolution_convert_fusion.5.query_ref.key_ref.value_ref, ...), custom_call_target="tpu_custom_call" | custom-call | flops 2415919104 | bytes 9437184 | tf_op jit(solution)/shard_map/pallas_call | solution.py:152
  419.1 6.9 %fusion.25 = (f32[768]{0:T(1024)}, f32[512]{0:T(512)}, f32[512]{0:T(512)}, f32[768]{0:T(1024)}, bf16[512,768]{1,0:T(8,128)(2,1)S(1)}, /*index=5*/f32[512,768]{1,0:T(8,128)}) fusion(f32[512]{0:T(512)S(1)} %rsqrt.31, f32[512]{0:T(512)S(1)} %div.49, bf16[8,32,768]{2,1,0:T(8,128)(2,1)S(1)} %copy-done.8, bf16[8,32,768]{2,1,0:T(8,128)(2,1)S(1)} %copy-done.11, ...), kind=kOutput, calls=%fused_computation.45 | convolution fusion | flops 1818228224 | bytes 9064448 | tf_op jit(solution)/shard_map/dot_general | solution.py:25
  426.1 3.8 convolution_convert_fusion.4
  429.9 6.5 reshape.317
  436.4 4.2 bitcast_dynamic-update-slice_fusion
  440.7 1.8 bitcast_dynamic-update-slice_fusion.4
  442.5 1.8 bitcast_dynamic-update-slice_fusion.3
  444.3 3.0 bitcast_dynamic-update-slice_fusion.1
  447.4 1.8 bitcast_dynamic-update-slice_fusion.2
  449.2 9.6 %copy.59 = bf16[8,2,768,384]{3,2,1,0:T(8,128)(2,1)} copy(bf16[8,2,768,384]{3,1,0,2:T(2,128)(2,1)} %bitcast_dynamic-update-slice_fusion.2) | data formatting | bytes 18874368 | tf_op jit(solution)/shard_map/concatenate | solution.py:284
  458.8 1.7 copy-done.24
  460.5 14.6 %convolution_convert_fusion.1 = bf16[4608,768]{1,0:T(8,128)(2,1)S(1)} fusion(bf16[4608,1536]{1,0:T(8,128)(2,1)} %get-tuple-element.30, bf16[768,1536]{0,1:T(8,128)(2,1)S(1)} %bitcast.228), kind=kOutput, calls=%fused_computation.4 | convolution fusion | flops 10875174912 | bytes 23592960 | tf_op jit(solution)/shard_map/dot_general | solution.py:25
  475.1 2.0 constant_dynamic-slice_fusion
  477.1 2.4 copy-done.14
  479.5 1.5 collective-permute-start.4
  481.1 8.5 %add_convert_fusion = bf16[512,768]{1,0:T(8,128)(2,1)S(1)} fusion(f32[512,768]{1,0:T(8,128)S(1)} %copy-done.3, bf16[768,3072]{0,1:T(8,128)(2,1)} %bitcast.213, f32[512,3072]{1,0:T(8,128)} %copy-done.52), kind=kOutput, calls=%fused_computation.52 | convolution fusion | flops 2430861312 | bytes 13369344 | tf_op jit(solution)/shard_map/dot_general | solution.py:25
  491.1 1.6 collective-permute-start.3
  492.7 140.8 %psum.7 = f32[6,768]{1,0:T(8,128)S(1)} all-reduce(f32[6,768]{1,0:T(8,128)S(1)} %stack.98), channel_id=1, replica_groups=mesh['dp'=16,'mp'=2] {'dp','mp'}, use_global_device_ids=true, to_apply=%region_20.21 | all-reduce | flops 4608 | bytes 36864 | tf_op jit(solution)/shard_map/psum | solution.py:304
  638.0 5.1 broadcast_select_fusion.1
  643.2 8.2 %maximum_convert_fusion = f32[16,288,768]{2,1,0:T(8,128)} fusion(bf16[8,288,768]{2,1,0:T(8,128)(2,1)} %get-tuple-element.50, bf16[8,288,768]{2,1,0:T(8,128)(2,1)S(1)} %get-tuple-element.49), kind=kLoop, calls=%fused_computation.5 | loop fusion | flops 7077888 | bytes 21233664 | tf_op jit(solution)/shard_map/convert_element_type | solution.py:308
  (191 shorter events, 33.7 us)
Async XLA Ops:
  7.2 14.2 %copy-start.31 = (bf16[16,32,768]{2,1,0:T(8,128)(2,1)S(1)}, bf16[16,32,768]{2,1,0:T(8,128)(2,1)}, u32[]{:S(2)}) copy-start(bf16[16,32,768]{2,1,0:T(8,128)(2,1)} %param.39) | copy-start | bytes 2359300
  7.2 17.3 %copy-start.32 = (bf16[16,32,768]{2,1,0:T(8,128)(2,1)S(1)}, bf16[16,32,768]{2,1,0:T(8,128)(2,1)}, u32[]{:S(2)}) copy-start(bf16[16,32,768]{2,1,0:T(8,128)(2,1)} %param.20) | copy-start | bytes 2359300
  7.2 93.1 %all-gather.5.cloned.1.call-start = ((), (), s32[]{:S(2)}) async-start(), calls=%async_computation.3 | async-start | bytes 9732096 | tf_op jit(solution)/shard_map/all_gather | solution.py:273
  9.7 15.0 %copy-start.51 = (s32[16]{0:T(128)S(1)}, s32[16]{0:T(128)}, u32[]{:S(2)}) copy-start(s32[16]{0:T(128)} %param.22) | copy-start | bytes 196
  13.6 0.7 copy-start.33
  14.3 169.6 %all-gather.3.cloned.1.call-start = ((), (), s32[]{:S(2)}) async-start(), calls=%async_computation.2 | async-start | bytes 9732096 | tf_op jit(solution)/shard_map/all_gather | solution.py:273
  20.6 0.7 copy-start.34
  21.4 630.0 %reduce-scatter.5.cloned.1.call-start = ((), (), s32[]{:S(2)}) async-start(), calls=%async_computation.5 | async-start | bytes 9732096 | tf_op jit(solution)/shard_map/reduce_scatter | solution.py:285
  21.5 15.1 %collective-permute-start.2 = (bf16[8,32,768]{2,1,0:T(8,128)(2,1)S(1)}, bf16[8,32,768]{2,1,0:T(8,128)(2,1)S(1)}, u32[]{:S(2)}, u32[]{:S(2)}) collective-permute-start(bf16[8,32,768]{2,1,0:T(8,128)(2,1)S(1)} %constant_dynamic-slice_fusion.2), channel_id=1, source_target_pairs={{0,1},{1,0},{2,3},{3,2},{4,5},{5,4},{6,7},{7,6},{8,9},{9,8},{10,11... | collective-permute-start | bytes 1179656 | tf_op jit(solution)/shard_map/ppermute | solution.py:226
  24.6 19.6 %collective-permute-start = (bf16[8,32,768]{2,1,0:T(8,128)(2,1)S(1)}, bf16[8,32,768]{2,1,0:T(8,128)(2,1)S(1)}, u32[]{:S(2)}, u32[]{:S(2)}) collective-permute-start(bf16[8,32,768]{2,1,0:T(8,128)(2,1)S(1)} %constant_dynamic-slice_fusion.5), channel_id=1, source_target_pairs={{0,1},{1,0},{2,3},{3,2},{4,5},{5,4},{6,7},{7,6},{8,9},{9,8},{10,11... | collective-permute-start | bytes 1179656 | tf_op jit(solution)/shard_map/ppermute | solution.py:226
  44.3 2.5 copy-start.7
  44.3 2.5 copy-start.10
  45.4 1.4 copy-start.35
  45.4 1.4 copy-start.38
  184.0 1.7 slice-start
  194.6 2.0 slice-start.1
  200.4 1.7 copy-start.30
  202.0 16.9 %copy-start.27 = (bf16[768,1,2,384]{0,3,2,1:T(8,128)(2,1)}, bf16[768,1,2,384]{0,3,2,1:T(8,128)(2,1)S(1)}, u32[]{:S(2)}) copy-start(bf16[768,1,2,384]{0,3,2,1:T(8,128)(2,1)S(1)} %copy.50) | copy-start | bytes 3538948
  218.9 2.7 copy-start.23
  221.3 33.8 %copy-start.4 = (f32[512,768]{1,0:T(8,128)}, f32[512,768]{1,0:T(8,128)S(1)}, u32[]{:S(2)}) copy-start(f32[512,768]{1,0:T(8,128)S(1)} %get-tuple-element.82) | copy-start | bytes 4718596
  221.6 17.2 %copy-start.28 = (bf16[768,1,2,384]{0,3,2,1:T(8,128)(2,1)S(1)}, bf16[768,1,2,384]{0,3,2,1:T(8,128)(2,1)}, u32[]{:S(2)}) copy-start(bf16[768,1,2,384]{0,3,2,1:T(8,128)(2,1)} %copy.51) | copy-start | bytes 3538948
  221.7 17.2 %copy-start.46 = (f32[768]{0:T(1024)S(1)}, f32[768]{0:T(1024)}, u32[]{:S(2)}) copy-start(f32[768]{0:T(1024)} %param.35) | copy-start | bytes 9220
  221.7 17.1 %copy-start.50 = (f32[768]{0:T(1024)S(1)}, f32[768]{0:T(1024)}, u32[]{:S(2)}) copy-start(f32[768]{0:T(1024)} %param.36) | copy-start | bytes 9220
  257.5 78.5 %copy-start.2 = (f32[512,768]{1,0:T(8,128)}, f32[512,768]{1,0:T(8,128)S(1)}, u32[]{:S(2)}) copy-start(f32[512,768]{1,0:T(8,128)S(1)} %get-tuple-element.84) | copy-start | bytes 4718596
  257.5 0.7 copy-start.37
  257.5 0.7 copy-start.49
  258.3 4.9 copy-start.21
  258.3 9.6 %slice-start.2 = ((s8[4718592]{0:T(1024)(128)(4,1)}), s8[4194304]{0:T(1024)(128)(4,1)S(1)}, s32[]{:S(2)}) async-start(s8[4718592]{0:T(1024)(128)(4,1)} %bitcast.214), calls=%async_computation.8 | async-start | bytes 8388608
  263.1 4.7 copy-start.52
  263.2 4.7 slice-start.3
  328.9 323.5 %reduce-scatter.3.cloned.1.call-start = ((), (), s32[]{:S(2)}) async-start(), calls=%async_computation.4 | async-start | bytes 9732096 | tf_op jit(solution)/shard_map/reduce_scatter | solution.py:285
  329.1 6.9 %copy-start.22 = (bf16[8,64,768]{2,1,0:T(8,128)(2,1)S(1)}, bf16[8,64,768]{2,1,0:T(8,128)(2,1)}, u32[]{:S(2)}) copy-start(bf16[8,64,768]{2,1,0:T(8,128)(2,1)} %pad_maximum_fusion.3) | copy-start | bytes 2359300
  336.0 1.3 copy-start.19
  376.3 6.0 copy-start.20
  384.1 4.9 copy-start.5
  396.9 3.4 copy-start.6
  400.3 1.2 copy-start.29
  401.5 3.7 copy-start
  408.2 10.9 %copy-start.8 = (bf16[8,32,768]{2,1,0:T(8,128)(2,1)S(1)}, bf16[8,32,768]{2,1,0:T(8,128)(2,1)}, u32[]{:S(2)}) copy-start(bf16[8,32,768]{2,1,0:T(8,128)(2,1)} %copy-done.7) | copy-start | bytes 1179652
  408.2 10.9 %copy-start.11 = (bf16[8,32,768]{2,1,0:T(8,128)(2,1)S(1)}, bf16[8,32,768]{2,1,0:T(8,128)(2,1)}, u32[]{:S(2)}) copy-start(bf16[8,32,768]{2,1,0:T(8,128)(2,1)} %copy-done.10) | copy-start | bytes 1179652
  408.2 10.9 %copy-start.36 = (f32[768]{0:T(1024)S(1)}, f32[768]{0:T(1024)}, u32[]{:S(2)}) copy-start(f32[768]{0:T(1024)} %param.33) | copy-start | bytes 9220
  408.2 10.9 %copy-start.39 = (f32[768]{0:T(1024)S(1)}, f32[768]{0:T(1024)}, u32[]{:S(2)}) copy-start(f32[768]{0:T(1024)} %param.34) | copy-start | bytes 9220
  419.1 7.0 %copy-start.25 = (bf16[512,2304]{1,0:T(8,128)(2,1)S(1)}, bf16[512,2304]{1,0:T(8,128)(2,1)}, u32[]{:S(2)}) copy-start(bf16[512,2304]{1,0:T(8,128)(2,1)} %shard_map.342) | copy-start | bytes 7077892
  436.4 4.2 copy-start.18
  440.7 1.8 copy-start.17
  442.5 1.8 copy-start.13
  444.3 3.0 copy-start.16
  458.8 1.7 copy-start.24
  475.0 4.4 copy-start.14
  475.1 6.0 copy-start.3
  479.5 157.3 %collective-permute-start.4 = (bf16[8,288,768]{2,1,0:T(8,128)(2,1)}, bf16[8,288,768]{2,1,0:T(8,128)(2,1)}, u32[]{:S(2)}, u32[]{:S(2)}) collective-permute-start(bf16[8,288,768]{2,1,0:T(8,128)(2,1)} %constant_dynamic-slice_fusion), channel_id=1, source_target_pairs={{0,1},{1,0},{2,3},{3,2},{4,5},{5,4},{6,7},{7,6},{8,9},{9,8},{10,11... | collective-permute-start | bytes 10616840 | tf_op jit(solution)/shard_map/ppermute | solution.py:226
  481.0 9.2 %copy-start.48 = (f32[512]{0:T(512)S(1)}, f32[512]{0:T(512)}, u32[]{:S(2)}) copy-start(f32[512]{0:T(512)} %get-tuple-element.36) | copy-start | bytes 6148
  481.0 9.2 %copy-start.47 = (f32[512]{0:T(512)S(1)}, f32[512]{0:T(512)}, u32[]{:S(2)}) copy-start(f32[512]{0:T(512)} %get-tuple-element.37) | copy-start | bytes 6148
  481.0 9.2 %copy-start.1 = (f32[512,768]{1,0:T(8,128)S(1)}, f32[512,768]{1,0:T(8,128)}, u32[]{:S(2)}) copy-start(f32[512,768]{1,0:T(8,128)} %copy-done) | copy-start | bytes 4718596
  481.0 9.2 %copy-start.9 = (bf16[8,32,768]{2,1,0:T(8,128)(2,1)S(1)}, bf16[8,32,768]{2,1,0:T(8,128)(2,1)}, u32[]{:S(2)}) copy-start(bf16[8,32,768]{2,1,0:T(8,128)(2,1)} %copy-done.7) | copy-start | bytes 1179652
  481.1 9.2 %copy-start.12 = (bf16[8,32,768]{2,1,0:T(8,128)(2,1)S(1)}, bf16[8,32,768]{2,1,0:T(8,128)(2,1)}, u32[]{:S(2)}) copy-start(bf16[8,32,768]{2,1,0:T(8,128)(2,1)} %copy-done.10) | copy-start | bytes 1179652
  481.1 9.2 %copy-start.26 = (f32[512,768]{1,0:T(8,128)S(1)}, f32[512,768]{1,0:T(8,128)}, u32[]{:S(2)}) copy-start(f32[512,768]{1,0:T(8,128)} %get-tuple-element.87) | copy-start | bytes 4718596
  489.7 144.5 %collective-permute-start.1 = (bf16[8,32,768]{2,1,0:T(8,128)(2,1)S(1)}, bf16[8,32,768]{2,1,0:T(8,128)(2,1)S(1)}, u32[]{:S(2)}, u32[]{:S(2)}) collective-permute-start(bf16[8,32,768]{2,1,0:T(8,128)(2,1)S(1)} %constant_dynamic-slice_fusion.3), channel_id=1, source_target_pairs={{0,1},{1,0},{2,3},{3,2},{4,5},{5,4},{6,7},{7,6},{8,9},{9,8},{10,11... | collective-permute-start | bytes 1179656 | tf_op jit(solution)/shard_map/ppermute | solution.py:226
  490.3 0.7 copy-start.43
  490.3 0.7 copy-start.45
  490.3 0.7 copy-start.44
  490.3 0.7 copy-start.42
  491.1 144.2 %collective-permute-start.3 = (bf16[8,32,768]{2,1,0:T(8,128)(2,1)S(1)}, bf16[8,32,768]{2,1,0:T(8,128)(2,1)S(1)}, u32[]{:S(2)}, u32[]{:S(2)}) collective-permute-start(bf16[8,32,768]{2,1,0:T(8,128)(2,1)S(1)} %constant_dynamic-slice_fusion.1), channel_id=1, source_target_pairs={{0,1},{1,0},{2,3},{3,2},{4,5},{5,4},{6,7},{7,6},{8,9},{9,8},{10,11... | collective-permute-start | bytes 1179656 | tf_op jit(solution)/shard_map/ppermute | solution.py:226
  634.2 3.9 copy-start.15
  (2 other events, 1.4 us)
Sparse Core Ops, SparseCore 0:
  14.5 85.8 all-gather.4
  103.9 80.0 all-gather.2
  329.1 134.7 reduce-scatter.4
  469.6 157.8 reduce-scatter.2

commit v4 on v3

--- a/solution.py
+++ b/solution.py
@@ -195,7 +195,7 @@
     hidden = hidden.astype(bf16)
     layer_out = stream_two + matmul_t(hidden, contract)
     grad_pre = (slope * matmul(cotangent, contract)).astype(bf16)
-    forward_grads = scatter_grads([weight_grad(normed_three, grad_pre), weight_grad(cotangent, hidden)])
+    forward_grads = scatter_grads([weight_grad(normed_three, grad_pre), weight_grad(cotangent, hidden)], True)
     grad_normed = matmul_t(grad_pre, expand)
     grad_input, gain_three, shift_three = norm_back(normal_three, inverse_three, third_gain, grad_normed)
     grad_stream = cotangent.astype(f32) + grad_input
@@ -244,16 +244,6 @@
     return jnp.concatenate([low, high], axis=0)
 
 
-def pack(shards):
-    narrow = shards[0].shape[1]
-    parts = []
-    for shard, turned in zip(shards, TURNED):
-        flat = shard.T if turned else shard
-        for j in range(flat.shape[1] // narrow):
-            parts.append(flat[:, j * narrow : (j + 1) * narrow])
-    return jnp.stack(parts)
-
-
 def unpack(packed):
     chunks = (packed.shape[0] - 8) // 2
     groups = [[packed[i]] for i in range(8)]
@@ -269,18 +259,249 @@
 TURNED = (False, False, False, True, False, False, False, True, False, True)
 
 
-def gather_weights(packed, counts):
-    full = lax.all_gather(packed, ("mp", "dp"), axis=1, tiled=True)
-    outs, start = [], 0
-    for count in counts:
-        sides = full[start : start + count].reshape(count, 2, D, -1)
-        outs.append(sides.transpose(2, 0, 1, 3).reshape(D, -1))
-        start += count
-    return outs
-
-
-def scatter_grads(grads):
-    sides = [g.astype(bf16).reshape(D, g.shape[1] // D, 2, D // 2).transpose(1, 2, 0, 3) for g in grads]
+MESH = pl.DeviceIdType.MESH
+DEPTH = 4
+BUNDLE = 4
+
+
+def place():
+    index = lax.axis_index("dp")
+    return index // 4, index // 2 % 2, index % 2, lax.axis_index("mp")
+
+
+def greet(z, x, c, y):
+    barrier = pltpu.get_barrier_semaphore()
+
+    def hello(z_to, x_to, c_to, y_to):
+        pl.semaphore_signal(barrier, inc=1, device_id=(z_to * 4 + x_to * 2 + c_to, y_to), device_id_type=MESH)
+
+    hello(z, 1 - x, c, y)
+    hello(z, x, 1 - c, y)
+    hello(z, x, c, 1 - y)
+
+    @pl.when(z > 0)
+    def _():
+        hello(z - 1, x, c, y)
+
+    @pl.when(z < DEPTH - 1)
+    def _():
+        hello(z + 1, x, c, y)
+
+    pl.semaphore_wait(barrier, 3 + jnp.where(z > 0, 1, 0) + jnp.where(z < DEPTH - 1, 1, 0))
+
+
+def gather_kernel(att_in, exp_in, con_in, att, exp, con, own_sem, side_send, up_send, down_send, far_send, mate_send, recv, mate_recv):
+    z, x, c, y = place()
+    half, wide = att_in.shape[2], exp_in.shape[1]
+    greet(z, x, c, y)
+
+    def stream(index):
+        early = index % 2 == 0
+        part = index // 2
+
+        def own():
+            if early:
+                return att_in.at[pl.ds(part * BUNDLE, BUNDLE)]
+            return (exp_in, con_in)[part].at[...]
+
+        def region(w, z_from, u, core):
+            x_from = (x + (w if early else u)) % 2
+            y_from = (y + (u if early else w)) % 2
+            row = z_from * 4 + x_from * 2 + core
+            if early:
+                return att.at[pl.ds(part * BUNDLE, BUNDLE), row, :, pl.ds(pl.multiple_of(y_from * half, 128), half)]
+            return (exp, con)[part].at[row, :, pl.ds(pl.multiple_of(y_from * wide, 128), wide)]
+
+        if early:
+            beside, far = (z * 4 + (1 - x) * 2 + c, y), (z * 4 + x * 2 + c, 1 - y)
+        else:
+            beside, far = (z * 4 + x * 2 + c, 1 - y), (z * 4 + (1 - x) * 2 + c, y)
+
+        def copy(src, dst, send, receive, device):
+            return pltpu.make_async_remote_copy(
+                src_ref=src, dst_ref=dst, send_sem=send, recv_sem=receive, device_id=device, device_id_type=MESH
+            )
+
+        mine = z * 4 + x * 2 + c
+
+        def to_beside():
+            return copy(own(), region(0, z, 0, c), side_send.at[index], recv.at[index, 1, z, 0], beside)
+
+        def to_up(w, z_from, src):
+            return copy(src, region(w, z_from, 0, c), up_send.at[index, w, z_from], recv.at[index, w, z_from, 0], (mine + 4, y))
+
+        def to_down(w, z_from, src):
+            return copy(src, region(w, z_from, 0, c), down_send.at[index, w, z_from], recv.at[index, w, z_from, 0], (mine - 4, y))
+
+        def to_far(w, z_from, src):
+            return copy(src, region(w, z_from, 0, c), far_send.at[index, w, z_from], recv.at[index, w, z_from, 1], far)
+
+        def to_mate(w, z_from, u, src):
+            return copy(
+                src,
+                region(w, z_from, u, c),
+                mate_send.at[index, w, z_from, u],
+                mate_recv.at[index, w, z_from, u],
+                (z * 4 + x * 2 + 1 - c, y),
+            )
+
+        def keep():
+            return pltpu.make_async_copy(own(), region(0, z, 0, c), own_sem.at[index])
+
+        def arrive(w, z_from, u):
+            spot = region(w, z_from, u, c)
+            copy(spot, spot, far_send.at[index, w, z_from], recv.at[index, w, z_from, u], far).wait_recv()
+
+        def arrive_mate(w, z_from, u):
+            spot = region(w, z_from, u, 1 - c)
+            copy(spot, spot, far_send.at[index, w, z_from], mate_recv.at[index, w, z_from, u], far).wait_recv()
+
+        def pass_on(w, z_from, src, up, down):
+            @pl.when(up)
+            def _():
+                to_up(w, z_from, src).start()
+
+            @pl.when(down)
+            def _():
+                to_down(w, z_from, src).start()
+
+            to_far(w, z_from, src).start()
+            to_mate(w, z_from, 0, src).start()
+
+        def first():
+            to_beside().start()
+            pass_on(0, z, own(), z < DEPTH - 1, z > 0)
+            keep().start()
+
+        def second():
+            arrive(1, z, 0)
+            pass_on(1, z, region(1, z, 0, c), z < DEPTH - 1, z > 0)
+
+        def along(w, distance):
+            @pl.when(z >= distance)
+            def _():
+                z_from = z - distance
+                arrive(w, z_from, 0)
+                pass_on(w, z_from, region(w, z_from, 0, c), z < DEPTH - 1, z < 0)
+
+            @pl.when(z + distance < DEPTH)
+            def _():
+                z_from = z + distance
+                arrive(w, z_from, 0)
+                pass_on(w, z_from, region(w, z_from, 0, c), z < 0, z > 0)
+
+        def across(w, z_from):
+            arrive(w, z_from, 1)
+            to_mate(w, z_from, 1, region(w, z_from, 1, c)).start()
+
+        def across_at(w, distance):
+            if distance == 0:
+                across(w, z)
+                return
+
+            @pl.when(z >= distance)
+            def _():
+                across(w, z - distance)
+
+            @pl.when(z + distance < DEPTH)
+            def _():
+                across(w, z + distance)
+
+        def finish():
+            keep().wait()
+            to_beside().wait_send()
+
+            def each(number, _):
+                w, z_from = number // DEPTH, number % DEPTH
+                spot = region(w, z_from, 0, c)
+
+                @pl.when((z < DEPTH - 1) & (z_from <= z))
+                def _():
+                    to_up(w, z_from, spot).wait_send()
+
+                @pl.when((z > 0) & (z_from >= z))
+                def _():
+                    to_down(w, z_from, spot).wait_send()
+
+                to_far(w, z_from, spot).wait_send()
+                for u in range(2):
+                    to_mate(w, z_from, u, spot).wait_send()
+                    arrive_mate(w, z_from, u)
+                return 0
+
+            lax.fori_loop(0, 2 * DEPTH, each, 0)
+
+        return first, second, along, across_at, finish
+
+    streams = [stream(index) for index in range(4)]
+    for first, _, _, _, _ in streams:
+        first()
+    for _, second, _, _, _ in streams:
+        second()
+    for distance in range(1, DEPTH + 1):
+        for w in range(2):
+            for _, _, along, across_at, _ in streams:
+                if distance < DEPTH:
+                    along(w, distance)
+                across_at(w, distance - 1)
+    for streamed in streams:
+        streamed[4]()
+
+
+def gather_near(att, exp, con):
+    dp = lax.axis_size("dp")
+    rows, half, wide = att.shape[1], att.shape[2], exp.shape[1]
+    vmem = pl.BlockSpec(memory_space=pltpu.VMEM)
+    anywhere = pl.BlockSpec(memory_space=pl.ANY)
+    dma = pltpu.SemaphoreType.DMA
+    return pl.pallas_call(
+        gather_kernel,
+        in_specs=[vmem] * 3,
+        out_specs=[anywhere] * 3,
+        out_shape=[
+            jax.ShapeDtypeStruct((att.shape[0], dp, rows, 2 * half), bf16),
+            jax.ShapeDtypeStruct((dp, rows, 2 * wide), bf16),
+            jax.ShapeDtypeStruct((dp, rows, 2 * wide), bf16),
+        ],
+        scratch_shapes=[
+            dma((4,)),
+            dma((4,)),
+            dma((4, 2, DEPTH)),
+            dma((4, 2, DEPTH)),
+            dma((4, 2, DEPTH)),
+            dma((4, 2, DEPTH, 2)),
+            dma((4, 2, DEPTH, 2)),
+            dma((4, 2, DEPTH, 2)),
+        ],
+        compiler_params=pltpu.CompilerParams(collective_id=0, has_side_effects=True),
+    )(att, exp, con)
+
+
+def gather_weights(att, exp, con):
+    count, width = att.shape[0], D
+    if lax.axis_size("dp") == 4 * DEPTH:
+        att, exp, con = gather_near(att, exp, con)
+        att = att.reshape(count, width, -1)
+        exp, con = exp.reshape(width, -1), con.reshape(width, -1)
+    else:
+        chunks = exp.shape[1] // att.shape[2]
+        narrow = [g[:, j * att.shape[2] : (j + 1) * att.shape[2]] for g in (exp, con) for j in range(chunks)]
+        sides = lax.all_gather(att, ("mp", "dp"), axis=1, tiled=True).reshape(count, 2, width, -1)
+        att = sides.transpose(0, 2, 1, 3).reshape(count, width, -1)
+        sides = lax.all_gather(jnp.stack(narrow), ("mp", "dp"), axis=1, tiled=True).reshape(2, chunks, 2, width, -1)
+        exp, con = sides.transpose(0, 3, 2, 1, 4).reshape(2, width, -1)
+    project_self = jnp.concatenate([att[0], att[1], att[2]], axis=1)
+    project_patch = jnp.concatenate([att[5], att[6]], axis=1)
+    return project_self, att[3], att[4], project_patch, att[7], exp, con
+
+
+def scatter_grads(grads, natural):
+    sides = []
+    for g in grads:
+        if natural:
+            sides.append(g.astype(bf16).reshape(D, 2, g.shape[1] // D, D // 2).transpose(2, 1, 0, 3))
+        else:
+            sides.append(g.astype(bf16).reshape(D, g.shape[1] // D, 2, D // 2).transpose(1, 2, 0, 3))
     stacked = jnp.concatenate(sides).reshape(-1, 2 * D, D // 2)
     return lax.psum_scatter(stacked, ("mp", "dp"), scatter_dimension=1, tiled=True).astype(f32)
 
@@ -290,9 +511,8 @@
     side = lax.axis_index("mp")
     half = text_tokens.shape[0] // 2
     width = text_tokens.shape[2]
-    packed = pack(shards)
-    chunks = (packed.shape[0] - 8) // 2
-    weights = gather_weights(packed[:8], (3, 1, 1, 2, 1)) + gather_weights(packed[8:], (chunks, chunks))
+    flat = [shard.T if turned else shard for shard, turned in zip(shards, TURNED)]
+    weights = gather_weights(jnp.stack(flat[:8]), flat[8], flat[9])
     text = to_captions(text_tokens, side)
     grad_out = to_captions(cotangent, side)
     patches = lax.dynamic_slice_in_dim(image_tokens, side * half, half, 0)
@@ -300,7 +520,7 @@
     layer_out, text_grad, patch_grad, attention_grads, forward_grads, norm_grads = layer(
         weights, norms, text.reshape(-1, width), grad_out.reshape(-1, width), patches.reshape(-1, width), flags
     )
-    weight_outs = unpack(jnp.concatenate([scatter_grads(attention_grads), forward_grads]))
+    weight_outs = unpack(jnp.concatenate([scatter_grads(attention_grads, False), forward_grads]))
     norm_outs = lax.psum(norm_grads, BOTH)
     return (
         to_positions(layer_out.reshape(half, LEN, width), side),

time: 670 us -> 578 us (0.86)
  waiting for transfers between devices: 126 us -> 0.07 us
  Pallas kernels: 56.1 us -> 149 us
  local copies, waits for them, and re-layouts: 153 us -> 111 us
  blocking collectives: 141 us -> 131 us
  matrix products: 124 us -> 117 us
    all_gather x2 -> x0, waiting for transfers between devices: 114 us -> none  [gather_weights(): full = lax.all_gather(packed, ('mp', 'dp'), axis=1, tiled=True)]
    pallas_call x0 -> x1, Pallas kernels: none -> 92.9 us  [gather_near(): pl.pallas_call(gather_kernel, in_specs=[vmem] * 3, out_specs=[anywhere] *...]
    transpose x7 -> x0, local copies, waits for them, and re-layouts: 24.5 us -> none  [gather_weights(): outs.append(sides.transpose(2, 0, 1, 3).reshape(D, -1))]
    reshape x7 -> x5, local copies, waits for them, and re-layouts: 48.3 us -> 25.2 us  [scatter_grads(): g.astype(bf16).reshape(D, g.shape[1] // D, 2, D // 2).transpose(1, 2, 0, 3)]
    reshape x0 -> x2, local copies, waits for them, and re-layouts: none -> 19.5 us  [scatter_grads(): g.astype(bf16).reshape(D, 2, g.shape[1] // D, D // 2).transpose(2, 1, 0, 3)]
    ppermute x5, waiting for transfers between devices: 12.4 us -> 0.01 us  [swap(): return lax.ppermute(rows, 'mp', [(0, 1), (1, 0)])]
    psum x1, blocking collectives: 141 us -> 131 us  [body(): norm_outs = lax.psum(norm_grads, BOTH)]
    slice x6 -> x1, local copies, waits for them, and re-layouts: 15.5 us -> 6.52 us  [gather_weights(): return (project_self, att[3], att[4], project_patch, att[7], exp, con)]
  transfers between devices with their start and end apart: 9 -> 7, of which waited for: 4 -> 0; matrix products, arithmetic and copies ran while one was open for 27% -> 30% of each run, Pallas kernels for 5% -> 22%
where the time goes in v4:
time: 578 us; the launch traced here: 572 us
  Pallas kernels  149 us (26%)
  blocking collectives  131 us (23%)
  matrix products  117 us (20%)
  local copies, waits for them, and re-layouts  111 us (19%)
  other arithmetic  41.8 us (7%)
  between operations  15.3 us (3%)
  starting transfers between devices  6.8 us (1%)
    psum x1, blocking collectives, body(): norm_outs = lax.psum(norm_grads, BOTH)  131 us
    dot_general x21, matrix products, dot(): lax.dot_general(left, right, (((left_dim,), (right_dim,)), ((), ())), pre...  117 us
    pallas_call x1, Pallas kernels, gather_near(): pl.pallas_call(gather_kernel, in_specs=[vmem] * 3, out_specs=[anywhere] *...  92.9 us
    pallas_call x2, Pallas kernels, attend_back(): pl.pallas_call(attend_back_kernel, grid=(count,), in_specs=[column(LEN, w...  30.7 us
    pallas_call x2, Pallas kernels, attend(): pl.pallas_call(functools.partial(attend_kernel, causal), grid_spec=grid_s...  25.4 us
    reshape x5, local copies, waits for them, and re-layouts, scatter_grads(): g.astype(bf16).reshape(D, g.shape[1] // D, 2, D // 2).transpose(1, 2, 0, 3)  25.2 us
    unnamed x153, local copies, waits for them, and re-layouts  24.5 us
    concatenate x3, local copies, waits for them, and re-layouts, scatter_grads(): stacked = jnp.concatenate(sides).reshape(-1, 2 * D, D // 2)  21.1 us
  transfers between devices with their start and end apart: 7, of which 0 were waited for; matrix products, arithmetic and copies ran while one was open for 30% of the time, Pallas kernels for 22%

profile of v4, /device:TPU:0, one launch (start us, length us, event | category | flops | bytes accessed | tf_op | source)
XLA Modules:
  0.0 571.7 jit_solution(12800937793123339581)
XLA Ops:
  7.3 1.0 constant_dynamic-slice_fusion.2
  8.4 3.1 collective-permute-start.2
  11.4 1.0 constant_dynamic-slice_fusion.5
  13.5 92.9 %shard_map.339 = (bf16[8,16,48,768]{3,2,1,0:T(8,128)(2,1)}, bf16[16,48,3072]{2,1,0:T(8,128)(2,1)}, bf16[16,48,3072]{2,1,0:T(8,128)(2,1)}) custom-call(bf16[8,48,384]{2,1,0:T(8,128)(2,1)} %copy-done.42, bf16[48,1536]{1,0:T(8,128)(2,1)} %exp_in.1, bf16[48,1536]{1,0:T(8,128)(2,1)} %bitcast.182), custom_call_target="tpu_custom_call" | custom-call | tf_op jit(solution)/shard_map/pallas_call | solution.py:457
  106.3 6.5 %fusion.32 = (bf16[1,16,48,768]{3,2,1,0:T(8,128)(2,1)}, bf16[1,16,48,768]{3,2,1,0:T(8,128)(2,1)}, bf16[1,16,48,768]{3,2,1,0:T(8,128)(2,1)}, bf16[1,16,48,768]{3,...) fusion(bf16[8,16,48,768]{3,2,1,0:T(8,128)(2,1)} %get-tuple-elem, ...), kind=kLoop, calls=%fused_computation.142 | loop fusion | bytes 18874368 | tf_op jit(solution)/shard_map/slice | solution.py:495
  112.9 4.3 constant_dynamic-slice_fusion.4
  117.3 2.9 copy-done.13
  120.2 14.0 %convolution_convert_fusion.key_ref.value_ref = bf16[4608,1536]{1,0:T(8,128)(2,1)} fusion(bf16[4608,768]{1,0:T(8,128)(2,1)S(1)} %bitcast.155, bf16[768,768]{1,0:T(8,128)(2,1)S(1)} %bitcast.171, bf16[768,768]{1,0:T(8,128)(2,1)S(1)} %bitcast.173), kind=kOutput, calls=%fused_computation | convolution fusion | flops 10883432448 | bytes 23592960 | tf_op jit(solution)/shard_map/dot_general | solution.py:25
  135.5 2.2 broadcast_select_fusion.5
  139.4 1.1 fusion.15
  141.5 3.9 convolution_convert_fusion.5.query_ref.key_ref.value_ref
  145.4 11.1 %shard_map.340 = (bf16[512,768]{1,0:T(8,128)(2,1)}, bf16[512,768]{1,0:T(8,128)(2,1)}) custom-call(s32[8]{0:T(128)} %dynamic_slice.38.flag_ref, bf16[512,2304]{1,0:T(8,128)(2,1)} %convolution_convert_fusion.5.query_ref.key_ref.value_ref, bf16[512,2304]{1,0:T(8,128)(2,1)} %convolution_convert_fusion.5.query_ref.key_ref.value_ref, ...), custom_call_target="tpu_custom_call" | custom-call | flops 1207959552 | bytes 4718592 | tf_op jit(solution)/shard_map/pallas_call | solution.py:137
  156.6 2.3 fusion.33
  159.2 1.5 copy-done.36
  160.7 1.8 convolution_convert_fusion.12.query_ref
  162.5 14.3 %shard_map.341 = (bf16[512,768]{1,0:T(8,128)(2,1)}, bf16[4608,768]{1,0:T(8,128)(2,1)}) custom-call(s32[8]{0:T(128)} %dynamic_slice.38.flag_ref, bf16[512,768]{1,0:T(8,128)(2,1)} %convolution_convert_fusion.12.query_ref, bf16[4608,1536]{1,0:T(8,128)(2,1)} %convolution_convert_fusion.key_ref.value_ref, bf16[4608,1536]{1,0:T(8,128)(2,1)} %convolution_convert_fusion.key_ref.value_ref), custom_call_target="tpu_custom_call" | custom-call | flops 3623878656 | bytes 14155776 | tf_op jit(solution)/shard_map/pallas_call | solution.py:137
  176.8 2.4 fusion.34
  180.6 5.0 fusion.31
  185.6 4.7 convolution_convert_fusion.2
  190.3 6.8 %fusion.6 = bf16[512,3072]{1,0:T(8,128)(2,1)} fusion(f32[512,3072]{1,0:T(8,128)S(1)} %fusion.31, bf16[512,768]{1,0:T(8,128)(2,1)S(1)} %bitcast.162, bf16[768,3072]{1,0:T(8,128)(2,1)S(1)} %bitcast.186), kind=kOutput, calls=%fused_computation.12 | convolution fusion | flops 2445803520 | bytes 14942208 | tf_op jit(solution)/shard_map/dot_general | solution.py:25
  197.1 9.7 %reshape.206 = bf16[768,2,4,384]{3,2,1,0:T(4,128)(2,1)} reshape(bf16[768,3072]{1,0:T(8,128)(2,1)} %convolution_convert_fusion.2) | data formatting | bytes 9437184 | tf_op jit(solution)/shard_map/reshape | solution.py:502
  206.8 6.4 %convolution_convert_fusion.3 = bf16[768,3072]{1,0:T(8,128)(2,1)} fusion(bf16[512,3072]{1,0:T(8,128)(2,1)} %fusion.6, f32[512,768]{1,0:T(8,128)S(1)} %get-tuple-element.92, f32[768]{0:T(1024)S(1)} %copy-done.64, f32[768]{0:T(1024)S(1)} %copy-done.57, f32[512]{0:T(512)S(1)} %add_rsqrt_fusion.1, f32[512]{0:T(512)S(1)} %broadcast_multiply_fusion.7), kind=kOutput, calls=%fused_computation.15 | convolution fusion | flops 2420244480 | bytes 9447424 | tf_op jit(solution)/shard_map/dot_general | solution.py:25
  213.2 9.8 %reshape.205 = bf16[768,2,4,384]{3,2,1,0:T(4,128)(2,1)} reshape(bf16[768,3072]{1,0:T(8,128)(2,1)} %convolution_convert_fusion.3) | data formatting | bytes 9437184 | tf_op jit(solution)/shard_map/reshape | solution.py:502
  223.0 12.1 %pad_maximum_fusion = bf16[8,2,768,384]{3,0,1,2:T(8,128)(2,1)} fusion(bf16[4,2,768,384]{3,0,1,2:T(4,128)(2,1)} %bitcast.151, bf16[4,2,768,384]{3,0,1,2:T(4,128)(2,1)} %bitcast.152), kind=kLoop, calls=%fused_computation.3 | loop fusion | flops 18874368 | bytes 18874368 | tf_op jit(solution)/shard_map/concatenate | solution.py:505
  235.1 9.6 %copy.43 = bf16[8,2,768,384]{3,2,1,0:T(8,128)(2,1)} copy(bf16[8,2,768,384]{3,0,1,2:T(8,128)(2,1)} %pad_maximum_fusion) | data formatting | bytes 18874368 | tf_op jit(solution)/shard_map/concatenate | solution.py:505
  244.8 7.0 %multiply_reduce_fusion = (f32[768]{0:T(1024)}, f32[512]{0:T(512)S(1)}, f32[512]{0:T(512)S(1)}, f32[768]{0:T(1024)}, f32[512,768]{1,0:T(8,128)S(1)}) fusion(f32[512,768]{1,0:T(8,128)S(1)} %get-tuple-element.92, f32[512]{0:T(512)S(1)} %add_rsqrt_fusion.1, f32[512]{0:T(512)S(1)} %broadcast_multiply_fusion.7, f32[768]{0:T(1024)S(1)} %copy-done.57, ...), kind=kOutput, calls=%fused_computation.44 | convolution fusion | flops 2419455488 | bytes 11027456 | tf_op jit(solution)/shard_map/dot_general | solution.py:25
  253.1 1.7 convolution_convert_fusion.11.grad_ref
  254.8 20.1 %shard_map.342 = (bf16[512,768]{1,0:T(8,128)(2,1)}, bf16[4608,1536]{1,0:T(8,128)(2,1)}) custom-call(bf16[512,768]{1,0:T(8,128)(2,1)} %convolution_convert_fusion.12.query_ref, bf16[4608,1536]{1,0:T(8,128)(2,1)} %convolution_convert_fusion.key_ref.value_ref, bf16[4608,1536]{1,0:T(8,128)(2,1)} %convolution_convert_fusion.key_ref.value_ref, ...), custom_call_target="tpu_custom_call" | custom-call | flops 7247757312 | bytes 28311552 | tf_op jit(solution)/shard_map/pallas_call | solution.py:152
  274.9 17.4 %convolution_convert_fusion.6 = bf16[768,1536]{1,0:T(8,128)(2,1)} fusion(bf16[4608,768]{1,0:T(8,128)(2,1)} %bitcast.156, bf16[4608,1536]{1,0:T(8,128)(2,1)} %get-tuple-element.36), kind=kOutput, calls=%fused_computation.22 | convolution fusion | flops 10872815616 | bytes 23592960 | tf_op jit(solution)/shard_map/dot_general | solution.py:25
  292.3 6.0 %reshape.202 = bf16[768,2,2,384]{3,2,1,0:T(2,128)(2,1)} reshape(bf16[768,1536]{1,0:T(8,128)(2,1)} %convolution_convert_fusion.6) | data formatting | bytes 4718592 | tf_op jit(solution)/shard_map/reshape | solution.py:504
  298.3 1.8 convolution_convert_fusion.7
  300.2 4.9 copy.41
  305.1 3.1 convolution_convert_fusion.8
  308.2 4.8 copy.40
  313.0 3.4 multiply_reduce_fusion.1
  318.4 2.8 copy.39
  321.3 3.0 convolution_convert_fusion.10.grad_ref
  324.3 10.6 %shard_map.343 = bf16[512,2304]{1,0:T(8,128)(2,1)} custom-call(bf16[512,2304]{1,0:T(8,128)(2,1)} %convolution_convert_fusion.5.query_ref.key_ref.value_ref, bf16[512,2304]{1,0:T(8,128)(2,1)} %convolution_convert_fusion.5.query_ref.key_ref.value_ref, bf16[512,2304]{1,0:T(8,128)(2,1)} %convolution_convert_fusion.5.query_ref.key_ref.value_ref, ...), custom_call_target="tpu_custom_call" | custom-call | flops 2415919104 | bytes 9437184 | tf_op jit(solution)/shard_map/pallas_call | solution.py:152
  334.9 5.5 convolution_convert_fusion.4
  340.4 6.6 %reshape.199 = bf16[768,3,2,384]{3,2,1,0:T(2,128)(2,1)S(1)} reshape(bf16[768,2304]{1,0:T(8,128)(2,1)} %convolution_convert_fusion.4) | data formatting | bytes 7077888 | tf_op jit(solution)/shard_map/reshape | solution.py:504
  347.1 4.2 bitcast_dynamic-update-slice_fusion
  351.3 1.8 bitcast_dynamic-update-slice_fusion.4
  353.1 1.8 bitcast_dynamic-update-slice_fusion.3
  355.0 3.0 bitcast_dynamic-update-slice_fusion.1
  358.0 1.8 bitcast_dynamic-update-slice_fusion.2
  359.8 9.7 %copy.42 = bf16[8,2,768,384]{3,2,1,0:T(8,128)(2,1)} copy(bf16[8,2,768,384]{3,1,0,2:T(2,128)(2,1)} %bitcast_dynamic-update-slice_fusion.2) | data formatting | bytes 18874368 | tf_op jit(solution)/shard_map/concatenate | solution.py:505
  369.5 1.2 copy-done.32
  371.1 14.7 %convolution_convert_fusion.1 = bf16[4608,768]{1,0:T(8,128)(2,1)S(1)} fusion(bf16[4608,1536]{1,0:T(8,128)(2,1)} %get-tuple-element.36, bf16[768,768]{1,0:T(8,128)(2,1)S(1)} %bitcast.172, bf16[768,768]{1,0:T(8,128)(2,1)S(1)} %bitcast.174), kind=kOutput, calls=%fused_computation.4 | convolution fusion | flops 10879893504 | bytes 23592960 | tf_op jit(solution)/shard_map/dot_general | solution.py:25
  386.1 2.7 copy-done.12
  388.8 1.6 collective-permute-start.4
  390.4 9.1 %add_convert_fusion = bf16[512,768]{1,0:T(8,128)(2,1)S(1)} fusion(f32[512,768]{1,0:T(8,128)S(1)} %copy-done.3, bf16[768,3072]{1,0:T(8,128)(2,1)} %bitcast.183, f32[512,3072]{1,0:T(8,128)} %copy-done.68), kind=kOutput, calls=%fused_computation.50 | convolution fusion | flops 2430861312 | bytes 13369344 | tf_op jit(solution)/shard_map/dot_general | solution.py:25
  400.7 2.4 fusion.21
  405.9 1.8 collective-permute-start.3
  407.7 1.3 stack.63
  409.0 130.6 %psum.7 = f32[6,768]{1,0:T(8,128)} all-reduce(f32[6,768]{1,0:T(8,128)} %stack.63), channel_id=1, replica_groups=mesh['dp'=16,'mp'=2] {'dp','mp'}, use_global_device_ids=true, to_apply=%region_20.21 | all-reduce | flops 4608 | bytes 36864 | tf_op jit(solution)/shard_map/psum | solution.py:524
  539.6 1.6 slice_reduce_fusion
  541.2 1.3 broadcast_select_fusion.7
  542.6 0.9 pad_maximum_fusion.8
  543.5 1.1 broadcast_select_fusion.3
  544.7 1.2 maximum_convert_fusion.1
  545.9 6.1 %broadcast_select_fusion.1 = (bf16[8,288,768]{2,1,0:T(8,128)(2,1)S(1)}, bf16[8,288,768]{2,1,0:T(8,128)(2,1)}) fusion(bf16[8,288,768]{2,1,0:T(8,128)(2,1)} %collective-permute-done.4, pred[]{:T(512)S(6)} %eq.2, bf16[8,576,768]{2,1,0:T(8,128)(2,1)} %bitcast.154, s32[]{:T(128)S(6)} %select_n.86), kind=kLoop, calls=%fused_computation.21 | loop fusion | flops 3538944 | bytes 14155781 | tf_op jit(solution)/shard_map/jit(_where)/select_n | solution.py:242
  552.0 8.2 %maximum_convert_fusion = f32[16,288,768]{2,1,0:T(8,128)} fusion(bf16[8,288,768]{2,1,0:T(8,128)(2,1)} %get-tuple-element.56, bf16[8,288,768]{2,1,0:T(8,128)(2,1)S(1)} %get-tuple-element.55), kind=kLoop, calls=%fused_computation.5 | loop fusion | flops 7077888 | bytes 21233664 | tf_op jit(solution)/shard_map/convert_element_type | solution.py:528
  560.2 1.0 convert_element_type.120
  561.3 1.0 convert_element_type.117
  (198 shorter events, 16.7 us)
Async XLA Ops:
  7.2 5.3 copy-start.43
  7.2 5.3 copy-start.44
  7.2 5.4 copy-start.45
  7.2 5.4 copy-start.46
  7.2 5.4 copy-start.47
  7.2 5.4 copy-start.48
  7.3 5.4 copy-start.49
  7.3 5.5 copy-start.50
  7.3 552.9 %reduce-scatter.5.cloned.1.call-start = ((), (), s32[]{:S(2)}) async-start(), calls=%async_computation.3 | async-start | bytes 9732096 | tf_op jit(solution)/shard_map/reduce_scatter | solution.py:506
  8.4 126.4 %collective-permute-start.2 = (bf16[8,32,768]{2,1,0:T(8,128)(2,1)S(1)}, bf16[8,32,768]{2,1,0:T(8,128)(2,1)S(1)}, u32[]{:S(2)}, u32[]{:S(2)}) collective-permute-start(bf16[8,32,768]{2,1,0:T(8,128)(2,1)S(1)} %constant_dynamic-slice_fusion.2), channel_id=1, source_target_pairs={{0,1},{1,0},{2,3},{3,2},{4,5},{5,4},{6,7},{7,6},{8,9},{9,8},{10,11... | collective-permute-start | bytes 1179656 | tf_op jit(solution)/shard_map/ppermute | solution.py:226
  12.4 123.1 %collective-permute-start = (bf16[8,32,768]{2,1,0:T(8,128)(2,1)S(1)}, bf16[8,32,768]{2,1,0:T(8,128)(2,1)}, u32[]{:S(2)}, u32[]{:S(2)}) collective-permute-start(bf16[8,32,768]{2,1,0:T(8,128)(2,1)S(1)} %constant_dynamic-slice_fusion.5), channel_id=1, source_target_pairs={{0,1},{1,0},{2,3},{3,2},{4,5},{5,4},{6,7},{7,6},{8,9},{9,8},{10,11... | collective-permute-start | bytes 1179656 | tf_op jit(solution)/shard_map/ppermute | solution.py:226
  112.9 27.7 %copy-start.25 = (bf16[1,16,48,768]{3,2,1,0:T(8,128)(2,1)}, bf16[1,16,48,768]{3,2,1,0:T(8,128)(2,1)S(1)}, u32[]{:S(2)}) copy-start(bf16[1,16,48,768]{3,2,1,0:T(8,128)(2,1)S(1)} %get-tuple-element.62) | copy-start | bytes 3538948
  112.9 27.7 %copy-start.27 = (bf16[1,16,48,768]{3,2,1,0:T(8,128)(2,1)}, bf16[1,16,48,768]{3,2,1,0:T(8,128)(2,1)S(1)}, u32[]{:S(2)}) copy-start(bf16[1,16,48,768]{3,2,1,0:T(8,128)(2,1)S(1)} %get-tuple-element.63) | copy-start | bytes 3538948
  112.9 7.3 %copy-start.31 = (bf16[1,16,48,768]{3,2,1,0:T(8,128)(2,1)S(1)}, bf16[1,16,48,768]{3,2,1,0:T(8,128)(2,1)}, u32[]{:S(2)}) copy-start(bf16[1,16,48,768]{3,2,1,0:T(8,128)(2,1)} %get-tuple-element.58) | copy-start | bytes 3538948
  112.9 7.3 %copy-start.33 = (bf16[1,16,48,768]{3,2,1,0:T(8,128)(2,1)S(1)}, bf16[1,16,48,768]{3,2,1,0:T(8,128)(2,1)}, u32[]{:S(2)}) copy-start(bf16[1,16,48,768]{3,2,1,0:T(8,128)(2,1)} %get-tuple-element.59) | copy-start | bytes 3538948
  117.2 3.0 copy-start.13
  120.2 14.0 %copy-start.67 = (s32[16]{0:T(128)S(1)}, s32[16]{0:T(128)}, u32[]{:S(2)}) copy-start(s32[16]{0:T(128)} %param.22) | copy-start | bytes 196
  137.8 1.6 copy-start.7
  137.8 1.6 copy-start.9
  137.8 1.6 copy-start.55
  138.0 2.5 copy-start.51
  139.4 6.0 %copy-start.53 = (f32[512]{0:T(512)}, f32[512]{0:T(512)S(1)}, u32[]{:S(2)}) copy-start(f32[512]{0:T(512)S(1)} %rsqrt.28) | copy-start | bytes 6148
  139.4 2.1 copy-start.29
  145.4 11.1 %copy-start.35 = (bf16[1,16,48,768]{3,2,1,0:T(8,128)(2,1)S(1)}, bf16[1,16,48,768]{3,2,1,0:T(8,128)(2,1)}, u32[]{:S(2)}) copy-start(bf16[1,16,48,768]{3,2,1,0:T(8,128)(2,1)} %get-tuple-element.61) | copy-start | bytes 3538948
  158.8 18.0 %copy-start.4 = (f32[512,768]{1,0:T(8,128)}, f32[512,768]{1,0:T(8,128)S(1)}, u32[]{:S(2)}) copy-start(f32[512,768]{1,0:T(8,128)S(1)} %get-tuple-element.90) | copy-start | bytes 4718596
  158.8 1.8 copy-start.36
  158.8 1.8 copy-start.62
  158.8 1.8 copy-start.65
  179.2 72.6 %copy-start.2 = (f32[512,768]{1,0:T(8,128)}, f32[512,768]{1,0:T(8,128)S(1)}, u32[]{:S(2)}) copy-start(f32[512,768]{1,0:T(8,128)S(1)} %get-tuple-element.92) | copy-start | bytes 4718596
  180.5 9.8 %copy-start.19 = (bf16[8,64,768]{2,1,0:T(8,128)(2,1)}, bf16[8,64,768]{2,1,0:T(8,128)(2,1)S(1)}, u32[]{:S(2)}) copy-start(bf16[8,64,768]{2,1,0:T(8,128)(2,1)S(1)} %pad_maximum_fusion.9) | copy-start | bytes 2359300
  180.5 9.7 %slice-start = ((s8[4718592]{0:T(1024)(128)(4,1)}), s8[4194304]{0:T(1024)(128)(4,1)S(1)}, s32[]{:S(2)}) async-start(s8[4718592]{0:T(1024)(128)(4,1)} %bitcast.184), calls=%async_computation.4 | async-start | bytes 8388608
  185.6 4.7 copy-start.68
  185.6 4.7 slice-start.1
  244.7 7.0 %copy-start.58 = (f32[768]{0:T(1024)S(1)}, f32[768]{0:T(1024)}, u32[]{:S(2)}) copy-start(f32[768]{0:T(1024)} %param.37) | copy-start | bytes 9220
  244.7 316.5 %reduce-scatter.3.cloned.1.call-start = ((), (), s32[]{:S(2)}) async-start(), calls=%async_computation.2 | async-start | bytes 9732096 | tf_op jit(solution)/shard_map/reduce_scatter | solution.py:506
  244.8 7.0 %copy-start.20 = (bf16[8,64,768]{2,1,0:T(8,128)(2,1)S(1)}, bf16[8,64,768]{2,1,0:T(8,128)(2,1)}, u32[]{:S(2)}) copy-start(bf16[8,64,768]{2,1,0:T(8,128)(2,1)} %copy-done.19) | copy-start | bytes 2359300
  292.3 6.0 %copy-start.18 = (bf16[512,768]{1,0:T(8,128)(2,1)S(1)}, bf16[512,768]{1,0:T(8,128)(2,1)}, u32[]{:S(2)}) copy-start(bf16[512,768]{1,0:T(8,128)(2,1)} %get-tuple-element.30) | copy-start | bytes 2359300
  300.2 4.9 copy-start.5
  300.2 4.9 copy-start.63
  300.2 4.9 copy-start.66
  313.0 3.4 copy-start.6
  317.6 3.7 copy-start
  324.3 10.6 %copy-start.39 = (bf16[512,768]{1,0:T(8,128)(2,1)S(1)}, bf16[512,768]{1,0:T(8,128)(2,1)}, u32[]{:S(2)}) copy-start(bf16[512,768]{1,0:T(8,128)(2,1)} %copy-done.38) | copy-start | bytes 2359300
  347.1 4.2 copy-start.17
  351.3 1.8 copy-start.16
  353.1 1.8 copy-start.11
  355.0 3.0 copy-start.15
  385.8 3.0 copy-start.12
  385.8 4.6 copy-start.3
  388.7 11.9 %copy-start.8 = (bf16[8,32,768]{2,1,0:T(8,128)(2,1)S(1)}, bf16[8,32,768]{2,1,0:T(8,128)(2,1)}, u32[]{:S(2)}) copy-start(bf16[8,32,768]{2,1,0:T(8,128)(2,1)} %copy-done.7) | copy-start | bytes 1179652
  388.7 11.9 %copy-start.10 = (bf16[8,32,768]{2,1,0:T(8,128)(2,1)S(1)}, bf16[8,32,768]{2,1,0:T(8,128)(2,1)}, u32[]{:S(2)}) copy-start(bf16[8,32,768]{2,1,0:T(8,128)(2,1)} %copy-done.9) | copy-start | bytes 1179652
  388.7 11.9 %copy-start.23 = (bf16[512,2304]{1,0:T(8,128)(2,1)S(1)}, bf16[512,2304]{1,0:T(8,128)(2,1)}, u32[]{:S(2)}) copy-start(bf16[512,2304]{1,0:T(8,128)(2,1)} %shard_map.343) | copy-start | bytes 7077892
  388.7 11.9 %copy-start.26 = (bf16[1,16,48,768]{3,2,1,0:T(8,128)(2,1)S(1)}, bf16[1,16,48,768]{3,2,1,0:T(8,128)(2,1)}, u32[]{:S(2)}) copy-start(bf16[1,16,48,768]{3,2,1,0:T(8,128)(2,1)} %copy-done.25) | copy-start | bytes 3538948
  388.8 11.9 %copy-start.28 = (bf16[1,16,48,768]{3,2,1,0:T(8,128)(2,1)S(1)}, bf16[1,16,48,768]{3,2,1,0:T(8,128)(2,1)}, u32[]{:S(2)}) copy-start(bf16[1,16,48,768]{3,2,1,0:T(8,128)(2,1)} %copy-done.27) | copy-start | bytes 3538948
  388.8 11.9 %copy-start.30 = (bf16[1,16,48,768]{3,2,1,0:T(8,128)(2,1)S(1)}, bf16[1,16,48,768]{3,2,1,0:T(8,128)(2,1)}, u32[]{:S(2)}) copy-start(bf16[1,16,48,768]{3,2,1,0:T(8,128)(2,1)} %get-tuple-element.64) | copy-start | bytes 3538948
  388.8 11.9 %copy-start.52 = (f32[512]{0:T(512)S(1)}, f32[512]{0:T(512)}, u32[]{:S(2)}) copy-start(f32[512]{0:T(512)} %copy-done.51) | copy-start | bytes 6148
  388.8 11.9 %copy-start.54 = (f32[512]{0:T(512)S(1)}, f32[512]{0:T(512)}, u32[]{:S(2)}) copy-start(f32[512]{0:T(512)} %copy-done.53) | copy-start | bytes 6148
  388.8 11.9 %copy-start.56 = (f32[768]{0:T(1024)S(1)}, f32[768]{0:T(1024)}, u32[]{:S(2)}) copy-start(f32[768]{0:T(1024)} %param.33) | copy-start | bytes 9220
  388.8 157.1 %collective-permute-start.4 = (bf16[8,288,768]{2,1,0:T(8,128)(2,1)S(1)}, bf16[8,288,768]{2,1,0:T(8,128)(2,1)}, u32[]{:S(2)}, u32[]{:S(2)}) collective-permute-start(bf16[8,288,768]{2,1,0:T(8,128)(2,1)S(1)} %constant_dynamic-slice_fusion), channel_id=1, source_target_pairs={{0,1},{1,0},{2,3},{3,2},{4,5},{5,4},{6,7},{7,6},{8,9},{9,8},{10,11... | collective-permute-start | bytes 10616840 | tf_op jit(solution)/shard_map/ppermute | solution.py:226
  399.5 3.6 copy-start.40
  400.3 2.8 copy-start.1
  400.3 140.9 %collective-permute-start.1 = (bf16[8,32,768]{2,1,0:T(8,128)(2,1)}, bf16[8,32,768]{2,1,0:T(8,128)(2,1)}, u32[]{:S(2)}, u32[]{:S(2)}) collective-permute-start(bf16[8,32,768]{2,1,0:T(8,128)(2,1)} %constant_dynamic-slice_fusion.3), channel_id=1, source_target_pairs={{0,1},{1,0},{2,3},{3,2},{4,5},{5,4},{6,7},{7,6},{8,9},{9,8},{10,11... | collective-permute-start | bytes 1179656 | tf_op jit(solution)/shard_map/ppermute | solution.py:226
  405.9 137.6 %collective-permute-start.3 = (bf16[8,32,768]{2,1,0:T(8,128)(2,1)}, bf16[8,32,768]{2,1,0:T(8,128)(2,1)}, u32[]{:S(2)}, u32[]{:S(2)}) collective-permute-start(bf16[8,32,768]{2,1,0:T(8,128)(2,1)} %constant_dynamic-slice_fusion.1), channel_id=1, source_target_pairs={{0,1},{1,0},{2,3},{3,2},{4,5},{5,4},{6,7},{7,6},{8,9},{9,8},{10,11... | collective-permute-start | bytes 1179656 | tf_op jit(solution)/shard_map/ppermute | solution.py:226
  541.2 2.3 copy-start.22
  (14 other events, 15.7 us)
Sparse Core Ops, SparseCore 0:
  244.9 135.4 reduce-scatter.4
  386.2 152.3 reduce-scatter.2

commit v5 on v4

--- a/solution.py
+++ b/solution.py
@@ -195,7 +195,8 @@
     hidden = hidden.astype(bf16)
     layer_out = stream_two + matmul_t(hidden, contract)
     grad_pre = (slope * matmul(cotangent, contract)).astype(bf16)
-    forward_grads = scatter_grads([weight_grad(normed_three, grad_pre), weight_grad(cotangent, hidden)], True)
+    grad_expand = weight_grad(normed_three, grad_pre)
+    grad_contract = weight_grad(cotangent, hidden)
     grad_normed = matmul_t(grad_pre, expand)
     grad_input, gain_three, shift_three = norm_back(normal_three, inverse_three, third_gain, grad_normed)
     grad_stream = cotangent.astype(f32) + grad_input
@@ -218,8 +219,8 @@
     grad_input, gain_one, shift_one = norm_back(normal_one, inverse_one, first_gain, grad_normed)
     text_grad = (grad_stream + grad_input).astype(bf16)
     norm_grads = jnp.stack([gain_one, shift_one, gain_two, shift_two, gain_three, shift_three])
-    attention_grads = [grad_self, grad_mix_self, grad_query_cross, grad_patch, grad_mix_cross]
-    return layer_out.astype(bf16), text_grad, patch_grad, attention_grads, forward_grads, norm_grads
+    grads = [grad_expand, grad_contract, grad_self, grad_mix_self, grad_query_cross, grad_patch, grad_mix_cross]
+    return layer_out.astype(bf16), text_grad, patch_grad, [g.astype(bf16) for g in grads], norm_grads
 
 
 def swap(rows):
@@ -242,18 +243,6 @@
     low = jnp.where(side == 0, mine, other)
     high = jnp.where(side == 0, other, mine)
     return jnp.concatenate([low, high], axis=0)
-
-
-def unpack(packed):
-    chunks = (packed.shape[0] - 8) // 2
-    groups = [[packed[i]] for i in range(8)]
-    groups.append([packed[8 + j] for j in range(chunks)])
-    groups.append([packed[8 + chunks + j] for j in range(chunks)])
-    outs = []
-    for group, turned in zip(groups, TURNED):
-        flat = group[0] if len(group) == 1 else jnp.concatenate(group, axis=1)
-        outs.append(flat.T if turned else flat)
-    return tuple(outs)
 
 
 TURNED = (False, False, False, True, False, False, False, True, False, True)
@@ -495,15 +484,287 @@
     return project_self, att[3], att[4], project_patch, att[7], exp, con
 
 
-def scatter_grads(grads, natural):
+PIECES = 16
+SIDE_LAG = 2
+NORM_STEP = 2
+
+
+def scatter_kernel(exp, con, own, mix_own, ask, source, mix, norms, out, norm_out, acc, other, side, low, high, last, total, norm_buf, norm_line, *sems):
+    local_sem, mate_send, mate_recv, side_send, side_recv, line_send, low_recv, high_recv, last_send, last_recv, norm_send, norm_recv = sems
+    z, x, c, y = place()
+    half = out.shape[2]
+    mine = z * 4 + x * 2 + c
+    mate = (z * 4 + x * 2 + 1 - c, y)
+    greet(z, x, c, y)
+
+    def copy(src, dst, send, receive, device):
+        return pltpu.make_async_remote_copy(src_ref=src, dst_ref=dst, send_sem=send, recv_sem=receive, device_id=device, device_id_type=MESH)
+
+    early = [(ref, ref.shape[4] // 2, j * half) for ref in (exp, con) for j in range(4)]
+    late = [(own, half, 0), (own, half, 2 * half), (own, half, 4 * half), (mix_own, half, 0), (ask, half, 0)]
+    late += [(source, half, 0), (source, half, 2 * half), (mix, half, 0)]
+    pieces = [piece for pair in zip(early, late) for piece in pair]
+
+    for p, (ref, stride, offset) in enumerate(pieces):
+        for k in range(2):
+            columns = pl.ds(k * stride + offset, half)
+            spot = (p, slice(None), slice(None), k) if p % 2 == 0 else (p, slice(None), k)
+            copy(ref.at[:, :, 1 - c, :, columns], other.at[spot], mate_send.at[p, k], mate_recv.at[p, k], mate).start()
+            pltpu.make_async_copy(ref.at[:, :, c, :, columns], acc.at[spot], local_sem.at[p, k]).start()
+
+    def kind(p):
+        odd = p % 2
+        u = x * (1 - odd) + y * odd
+        w = y * (1 - odd) + x * odd
+        over_x = (z * 4 + (1 - x) * 2 + c, y)
+        over_y = (mine, 1 - y)
+        first = tuple(one * (1 - odd) + two * odd for one, two in zip(over_x, over_y))
+        second = tuple(two * (1 - odd) + one * odd for one, two in zip(over_x, over_y))
+        return u, w, first, second
+
+    def to_mate(p, k):
+        return copy(other.at[p, :, k], other.at[p, :, k], mate_send.at[p, k], mate_recv.at[p, k], mate)
+
+    def to_side(p):
+        u, w, first, second = kind(p)
+        return copy(acc.at[p, :, 1 - u], side.at[p], side_send.at[p], side_recv.at[p], first)
+
+    def to_low(p, unit):
+        u, w, first, second = kind(p)
+        return copy(acc.at[p, unit, u], low.at[p, unit], line_send.at[p, unit], low_recv.at[p, unit], (mine - 4, y))
+
+    def to_high(p, unit):
+        u, w, first, second = kind(p)
+        return copy(acc.at[p, unit, u], high.at[p, unit], line_send.at[p, unit], high_recv.at[p, unit], (mine + 4, y))
+
+    def to_last(p):
+        u, w, first, second = kind(p)
+        return copy(acc.at[p, z, u, 1 - w], last.at[p], last_send.at[p], last_recv.at[p], second)
+
+    def open_piece(p):
+        for k in range(2):
+            pltpu.make_async_copy(other.at[p, :, k], acc.at[p, :, k], local_sem.at[p, k]).wait()
+        for k in range(2):
+            to_mate(p, k).wait_recv()
+
+        def add(unit, _):
+            acc[p, unit] = (acc[p, unit].astype(f32) + other[p, unit].astype(f32)).astype(bf16)
+            return 0
+
+        lax.fori_loop(0, DEPTH, add, 0)
+        to_side(p).start()
+
+    def add_side(p):
+        u, w, first, second = kind(p)
+        to_side(p).wait_recv()
+
+        def add(unit, _):
+            acc[p, unit, u] = (acc[p, unit, u].astype(f32) + side[p, unit].astype(f32)).astype(bf16)
+            return 0
+
+        lax.fori_loop(0, DEPTH, add, 0)
+
+    def pass_line(p, buffer, inner, has_source, beyond, send):
+        u, w, first, second = kind(p)
+
+        def each(unit, _):
+            @pl.when(has_source & (beyond(unit) | (unit == z)))
+            def _():
+                inner(p, unit).wait_recv()
+
+            @pl.when(has_source & beyond(unit))
+            def _():
+                acc[p, unit, u] = (acc[p, unit, u].astype(f32) + buffer[p, unit].astype(f32)).astype(bf16)
+
+            @pl.when(beyond(unit))
+            def _():
+                send(p, unit).start()
+
+            return 0
+
+        lax.fori_loop(0, DEPTH, each, 0)
+
+    def close_line(p):
+        u, w, first, second = kind(p)
+        total[...] = acc[p, z, u].astype(f32)
+
+        @pl.when(z < DEPTH - 1)
+        def _():
+            total[...] += low[p, z].astype(f32)
+
+        @pl.when(z > 0)
+        def _():
+            total[...] += high[p, z].astype(f32)
+
+        acc[p, z, u, 1 - w] = total[1 - w].astype(bf16)
+        to_last(p).start()
+        out[p] = total[w]
+
+    def close_piece(p):
+        to_last(p).wait_recv()
+        out[p] += last[p].astype(f32)
+
+    def norm_pair(step):
+        device = (mate, (z * 4 + (1 - x) * 2 + c, y), (mine, 1 - y))[step]
+        return copy(norm_buf.at[step], norm_buf.at[3 + step], norm_send.at[step], norm_recv.at[step], device)
+
+    def norm_up(unit):
+        return copy(norm_line.at[unit], norm_line.at[unit], norm_send.at[3 + unit], norm_recv.at[3 + unit], (mine + 4, y))
+
+    def norm_down(unit):
+        return copy(norm_line.at[unit], norm_line.at[unit], norm_send.at[3 + DEPTH + unit], norm_recv.at[3 + unit], (mine - 4, y))
+
+    def norm_steps(t):
+        @pl.when(t == 0)
+        def _():
+            norm_buf[0] = norms[...]
+            norm_pair(0).start()
+
+        for step in range(1, 4):
+
+            @pl.when(t == step * NORM_STEP)
+            def _():
+                norm_pair(step - 1).wait_recv()
+                summed = norm_buf[step - 1] + norm_buf[2 + step]
+                if step < 3:
+                    norm_buf[step] = summed
+                    norm_pair(step).start()
+                else:
+                    norm_line[z] = summed
+
+                    @pl.when(z < DEPTH - 1)
+                    def _():
+                        norm_up(z).start()
+
+                    @pl.when(z > 0)
+                    def _():
+                        norm_down(z).start()
+
+        for distance in range(1, DEPTH):
+
+            @pl.when((t == (3 + distance) * NORM_STEP) & (z >= distance))
+            def _():
+                norm_up(z - distance).wait_recv()
+
+                @pl.when(z < DEPTH - 1)
+                def _():
+                    norm_up(z - distance).start()
+
+            @pl.when((t == (3 + distance) * NORM_STEP) & (z + distance < DEPTH))
+            def _():
+                norm_down(z + distance).wait_recv()
+
+                @pl.when(z > 0)
+                def _():
+                    norm_down(z + distance).start()
+
+    def at(p, work):
+        @pl.when((p >= 0) & (p < PIECES))
+        def _():
+            work(p)
+
+    def step(t, _):
+        at(t, open_piece)
+        at(t - SIDE_LAG, add_side)
+        at(
+            t - SIDE_LAG - (DEPTH - 1 - z),
+            lambda p: pass_line(p, low, to_low, z < DEPTH - 1, lambda unit: unit < z, to_low),
+        )
+        at(t - SIDE_LAG - z, lambda p: pass_line(p, high, to_high, z > 0, lambda unit: unit > z, to_high))
+        norm_steps(t)
+        at(t - SIDE_LAG - DEPTH, close_line)
+        at(t - SIDE_LAG - DEPTH - 2, close_piece)
+        return 0
+
+    lax.fori_loop(0, PIECES + SIDE_LAG + DEPTH + 2, step, 0)
+    norm_out[...] = norm_line[0] + norm_line[1] + norm_line[2] + norm_line[3]
+
+    def drain(p, _):
+        for k in range(2):
+            to_mate(p, k).wait_send()
+        to_side(p).wait_send()
+
+        def each(unit, _):
+            @pl.when(unit != z)
+            def _():
+                to_low(p, unit).wait_send()
+
+            return 0
+
+        lax.fori_loop(0, DEPTH, each, 0)
+        to_last(p).wait_send()
+        return 0
+
+    lax.fori_loop(0, PIECES, drain, 0)
+    for index in range(3):
+        norm_pair(index).wait_send()
+    for unit in range(DEPTH):
+
+        @pl.when((z < DEPTH - 1) & (unit <= z))
+        def _():
+            norm_up(unit).wait_send()
+
+        @pl.when((z > 0) & (unit >= z))
+        def _():
+            norm_down(unit).wait_send()
+
+
+def scatter_near(exp, con, own, mix_own, ask, source, mix, norms):
+    rows, half = D // (4 * DEPTH), D // 2
+    grads = [g.reshape(DEPTH, 2, 2, rows, g.shape[1]) for g in (exp, con, own, mix_own, ask, source, mix)]
+    vmem = pl.BlockSpec(memory_space=pltpu.VMEM)
+    anywhere = pl.BlockSpec(memory_space=pl.ANY)
+    dma = pltpu.SemaphoreType.DMA
+    return pl.pallas_call(
+        scatter_kernel,
+        in_specs=[anywhere] * 7 + [vmem],
+        out_specs=[vmem] * 2,
+        out_shape=[jax.ShapeDtypeStruct((PIECES, rows, half), f32), jax.ShapeDtypeStruct(norms.shape, f32)],
+        scratch_shapes=[
+            pltpu.VMEM((PIECES, DEPTH, 2, 2, rows, half), bf16),
+            pltpu.VMEM((PIECES, DEPTH, 2, 2, rows, half), bf16),
+            pltpu.VMEM((PIECES, DEPTH, 2, rows, half), bf16),
+            pltpu.VMEM((PIECES, DEPTH, 2, rows, half), bf16),
+            pltpu.VMEM((PIECES, DEPTH, 2, rows, half), bf16),
+            pltpu.VMEM((PIECES, rows, half), bf16),
+            pltpu.VMEM((2, rows, half), f32),
+            pltpu.VMEM((6, *norms.shape), f32),
+            pltpu.VMEM((DEPTH, *norms.shape), f32),
+            dma((PIECES, 2)),
+            dma((PIECES, 2)),
+            dma((PIECES, 2)),
+            dma((PIECES,)),
+            dma((PIECES,)),
+            dma((PIECES, DEPTH)),
+            dma((PIECES, DEPTH)),
+            dma((PIECES, DEPTH)),
+            dma((PIECES,)),
+            dma((PIECES,)),
+            dma((3 + 2 * DEPTH,)),
+            dma((3 + DEPTH,)),
+        ],
+        cost_estimate=pl.CostEstimate(flops=0, bytes_accessed=PIECES * D * D * 16, transcendentals=0),
+        compiler_params=pltpu.CompilerParams(collective_id=1, has_side_effects=True, vmem_limit_bytes=60 * 2**20),
+    )(*grads, norms)
+
+
+def scatter_grads(grads, norms):
+    exp, con, own, mix_own, ask, source, mix = grads
+    if lax.axis_size("dp") == 4 * DEPTH:
+        parts, norm_sums = scatter_near(*grads, jnp.pad(norms, ((0, 8 - norms.shape[0]), (0, 0))))
+        late = [parts[2 * i + 1] for i in range(8)]
+        exp, con = (jnp.concatenate([parts[2 * i] for i in part], axis=1) for part in (range(4), range(4, 8)))
+        return [*late, exp, con], norm_sums
     sides = []
-    for g in grads:
-        if natural:
-            sides.append(g.astype(bf16).reshape(D, 2, g.shape[1] // D, D // 2).transpose(2, 1, 0, 3))
-        else:
-            sides.append(g.astype(bf16).reshape(D, g.shape[1] // D, 2, D // 2).transpose(1, 2, 0, 3))
+    for g in (own, mix_own, ask, source, mix):
+        sides.append(g.reshape(D, g.shape[1] // D, 2, D // 2).transpose(1, 2, 0, 3))
+    for g in (exp, con):
+        sides.append(g.reshape(D, 2, g.shape[1] // D, D // 2).transpose(2, 1, 0, 3))
     stacked = jnp.concatenate(sides).reshape(-1, 2 * D, D // 2)
-    return lax.psum_scatter(stacked, ("mp", "dp"), scatter_dimension=1, tiled=True).astype(f32)
+    parts = lax.psum_scatter(stacked, ("mp", "dp"), scatter_dimension=1, tiled=True).astype(f32)
+    chunks = (parts.shape[0] - 8) // 2
+    exp, con = (jnp.concatenate(list(parts[start : start + chunks]), axis=1) for start in (8, 8 + chunks))
+    return [*(parts[i] for i in range(8)), exp, con], lax.psum(norms, BOTH)
 
 
 def body(text_tokens, image_tokens, resolution, *rest):
@@ -517,11 +778,11 @@
     grad_out = to_captions(cotangent, side)
     patches = lax.dynamic_slice_in_dim(image_tokens, side * half, half, 0)
     flags = lax.dynamic_slice_in_dim(resolution, side * half, half, 0)
-    layer_out, text_grad, patch_grad, attention_grads, forward_grads, norm_grads = layer(
+    layer_out, text_grad, patch_grad, grads, norm_grads = layer(
         weights, norms, text.reshape(-1, width), grad_out.reshape(-1, width), patches.reshape(-1, width), flags
     )
-    weight_outs = unpack(jnp.concatenate([scatter_grads(attention_grads, False), forward_grads]))
-    norm_outs = lax.psum(norm_grads, BOTH)
+    weight_grads, norm_outs = scatter_grads(grads, norm_grads)
+    weight_outs = [g.T if turned else g for g, turned in zip(weight_grads, TURNED)]
     return (
         to_positions(layer_out.reshape(half, LEN, width), side),
         to_positions(text_grad.reshape(half, LEN, width), side).astype(f32),

time: 578 us -> 481 us (0.83)
  Pallas kernels: 149 us -> 298 us
  blocking collectives: 131 us -> 0 us
  local copies, waits for them, and re-layouts: 111 us -> 34.9 us
  other arithmetic: 41.8 us -> 28.2 us
  between operations: 15.3 us -> 1.73 us
  matrix products: 117 us -> 107 us
    pallas_call x0 -> x1, Pallas kernels: none -> 150 us  [scatter_near(): pl.pallas_call(scatter_kernel, in_specs=[anywhere] * 7 + [vmem], out_spec...]
    psum x1 -> x0, blocking collectives: 131 us -> none  [body(): norm_outs = lax.psum(norm_grads, BOTH)]
    reshape x7 -> x0, local copies, waits for them, and re-layouts: 44.6 us -> none  [the longest x5 25.2 us: scatter_grads(): g.astype(bf16).reshape(D, g.shape[1] // D, 2, D // 2).transpose(1, 2, 0, 3)]
    concatenate x3 -> x0, local copies, waits for them, and re-layouts: 21.1 us -> none  [scatter_grads(): stacked = jnp.concatenate(sides).reshape(-1, 2 * D, D // 2)]
    unnamed x153 -> x127, local copies, waits for them, and re-layouts: 24.5 us -> 10.1 us
    concatenate x2 -> x1, other arithmetic: 12.8 us -> 0.73 us  [scatter_grads(): jnp.concatenate([parts[2 * i] for i in part], axis=1)]
    dot_general x21, matrix products: 117 us -> 107 us  [dot(): lax.dot_general(left, right, (((left_dim,), (right_dim,)), ((), ())), pre...]
  transfers between devices with their start and end apart: 7 -> 5, of which waited for: 0 -> 0; matrix products, arithmetic and copies ran while one was open for 30% -> 16% of each run, Pallas kernels for 22% -> 51%
where the time goes in v5:
time: 481 us; the launch traced here: 476 us
  Pallas kernels  298 us (62%)
  matrix products  107 us (22%)
  local copies, waits for them, and re-layouts  34.9 us (7%)
  other arithmetic  28.2 us (6%)
  starting transfers between devices  6.62 us (1%)
    pallas_call x1, Pallas kernels, scatter_near(): pl.pallas_call(scatter_kernel, in_specs=[anywhere] * 7 + [vmem], out_spec...  150 us
    dot_general x21, matrix products, dot(): lax.dot_general(left, right, (((left_dim,), (right_dim,)), ((), ())), pre...  107 us
    pallas_call x1, Pallas kernels, gather_near(): pl.pallas_call(gather_kernel, in_specs=[vmem] * 3, out_specs=[anywhere] *...  92.2 us
    pallas_call x2, Pallas kernels, attend_back(): pl.pallas_call(attend_back_kernel, grid=(count,), in_specs=[column(LEN, w...  29.7 us
    pallas_call x2, Pallas kernels, attend(): pl.pallas_call(functools.partial(attend_kernel, causal), grid_spec=grid_s...  25.6 us
    unnamed x127, local copies, waits for them, and re-layouts  10.1 us
  transfers between devices with their start and end apart: 5, of which 0 were waited for; matrix products, arithmetic and copies ran while one was open for 16% of the time, Pallas kernels for 51%

profile of v5, /device:TPU:0, one launch (start us, length us, event | category | flops | bytes accessed | tf_op | source)
XLA Modules:
  0.0 475.9 jit_solution(14660049179794797554)
XLA Ops:
  0.7 1.1 constant_dynamic-slice_fusion.2
  1.8 3.1 collective-permute-start.2
  4.9 1.8 constant_dynamic-slice_fusion.5
  6.9 0.7 copy-done.28
  7.6 92.2 %shard_map.339 = (bf16[8,16,48,768]{3,2,1,0:T(8,128)(2,1)}, bf16[16,48,3072]{2,1,0:T(8,128)(2,1)}, bf16[16,48,3072]{2,1,0:T(8,128)(2,1)}) custom-call(bf16[8,48,384]{2,1,0:T(8,128)(2,1)} %copy-done.28, bf16[48,1536]{1,0:T(8,128)(2,1)} %exp_in.1, bf16[48,1536]{1,0:T(8,128)(2,1)} %bitcast.172), custom_call_target="tpu_custom_call" | custom-call | tf_op jit(solution)/shard_map/pallas_call | solution.py:446
  99.8 6.6 %fusion.32 = (bf16[1,16,48,768]{3,2,1,0:T(8,128)(2,1)S(1)}, bf16[1,16,48,768]{3,2,1,0:T(8,128)(2,1)S(1)}, bf16[1,16,48,768]{3,2,1,0:T(8,128)(2,1)}, bf16[1,16,48...) fusion(bf16[8,16,48,768]{3,2,1,0:T(8,128)(2,1)} %get-tuple-elem, ...), kind=kLoop, calls=%fused_computation.136 | loop fusion | bytes 18874368 | tf_op jit(solution)/shard_map/slice | solution.py:484
  106.5 4.3 constant_dynamic-slice_fusion.4
  110.8 2.8 copy-done.5
  113.6 14.0 %convolution_convert_fusion.key_ref.value_ref = bf16[4608,1536]{1,0:T(8,128)(2,1)} fusion(bf16[4608,768]{1,0:T(8,128)(2,1)S(1)} %bitcast.141, bf16[768,768]{1,0:T(8,128)(2,1)S(1)} %bitcast.155, bf16[768,768]{1,0:T(8,128)(2,1)S(1)} %bitcast.157), kind=kOutput, calls=%fused_computation | convolution fusion | flops 10883432448 | bytes 23592960 | tf_op jit(solution)/shard_map/dot_general | solution.py:25
  127.6 0.6 dynamic_slice.38.flag_ref
  128.2 2.1 broadcast_select_fusion.5
  131.0 0.9 pad_maximum_fusion.6
  132.0 1.1 fusion.15
  133.1 0.9 copy-done.23
  134.0 4.6 convolution_convert_fusion.5.query_ref.key_ref.value_ref
  138.7 11.0 %shard_map.340 = (bf16[512,768]{1,0:T(8,128)(2,1)}, bf16[512,768]{1,0:T(8,128)(2,1)}) custom-call(s32[8]{0:T(128)} %dynamic_slice.38.flag_ref, bf16[512,2304]{1,0:T(8,128)(2,1)} %convolution_convert_fusion.5.query_ref.key_ref.value_ref, bf16[512,2304]{1,0:T(8,128)(2,1)} %convolution_convert_fusion.5.query_ref.key_ref.value_ref, ...), custom_call_target="tpu_custom_call" | custom-call | flops 1207959552 | bytes 4718592 | tf_op jit(solution)/shard_map/pallas_call | solution.py:137
  149.7 2.6 fusion.33
  153.2 0.9 copy-done.21
  154.1 1.8 convolution_convert_fusion.12.query_ref
  156.0 14.6 %shard_map.341 = (bf16[512,768]{1,0:T(8,128)(2,1)}, bf16[4608,768]{1,0:T(8,128)(2,1)}) custom-call(s32[8]{0:T(128)} %dynamic_slice.38.flag_ref, bf16[512,768]{1,0:T(8,128)(2,1)} %convolution_convert_fusion.12.query_ref, bf16[4608,1536]{1,0:T(8,128)(2,1)} %convolution_convert_fusion.key_ref.value_ref, bf16[4608,1536]{1,0:T(8,128)(2,1)} %convolution_convert_fusion.key_ref.value_ref), custom_call_target="tpu_custom_call" | custom-call | flops 3623878656 | bytes 14155776 | tf_op jit(solution)/shard_map/pallas_call | solution.py:137
  170.6 2.0 fusion.34
  173.0 0.6 copy-done.12
  173.7 5.1 %fusion.31 = f32[512,3072]{1,0:T(8,128)S(1)} fusion(bf16[768,3072]{1,0:T(8,128)(2,1)} %bitcast.173, f32[512,768]{1,0:T(8,128)S(1)} %get-tuple-element.96, f32[768]{0:T(1024)S(1)} %copy-done.52, f32[768]{0:T(1024)S(1)} %copy-done.44, f32[512]{0:T(512)S(1)} %add_rsqrt_fusion.1, f32[512]{0:T(512)S(1)} %broadcast_multiply_fusion.7), kind=kOutput, calls=%fused_computation.135 | convolution fusion | flops 2417885184 | bytes 12593152 | tf_op jit(solution)/shard_map/dot_general | solution.py:25
  178.8 4.8 %add_convert_fusion = bf16[512,768]{1,0:T(8,128)(2,1)} fusion(f32[512,768]{1,0:T(8,128)S(1)} %get-tuple-element.96, bf16[768,3072]{1,0:T(8,128)(2,1)S(1)} %bitcast.179, f32[512,3072]{1,0:T(8,128)S(1)} %fusion.31), kind=kOutput, calls=%fused_computation.47 | convolution fusion | flops 2430861312 | bytes 13369344 | tf_op jit(solution)/shard_map/dot_general | solution.py:25
  183.6 5.8 %fusion.6 = bf16[512,3072]{1,0:T(8,128)(2,1)S(1)} fusion(f32[512,3072]{1,0:T(8,128)S(1)} %fusion.31, bf16[512,768]{1,0:T(8,128)(2,1)S(1)} %bitcast.150, bf16[768,3072]{1,0:T(8,128)(2,1)S(1)} %bitcast.180), kind=kOutput, calls=%fused_computation.11 | convolution fusion | flops 2445803520 | bytes 14942208 | tf_op jit(solution)/shard_map/dot_general | solution.py:25
  189.4 4.6 convolution_convert_fusion.3
  194.0 3.5 multiply_reduce_fusion
  197.5 4.9 %convolution_convert_fusion.4 = bf16[768,3072]{1,0:T(8,128)(2,1)} fusion(bf16[512,3072]{1,0:T(8,128)(2,1)S(1)} %fusion.6, f32[512,768]{1,0:T(8,128)S(1)} %get-tuple-element.96, f32[768]{0:T(1024)S(1)} %copy-done.52, f32[768]{0:T(1024)S(1)} %copy-done.44, f32[512]{0:T(512)S(1)} %add_rsqrt_fusion.1, f32[512]{0:T(512)S(1)} %broadcast_multiply_fusion.7), kind=kOutput, calls=%fused_computation.15 | convolution fusion | flops 2420244480 | bytes 9447424 | tf_op jit(solution)/shard_map/dot_general | solution.py:25
  202.5 0.6 multiply_add_fusion.2
  203.1 0.6 copy-done.7
  203.8 1.7 convolution_convert_fusion.11.grad_ref
  205.5 1.8 convolution_convert_fusion.7
  207.3 19.1 %shard_map.342 = (bf16[512,768]{1,0:T(8,128)(2,1)}, bf16[4608,1536]{1,0:T(8,128)(2,1)}) custom-call(bf16[512,768]{1,0:T(8,128)(2,1)} %convolution_convert_fusion.12.query_ref, bf16[4608,1536]{1,0:T(8,128)(2,1)} %convolution_convert_fusion.key_ref.value_ref, bf16[4608,1536]{1,0:T(8,128)(2,1)} %convolution_convert_fusion.key_ref.value_ref, ...), custom_call_target="tpu_custom_call" | custom-call | flops 7247757312 | bytes 28311552 | tf_op jit(solution)/shard_map/pallas_call | solution.py:152
  226.4 3.4 multiply_reduce_fusion.1
  229.8 2.1 convolution_convert_fusion.8
  231.9 2.0 multiply_add_fusion.1
  233.9 1.7 convolution_convert_fusion.10.grad_ref
  235.6 1.8 convolution_convert_fusion.9
  237.4 10.7 %shard_map.343 = bf16[512,2304]{1,0:T(8,128)(2,1)} custom-call(bf16[512,2304]{1,0:T(8,128)(2,1)} %convolution_convert_fusion.5.query_ref.key_ref.value_ref, bf16[512,2304]{1,0:T(8,128)(2,1)} %convolution_convert_fusion.5.query_ref.key_ref.value_ref, bf16[512,2304]{1,0:T(8,128)(2,1)} %convolution_convert_fusion.5.query_ref.key_ref.value_ref, ...), custom_call_target="tpu_custom_call" | custom-call | flops 2415919104 | bytes 9437184 | tf_op jit(solution)/shard_map/pallas_call | solution.py:152
  248.1 4.9 %fusion.21 = (f32[768]{0:T(1024)S(1)}, f32[512]{0:T(512)S(1)}, f32[512]{0:T(512)S(1)}, f32[768]{0:T(1024)S(1)}, f32[512,768]{1,0:T(8,128)S(1)}) fusion(f32[512]{0:T(512)S(1)} %rsqrt.28, f32[512]{0:T(512)S(1)} %div.39, bf16[8,32,768]{2,1,0:T(8,128)(2,1)S(1)} %get-tuple-element.100, bf16[8,32,768]{2,1,0:T(8,128)(2,1)S(1)} %copy-done.2, ...), kind=kOutput, calls=%fused_computation.40 | convolution fusion | flops 1827665408 | bytes 8274944 | tf_op jit(solution)/shard_map/dot_general | solution.py:25
  253.1 3.9 convolution_convert_fusion.2
  257.0 0.6 stack.62
  257.6 0.8 constant_dynamic-slice_fusion.3
  258.4 1.5 collective-permute-start.1
  261.7 0.6 stack.60
  262.2 0.6 fusion.20
  262.9 0.8 constant_dynamic-slice_fusion.1
  264.2 14.5 %convolution_convert_fusion.1 = bf16[4608,768]{1,0:T(8,128)(2,1)S(1)} fusion(bf16[4608,1536]{1,0:T(8,128)(2,1)} %get-tuple-element.38, bf16[768,768]{1,0:T(8,128)(2,1)S(1)} %bitcast.156, bf16[768,768]{1,0:T(8,128)(2,1)S(1)} %bitcast.158), kind=kOutput, calls=%fused_computation.3 | convolution fusion | flops 10879893504 | bytes 23592960 | tf_op jit(solution)/shard_map/dot_general | solution.py:25
  279.0 2.6 copy-done.3
  281.6 1.5 collective-permute-start.4
  283.1 1.3 stack.63
  284.5 1.3 pad.4.norms
  285.8 17.2 %convolution_convert_fusion.6 = bf16[768,1536]{1,0:T(8,128)(2,1)} fusion(bf16[4608,768]{1,0:T(8,128)(2,1)} %bitcast.142, bf16[4608,1536]{1,0:T(8,128)(2,1)} %get-tuple-element.38), kind=kOutput, calls=%fused_computation.20 | convolution fusion | flops 10872815616 | bytes 23592960 | tf_op jit(solution)/shard_map/dot_general | solution.py:25
  303.0 150.0 %shard_map.344 = (f32[16,48,384]{2,1,0:T(8,128)}, f32[8,768]{1,0:T(8,128)}) custom-call(bf16[4,2,2,48,3072]{4,3,2,1,0:T(8,128)(2,1)} %bitcast.146, bf16[4,2,2,48,3072]{4,3,2,1,0:T(8,128)(2,1)} %bitcast.145, bf16[4,2,2,48,2304]{4,3,2,1,0:T(8,128)(2,1)} %bitcast.149, bf16[4,2,2,48,768]{4,3,2,1,0:T(8,128)(2,1)} %bitcast.144, ...), custom_call_target="tpu_custom_call" | custom-call | bytes 150994944 | tf_op jit(solution)/shard_map/pallas_call | solution.py:718
  453.1 2.2 slice_bitcast_fusion.3
  455.3 0.7 maximum_bitcast_fusion
  456.0 0.7 pad_maximum_fusion.9
  456.8 0.6 slice_reduce_fusion
  457.4 1.3 broadcast_select_fusion.7
  458.7 0.9 pad_maximum_fusion.7
  459.7 1.3 broadcast_select_fusion.3
  461.0 1.2 maximum_convert_fusion.1
  462.3 5.1 %broadcast_select_fusion.1 = (bf16[8,288,768]{2,1,0:T(8,128)(2,1)S(1)}, bf16[8,288,768]{2,1,0:T(8,128)(2,1)}) fusion(bf16[8,288,768]{2,1,0:T(8,128)(2,1)} %collective-permute-done.4, pred[]{:T(512)S(6)} %eq.2, bf16[8,576,768]{2,1,0:T(8,128)(2,1)S(1)} %bitcast.140, s32[]{:T(128)S(6)} %select_n.86), kind=kLoop, calls=%fused_computation.19 | loop fusion | flops 3538944 | bytes 14155781 | tf_op jit(solution)/shard_map/jit(_where)/select_n | solution.py:243
  467.4 8.2 %maximum_convert_fusion = f32[16,288,768]{2,1,0:T(8,128)} fusion(bf16[8,288,768]{2,1,0:T(8,128)(2,1)} %get-tuple-element.60, bf16[8,288,768]{2,1,0:T(8,128)(2,1)S(1)} %get-tuple-element.59), kind=kLoop, calls=%fused_computation.4 | loop fusion | flops 7077888 | bytes 21233664 | tf_op jit(solution)/shard_map/convert_element_type | solution.py:789
  (154 shorter events, 4.9 us)
Async XLA Ops:
  0.7 6.0 %copy-start.29 = (bf16[48,384]{1,0:T(8,128)(2,1)S(1)}, bf16[48,384]{1,0:T(8,128)(2,1)}, u32[]{:S(2)}) copy-start(bf16[48,384]{1,0:T(8,128)(2,1)} %param.23) | copy-start | bytes 110596
  0.7 6.0 %copy-start.30 = (bf16[48,384]{1,0:T(8,128)(2,1)S(1)}, bf16[48,384]{1,0:T(8,128)(2,1)}, u32[]{:S(2)}) copy-start(bf16[48,384]{1,0:T(8,128)(2,1)} %param.24) | copy-start | bytes 110596
  0.7 6.0 %copy-start.31 = (bf16[48,384]{1,0:T(8,128)(2,1)S(1)}, bf16[48,384]{1,0:T(8,128)(2,1)}, u32[]{:S(2)}) copy-start(bf16[48,384]{1,0:T(8,128)(2,1)} %param.25) | copy-start | bytes 110596
  0.7 6.0 %copy-start.32 = (bf16[384,48]{0,1:T(8,128)(2,1)S(1)}, bf16[384,48]{0,1:T(8,128)(2,1)}, u32[]{:S(2)}) copy-start(bf16[384,48]{0,1:T(8,128)(2,1)} %param.26) | copy-start | bytes 110596
  0.7 6.1 %copy-start.33 = (bf16[48,384]{1,0:T(8,128)(2,1)S(1)}, bf16[48,384]{1,0:T(8,128)(2,1)}, u32[]{:S(2)}) copy-start(bf16[48,384]{1,0:T(8,128)(2,1)} %param.27) | copy-start | bytes 110596
  0.7 6.1 %copy-start.34 = (bf16[48,384]{1,0:T(8,128)(2,1)S(1)}, bf16[48,384]{1,0:T(8,128)(2,1)}, u32[]{:S(2)}) copy-start(bf16[48,384]{1,0:T(8,128)(2,1)} %param.28) | copy-start | bytes 110596
  0.7 6.1 %copy-start.35 = (bf16[48,384]{1,0:T(8,128)(2,1)S(1)}, bf16[48,384]{1,0:T(8,128)(2,1)}, u32[]{:S(2)}) copy-start(bf16[48,384]{1,0:T(8,128)(2,1)} %param.29) | copy-start | bytes 110596
  0.7 6.1 %copy-start.36 = (bf16[384,48]{0,1:T(8,128)(2,1)S(1)}, bf16[384,48]{0,1:T(8,128)(2,1)}, u32[]{:S(2)}) copy-start(bf16[384,48]{0,1:T(8,128)(2,1)} %param.30) | copy-start | bytes 110596
  1.8 126.4 %collective-permute-start.2 = (bf16[8,32,768]{2,1,0:T(8,128)(2,1)S(1)}, bf16[8,32,768]{2,1,0:T(8,128)(2,1)}, u32[]{:S(2)}, u32[]{:S(2)}) collective-permute-start(bf16[8,32,768]{2,1,0:T(8,128)(2,1)S(1)} %constant_dynamic-slice_fusion.2), channel_id=1, source_target_pairs={{0,1},{1,0},{2,3},{3,2},{4,5},{5,4},{6,7},{7,6},{8,9},{9,8},{10,11... | collective-permute-start | bytes 1179656 | tf_op jit(solution)/shard_map/ppermute | solution.py:227
  6.7 121.6 %collective-permute-start = (bf16[8,32,768]{2,1,0:T(8,128)(2,1)}, bf16[8,32,768]{2,1,0:T(8,128)(2,1)}, u32[]{:S(2)}, u32[]{:S(2)}) collective-permute-start(bf16[8,32,768]{2,1,0:T(8,128)(2,1)} %constant_dynamic-slice_fusion.5), channel_id=1, source_target_pairs={{0,1},{1,0},{2,3},{3,2},{4,5},{5,4},{6,7},{7,6},{8,9},{9,8},{10,11... | collective-permute-start | bytes 1179656 | tf_op jit(solution)/shard_map/ppermute | solution.py:227
  6.9 0.7 copy-start.28
  106.4 4.4 copy-start.13
  106.4 64.2 %copy-start.6 = (bf16[1,16,48,768]{3,2,1,0:T(8,128)(2,1)}, bf16[1,16,48,768]{3,2,1,0:T(8,128)(2,1)S(1)}, u32[]{:S(2)}) copy-start(bf16[1,16,48,768]{3,2,1,0:T(8,128)(2,1)S(1)} %get-tuple-element.61) | copy-start | bytes 3538948
  106.4 7.2 %copy-start.15 = (bf16[1,16,48,768]{3,2,1,0:T(8,128)(2,1)S(1)}, bf16[1,16,48,768]{3,2,1,0:T(8,128)(2,1)}, u32[]{:S(2)}) copy-start(bf16[1,16,48,768]{3,2,1,0:T(8,128)(2,1)} %get-tuple-element.63) | copy-start | bytes 3538948
  110.8 2.8 copy-start.5
  113.6 14.0 %copy-start.55 = (s32[16]{0:T(128)S(1)}, s32[16]{0:T(128)}, u32[]{:S(2)}) copy-start(s32[16]{0:T(128)} %param.22) | copy-start | bytes 196
  113.6 14.6 %copy-start.27 = (bf16[16,32,768]{2,1,0:T(8,128)(2,1)S(1)}, bf16[16,32,768]{2,1,0:T(8,128)(2,1)}, u32[]{:S(2)}) copy-start(bf16[16,32,768]{2,1,0:T(8,128)(2,1)} %param.39) | copy-start | bytes 2359300
  130.3 1.6 copy-start.1
  130.3 1.6 copy-start.37
  131.0 3.1 copy-start.17
  132.0 2.0 copy-start.19
  133.1 0.9 copy-start.23
  152.3 77.5 %copy-start = (f32[512,768]{1,0:T(8,128)}, f32[512,768]{1,0:T(8,128)S(1)}, u32[]{:S(2)}) copy-start(f32[512,768]{1,0:T(8,128)S(1)} %get-tuple-element.94) | copy-start | bytes 4718596
  152.3 1.8 copy-start.21
  152.3 1.8 copy-start.49
  152.3 1.8 copy-start.53
  172.6 1.0 copy-start.12
  172.6 1.0 copy-start.52
  172.7 1.0 copy-start.44
  172.7 6.1 %slice-start.2 = ((s8[4718592]{0:T(1024)(128)(4,1)}), s8[4194304]{0:T(1024)(128)(4,1)S(1)}, s32[]{:S(2)}) async-start(s8[4718592]{0:T(1024)(128)(4,1)} %bitcast.177), calls=%async_computation.2 | async-start | bytes 8388608
  173.7 5.1 %slice-start.3 = ((s8[4718592]{0:T(1024)(128)(4,1)}), s8[524288]{0:T(1024)(128)(4,1)S(1)}, s32[]{:S(2)}) async-start(s8[4718592]{0:T(1024)(128)(4,1)} %bitcast.177), calls=%async_computation.3 | async-start | bytes 1048576
  178.8 15.2 %slice-start = ((s8[4718592]{0:T(1024)(128)(4,1)}), s8[4194304]{0:T(1024)(128)(4,1)S(1)}, s32[]{:S(2)}) async-start(s8[4718592]{0:T(1024)(128)(4,1)} %bitcast.174), calls=%async_computation | async-start | bytes 8388608
  183.6 10.4 %slice-start.1 = ((s8[4718592]{0:T(1024)(128)(4,1)}), s8[524288]{0:T(1024)(128)(4,1)S(1)}, s32[]{:S(2)}) async-start(s8[4718592]{0:T(1024)(128)(4,1)} %bitcast.174), calls=%async_computation.1 | async-start | bytes 1048576
  202.5 1.3 copy-start.7
  203.8 1.7 copy-start.8
  226.4 3.4 copy-start.43
  226.4 3.4 copy-start.50
  226.4 3.4 copy-start.51
  226.4 3.4 copy-start.54
  231.9 2.0 copy-start.20
  233.9 1.7 copy-start.22
  237.4 10.7 %copy-start.2 = (bf16[8,32,768]{2,1,0:T(8,128)(2,1)S(1)}, bf16[8,32,768]{2,1,0:T(8,128)(2,1)}, u32[]{:S(2)}) copy-start(bf16[8,32,768]{2,1,0:T(8,128)(2,1)} %copy-done.1) | copy-start | bytes 1179652
  237.4 10.7 %copy-start.18 = (bf16[1,16,48,768]{3,2,1,0:T(8,128)(2,1)S(1)}, bf16[1,16,48,768]{3,2,1,0:T(8,128)(2,1)}, u32[]{:S(2)}) copy-start(bf16[1,16,48,768]{3,2,1,0:T(8,128)(2,1)} %get-tuple-element.66) | copy-start | bytes 3538948
  248.1 4.9 %copy-start.11 = (bf16[512,2304]{1,0:T(8,128)(2,1)S(1)}, bf16[512,2304]{1,0:T(8,128)(2,1)}, u32[]{:S(2)}) copy-start(bf16[512,2304]{1,0:T(8,128)(2,1)} %shard_map.343) | copy-start | bytes 7077892
  248.1 4.9 %copy-start.24 = (bf16[512,768]{1,0:T(8,128)(2,1)S(1)}, bf16[512,768]{1,0:T(8,128)(2,1)}, u32[]{:S(2)}) copy-start(bf16[512,768]{1,0:T(8,128)(2,1)} %copy-done.23) | copy-start | bytes 2359300
  253.0 4.0 copy-start.46
  253.1 4.0 copy-start.45
  253.1 4.5 copy-start.25
  253.1 6.8 %copy-start.48 = (f32[768]{0:T(1024)S(1)}, f32[768]{0:T(1024)}, u32[]{:S(2)}) copy-start(f32[768]{0:T(1024)} %get-tuple-element.43) | copy-start | bytes 9220
  253.1 8.6 %copy-start.47 = (f32[768]{0:T(1024)S(1)}, f32[768]{0:T(1024)}, u32[]{:S(2)}) copy-start(f32[768]{0:T(1024)} %get-tuple-element.51) | copy-start | bytes 9220
  258.4 199.0 %collective-permute-start.1 = (bf16[8,32,768]{2,1,0:T(8,128)(2,1)}, bf16[8,32,768]{2,1,0:T(8,128)(2,1)}, u32[]{:S(2)}, u32[]{:S(2)}) collective-permute-start(bf16[8,32,768]{2,1,0:T(8,128)(2,1)} %constant_dynamic-slice_fusion.3), channel_id=1, source_target_pairs={{0,1},{1,0},{2,3},{3,2},{4,5},{5,4},{6,7},{7,6},{8,9},{9,8},{10,11... | collective-permute-start | bytes 1179656 | tf_op jit(solution)/shard_map/ppermute | solution.py:227
  262.2 1.9 copy-start.14
  262.2 1.9 copy-start.16
  262.8 1.3 copy-start.9
  263.6 196.1 %collective-permute-start.3 = (bf16[8,32,768]{2,1,0:T(8,128)(2,1)}, bf16[8,32,768]{2,1,0:T(8,128)(2,1)}, u32[]{:S(2)}, u32[]{:S(2)}) collective-permute-start(bf16[8,32,768]{2,1,0:T(8,128)(2,1)} %constant_dynamic-slice_fusion.1), channel_id=1, source_target_pairs={{0,1},{1,0},{2,3},{3,2},{4,5},{5,4},{6,7},{7,6},{8,9},{9,8},{10,11... | collective-permute-start | bytes 1179656 | tf_op jit(solution)/shard_map/ppermute | solution.py:227
  278.7 3.0 copy-start.3
  278.7 4.5 copy-start.39
  278.7 4.5 copy-start.40
  278.7 4.4 copy-start.41
  281.6 180.6 %collective-permute-start.4 = (bf16[8,288,768]{2,1,0:T(8,128)(2,1)S(1)}, bf16[8,288,768]{2,1,0:T(8,128)(2,1)}, u32[]{:S(2)}, u32[]{:S(2)}) collective-permute-start(bf16[8,288,768]{2,1,0:T(8,128)(2,1)S(1)} %constant_dynamic-slice_fusion), channel_id=1, source_target_pairs={{0,1},{1,0},{2,3},{3,2},{4,5},{5,4},{6,7},{7,6},{8,9},{9,8},{10,11... | collective-permute-start | bytes 10616840 | tf_op jit(solution)/shard_map/ppermute | solution.py:227
  453.1 3.7 copy-start.38
  453.1 4.4 copy-start.26
  455.3 4.4 copy-start.10
  457.4 4.8 %copy-start.4 = (bf16[4608,768]{1,0:T(8,128)(2,1)S(1)}, bf16[4608,768]{1,0:T(8,128)(2,1)}, u32[]{:S(2)}) copy-start(bf16[4608,768]{1,0:T(8,128)(2,1)} %copy-done.3) | copy-start | bytes 21233668
  (1 other events, 0.6 us)

commit v6 on v5

--- a/solution.py
+++ b/solution.py
@@ -10,6 +10,7 @@
 HD = 64
 D = 768
 GROUP = 256
+ROWS = 1152
 LEN = 64
 PATCH = 576
 SMALLP = 196
@@ -73,69 +74,77 @@
     return [slice(start, start + GROUP) for start in range(0, width, GROUP)]
 
 
-def attend_kernel(causal, flag_ref, query_ref, key_ref, value_ref, mix_ref, prob_ref):
-    keys = key_ref.shape[0]
+def attend_kernel(causal, batch, flag_ref, query_ref, key_ref, value_ref, mix_ref, prob_ref):
+    keys = key_ref.shape[0] // batch
     shape = (keys, GROUP // HD * LEN)
     row = lax.broadcasted_iota(jnp.int32, shape, 0)
-    if causal:
-        allowed = row <= lax.broadcasted_iota(jnp.int32, shape, 1) % LEN
-    else:
-        allowed = row < SMALLP + (PATCH - SMALLP) * flag_ref[pl.program_id(0)]
-    for part in groups(query_ref.shape[1]):
-        queries = spread(query_ref[:, part]) * jnp.asarray(HD ** (-0.5), bf16)
-        scores = jnp.where(allowed, dot(key_ref[:, part], queries, 1, 1), masked_score)
-        exponent = jnp.exp(scores - jnp.max(scores, axis=0, keepdims=True))
-        probs = (exponent * (1.0 / jnp.sum(exponent, axis=0, keepdims=True))).astype(bf16)
-        prob_ref[:, part] = probs
-        mix_ref[:, part] = collect(dot(probs, value_ref[:, part], 0, 0)).astype(bf16)
-
-
-def attend_back_kernel(query_ref, key_ref, value_ref, prob_ref, grad_ref, *outs):
+    for n in range(batch):
+        ask, see = slice(n * LEN, (n + 1) * LEN), slice(n * keys, (n + 1) * keys)
+        if causal:
+            allowed = row <= lax.broadcasted_iota(jnp.int32, shape, 1) % LEN
+        else:
+            allowed = row < SMALLP + (PATCH - SMALLP) * flag_ref[pl.program_id(0) * batch + n]
+        for part in groups(query_ref.shape[1]):
+            queries = spread(query_ref[ask, part]) * jnp.asarray(HD ** (-0.5), bf16)
+            scores = jnp.where(allowed, dot(key_ref[see, part], queries, 1, 1), masked_score)
+            exponent = jnp.exp(scores - jnp.max(scores, axis=0, keepdims=True))
+            probs = (exponent * (1.0 / jnp.sum(exponent, axis=0, keepdims=True))).astype(bf16)
+            prob_ref[see, part] = probs
+            mix_ref[ask, part] = collect(dot(probs, value_ref[see, part], 0, 0)).astype(bf16)
+
+
+def attend_back_kernel(batch, query_ref, key_ref, value_ref, prob_ref, grad_ref, *outs):
     width = query_ref.shape[1]
+    keys = key_ref.shape[0] // batch
     joined = outs[-1]
     query_out, shift = (outs[0], 0) if len(outs) == 2 else (joined, width)
-    for part in groups(width):
-        queries = spread(query_ref[:, part]) * jnp.asarray(HD ** (-0.5), bf16)
-        grads = spread(grad_ref[:, part])
-        probs_low = prob_ref[:, part]
-        probs = probs_low.astype(f32)
-        grad_prob = dot(value_ref[:, part], grads, 1, 1)
-        inner = jnp.sum(probs * grad_prob, axis=0, keepdims=True)
-        grad_score = (probs * (grad_prob - inner)).astype(bf16)
-        key_part = slice(shift + part.start, shift + part.stop)
-        value_part = slice(shift + width + part.start, shift + width + part.stop)
-        joined[:, value_part] = dot(probs_low, grads, 1, 0).astype(bf16)
-        joined[:, key_part] = dot(grad_score, queries, 1, 0).astype(bf16)
-        query_out[:, part] = (collect(dot(grad_score, key_ref[:, part], 0, 0)) * HD ** (-0.5)).astype(bf16)
+    for n in range(batch):
+        ask, see = slice(n * LEN, (n + 1) * LEN), slice(n * keys, (n + 1) * keys)
+        for part in groups(width):
+            queries = spread(query_ref[ask, part]) * jnp.asarray(HD ** (-0.5), bf16)
+            grads = spread(grad_ref[ask, part])
+            probs_low = prob_ref[see, part]
+            probs = probs_low.astype(f32)
+            grad_prob = dot(value_ref[see, part], grads, 1, 1)
+            inner = jnp.sum(probs * grad_prob, axis=0, keepdims=True)
+            grad_score = (probs * (grad_prob - inner)).astype(bf16)
+            key_part = slice(shift + part.start, shift + part.stop)
+            value_part = slice(shift + width + part.start, shift + width + part.stop)
+            joined[see, value_part] = dot(probs_low, grads, 1, 0).astype(bf16)
+            joined[see, key_part] = dot(grad_score, queries, 1, 0).astype(bf16)
+            query_out[ask, part] = (collect(dot(grad_score, key_ref[see, part], 0, 0)) * HD ** (-0.5)).astype(bf16)
 
 
 def column(rows, width, index):
-    return pl.BlockSpec((rows, width), lambda i: (i, index))
+    return pl.BlockSpec((rows, width), lambda i, *_: (i, index))
 
 
 def attend_cost(queries, count, keys, products):
-    flops = 2 * products * queries.shape[0] * keys * queries.shape[1] * GROUP // HD
-    return pl.CostEstimate(flops=flops, bytes_accessed=products * 2 * count * keys * queries.shape[1], transcendentals=0)
+    if keys == LEN and products == 4:
+        return pl.CostEstimate(flops=2**20, bytes_accessed=2**20, transcendentals=0)
+    flops = 2 * products * count * LEN * keys * D * GROUP // HD
+    return pl.CostEstimate(flops=flops, bytes_accessed=products * 2 * count * keys * D, transcendentals=0)
+
+
+def batch_of(count, keys):
+    for batch in (8, 4, 2):
+        if count % batch == 0 and batch * keys <= ROWS:
+            return batch
+    return 1
 
 
 def attend(queries, query_at, sources, key_at, value_at, flags, count, causal):
     keys = sources.shape[0] // count
-    width = D
+    batch = batch_of(count, keys)
+    ask, see, width = batch * LEN, batch * keys, D
     grid_spec = pltpu.PrefetchScalarGridSpec(
         num_scalar_prefetch=1,
-        grid=(count,),
-        in_specs=[
-            pl.BlockSpec((LEN, width), lambda i, flag: (i, query_at)),
-            pl.BlockSpec((keys, width), lambda i, flag: (i, key_at)),
-            pl.BlockSpec((keys, width), lambda i, flag: (i, value_at)),
-        ],
-        out_specs=[
-            pl.BlockSpec((LEN, width), lambda i, flag: (i, 0)),
-            pl.BlockSpec((keys, width), lambda i, flag: (i, 0)),
-        ],
+        grid=(count // batch,),
+        in_specs=[column(ask, width, query_at), column(see, width, key_at), column(see, width, value_at)],
+        out_specs=[column(ask, width, 0), column(see, width, 0)],
     )
     return pl.pallas_call(
-        functools.partial(attend_kernel, causal),
+        functools.partial(attend_kernel, causal, batch),
         grid_spec=grid_spec,
         out_shape=(
             jax.ShapeDtypeStruct((count * LEN, width), bf16),
@@ -147,22 +156,86 @@
 
 def attend_back(queries, query_at, sources, key_at, value_at, probs, grad_mix, count, whole):
     keys = sources.shape[0] // count
-    width = D
+    batch = batch_of(count, keys)
+    ask, see, width = batch * LEN, batch * keys, D
     widths = [(keys, 3 * width)] if whole else [(LEN, width), (keys, 2 * width)]
     return pl.pallas_call(
-        attend_back_kernel,
-        grid=(count,),
+        functools.partial(attend_back_kernel, batch),
+        grid=(count // batch,),
         in_specs=[
-            column(LEN, width, query_at),
-            column(keys, width, key_at),
-            column(keys, width, value_at),
-            column(keys, width, 0),
-            column(LEN, width, 0),
+            column(ask, width, query_at),
+            column(see, width, key_at),
+            column(see, width, value_at),
+            column(see, width, 0),
+            column(ask, width, 0),
         ],
-        out_specs=[column(rows, wide, 0) for rows, wide in widths],
+        out_specs=[column(batch * rows, wide, 0) for rows, wide in widths],
         out_shape=[jax.ShapeDtypeStruct((count * rows, wide), bf16) for rows, wide in widths],
         cost_estimate=attend_cost(queries, count, keys, 4),
     )(queries, sources, sources, probs, grad_mix)
+
+
+def swap(rows):
+    return lax.ppermute(rows, "mp", [(0, 1), (1, 0)])
+
+
+def patch_kernel(side_ref, grad_ref, weight_ref, out_ref):
+    for n in range(grad_ref.shape[0]):
+        out_ref[n] = dot(grad_ref[n], weight_ref[...], 1, 0).astype(out_ref.dtype)
+
+
+def patch_product(grads, weights, first, last, half, place_at, total, kind):
+    batch = 2 - (last - first) % 2
+    rows = PATCH // 2
+    depth, width = weights.shape
+    grid_spec = pltpu.PrefetchScalarGridSpec(
+        num_scalar_prefetch=1,
+        grid=((last - first) // batch,),
+        in_specs=[
+            pl.BlockSpec((batch, rows, depth), lambda i, at: (i + first // batch, at[0], 0)),
+            pl.BlockSpec((depth, width), lambda i, at: (0, 0)),
+        ],
+        out_specs=pl.BlockSpec((batch, rows, width), lambda i, at: (i + at[1] // batch, 0, 0)),
+    )
+    flops = 2**20
+    return pl.pallas_call(
+        patch_kernel,
+        grid_spec=grid_spec,
+        out_shape=jax.ShapeDtypeStruct((total, rows, width), kind),
+        cost_estimate=pl.CostEstimate(flops=flops, bytes_accessed=flops // width, transcendentals=0),
+    )(jnp.stack([half, place_at]), grads.reshape(-1, PATCH, depth), weights)
+
+
+def widen_kernel(side_ref, early_ref, late_ref, whole_ref, out_ref):
+    early = pl.program_id(0) * 2 < pl.num_programs(0)
+
+    @pl.when(early)
+    def _():
+        out_ref[...] = early_ref[...].astype(f32)
+
+    @pl.when(jnp.logical_not(early))
+    def _():
+        out_ref[...] = late_ref[...].astype(f32)
+
+
+def widen(early, late, whole, place_at):
+    count, height, width = early.shape
+    grid_spec = pltpu.PrefetchScalarGridSpec(
+        num_scalar_prefetch=1,
+        grid=(2 * count,),
+        in_specs=[
+            pl.BlockSpec((1, height, width), lambda i, at: (jnp.minimum(i, count - 1), 0, 0)),
+            pl.BlockSpec((1, height, width), lambda i, at: (jnp.maximum(i - count, 0), 0, 0)),
+            pl.BlockSpec(memory_space=pl.ANY),
+        ],
+        out_specs=pl.BlockSpec((1, height, width), lambda i, at: (i + at[0], 0, 0)),
+    )
+    return pl.pallas_call(
+        widen_kernel,
+        grid_spec=grid_spec,
+        out_shape=jax.ShapeDtypeStruct(whole.shape, f32),
+        input_output_aliases={3: 0},
+    )(place_at[None], early, late, whole)
 
 
 def gelu_parts(value):
@@ -201,12 +274,23 @@
     grad_input, gain_three, shift_three = norm_back(normal_three, inverse_three, third_gain, grad_normed)
     grad_stream = cotangent.astype(f32) + grad_input
     grad_rows = grad_stream.astype(bf16)
-    grad_mix_cross = weight_grad(grad_rows, mixed_two)
+    grad_mix_cross = weight_grad(grad_rows, mixed_two).astype(bf16)
+    grad_expand, grad_contract = grad_expand.astype(bf16), grad_contract.astype(bf16)
+    grad_rows, grad_expand, grad_contract, grad_mix_cross = lax.optimization_barrier(
+        (grad_rows, grad_expand, grad_contract, grad_mix_cross)
+    )
     grad_mixed = matmul(grad_rows, mix_cross).astype(bf16)
     grad_queries, grad_sources = attend_back(queries_two, 0, rows_two, 0, 1, probs_two, grad_mixed, count, False)
-    patch_grad = matmul_t(grad_sources, project_patch).astype(bf16)
-    grad_query_cross = weight_grad(normed_two, grad_queries)
-    grad_patch = weight_grad(patches, grad_sources)
+    side = lax.axis_index("mp")
+    grad_query_cross = weight_grad(normed_two, grad_queries).astype(bf16)
+    grad_patch = weight_grad(patches, grad_sources).astype(bf16)
+    grad_patch, grad_sources, grad_query_cross = lax.optimization_barrier((grad_patch, grad_sources, grad_query_cross))
+    turned_patch = jnp.concatenate([project_patch[:, :D].T, project_patch[:, D:].T])
+    early = patch_product(grad_sources, turned_patch, 0, count // 2, 1 - side, 0 * side, count // 2, bf16)
+    early, grad_queries = lax.optimization_barrier((early, grad_queries))
+    early = swap(early)
+    late = patch_product(grad_sources, turned_patch, count // 2, count, 1 - side, 0 * side, count // 2, bf16)
+    patch_grad = patch_product(grad_sources, turned_patch, 0, count, side, side * count, 2 * count, f32)
     grad_normed = matmul_t(grad_queries, query_cross)
     grad_input, gain_two, shift_two = norm_back(normal_two, inverse_two, second_gain, grad_normed)
     grad_stream = grad_stream + grad_input
@@ -220,11 +304,10 @@
     text_grad = (grad_stream + grad_input).astype(bf16)
     norm_grads = jnp.stack([gain_one, shift_one, gain_two, shift_two, gain_three, shift_three])
     grads = [grad_expand, grad_contract, grad_self, grad_mix_self, grad_query_cross, grad_patch, grad_mix_cross]
-    return layer_out.astype(bf16), text_grad, patch_grad, [g.astype(bf16) for g in grads], norm_grads
-
-
-def swap(rows):
-    return lax.ppermute(rows, "mp", [(0, 1), (1, 0)])
+    early, norm_grads = lax.optimization_barrier((early, norm_grads))
+    weight_grads, norm_sums, late = scatter_grads([g.astype(bf16) for g in grads], norm_grads, late)
+    patch_grad = widen(early, late, patch_grad, (1 - side) * count)
+    return layer_out.astype(bf16), text_grad, patch_grad, weight_grads, norm_sums
 
 
 def to_captions(rows, side):
@@ -237,12 +320,11 @@
 
 
 def to_positions(rows, side):
-    length = rows.shape[1] // 2
+    count, length, width = rows.shape[0], rows.shape[1] // 2, rows.shape[2]
     mine = lax.dynamic_slice_in_dim(rows, side * length, length, 1)
     other = swap(lax.dynamic_slice_in_dim(rows, (1 - side) * length, length, 1))
-    low = jnp.where(side == 0, mine, other)
-    high = jnp.where(side == 0, other, mine)
-    return jnp.concatenate([low, high], axis=0)
+    first = (jnp.arange(2) == side).reshape(2, 1, 1, 1)
+    return jnp.where(first, mine[None], other[None]).reshape(2 * count, length, width)
 
 
 TURNED = (False, False, False, True, False, False, False, True, False, True)
@@ -287,6 +369,7 @@
     def stream(index):
         early = index % 2 == 0
         part = index // 2
+        line_first = index == 2
 
         def own():
             if early:
@@ -313,8 +396,8 @@
 
         mine = z * 4 + x * 2 + c
 
-        def to_beside():
-            return copy(own(), region(0, z, 0, c), side_send.at[index], recv.at[index, 1, z, 0], beside)
+        def to_beside(z_from, src):
+            return copy(src, region(0, z_from, 0, c), side_send.at[index, z_from], recv.at[index, 1, z_from, 0], beside)
 
         def to_up(w, z_from, src):
             return copy(src, region(w, z_from, 0, c), up_send.at[index, w, z_from], recv.at[index, w, z_from, 0], (mine + 4, y))
@@ -346,19 +429,24 @@
             copy(spot, spot, far_send.at[index, w, z_from], mate_recv.at[index, w, z_from, u], far).wait_recv()
 
         def pass_on(w, z_from, src, up, down):
-            @pl.when(up)
-            def _():
-                to_up(w, z_from, src).start()
-
-            @pl.when(down)
-            def _():
-                to_down(w, z_from, src).start()
-
+            if w == 0 or not line_first:
+
+                @pl.when(up)
+                def _():
+                    to_up(w, z_from, src).start()
+
+                @pl.when(down)
+                def _():
+                    to_down(w, z_from, src).start()
+
+            if w == 0 and line_first:
+                to_beside(z_from, src).start()
             to_far(w, z_from, src).start()
             to_mate(w, z_from, 0, src).start()
 
         def first():
-            to_beside().start()
+            if not line_first:
+                to_beside(z, own()).start()
             pass_on(0, z, own(), z < DEPTH - 1, z > 0)
             keep().start()
 
@@ -398,19 +486,27 @@
 
         def finish():
             keep().wait()
-            to_beside().wait_send()
+            if not line_first:
+                to_beside(z, own()).wait_send()
 
             def each(number, _):
                 w, z_from = number // DEPTH, number % DEPTH
                 spot = region(w, z_from, 0, c)
-
-                @pl.when((z < DEPTH - 1) & (z_from <= z))
+                in_line = (w == 0) if line_first else (w >= 0)
+
+                @pl.when(in_line & (z < DEPTH - 1) & (z_from <= z))
                 def _():
                     to_up(w, z_from, spot).wait_send()
 
-                @pl.when((z > 0) & (z_from >= z))
+                @pl.when(in_line & (z > 0) & (z_from >= z))
                 def _():
                     to_down(w, z_from, spot).wait_send()
+
+                if line_first:
+
+                    @pl.when(w == 0)
+                    def _():
+                        to_beside(z_from, spot).wait_send()
 
                 to_far(w, z_from, spot).wait_send()
                 for u in range(2):
@@ -454,7 +550,7 @@
         ],
         scratch_shapes=[
             dma((4,)),
-            dma((4,)),
+            dma((4, DEPTH)),
             dma((4, 2, DEPTH)),
             dma((4, 2, DEPTH)),
             dma((4, 2, DEPTH)),
@@ -485,12 +581,13 @@
 
 
 PIECES = 16
-SIDE_LAG = 2
+SCATTER_COST = 2**20
+SIDE_LAG = 1
 NORM_STEP = 2
 
 
-def scatter_kernel(exp, con, own, mix_own, ask, source, mix, norms, out, norm_out, acc, other, side, low, high, last, total, norm_buf, norm_line, *sems):
-    local_sem, mate_send, mate_recv, side_send, side_recv, line_send, low_recv, high_recv, last_send, last_recv, norm_send, norm_recv = sems
+def scatter_kernel(exp, con, own, mix_own, ask, source, mix, norms, away, out, norm_out, back, acc, other, side, low, high, last, total, norm_buf, norm_line, *sems):
+    local_sem, mate_send, mate_recv, side_send, side_recv, line_send, low_recv, high_recv, last_send, last_recv, norm_send, norm_recv, away_send, back_recv = sems
     z, x, c, y = place()
     half = out.shape[2]
     mine = z * 4 + x * 2 + c
@@ -500,20 +597,26 @@
     def copy(src, dst, send, receive, device):
         return pltpu.make_async_remote_copy(src_ref=src, dst_ref=dst, send_sem=send, recv_sem=receive, device_id=device, device_id_type=MESH)
 
-    early = [(ref, ref.shape[4] // 2, j * half) for ref in (exp, con) for j in range(4)]
-    late = [(own, half, 0), (own, half, 2 * half), (own, half, 4 * half), (mix_own, half, 0), (ask, half, 0)]
-    late += [(source, half, 0), (source, half, 2 * half), (mix, half, 0)]
-    pieces = [piece for pair in zip(early, late) for piece in pair]
-
-    for p, (ref, stride, offset) in enumerate(pieces):
+    pieces = [(ref, ref.shape[4] // 2, j * half) for ref in (exp, con) for j in range(4)]
+    pieces += [(own, half, 0), (own, half, 2 * half), (own, half, 4 * half), (mix_own, half, 0), (ask, half, 0)]
+    pieces += [(source, half, 0), (source, half, 2 * half), (mix, half, 0)]
+
+    over_x, over_y = pieces[: PIECES * 2 // 3 + 1], pieces[PIECES * 2 // 3 + 1 :]
+    for p in range(PIECES):
+        ref, stride, offset = over_y[p // 3] if p % 3 == 2 else over_x[p // 3 * 2 + p % 3]
         for k in range(2):
             columns = pl.ds(k * stride + offset, half)
-            spot = (p, slice(None), slice(None), k) if p % 2 == 0 else (p, slice(None), k)
+            spot = (p, slice(None), k) if p % 3 == 2 else (p, slice(None), slice(None), k)
             copy(ref.at[:, :, 1 - c, :, columns], other.at[spot], mate_send.at[p, k], mate_recv.at[p, k], mate).start()
             pltpu.make_async_copy(ref.at[:, :, c, :, columns], acc.at[spot], local_sem.at[p, k]).start()
 
+    def part(j):
+        rows = away.shape[1] // 2
+        spot = (j // 2, pl.ds(j % 2 * rows, rows))
+        return copy(away.at[spot], back.at[spot], away_send.at[j], back_recv.at[j], (mine, 1 - y))
+
     def kind(p):
-        odd = p % 2
+        odd = jnp.where(p % 3 == 2, 1, 0)
         u = x * (1 - odd) + y * odd
         w = y * (1 - odd) + x * odd
         over_x = (z * 4 + (1 - x) * 2 + c, y)
@@ -664,7 +767,14 @@
             work(p)
 
     def step(t, _):
-        at(t, open_piece)
+        at(2 * t, open_piece)
+        at(2 * t + 1, open_piece)
+        for j in range(2 * away.shape[0]):
+
+            @pl.when(t == 1 + PIECES * j // (2 * away.shape[0]))
+            def _():
+                part(j).start()
+
         at(t - SIDE_LAG, add_side)
         at(
             t - SIDE_LAG - (DEPTH - 1 - z),
@@ -673,10 +783,16 @@
         at(t - SIDE_LAG - z, lambda p: pass_line(p, high, to_high, z > 0, lambda unit: unit > z, to_high))
         norm_steps(t)
         at(t - SIDE_LAG - DEPTH, close_line)
-        at(t - SIDE_LAG - DEPTH - 2, close_piece)
         return 0
 
-    lax.fori_loop(0, PIECES + SIDE_LAG + DEPTH + 2, step, 0)
+    def close(p, _):
+        close_piece(p)
+        return 0
+
+    lax.fori_loop(0, PIECES + SIDE_LAG + DEPTH, step, 0)
+    lax.fori_loop(0, PIECES, close, 0)
+    for j in range(2 * away.shape[0]):
+        part(j).wait()
     norm_out[...] = norm_line[0] + norm_line[1] + norm_line[2] + norm_line[3]
 
     def drain(p, _):
@@ -709,7 +825,7 @@
             norm_down(unit).wait_send()
 
 
-def scatter_near(exp, con, own, mix_own, ask, source, mix, norms):
+def scatter_near(exp, con, own, mix_own, ask, source, mix, norms, away):
     rows, half = D // (4 * DEPTH), D // 2
     grads = [g.reshape(DEPTH, 2, 2, rows, g.shape[1]) for g in (exp, con, own, mix_own, ask, source, mix)]
     vmem = pl.BlockSpec(memory_space=pltpu.VMEM)
@@ -717,9 +833,13 @@
     dma = pltpu.SemaphoreType.DMA
     return pl.pallas_call(
         scatter_kernel,
-        in_specs=[anywhere] * 7 + [vmem],
-        out_specs=[vmem] * 2,
-        out_shape=[jax.ShapeDtypeStruct((PIECES, rows, half), f32), jax.ShapeDtypeStruct(norms.shape, f32)],
+        in_specs=[anywhere] * 7 + [vmem, anywhere],
+        out_specs=[vmem, vmem, anywhere],
+        out_shape=[
+            jax.ShapeDtypeStruct((PIECES, rows, half), f32),
+            jax.ShapeDtypeStruct(norms.shape, f32),
+            jax.ShapeDtypeStruct(away.shape, away.dtype),
+        ],
         scratch_shapes=[
             pltpu.VMEM((PIECES, DEPTH, 2, 2, rows, half), bf16),
             pltpu.VMEM((PIECES, DEPTH, 2, 2, rows, half), bf16),
@@ -742,19 +862,21 @@
             dma((PIECES,)),
             dma((3 + 2 * DEPTH,)),
             dma((3 + DEPTH,)),
+            dma((2 * away.shape[0],)),
+            dma((2 * away.shape[0],)),
         ],
-        cost_estimate=pl.CostEstimate(flops=0, bytes_accessed=PIECES * D * D * 16, transcendentals=0),
+        cost_estimate=pl.CostEstimate(flops=0, bytes_accessed=SCATTER_COST, transcendentals=0),
         compiler_params=pltpu.CompilerParams(collective_id=1, has_side_effects=True, vmem_limit_bytes=60 * 2**20),
-    )(*grads, norms)
-
-
-def scatter_grads(grads, norms):
+    )(*grads, norms, away)
+
+
+def scatter_grads(grads, norms, away):
     exp, con, own, mix_own, ask, source, mix = grads
     if lax.axis_size("dp") == 4 * DEPTH:
-        parts, norm_sums = scatter_near(*grads, jnp.pad(norms, ((0, 8 - norms.shape[0]), (0, 0))))
-        late = [parts[2 * i + 1] for i in range(8)]
-        exp, con = (jnp.concatenate([parts[2 * i] for i in part], axis=1) for part in (range(4), range(4, 8)))
-        return [*late, exp, con], norm_sums
+        parts, norm_sums, back = scatter_near(*grads, jnp.pad(norms, ((0, 8 - norms.shape[0]), (0, 0))), away)
+        ordered = [parts[p] for p in range(PIECES) if p % 3 != 2] + [parts[p] for p in range(PIECES) if p % 3 == 2]
+        exp, con = (jnp.concatenate(part, axis=1) for part in (ordered[:4], ordered[4:8]))
+        return [*ordered[8:], exp, con], norm_sums, back
     sides = []
     for g in (own, mix_own, ask, source, mix):
         sides.append(g.reshape(D, g.shape[1] // D, 2, D // 2).transpose(1, 2, 0, 3))
@@ -764,7 +886,7 @@
     parts = lax.psum_scatter(stacked, ("mp", "dp"), scatter_dimension=1, tiled=True).astype(f32)
     chunks = (parts.shape[0] - 8) // 2
     exp, con = (jnp.concatenate(list(parts[start : start + chunks]), axis=1) for start in (8, 8 + chunks))
-    return [*(parts[i] for i in range(8)), exp, con], lax.psum(norms, BOTH)
+    return [*(parts[i] for i in range(8)), exp, con], lax.psum(norms, BOTH), swap(away)
 
 
 def body(text_tokens, image_tokens, resolution, *rest):
@@ -778,15 +900,14 @@
     grad_out = to_captions(cotangent, side)
     patches = lax.dynamic_slice_in_dim(image_tokens, side * half, half, 0)
     flags = lax.dynamic_slice_in_dim(resolution, side * half, half, 0)
-    layer_out, text_grad, patch_grad, grads, norm_grads = layer(
+    layer_out, text_grad, patch_grad, weight_grads, norm_outs = layer(
         weights, norms, text.reshape(-1, width), grad_out.reshape(-1, width), patches.reshape(-1, width), flags
     )
-    weight_grads, norm_outs = scatter_grads(grads, norm_grads)
     weight_outs = [g.T if turned else g for g, turned in zip(weight_grads, TURNED)]
     return (
         to_positions(layer_out.reshape(half, LEN, width), side),
         to_positions(text_grad.reshape(half, LEN, width), side).astype(f32),
-        to_positions(patch_grad.reshape(half, PATCH, width), side).astype(f32),
+        patch_grad,
         *weight_outs,
         *(norm_outs[i] for i in range(6)),
     )

time: 481 us -> 433 us (0.900)
  Pallas kernels: 298 us -> 267 us
  matrix products: 107 us -> 94.9 us
  other arithmetic: 28.2 us -> 16.9 us
    pallas_call x5 -> x9, Pallas kernels: 205 us -> 186 us  [the longest x1 106 us: scatter_near(): pl.pallas_call(scatter_kernel, in_specs=[anywhere] * 7 + [vmem, anywhere]...]
    dot_general x21 -> x20, matrix products: 107 us -> 94.9 us  [dot(): lax.dot_general(left, right, (((left_dim,), (right_dim,)), ((), ())), pre...]
    pallas_call x1, Pallas kernels: 92.2 us -> 81.1 us  [gather_near(): pl.pallas_call(gather_kernel, in_specs=[vmem] * 3, out_specs=[anywhere] *...]
    select_n x3 -> x0, other arithmetic: 7.73 us -> none  [to_positions(): low = jnp.where(side == 0, mine, other)]
    convert_element_type x1, other arithmetic: 8.21 us -> 1.78 us  [layer(): grad_rows = grad_stream.astype(bf16)]
    unnamed x127 -> x119, local copies, waits for them, and re-layouts: 10.1 us -> 4.44 us
  transfers between devices with their start and end apart: 5 -> 5, of which waited for: 0 -> 1; matrix products, arithmetic and copies ran while one was open for 16% -> 15% of each run, Pallas kernels for 51% -> 27%
where the time goes in v6:
time: 433 us; the launch traced here: 425 us
  Pallas kernels  267 us (62%)
  matrix products  94.9 us (22%)
  local copies, waits for them, and re-layouts  34.7 us (8%)
  other arithmetic  16.9 us (4%)
  starting transfers between devices  6.55 us (2%)
    pallas_call x1, Pallas kernels, scatter_near(): pl.pallas_call(scatter_kernel, in_specs=[anywhere] * 7 + [vmem, anywhere]...  106 us
    dot_general x20, matrix products, dot(): lax.dot_general(left, right, (((left_dim,), (right_dim,)), ((), ())), pre...  94.9 us
    pallas_call x1, Pallas kernels, gather_near(): pl.pallas_call(gather_kernel, in_specs=[vmem] * 3, out_specs=[anywhere] *...  81.1 us
    pallas_call x2, Pallas kernels, attend_back(): pl.pallas_call(functools.partial(attend_back_kernel, batch), grid=(count...  28.3 us
    pallas_call x3, Pallas kernels, patch_product(): pl.pallas_call(patch_kernel, grid_spec=grid_spec, out_shape=jax.ShapeDtyp...  25.5 us
    pallas_call x2, Pallas kernels, attend(): pl.pallas_call(functools.partial(attend_kernel, causal, batch), grid_spec...  19.3 us
  transfers between devices with their start and end apart: 5, of which 1 were waited for; matrix products, arithmetic and copies ran while one was open for 15% of the time, Pallas kernels for 27%

profile of v6, /device:TPU:0, one launch (start us, length us, event | category | flops | bytes accessed | tf_op | source)
XLA Modules:
  0.0 425.1 jit_solution(13990421872284669701)
XLA Ops:
  0.7 1.8 constant_dynamic-slice_fusion.2
  2.5 3.0 collective-permute-start.2
  5.5 1.8 constant_dynamic-slice_fusion.6
  7.3 0.6 broadcast_in_dim.78
  7.9 0.6 dynamic_slice.32.flag_ref
  8.6 6.3 %constant_dynamic-slice_fusion.5 = bf16[8,576,768]{2,1,0:T(8,128)(2,1)} fusion(bf16[16,576,768]{2,1,0:T(8,128)(2,1)} %param.21, s32[]{:T(128)S(6)} %select_n.48), kind=kLoop, calls=%fused_computation.113 | loop fusion | bytes 14155780 | tf_op jit(solution)/shard_map/dynamic_slice | solution.py:901
  15.1 0.7 copy-done.19
  15.8 81.1 %shard_map.339 = (bf16[8,16,48,768]{3,2,1,0:T(8,128)(2,1)}, bf16[16,48,3072]{2,1,0:T(8,128)(2,1)}, bf16[16,48,3072]{2,1,0:T(8,128)(2,1)}) custom-call(bf16[8,48,384]{2,1,0:T(8,128)(2,1)} %copy-done.19, bf16[48,1536]{1,0:T(8,128)(2,1)} %exp_in.1, bf16[48,1536]{1,0:T(8,128)(2,1)} %bitcast.191), custom_call_target="tpu_custom_call" | custom-call | tf_op jit(solution)/shard_map/pallas_call | solution.py:542
  96.9 6.3 %fusion.34 = (bf16[1,16,48,768]{3,2,1,0:T(8,128)(2,1)S(1)}, bf16[1,16,48,768]{3,2,1,0:T(8,128)(2,1)S(1)}, bf16[1,16,48,768]{3,2,1,0:T(8,128)(2,1)S(1)}, bf16[1,1...) fusion(bf16[8,16,48,768]{3,2,1,0:T(8,128)(2,1)} %get-tuple-elem, ...), kind=kLoop, calls=%fused_computation.134 | loop fusion | bytes 18874368 | tf_op jit(solution)/shard_map/slice | solution.py:580
  103.3 1.4 copy.43
  104.7 1.5 copy.42
  106.2 17.1 %convolution_convert_fusion.key_ref.value_ref = bf16[4608,1536]{1,0:T(8,128)(2,1)} fusion(bf16[4608,768]{1,0:T(8,128)(2,1)} %bitcast.160, bf16[768,768]{1,0:T(8,128)(2,1)S(1)} %bitcast.163, bf16[768,768]{1,0:T(8,128)(2,1)S(1)} %bitcast.165), kind=kOutput, calls=%fused_computation | convolution fusion | flops 10883432448 | bytes 23592960 | tf_op jit(solution)/shard_map/dot_general | solution.py:26
  123.3 0.6 pad_add_fusion.side_ref
  123.9 0.6 pad_add_fusion.1.side_ref
  124.5 3.3 pad_maximum_fusion.1.weight_ref
  127.8 2.0 broadcast_select_fusion.1
  130.4 0.9 pad_maximum_fusion.4
  131.5 1.1 fusion.18
  132.6 0.9 copy-done.14
  133.5 4.7 %convolution_convert_fusion.4.query_ref.key_ref.value_ref = bf16[512,2304]{1,0:T(8,128)(2,1)} fusion(bf16[512,768]{1,0:T(8,128)(2,1)S(1)} %fusion.18, bf16[768,768]{1,0:T(8,128)(2,1)S(1)} %bitcast.178, bf16[768,768]{1,0:T(8,128)(2,1)S(1)} %bitcast.181, bf16[768,768]{1,0:T(8,128)(2,1)} %bitcast.182), kind=kOutput, calls=%fused_computation.14 | convolution fusion | flops 1823735808 | bytes 6684672 | tf_op jit(solution)/shard_map/dot_general | solution.py:26
  138.2 6.0 %shard_map.340 = (bf16[512,768]{1,0:T(8,128)(2,1)}, bf16[512,768]{1,0:T(8,128)(2,1)}) custom-call(s32[8]{0:T(128)} %dynamic_slice.32.flag_ref, bf16[512,2304]{1,0:T(8,128)(2,1)} %convolution_convert_fusion.4.query_ref.key_ref.value_ref, bf16[512,2304]{1,0:T(8,128)(2,1)} %convolution_convert_fusion.4.query_ref.key_ref.value_ref, ...), custom_call_target="tpu_custom_call" | custom-call | flops 402653184 | bytes 1572864 | tf_op jit(solution)/shard_map/pallas_call | solution.py:146
  144.2 2.6 fusion.35
  148.1 1.8 convolution_convert_fusion.11.query_ref
  149.9 13.3 %shard_map.341 = (bf16[512,768]{1,0:T(8,128)(2,1)}, bf16[4608,768]{1,0:T(8,128)(2,1)}) custom-call(s32[8]{0:T(128)} %dynamic_slice.32.flag_ref, bf16[512,768]{1,0:T(8,128)(2,1)} %convolution_convert_fusion.11.query_ref, bf16[4608,1536]{1,0:T(8,128)(2,1)} %convolution_convert_fusion.key_ref.value_ref, bf16[4608,1536]{1,0:T(8,128)(2,1)} %convolution_convert_fusion.key_ref.value_ref), custom_call_target="tpu_custom_call" | custom-call | flops 3623878656 | bytes 14155776 | tf_op jit(solution)/shard_map/pallas_call | solution.py:146
  163.3 2.0 fusion.36
  165.6 0.6 copy-done.5
  166.4 5.1 %fusion.32 = f32[512,3072]{1,0:T(8,128)S(1)} fusion(bf16[768,3072]{1,0:T(8,128)(2,1)} %bitcast.192, f32[512,768]{1,0:T(8,128)S(1)} %get-tuple-element.122, f32[768]{0:T(1024)S(1)} %copy-done.48, f32[768]{0:T(1024)S(1)} %copy-done.42, f32[512]{0:T(512)S(1)} %add_rsqrt_fusion.1, f32[512]{0:T(512)S(1)} %broadcast_multiply_fusion.7), kind=kOutput, calls=%fused_computation.132 | convolution fusion | flops 2417885184 | bytes 12593152 | tf_op jit(solution)/shard_map/dot_general | solution.py:26
  171.5 5.1 %add_convert_fusion = bf16[512,768]{1,0:T(8,128)(2,1)} fusion(f32[512,768]{1,0:T(8,128)S(1)} %get-tuple-element.122, bf16[768,3072]{1,0:T(8,128)(2,1)S(1)} %bitcast.198, f32[512,3072]{1,0:T(8,128)S(1)} %fusion.32), kind=kOutput, calls=%fused_computation.46 | convolution fusion | flops 2430861312 | bytes 13369344 | tf_op jit(solution)/shard_map/dot_general | solution.py:26
  176.6 5.8 %fusion.6 = bf16[512,3072]{1,0:T(8,128)(2,1)S(1)} fusion(f32[512,3072]{1,0:T(8,128)S(1)} %fusion.32, bf16[512,768]{1,0:T(8,128)(2,1)S(1)} %bitcast.174, bf16[768,3072]{1,0:T(8,128)(2,1)S(1)} %bitcast.199), kind=kOutput, calls=%fused_computation.9 | convolution fusion | flops 2445803520 | bytes 14942208 | tf_op jit(solution)/shard_map/dot_general | solution.py:26
  182.3 4.6 %convolution_convert_fusion.2 = bf16[768,3072]{1,0:T(8,128)(2,1)} fusion(bf16[512,768]{1,0:T(8,128)(2,1)S(1)} %bitcast.175, f32[512,3072]{1,0:T(8,128)S(1)} %fusion.32), kind=kOutput, calls=%fused_computation.12 | convolution fusion | flops 2432434176 | bytes 11796480 | tf_op jit(solution)/shard_map/dot_general | solution.py:26
  186.9 3.5 multiply_reduce_fusion
  190.4 4.8 %convolution_convert_fusion.3 = bf16[768,3072]{1,0:T(8,128)(2,1)} fusion(bf16[512,3072]{1,0:T(8,128)(2,1)S(1)} %fusion.6, f32[512,768]{1,0:T(8,128)S(1)} %get-tuple-element.122, f32[768]{0:T(1024)S(1)} %copy-done.48, f32[768]{0:T(1024)S(1)} %copy-done.42, f32[512]{0:T(512)S(1)} %add_rsqrt_fusion.1, f32[512]{0:T(512)S(1)} %broadcast_multiply_fusion.7), kind=kOutput, calls=%fused_computation.13 | convolution fusion | flops 2420244480 | bytes 9447424 | tf_op jit(solution)/shard_map/dot_general | solution.py:26
  195.3 1.8 fusion.33
  197.0 1.8 convolution_convert_fusion.8
  198.9 1.7 convolution_convert_fusion.10.grad_ref
  200.6 18.6 %shard_map.342 = (bf16[512,768]{1,0:T(8,128)(2,1)}, bf16[4608,1536]{1,0:T(8,128)(2,1)}) custom-call(bf16[512,768]{1,0:T(8,128)(2,1)} %convolution_convert_fusion.11.query_ref, bf16[4608,1536]{1,0:T(8,128)(2,1)} %convolution_convert_fusion.key_ref.value_ref, bf16[4608,1536]{1,0:T(8,128)(2,1)} %convolution_convert_fusion.key_ref.value_ref, ...), custom_call_target="tpu_custom_call" | custom-call | flops 7247757312 | bytes 28311552 | tf_op jit(solution)/shard_map/pallas_call | solution.py:162
  219.2 17.0 %convolution_convert_fusion.5 = bf16[768,1536]{1,0:T(8,128)(2,1)} fusion(bf16[4608,768]{1,0:T(8,128)(2,1)} %bitcast.161, bf16[4608,1536]{1,0:T(8,128)(2,1)} %get-tuple-element.51), kind=kOutput, calls=%fused_computation.16 | convolution fusion | flops 10872815616 | bytes 23592960 | tf_op jit(solution)/shard_map/dot_general | solution.py:26
  236.2 0.9 constant_dynamic-slice_fusion.4
  237.2 1.5 collective-permute-start.1
  238.7 2.1 convolution_convert_fusion.7
  240.8 7.2 %shard_map.343 = bf16[4,288,768]{2,1,0:T(8,128)(2,1)} custom-call(s32[2]{0:T(128)} %pad_add_fusion.side_ref, bf16[8,576,1536]{2,1,0:T(8,128)(2,1)} %bitcast.157, bf16[1536,768]{1,0:T(8,128)(2,1)} %pad_maximum_fusion.1.weight_ref), custom_call_target="tpu_custom_call" | custom-call | flops 1048576 | bytes 1365 | tf_op jit(solution)/shard_map/pallas_call | solution.py:201
  248.1 3.0 multiply_reduce_fusion.1
  251.7 0.7 copy-done.9
  252.4 1.7 convolution_convert_fusion.9.grad_ref
  254.6 9.7 %shard_map.344 = bf16[512,2304]{1,0:T(8,128)(2,1)} custom-call(bf16[512,2304]{1,0:T(8,128)(2,1)} %convolution_convert_fusion.4.query_ref.key_ref.value_ref, bf16[512,2304]{1,0:T(8,128)(2,1)} %convolution_convert_fusion.4.query_ref.key_ref.value_ref, bf16[512,2304]{1,0:T(8,128)(2,1)} %convolution_convert_fusion.4.query_ref.key_ref.value_ref, ...), custom_call_target="tpu_custom_call" | custom-call | flops 1048576 | bytes 1048576 | tf_op jit(solution)/shard_map/pallas_call | solution.py:162
  264.3 4.7 %fusion.24 = (f32[768]{0:T(1024)S(1)}, f32[512]{0:T(512)S(1)}, f32[512]{0:T(512)S(1)}, f32[768]{0:T(1024)S(1)}, f32[512,768]{1,0:T(8,128)S(1)}) fusion(f32[512]{0:T(512)S(1)} %rsqrt.28, f32[512]{0:T(512)S(1)} %div.39, bf16[8,32,768]{2,1,0:T(8,128)(2,1)S(1)} %get-tuple-element.126, bf16[8,32,768]{2,1,0:T(8,128)(2,1)S(1)} %copy-done.1, ...), kind=kOutput, calls=%fused_computation.39 | convolution fusion | flops 1827665408 | bytes 8274944 | tf_op jit(solution)/shard_map/dot_general | solution.py:26
  269.1 0.6 stack.81
  272.0 0.6 fusion.23
  272.7 0.8 constant_dynamic-slice_fusion.1
  273.5 1.5 collective-permute-start.3
  275.0 0.6 stack.82
  275.7 6.9 %shard_map.345.away = bf16[4,288,768]{2,1,0:T(8,128)(2,1)} custom-call(s32[2]{0:T(128)} %pad_add_fusion.side_ref, bf16[8,576,1536]{2,1,0:T(8,128)(2,1)} %bitcast.158, bf16[1536,768]{1,0:T(8,128)(2,1)} %pad_maximum_fusion.1.weight_ref), custom_call_target="tpu_custom_call" | custom-call | flops 1048576 | bytes 1365 | tf_op jit(solution)/shard_map/pallas_call | solution.py:201
  282.6 11.3 %shard_map.347.whole_ref = f32[16,288,768]{2,1,0:T(8,128)} custom-call(s32[2]{0:T(128)} %pad_add_fusion.1.side_ref, bf16[8,576,1536]{2,1,0:T(8,128)(2,1)} %bitcast.159, bf16[1536,768]{1,0:T(8,128)(2,1)} %pad_maximum_fusion.1.weight_ref), custom_call_target="tpu_custom_call" | custom-call | flops 1048576 | bytes 1365 | tf_op jit(solution)/shard_map/pallas_call | solution.py:201
  294.0 1.8 convolution_convert_fusion.6
  296.0 3.8 convolution_convert_fusion.1
  299.8 3.5 collective-permute-done.3
  303.4 2.8 fusion.26
  306.2 0.6 pad.4.norms
  306.8 105.7 %shard_map.346 = (f32[16,48,384]{2,1,0:T(8,128)}, f32[8,768]{1,0:T(8,128)}, bf16[4,288,768]{2,1,0:T(8,128)(2,1)}) custom-call(bf16[4,2,2,48,3072]{4,3,2,1,0:T(8,128)(2,1)} %bitcast.171, bf16[4,2,2,48,3072]{4,3,2,1,0:T(8,128)(2,1)} %bitcast.170, bf16[4,2,2,48,2304]{4,3,2,1,0:T(8,128)(2,1)} %bitcast.173, bf16[4,2,2,48,768]{4,3,2,1,0:T(8,128)(2,1)} %bitcast.172, ...), custom_call_target="tpu_custom_call" | custom-call | bytes 1048576 | tf_op jit(solution)/shard_map/pallas_call | solution.py:834
  412.5 1.6 slice_reduce_fusion
  414.1 2.1 slice_bitcast_fusion.3
  416.3 7.1 %shard_map.348 = f32[16,288,768]{2,1,0:T(8,128)} custom-call(s32[1]{0:T(128)} %bitcast.34.side_ref, bf16[4,288,768]{2,1,0:T(8,128)(2,1)} %collective-permute-done.4.early_ref, bf16[4,288,768]{2,1,0:T(8,128)(2,1)} %get-tuple-element.62.late_ref, f32[16,288,768]{2,1,0:T(8,128)} %shard_map.347.whole_ref), custom_call_target="tpu_custom_call", output_to_operand_aliasing={{}: (3, {})} | custom-call | tf_op jit(solution)/shard_map/pallas_call | solution.py:233
  423.4 0.7 maximum_bitcast_fusion
  424.2 0.7 pad_maximum_fusion.6
  (151 shorter events, 6.3 us)
Async XLA Ops:
  0.7 7.2 %copy-start.21 = (bf16[48,384]{1,0:T(8,128)(2,1)S(1)}, bf16[48,384]{1,0:T(8,128)(2,1)}, u32[]{:S(2)}) copy-start(bf16[48,384]{1,0:T(8,128)(2,1)} %param.23) | copy-start | bytes 110596
  0.7 7.2 %copy-start.51 = (s32[16]{0:T(128)S(1)}, s32[16]{0:T(128)}, u32[]{:S(2)}) copy-start(s32[16]{0:T(128)} %param.22) | copy-start | bytes 196
  2.5 125.3 %collective-permute-start.2 = (bf16[8,32,768]{2,1,0:T(8,128)(2,1)}, bf16[8,32,768]{2,1,0:T(8,128)(2,1)}, u32[]{:S(2)}, u32[]{:S(2)}) collective-permute-start(bf16[8,32,768]{2,1,0:T(8,128)(2,1)} %constant_dynamic-slice_fusion.2), channel_id=1, source_target_pairs={{0,1},{1,0},{2,3},{3,2},{4,5},{5,4},{6,7},{7,6},{8,9},{9,8},{10,11... | collective-permute-start | bytes 1179656 | tf_op jit(solution)/shard_map/ppermute | solution.py:179
  7.2 120.6 %collective-permute-start = (bf16[8,32,768]{2,1,0:T(8,128)(2,1)}, bf16[8,32,768]{2,1,0:T(8,128)(2,1)}, u32[]{:S(2)}, u32[]{:S(2)}) collective-permute-start(bf16[8,32,768]{2,1,0:T(8,128)(2,1)} %constant_dynamic-slice_fusion.6), channel_id=1, source_target_pairs={{0,1},{1,0},{2,3},{3,2},{4,5},{5,4},{6,7},{7,6},{8,9},{9,8},{10,11... | collective-permute-start | bytes 1179656 | tf_op jit(solution)/shard_map/ppermute | solution.py:179
  8.5 6.4 %copy-start.22 = (bf16[48,384]{1,0:T(8,128)(2,1)S(1)}, bf16[48,384]{1,0:T(8,128)(2,1)}, u32[]{:S(2)}) copy-start(bf16[48,384]{1,0:T(8,128)(2,1)} %param.24) | copy-start | bytes 110596
  8.5 6.4 %copy-start.23 = (bf16[48,384]{1,0:T(8,128)(2,1)S(1)}, bf16[48,384]{1,0:T(8,128)(2,1)}, u32[]{:S(2)}) copy-start(bf16[48,384]{1,0:T(8,128)(2,1)} %param.25) | copy-start | bytes 110596
  8.5 6.4 %copy-start.24 = (bf16[384,48]{0,1:T(8,128)(2,1)S(1)}, bf16[384,48]{0,1:T(8,128)(2,1)}, u32[]{:S(2)}) copy-start(bf16[384,48]{0,1:T(8,128)(2,1)} %param.26) | copy-start | bytes 110596
  8.5 6.5 %copy-start.25 = (bf16[48,384]{1,0:T(8,128)(2,1)S(1)}, bf16[48,384]{1,0:T(8,128)(2,1)}, u32[]{:S(2)}) copy-start(bf16[48,384]{1,0:T(8,128)(2,1)} %param.27) | copy-start | bytes 110596
  8.5 6.5 %copy-start.26 = (bf16[48,384]{1,0:T(8,128)(2,1)S(1)}, bf16[48,384]{1,0:T(8,128)(2,1)}, u32[]{:S(2)}) copy-start(bf16[48,384]{1,0:T(8,128)(2,1)} %param.28) | copy-start | bytes 110596
  8.5 6.5 %copy-start.27 = (bf16[48,384]{1,0:T(8,128)(2,1)S(1)}, bf16[48,384]{1,0:T(8,128)(2,1)}, u32[]{:S(2)}) copy-start(bf16[48,384]{1,0:T(8,128)(2,1)} %param.29) | copy-start | bytes 110596
  8.5 6.5 %copy-start.28 = (bf16[384,48]{0,1:T(8,128)(2,1)S(1)}, bf16[384,48]{0,1:T(8,128)(2,1)}, u32[]{:S(2)}) copy-start(bf16[384,48]{0,1:T(8,128)(2,1)} %param.30) | copy-start | bytes 110596
  15.1 0.7 copy-start.19
  124.5 3.3 copy-start.17
  124.5 3.3 copy-start.18
  129.8 1.6 copy-start
  129.8 1.6 copy-start.29
  130.4 3.1 copy-start.6
  131.5 2.0 copy-start.8
  132.6 0.9 copy-start.14
  146.8 1.3 copy-start.10
  146.8 1.3 copy-start.43
  146.8 1.3 copy-start.49
  147.2 0.6 copy-start.35
  165.3 1.0 copy-start.5
  165.3 1.0 copy-start.48
  165.3 1.0 copy-start.42
  165.3 6.1 %slice-start.2 = ((s8[4718592]{0:T(1024)(128)(4,1)}), s8[4194304]{0:T(1024)(128)(4,1)S(1)}, s32[]{:S(2)}) async-start(s8[4718592]{0:T(1024)(128)(4,1)} %bitcast.196), calls=%async_computation.2 | async-start | bytes 8388608
  166.4 5.1 %slice-start.3 = ((s8[4718592]{0:T(1024)(128)(4,1)}), s8[524288]{0:T(1024)(128)(4,1)S(1)}, s32[]{:S(2)}) async-start(s8[4718592]{0:T(1024)(128)(4,1)} %bitcast.196), calls=%async_computation.3 | async-start | bytes 1048576
  171.5 15.4 %slice-start = ((s8[4718592]{0:T(1024)(128)(4,1)}), s8[4194304]{0:T(1024)(128)(4,1)S(1)}, s32[]{:S(2)}) async-start(s8[4718592]{0:T(1024)(128)(4,1)} %bitcast.193), calls=%async_computation | async-start | bytes 8388608
  176.6 10.4 %slice-start.1 = ((s8[4718592]{0:T(1024)(128)(4,1)}), s8[524288]{0:T(1024)(128)(4,1)S(1)}, s32[]{:S(2)}) async-start(s8[4718592]{0:T(1024)(128)(4,1)} %bitcast.193), calls=%async_computation.1 | async-start | bytes 1048576
  195.3 1.8 copy-start.13
  219.2 17.0 %copy-start.16 = (bf16[512,768]{1,0:T(8,128)(2,1)S(1)}, bf16[512,768]{1,0:T(8,128)(2,1)}, u32[]{:S(2)}) copy-start(bf16[512,768]{1,0:T(8,128)(2,1)} %add_convert_fusion) | copy-start | bytes 2359300
  236.2 2.5 copy-start.36
  236.2 2.5 copy-start.44
  236.2 2.5 copy-start.47
  236.2 2.5 copy-start.50
  237.2 62.7 %collective-permute-start.1 = (bf16[8,32,768]{2,1,0:T(8,128)(2,1)}, bf16[8,32,768]{2,1,0:T(8,128)(2,1)}, u32[]{:S(2)}, u32[]{:S(2)}) collective-permute-start(bf16[8,32,768]{2,1,0:T(8,128)(2,1)} %get-tuple-element.116), channel_id=1, source_target_pairs={{0,1},{1,0},{2,3},{3,2},{4,5},{5,4},{6,7},{7,6},{8,9},{9,8},{10,11... | collective-permute-start | bytes 1179656 | tf_op jit(solution)/shard_map/ppermute | solution.py:179
  240.8 7.2 %copy-start.11 = (bf16[1,16,48,768]{3,2,1,0:T(8,128)(2,1)S(1)}, bf16[1,16,48,768]{3,2,1,0:T(8,128)(2,1)}, u32[]{:S(2)}) copy-start(bf16[1,16,48,768]{3,2,1,0:T(8,128)(2,1)} %get-tuple-element.88) | copy-start | bytes 3538948
  248.0 3.1 copy-start.2
  248.0 3.1 copy-start.37
  248.0 3.1 copy-start.45
  251.1 1.3 copy-start.9
  254.1 52.2 %collective-permute-start.4 = (bf16[4,288,768]{2,1,0:T(8,128)(2,1)}, bf16[4,288,768]{2,1,0:T(8,128)(2,1)}, u32[]{:S(2)}, u32[]{:S(2)}) collective-permute-start(bf16[4,288,768]{2,1,0:T(8,128)(2,1)} %shard_map.343), channel_id=1, source_target_pairs={{0,1},{1,0},{2,3},{3,2},{4,5},{5,4},{6,7},{7,6},{8,9},{9,8},{10,11... | collective-permute-start | bytes 5308424 | tf_op jit(solution)/shard_map/ppermute | solution.py:179
  254.6 9.7 %copy-start.1 = (bf16[8,32,768]{2,1,0:T(8,128)(2,1)S(1)}, bf16[8,32,768]{2,1,0:T(8,128)(2,1)}, u32[]{:S(2)}) copy-start(bf16[8,32,768]{2,1,0:T(8,128)(2,1)} %copy-done) | copy-start | bytes 1179652
  254.6 9.7 %copy-start.7 = (bf16[1,16,48,768]{3,2,1,0:T(8,128)(2,1)S(1)}, bf16[1,16,48,768]{3,2,1,0:T(8,128)(2,1)}, u32[]{:S(2)}) copy-start(bf16[1,16,48,768]{3,2,1,0:T(8,128)(2,1)} %get-tuple-element.90) | copy-start | bytes 3538948
  264.3 4.8 %copy-start.39 = (f32[768]{0:T(1024)S(1)}, f32[768]{0:T(1024)}, u32[]{:S(2)}) copy-start(f32[768]{0:T(1024)} %get-tuple-element.65) | copy-start | bytes 9220
  264.3 4.8 %copy-start.38 = (f32[768]{0:T(1024)S(1)}, f32[768]{0:T(1024)}, u32[]{:S(2)}) copy-start(f32[768]{0:T(1024)} %get-tuple-element.74) | copy-start | bytes 9220
  264.3 5.4 %copy-start.41 = (f32[768]{0:T(1024)S(1)}, f32[768]{0:T(1024)}, u32[]{:S(2)}) copy-start(f32[768]{0:T(1024)} %get-tuple-element.67) | copy-start | bytes 9220
  264.3 7.1 %copy-start.40 = (f32[768]{0:T(1024)S(1)}, f32[768]{0:T(1024)}, u32[]{:S(2)}) copy-start(f32[768]{0:T(1024)} %get-tuple-element.75) | copy-start | bytes 9220
  272.6 2.4 copy-start.30
  272.6 2.4 copy-start.31
  272.6 2.4 copy-start.32
  272.6 2.4 copy-start.33
  272.7 2.4 copy-start.34
  273.5 29.9 %collective-permute-start.3 = (bf16[8,32,768]{2,1,0:T(8,128)(2,1)}, bf16[8,32,768]{2,1,0:T(8,128)(2,1)}, u32[]{:S(2)}, u32[]{:S(2)}) collective-permute-start(bf16[8,32,768]{2,1,0:T(8,128)(2,1)} %get-tuple-element.114), channel_id=1, source_target_pairs={{0,1},{1,0},{2,3},{3,2},{4,5},{5,4},{6,7},{7,6},{8,9},{9,8},{10,11... | collective-permute-start | bytes 1179656 | tf_op jit(solution)/shard_map/ppermute | solution.py:179
  282.6 11.3 %copy-start.12 = (bf16[512,768]{1,0:T(8,128)(2,1)S(1)}, bf16[512,768]{1,0:T(8,128)(2,1)}, u32[]{:S(2)}) copy-start(bf16[512,768]{1,0:T(8,128)(2,1)} %get-tuple-element.43) | copy-start | bytes 2359300
  293.9 1.8 copy-start.3
  293.9 2.1 copy-start.15
  296.0 7.4 %copy-start.4 = (bf16[8,32,768]{2,1,0:T(8,128)(2,1)S(1)}, bf16[8,32,768]{2,1,0:T(8,128)(2,1)}, u32[]{:S(2)}) copy-start(bf16[8,32,768]{2,1,0:T(8,128)(2,1)} %get-tuple-element.115) | copy-start | bytes 1179652
  296.0 7.4 %copy-start.46 = (pred[16]{0:T(512)(128)(4,1)S(1)}, pred[16]{0:T(512)(128)(4,1)}, u32[]{:S(2)}) copy-start(pred[16]{0:T(512)(128)(4,1)} %broadcast_in_dim.78) | copy-start | bytes 52
  303.4 2.8 copy-start.20

commit v7 on v6

--- a/solution.py
+++ b/solution.py
@@ -51,7 +51,7 @@
     mean_one = jnp.mean(scaled, axis=-1, keepdims=True)
     mean_two = jnp.mean(scaled * normal, axis=-1, keepdims=True)
     grad_value = (scaled - mean_one - normal * mean_two) * inverse
-    return grad_value, jnp.sum(grad * normal, axis=0), jnp.sum(grad, axis=0)
+    return grad_value, jnp.sum(grad * normal, axis=0, keepdims=True), jnp.sum(grad, axis=0, keepdims=True)
 
 
 def spread(rows):
@@ -115,8 +115,8 @@
             query_out[ask, part] = (collect(dot(grad_score, key_ref[see, part], 0, 0)) * HD ** (-0.5)).astype(bf16)
 
 
-def column(rows, width, index):
-    return pl.BlockSpec((rows, width), lambda i, *_: (i, index))
+def column(rows, width):
+    return pl.BlockSpec((rows, width), lambda i, *_: (i, 0))
 
 
 def attend_cost(queries, count, keys, products):
@@ -133,15 +133,15 @@
     return 1
 
 
-def attend(queries, query_at, sources, key_at, value_at, flags, count, causal):
+def attend(queries, sources, values, flags, count, causal):
     keys = sources.shape[0] // count
     batch = batch_of(count, keys)
     ask, see, width = batch * LEN, batch * keys, D
     grid_spec = pltpu.PrefetchScalarGridSpec(
         num_scalar_prefetch=1,
         grid=(count // batch,),
-        in_specs=[column(ask, width, query_at), column(see, width, key_at), column(see, width, value_at)],
-        out_specs=[column(ask, width, 0), column(see, width, 0)],
+        in_specs=[column(ask, width), column(see, width), column(see, width)],
+        out_specs=[column(ask, width), column(see, width)],
     )
     return pl.pallas_call(
         functools.partial(attend_kernel, causal, batch),
@@ -151,10 +151,10 @@
             jax.ShapeDtypeStruct((count * keys, width), bf16),
         ),
         cost_estimate=attend_cost(queries, count, keys, 2),
-    )(flags, queries, sources, sources)
-
-
-def attend_back(queries, query_at, sources, key_at, value_at, probs, grad_mix, count, whole):
+    )(flags, queries, sources, values)
+
+
+def attend_back(queries, sources, values, probs, grad_mix, count, whole):
     keys = sources.shape[0] // count
     batch = batch_of(count, keys)
     ask, see, width = batch * LEN, batch * keys, D
@@ -163,37 +163,40 @@
         functools.partial(attend_back_kernel, batch),
         grid=(count // batch,),
         in_specs=[
-            column(ask, width, query_at),
-            column(see, width, key_at),
-            column(see, width, value_at),
-            column(see, width, 0),
-            column(ask, width, 0),
+            column(ask, width),
+            column(see, width),
+            column(see, width),
+            column(see, width),
+            column(ask, width),
         ],
-        out_specs=[column(batch * rows, wide, 0) for rows, wide in widths],
+        out_specs=[column(batch * rows, wide) for rows, wide in widths],
         out_shape=[jax.ShapeDtypeStruct((count * rows, wide), bf16) for rows, wide in widths],
         cost_estimate=attend_cost(queries, count, keys, 4),
-    )(queries, sources, sources, probs, grad_mix)
+    )(queries, sources, values, probs, grad_mix)
 
 
 def swap(rows):
     return lax.ppermute(rows, "mp", [(0, 1), (1, 0)])
 
 
-def patch_kernel(side_ref, grad_ref, weight_ref, out_ref):
+def patch_kernel(side_ref, grad_ref, key_ref, value_ref, out_ref):
+    width = key_ref.shape[1]
     for n in range(grad_ref.shape[0]):
-        out_ref[n] = dot(grad_ref[n], weight_ref[...], 1, 0).astype(out_ref.dtype)
-
-
-def patch_product(grads, weights, first, last, half, place_at, total, kind):
+        product = dot(grad_ref[n, :, :width], key_ref[...], 1, 1) + dot(grad_ref[n, :, width:], value_ref[...], 1, 1)
+        out_ref[n] = product.astype(out_ref.dtype)
+
+
+def patch_product(grads, key_w, value_w, first, last, half, place_at, total, kind):
     batch = 2 - (last - first) % 2
     rows = PATCH // 2
-    depth, width = weights.shape
+    width, depth = key_w.shape[0], 2 * key_w.shape[1]
     grid_spec = pltpu.PrefetchScalarGridSpec(
         num_scalar_prefetch=1,
         grid=((last - first) // batch,),
         in_specs=[
             pl.BlockSpec((batch, rows, depth), lambda i, at: (i + first // batch, at[0], 0)),
-            pl.BlockSpec((depth, width), lambda i, at: (0, 0)),
+            pl.BlockSpec(key_w.shape, lambda i, at: (0, 0)),
+            pl.BlockSpec(value_w.shape, lambda i, at: (0, 0)),
         ],
         out_specs=pl.BlockSpec((batch, rows, width), lambda i, at: (i + at[1] // batch, 0, 0)),
     )
@@ -203,11 +206,11 @@
         grid_spec=grid_spec,
         out_shape=jax.ShapeDtypeStruct((total, rows, width), kind),
         cost_estimate=pl.CostEstimate(flops=flops, bytes_accessed=flops // width, transcendentals=0),
-    )(jnp.stack([half, place_at]), grads.reshape(-1, PATCH, depth), weights)
-
-
-def widen_kernel(side_ref, early_ref, late_ref, whole_ref, out_ref):
-    early = pl.program_id(0) * 2 < pl.num_programs(0)
+    )(jnp.stack([half, place_at]), grads.reshape(-1, PATCH, depth), key_w, value_w)
+
+
+def widen_kernel(first, side_ref, early_ref, late_ref, whole_ref, out_ref):
+    early = pl.program_id(0) < first
 
     @pl.when(early)
     def _():
@@ -222,7 +225,7 @@
     count, height, width = early.shape
     grid_spec = pltpu.PrefetchScalarGridSpec(
         num_scalar_prefetch=1,
-        grid=(2 * count,),
+        grid=(count + late.shape[0],),
         in_specs=[
             pl.BlockSpec((1, height, width), lambda i, at: (jnp.minimum(i, count - 1), 0, 0)),
             pl.BlockSpec((1, height, width), lambda i, at: (jnp.maximum(i - count, 0), 0, 0)),
@@ -231,7 +234,7 @@
         out_specs=pl.BlockSpec((1, height, width), lambda i, at: (i + at[0], 0, 0)),
     )
     return pl.pallas_call(
-        widen_kernel,
+        functools.partial(widen_kernel, count),
         grid_spec=grid_spec,
         out_shape=jax.ShapeDtypeStruct(whole.shape, f32),
         input_output_aliases={3: 0},
@@ -248,19 +251,19 @@
 
 def layer(weights, norms, text, cotangent, patches, resolution):
     count = text.shape[0] // LEN
-    project_self, mix_self, query_cross, project_patch, mix_cross, expand, contract = weights
+    query_self, key_self, value_self, mix_self, query_cross, key_cross, value_cross, mix_cross, expand, contract = weights
     first_gain, first_shift, second_gain, second_shift, third_gain, third_shift = norms
     stream = text.astype(f32)
     normal_one, inverse_one = norm_stats(stream)
     normed_one = (normal_one * first_gain + first_shift).astype(bf16)
-    rows_one = matmul(normed_one, project_self).astype(bf16)
-    mixed_one, probs_one = attend(rows_one, 0, rows_one, 1, 2, resolution, count, True)
+    queries_one, keys_one, values_one = (matmul(normed_one, w).astype(bf16) for w in (query_self, key_self, value_self))
+    mixed_one, probs_one = attend(queries_one, keys_one, values_one, resolution, count, True)
     stream_one = stream + matmul_t(mixed_one, mix_self)
     normal_two, inverse_two = norm_stats(stream_one)
     normed_two = (normal_two * second_gain + second_shift).astype(bf16)
     queries_two = matmul(normed_two, query_cross).astype(bf16)
-    rows_two = matmul(patches, project_patch).astype(bf16)
-    mixed_two, probs_two = attend(queries_two, 0, rows_two, 0, 1, resolution, count, False)
+    keys_two, values_two = (matmul(patches, w).astype(bf16) for w in (key_cross, value_cross))
+    mixed_two, probs_two = attend(queries_two, keys_two, values_two, resolution, count, False)
     stream_two = stream_one + matmul_t(mixed_two, mix_cross)
     normal_three, inverse_three = norm_stats(stream_two)
     normed_three = (normal_three * third_gain + third_shift).astype(bf16)
@@ -276,55 +279,66 @@
     grad_rows = grad_stream.astype(bf16)
     grad_mix_cross = weight_grad(grad_rows, mixed_two).astype(bf16)
     grad_expand, grad_contract = grad_expand.astype(bf16), grad_contract.astype(bf16)
-    grad_rows, grad_expand, grad_contract, grad_mix_cross = lax.optimization_barrier(
-        (grad_rows, grad_expand, grad_contract, grad_mix_cross)
+    layer_out = layer_out.astype(bf16)
+    grad_rows, grad_expand, grad_contract, grad_mix_cross, layer_out = lax.optimization_barrier(
+        (grad_rows, grad_expand, grad_contract, grad_mix_cross, layer_out)
     )
     grad_mixed = matmul(grad_rows, mix_cross).astype(bf16)
-    grad_queries, grad_sources = attend_back(queries_two, 0, rows_two, 0, 1, probs_two, grad_mixed, count, False)
+    grad_queries, grad_sources = attend_back(queries_two, keys_two, values_two, probs_two, grad_mixed, count, False)
     side = lax.axis_index("mp")
     grad_query_cross = weight_grad(normed_two, grad_queries).astype(bf16)
     grad_patch = weight_grad(patches, grad_sources).astype(bf16)
     grad_patch, grad_sources, grad_query_cross = lax.optimization_barrier((grad_patch, grad_sources, grad_query_cross))
-    turned_patch = jnp.concatenate([project_patch[:, :D].T, project_patch[:, D:].T])
-    early = patch_product(grad_sources, turned_patch, 0, count // 2, 1 - side, 0 * side, count // 2, bf16)
+    first = count * 5 // 8
+    near, far = (0, first), (first, count)
+    early = patch_product(grad_sources, key_cross, value_cross, *near, 1 - side, 0 * side, first, bf16)
     early, grad_queries = lax.optimization_barrier((early, grad_queries))
     early = swap(early)
-    late = patch_product(grad_sources, turned_patch, count // 2, count, 1 - side, 0 * side, count // 2, bf16)
-    patch_grad = patch_product(grad_sources, turned_patch, 0, count, side, side * count, 2 * count, f32)
+    late = patch_product(grad_sources, key_cross, value_cross, *far, 1 - side, 0 * side, count - first, bf16)
     grad_normed = matmul_t(grad_queries, query_cross)
     grad_input, gain_two, shift_two = norm_back(normal_two, inverse_two, second_gain, grad_normed)
     grad_stream = grad_stream + grad_input
     grad_rows = grad_stream.astype(bf16)
     grad_mix_self = weight_grad(grad_rows, mixed_one)
     grad_mixed = matmul(grad_rows, mix_self).astype(bf16)
-    (grad_one,) = attend_back(rows_one, 0, rows_one, 1, 2, probs_one, grad_mixed, count, True)
+    (grad_one,) = attend_back(queries_one, keys_one, values_one, probs_one, grad_mixed, count, True)
     grad_self = weight_grad(normed_one, grad_one)
-    grad_normed = matmul_t(grad_one, project_self)
+    grad_normed = sum(matmul_t(grad_one[:, i * D : (i + 1) * D], w) for i, w in enumerate((query_self, key_self, value_self)))
     grad_input, gain_one, shift_one = norm_back(normal_one, inverse_one, first_gain, grad_normed)
     text_grad = (grad_stream + grad_input).astype(bf16)
-    norm_grads = jnp.stack([gain_one, shift_one, gain_two, shift_two, gain_three, shift_three])
+    norm_grads = [gain_one, shift_one, gain_two, shift_two, gain_three, shift_three]
     grads = [grad_expand, grad_contract, grad_self, grad_mix_self, grad_query_cross, grad_patch, grad_mix_cross]
-    early, norm_grads = lax.optimization_barrier((early, norm_grads))
-    weight_grads, norm_sums, late = scatter_grads([g.astype(bf16) for g in grads], norm_grads, late)
-    patch_grad = widen(early, late, patch_grad, (1 - side) * count)
-    return layer_out.astype(bf16), text_grad, patch_grad, weight_grads, norm_sums
-
-
-def to_captions(rows, side):
+    early, norm_grads[0] = lax.optimization_barrier((early, norm_grads[0]))
+    grads = [g.astype(bf16) for g in grads]
+    layer_mine, layer_away = split_positions(layer_out.reshape(count, LEN, D), side)
+    text_mine, text_away = split_positions(text_grad.reshape(count, LEN, D), side)
+    weight_grads, norm_sums, patch_grad, text_back, layer_back = scatter_grads(
+        grads, norm_grads, grad_sources, early, late, key_cross, value_cross, text_away, layer_away
+    )
+    layer_out = join_positions(layer_mine, layer_back, side)
+    text_grad = join_positions(text_mine, text_back, side).astype(f32)
+    return layer_out, text_grad, patch_grad, weight_grads, norm_sums
+
+
+def split_captions(rows, side):
     half = rows.shape[0] // 2
-    mine = lax.dynamic_slice_in_dim(rows, side * half, half, 0)
-    other = swap(lax.dynamic_slice_in_dim(rows, (1 - side) * half, half, 0))
+    return tuple(lax.dynamic_slice_in_dim(rows, at * half, half, 0) for at in (side, 1 - side))
+
+
+def join_captions(mine, other, side):
     low = jnp.where(side == 0, mine, other)
     high = jnp.where(side == 0, other, mine)
     return jnp.concatenate([low, high], axis=1)
 
 
-def to_positions(rows, side):
-    count, length, width = rows.shape[0], rows.shape[1] // 2, rows.shape[2]
-    mine = lax.dynamic_slice_in_dim(rows, side * length, length, 1)
-    other = swap(lax.dynamic_slice_in_dim(rows, (1 - side) * length, length, 1))
+def split_positions(rows, side):
+    half = rows.shape[1] // 2
+    return tuple(lax.dynamic_slice_in_dim(rows, at * half, half, 1) for at in (side, 1 - side))
+
+
+def join_positions(mine, other, side):
     first = (jnp.arange(2) == side).reshape(2, 1, 1, 1)
-    return jnp.where(first, mine[None], other[None]).reshape(2 * count, length, width)
+    return jnp.where(first, mine[None], other[None]).reshape(2 * mine.shape[0], *mine.shape[1:])
 
 
 TURNED = (False, False, False, True, False, False, False, True, False, True)
@@ -361,7 +375,28 @@
     pl.semaphore_wait(barrier, 3 + jnp.where(z > 0, 1, 0) + jnp.where(z < DEPTH - 1, 1, 0))
 
 
-def gather_kernel(att_in, exp_in, con_in, att, exp, con, own_sem, side_send, up_send, down_send, far_send, mate_send, recv, mate_recv):
+class Bundle:
+    def __init__(self, copies, total):
+        self.copies, self.total = copies, total
+
+    def start(self):
+        for one in self.copies:
+            one.start()
+
+    def wait(self):
+        self.total.wait()
+
+    def wait_send(self):
+        self.total.wait_send()
+
+    def wait_recv(self):
+        self.total.wait_recv()
+
+
+def gather_kernel(att_in, exp_in, con_in, text_in, grad_in, image, *refs):
+    att, refs = refs[: att_in.shape[0]], refs[att_in.shape[0] :]
+    exp, con, text_out, grad_out, patches, image_buf, own_sem, side_send, up_send, down_send = refs[:10]
+    far_send, mate_send, recv, mate_recv, trade_send, trade_recv, load_sem, store_sem = refs[10:]
     z, x, c, y = place()
     half, wide = att_in.shape[2], exp_in.shape[1]
     greet(z, x, c, y)
@@ -371,18 +406,19 @@
         part = index // 2
         line_first = index == 2
 
+        bundle = range(part * BUNDLE, (part + 1) * BUNDLE)
+        whole = att_in.at[pl.ds(part * BUNDLE, BUNDLE)] if early else (exp_in, con_in)[part].at[...]
+
         def own():
-            if early:
-                return att_in.at[pl.ds(part * BUNDLE, BUNDLE)]
-            return (exp_in, con_in)[part].at[...]
+            return [att_in.at[i] for i in bundle] if early else [whole]
 
         def region(w, z_from, u, core):
             x_from = (x + (w if early else u)) % 2
             y_from = (y + (u if early else w)) % 2
             row = z_from * 4 + x_from * 2 + core
             if early:
-                return att.at[pl.ds(part * BUNDLE, BUNDLE), row, :, pl.ds(pl.multiple_of(y_from * half, 128), half)]
-            return (exp, con)[part].at[row, :, pl.ds(pl.multiple_of(y_from * wide, 128), wide)]
+                return [att[i].at[row, :, pl.ds(pl.multiple_of(y_from * half, 128), half)] for i in bundle]
+            return [(exp, con)[part].at[row, :, pl.ds(pl.multiple_of(y_from * wide, 128), wide)]]
 
         if early:
             beside, far = (z * 4 + (1 - x) * 2 + c, y), (z * 4 + x * 2 + c, 1 - y)
@@ -390,9 +426,12 @@
             beside, far = (z * 4 + x * 2 + c, 1 - y), (z * 4 + (1 - x) * 2 + c, y)
 
         def copy(src, dst, send, receive, device):
-            return pltpu.make_async_remote_copy(
-                src_ref=src, dst_ref=dst, send_sem=send, recv_sem=receive, device_id=device, device_id_type=MESH
-            )
+            def make(one, two):
+                return pltpu.make_async_remote_copy(
+                    src_ref=one, dst_ref=two, send_sem=send, recv_sem=receive, device_id=device, device_id_type=MESH
+                )
+
+            return Bundle([make(one, two) for one, two in zip(src, dst)], make(whole, whole))
 
         mine = z * 4 + x * 2 + c
 
@@ -418,7 +457,10 @@
             )
 
         def keep():
-            return pltpu.make_async_copy(own(), region(0, z, 0, c), own_sem.at[index])
+            def make(one, two):
+                return pltpu.make_async_copy(one, two, own_sem.at[index])
+
+            return Bundle([make(one, two) for one, two in zip(own(), region(0, z, 0, c))], make(whole, whole))
 
         def arrive(w, z_from, u):
             spot = region(w, z_from, u, c)
@@ -518,11 +560,37 @@
 
         return first, second, along, across_at, finish
 
+    def trade(k):
+        src, dst = ((text_in, text_out), (grad_in, grad_out))[k]
+        return pltpu.make_async_remote_copy(
+            src_ref=src,
+            dst_ref=dst,
+            send_sem=trade_send.at[k],
+            recv_sem=trade_recv.at[k],
+            device_id=(z * 4 + x * 2 + c, 1 - y),
+            device_id_type=MESH,
+        )
+
+    count = patches.shape[0]
+
+    def load(n):
+        return pltpu.make_async_copy(image.at[y * count + n], image_buf.at[n], load_sem.at[n])
+
+    def store(n):
+        return pltpu.make_async_copy(image_buf.at[n], patches.at[n], store_sem.at[n])
+
     streams = [stream(index) for index in range(4)]
     for first, _, _, _, _ in streams:
         first()
+    for n in range(count):
+        load(n).start()
     for _, second, _, _, _ in streams:
         second()
+    for k in range(2):
+        trade(k).start()
+    for n in range(count):
+        load(n).wait()
+        store(n).start()
     for distance in range(1, DEPTH + 1):
         for w in range(2):
             for _, _, along, across_at, _ in streams:
@@ -531,24 +599,33 @@
                 across_at(w, distance - 1)
     for streamed in streams:
         streamed[4]()
-
-
-def gather_near(att, exp, con):
+    for k in range(2):
+        trade(k).wait()
+    for n in range(count):
+        store(n).wait()
+
+
+def gather_near(att, exp, con, text, grad, image):
     dp = lax.axis_size("dp")
+    count = image.shape[0] // 2
     rows, half, wide = att.shape[1], att.shape[2], exp.shape[1]
     vmem = pl.BlockSpec(memory_space=pltpu.VMEM)
     anywhere = pl.BlockSpec(memory_space=pl.ANY)
     dma = pltpu.SemaphoreType.DMA
     return pl.pallas_call(
         gather_kernel,
-        in_specs=[vmem] * 3,
-        out_specs=[anywhere] * 3,
-        out_shape=[
-            jax.ShapeDtypeStruct((att.shape[0], dp, rows, 2 * half), bf16),
+        in_specs=[vmem] * 3 + [anywhere] * 3,
+        out_specs=[anywhere] * (att.shape[0] + 5),
+        out_shape=[jax.ShapeDtypeStruct((dp, rows, 2 * half), bf16)] * att.shape[0]
+        + [
             jax.ShapeDtypeStruct((dp, rows, 2 * wide), bf16),
             jax.ShapeDtypeStruct((dp, rows, 2 * wide), bf16),
+            jax.ShapeDtypeStruct(text.shape, bf16),
+            jax.ShapeDtypeStruct(grad.shape, bf16),
+            jax.ShapeDtypeStruct((count, *image.shape[1:]), bf16),
         ],
         scratch_shapes=[
+            pltpu.VMEM((count, *image.shape[1:]), bf16),
             dma((4,)),
             dma((4, DEPTH)),
             dma((4, 2, DEPTH)),
@@ -557,16 +634,20 @@
             dma((4, 2, DEPTH, 2)),
             dma((4, 2, DEPTH, 2)),
             dma((4, 2, DEPTH, 2)),
+            dma((2,)),
+            dma((2,)),
+            dma((count,)),
+            dma((count,)),
         ],
         compiler_params=pltpu.CompilerParams(collective_id=0, has_side_effects=True),
-    )(att, exp, con)
-
-
-def gather_weights(att, exp, con):
+    )(att, exp, con, text, grad, image)
+
+
+def gather_weights(att, exp, con, text, grad, image):
     count, width = att.shape[0], D
     if lax.axis_size("dp") == 4 * DEPTH:
-        att, exp, con = gather_near(att, exp, con)
-        att = att.reshape(count, width, -1)
+        *att, exp, con, text, grad, patches = gather_near(att, exp, con, text, grad, image)
+        att = [w.reshape(width, -1) for w in att]
         exp, con = exp.reshape(width, -1), con.reshape(width, -1)
     else:
         chunks = exp.shape[1] // att.shape[2]
@@ -575,19 +656,25 @@
         att = sides.transpose(0, 2, 1, 3).reshape(count, width, -1)
         sides = lax.all_gather(jnp.stack(narrow), ("mp", "dp"), axis=1, tiled=True).reshape(2, chunks, 2, width, -1)
         exp, con = sides.transpose(0, 3, 2, 1, 4).reshape(2, width, -1)
-    project_self = jnp.concatenate([att[0], att[1], att[2]], axis=1)
-    project_patch = jnp.concatenate([att[5], att[6]], axis=1)
-    return project_self, att[3], att[4], project_patch, att[7], exp, con
+        text, grad = swap(text), swap(grad)
+        patches, _ = split_captions(image, lax.axis_index("mp"))
+    return [*(att[i] for i in range(8)), exp, con], text, grad, patches
 
 
 PIECES = 16
 SCATTER_COST = 2**20
 SIDE_LAG = 1
 NORM_STEP = 2
-
-
-def scatter_kernel(exp, con, own, mix_own, ask, source, mix, norms, away, out, norm_out, back, acc, other, side, low, high, last, total, norm_buf, norm_line, *sems):
-    local_sem, mate_send, mate_recv, side_send, side_recv, line_send, low_recv, high_recv, last_send, last_recv, norm_send, norm_recv, away_send, back_recv = sems
+NORMS = 6
+
+
+def scatter_kernel(exp, con, own, mix_own, ask, source, mix, *rest):
+    norms, rest = rest[:NORMS], rest[NORMS:]
+    scatter_body(exp, con, own, mix_own, ask, source, mix, norms, *rest)
+
+
+def scatter_body(exp, con, own, mix_own, ask, source, mix, norms, away, early, kept, key_w, value_w, text, result, out, norm_out, whole, text_back, result_back, acc, other, side, low, high, last, total, norm_buf, norm_line, back, early_buf, kept_buf, weight_buf, wide, *sems):
+    local_sem, mate_send, mate_recv, side_send, side_recv, line_send, low_recv, high_recv, last_send, last_recv, norm_send, norm_recv, away_send, back_recv, load_sem, wide_sem, trade_send, trade_recv = sems
     z, x, c, y = place()
     half = out.shape[2]
     mine = z * 4 + x * 2 + c
@@ -610,9 +697,69 @@
             copy(ref.at[:, :, 1 - c, :, columns], other.at[spot], mate_send.at[p, k], mate_recv.at[p, k], mate).start()
             pltpu.make_async_copy(ref.at[:, :, c, :, columns], acc.at[spot], local_sem.at[p, k]).start()
 
+    count, given = kept.shape[0], away.shape[0]
+
+    def load(n):
+        return pltpu.make_async_copy(kept.at[n, y], kept_buf.at[n], load_sem.at[n])
+
+    def load_early():
+        return pltpu.make_async_copy(early, early_buf, load_sem.at[count])
+
+    def load_weight(k):
+        return pltpu.make_async_copy((key_w, value_w)[k], weight_buf.at[k], load_sem.at[count + 1 + k])
+
+    for k in range(2):
+        load_weight(k).start()
+    for n in range(count):
+        load(n).start()
+    load_early().start()
+
+    def put(item):
+        place_at = jnp.where(item < count, y * count + item, (1 - y) * count + item - count)
+        return pltpu.make_async_copy(wide.at[item % 2], whole.at[place_at], wide_sem.at[item % 2])
+
+    def room(item):
+        @pl.when(item >= 2)
+        def _():
+            put(item - 2).wait()
+
+    def keep(item):
+        @pl.when(item == 0)
+        def _():
+            for k in range(2):
+                load_weight(k).wait()
+
+        load(item).wait()
+        room(item)
+        rows, width = kept_buf.at[item], weight_buf.shape[1]
+        product = dot(rows[:, :width], weight_buf[0], 1, 1) + dot(rows[:, width:], weight_buf[1], 1, 1)
+        wide[item % 2] = product.astype(bf16)
+        put(item).start()
+
+    def widen_early(item):
+        @pl.when(item == count)
+        def _():
+            load_early().wait()
+
+        room(item)
+        wide[item % 2] = early_buf[item - count]
+        put(item).start()
+
+    def widen_late(item):
+        n = item - 2 * count + given
+        for k in range(2):
+            part(2 * n + k).wait_recv()
+        room(item)
+        wide[item % 2] = back[n]
+        put(item).start()
+
+    def trade(k):
+        src, dst = ((text, text_back), (result, result_back))[k]
+        return copy(src, dst, trade_send.at[k], trade_recv.at[k], (mine, 1 - y))
+
     def part(j):
         rows = away.shape[1] // 2
-        spot = (j // 2, pl.ds(j % 2 * rows, rows))
+        spot = (j // 2, pl.ds(pl.multiple_of(j % 2 * rows, 16), rows))
         return copy(away.at[spot], back.at[spot], away_send.at[j], back_recv.at[j], (mine, 1 - y))
 
     def kind(p):
@@ -720,7 +867,9 @@
     def norm_steps(t):
         @pl.when(t == 0)
         def _():
-            norm_buf[0] = norms[...]
+            norm_buf[0] = jnp.zeros(norm_buf.shape[1:], f32)
+            for i, row in enumerate(norms):
+                norm_buf[0, i : i + 1] = row[...]
             norm_pair(0).start()
 
         for step in range(1, 4):
@@ -774,6 +923,12 @@
             @pl.when(t == 1 + PIECES * j // (2 * away.shape[0]))
             def _():
                 part(j).start()
+
+        for k in range(2):
+
+            @pl.when(t == 3 + 4 * k)
+            def _():
+                trade(k).start()
 
         at(t - SIDE_LAG, add_side)
         at(
@@ -783,6 +938,20 @@
         at(t - SIDE_LAG - z, lambda p: pass_line(p, high, to_high, z > 0, lambda unit: unit > z, to_high))
         norm_steps(t)
         at(t - SIDE_LAG - DEPTH, close_line)
+        item = t - 2
+
+        @pl.when((item >= 0) & (item < count))
+        def _():
+            keep(item)
+
+        @pl.when((item >= count) & (item < 2 * count - given))
+        def _():
+            widen_early(item)
+
+        @pl.when((item >= 2 * count - given) & (item < 2 * count))
+        def _():
+            widen_late(item)
+
         return 0
 
     def close(p, _):
@@ -791,8 +960,12 @@
 
     lax.fori_loop(0, PIECES + SIDE_LAG + DEPTH, step, 0)
     lax.fori_loop(0, PIECES, close, 0)
-    for j in range(2 * away.shape[0]):
-        part(j).wait()
+    for k in range(2):
+        trade(k).wait()
+    for j in range(2 * given):
+        part(j).wait_send()
+    for item in (2 * count - 2, 2 * count - 1):
+        put(item).wait()
     norm_out[...] = norm_line[0] + norm_line[1] + norm_line[2] + norm_line[3]
 
     def drain(p, _):
@@ -825,20 +998,23 @@
             norm_down(unit).wait_send()
 
 
-def scatter_near(exp, con, own, mix_own, ask, source, mix, norms, away):
+def scatter_near(exp, con, own, mix_own, ask, source, mix, norms, away, early, kept, key_w, value_w, text, result):
     rows, half = D // (4 * DEPTH), D // 2
+    count, height = kept.shape[0], kept.shape[2]
     grads = [g.reshape(DEPTH, 2, 2, rows, g.shape[1]) for g in (exp, con, own, mix_own, ask, source, mix)]
     vmem = pl.BlockSpec(memory_space=pltpu.VMEM)
     anywhere = pl.BlockSpec(memory_space=pl.ANY)
     dma = pltpu.SemaphoreType.DMA
     return pl.pallas_call(
         scatter_kernel,
-        in_specs=[anywhere] * 7 + [vmem, anywhere],
-        out_specs=[vmem, vmem, anywhere],
+        in_specs=[anywhere] * 7 + [vmem] * NORMS + [anywhere] * 7,
+        out_specs=[vmem, vmem, anywhere, anywhere, anywhere],
         out_shape=[
             jax.ShapeDtypeStruct((PIECES, rows, half), f32),
-            jax.ShapeDtypeStruct(norms.shape, f32),
-            jax.ShapeDtypeStruct(away.shape, away.dtype),
+            jax.ShapeDtypeStruct((8, D), f32),
+            jax.ShapeDtypeStruct((2 * count, height, D), bf16),
+            jax.ShapeDtypeStruct(text.shape, bf16),
+            jax.ShapeDtypeStruct(result.shape, bf16),
         ],
         scratch_shapes=[
             pltpu.VMEM((PIECES, DEPTH, 2, 2, rows, half), bf16),
@@ -848,8 +1024,13 @@
             pltpu.VMEM((PIECES, DEPTH, 2, rows, half), bf16),
             pltpu.VMEM((PIECES, rows, half), bf16),
             pltpu.VMEM((2, rows, half), f32),
-            pltpu.VMEM((6, *norms.shape), f32),
-            pltpu.VMEM((DEPTH, *norms.shape), f32),
+            pltpu.VMEM((6, 8, D), f32),
+            pltpu.VMEM((DEPTH, 8, D), f32),
+            pltpu.VMEM(away.shape, bf16),
+            pltpu.VMEM(early.shape, bf16),
+            pltpu.VMEM((count, height, 2 * D), bf16),
+            pltpu.VMEM((2, D, D), bf16),
+            pltpu.VMEM((2, height, D), bf16),
             dma((PIECES, 2)),
             dma((PIECES, 2)),
             dma((PIECES, 2)),
@@ -864,19 +1045,28 @@
             dma((3 + DEPTH,)),
             dma((2 * away.shape[0],)),
             dma((2 * away.shape[0],)),
+            dma((count + 3,)),
+            dma((2,)),
+            dma((2,)),
+            dma((2,)),
         ],
         cost_estimate=pl.CostEstimate(flops=0, bytes_accessed=SCATTER_COST, transcendentals=0),
         compiler_params=pltpu.CompilerParams(collective_id=1, has_side_effects=True, vmem_limit_bytes=60 * 2**20),
-    )(*grads, norms, away)
-
-
-def scatter_grads(grads, norms, away):
+    )(*grads, *norms, away, early, kept, key_w, value_w, text, result)
+
+
+def scatter_grads(grads, norms, sources, early, late, key_w, value_w, text, result):
     exp, con, own, mix_own, ask, source, mix = grads
+    count = sources.shape[0] // PATCH
     if lax.axis_size("dp") == 4 * DEPTH:
-        parts, norm_sums, back = scatter_near(*grads, jnp.pad(norms, ((0, 8 - norms.shape[0]), (0, 0))), away)
+        kept = sources.reshape(count, 2, PATCH // 2, -1)
+        parts, norm_sums, whole, text, result = scatter_near(*grads, norms, late, early, kept, key_w, value_w, text, result)
         ordered = [parts[p] for p in range(PIECES) if p % 3 != 2] + [parts[p] for p in range(PIECES) if p % 3 == 2]
         exp, con = (jnp.concatenate(part, axis=1) for part in (ordered[:4], ordered[4:8]))
-        return [*ordered[8:], exp, con], norm_sums, back
+        return [*ordered[8:], exp, con], norm_sums, whole.astype(f32), text, result
+    side = lax.axis_index("mp")
+    whole = patch_product(sources, key_w, value_w, 0, count, side, side * count, 2 * count, f32)
+    whole = widen(early, swap(late), whole, (1 - side) * count)
     sides = []
     for g in (own, mix_own, ask, source, mix):
         sides.append(g.reshape(D, g.shape[1] // D, 2, D // 2).transpose(1, 2, 0, 3))
@@ -886,7 +1076,7 @@
     parts = lax.psum_scatter(stacked, ("mp", "dp"), scatter_dimension=1, tiled=True).astype(f32)
     chunks = (parts.shape[0] - 8) // 2
     exp, con = (jnp.concatenate(list(parts[start : start + chunks]), axis=1) for start in (8, 8 + chunks))
-    return [*(parts[i] for i in range(8)), exp, con], lax.psum(norms, BOTH), swap(away)
+    return [*(parts[i] for i in range(8)), exp, con], lax.psum(jnp.concatenate(norms), BOTH), whole, swap(text), swap(result)
 
 
 def body(text_tokens, image_tokens, resolution, *rest):
@@ -895,18 +1085,21 @@
     half = text_tokens.shape[0] // 2
     width = text_tokens.shape[2]
     flat = [shard.T if turned else shard for shard, turned in zip(shards, TURNED)]
-    weights = gather_weights(jnp.stack(flat[:8]), flat[8], flat[9])
-    text = to_captions(text_tokens, side)
-    grad_out = to_captions(cotangent, side)
-    patches = lax.dynamic_slice_in_dim(image_tokens, side * half, half, 0)
+    text_mine, text_away = split_captions(text_tokens, side)
+    grad_mine, grad_away = split_captions(cotangent, side)
+    weights, text_back, grad_back, patches = gather_weights(
+        jnp.stack(flat[:8]), flat[8], flat[9], text_away, grad_away, image_tokens
+    )
+    text = join_captions(text_mine, text_back, side)
+    grad_out = join_captions(grad_mine, grad_back, side)
     flags = lax.dynamic_slice_in_dim(resolution, side * half, half, 0)
     layer_out, text_grad, patch_grad, weight_grads, norm_outs = layer(
         weights, norms, text.reshape(-1, width), grad_out.reshape(-1, width), patches.reshape(-1, width), flags
     )
     weight_outs = [g.T if turned else g for g, turned in zip(weight_grads, TURNED)]
     return (
-        to_positions(layer_out.reshape(half, LEN, width), side),
-        to_positions(text_grad.reshape(half, LEN, width), side).astype(f32),
+        layer_out,
+        text_grad,
         patch_grad,
         *weight_outs,
         *(norm_outs[i] for i in range(6)),

time: 433 us -> 411 us (0.949)
  local copies, waits for them, and re-layouts: 34.7 us -> 19.1 us
  Pallas kernels: 267 us -> 257 us
  matrix products: 94.9 us -> 104 us
  starting transfers between devices: 6.55 us -> 0.51 us
    pallas_call x3 -> x2, Pallas kernels: 25.5 us -> 15.5 us  [patch_product(): pl.pallas_call(patch_kernel, grid_spec=grid_spec, out_shape=jax.ShapeDtyp...]
    dot_general x20 -> x25, matrix products: 94.9 us -> 104 us  [dot(): lax.dot_general(left, right, (((left_dim,), (right_dim,)), ((), ())), pre...]
    convert_element_type x1 -> x2, other arithmetic: 2.82 us -> 11.5 us  [the longest x1 9.85 us: scatter_grads(): whole.astype(f32)]
    dynamic_slice x5 -> x4, local copies, waits for them, and re-layouts: 11.6 us -> 5.16 us  [the longest x2 3.53 us: split_captions(): lax.dynamic_slice_in_dim(rows, at * half, half, 0)]
    slice x1 -> x0, local copies, waits for them, and re-layouts: 6.34 us -> none  [gather_weights(): return (project_self, att[3], att[4], project_patch, att[7], exp, con)]
    ppermute x5 -> x1, starting transfers between devices: 6.55 us -> 0.51 us  [swap(): return lax.ppermute(rows, 'mp', [(0, 1), (1, 0)])]
    pallas_call x3 -> x2, Pallas kernels: 194 us -> 194 us  [the longest x1 110 us: scatter_near(): pl.pallas_call(scatter_kernel, in_specs=[anywhere] * 7 + [vmem] * NORMS +...]
  transfers between devices with their start and end apart: 5 -> 1, of which waited for: 1 -> 1; matrix products, arithmetic and copies ran while one was open for 15% -> 8% of each run, Pallas kernels for 27% -> 4%
where the time goes in v7:
time: 411 us; the launch traced here: 405 us
  Pallas kernels  257 us (63%)
  matrix products  104 us (25%)
  other arithmetic  20.7 us (5%)
  local copies, waits for them, and re-layouts  19.1 us (5%)
    pallas_call x1, Pallas kernels, scatter_near(): pl.pallas_call(scatter_kernel, in_specs=[anywhere] * 7 + [vmem] * NORMS +...  110 us
    dot_general x25, matrix products, dot(): lax.dot_general(left, right, (((left_dim,), (right_dim,)), ((), ())), pre...  104 us
    pallas_call x1, Pallas kernels, gather_near(): pl.pallas_call(gather_kernel, in_specs=[vmem] * 3 + [anywhere] * 3, out_s...  84.5 us
    pallas_call x2, Pallas kernels, attend_back(): pl.pallas_call(functools.partial(attend_back_kernel, batch), grid=(count...  27.7 us
    pallas_call x2, Pallas kernels, attend(): pl.pallas_call(functools.partial(attend_kernel, causal, batch), grid_spec...  19.2 us
    pallas_call x2, Pallas kernels, patch_product(): pl.pallas_call(patch_kernel, grid_spec=grid_spec, out_shape=jax.ShapeDtyp...  15.5 us
    convert_element_type x1, other arithmetic, scatter_grads(): whole.astype(f32)  9.85 us
  transfers between devices with their start and end apart: 1, of which 1 were waited for; matrix products, arithmetic and copies ran while one was open for 8% of the time, Pallas kernels for 4%

profile of v7, /device:TPU:0, one launch (start us, length us, event | category | flops | bytes accessed | tf_op | source)
XLA Modules:
  0.0 404.7 jit_solution(17652414381426913194)
XLA Ops:
  0.7 0.8 bitcast_dynamic-update-slice_fusion.7
  1.6 1.8 constant_dynamic-slice_fusion.5.text_in
  3.3 1.8 constant_dynamic-slice_fusion.4.grad_in
  5.3 0.7 copy-done.15
  6.0 84.5 %shard_map.339 = (bf16[16,48,768]{2,1,0:T(8,128)(2,1)}, bf16[16,48,768]{2,1,0:T(8,128)(2,1)}, bf16[16,48,768]{2,1,0:T(8,128)(2,1)}, bf16[16,48,768]{2,1,0:T(8,12...) custom-call(bf16[8,48,384]{2,1,0:T(8,128)(2,1)} %copy-done.15, ...), custom_call_target="tpu_custom_call" | custom-call | tf_op jit(solution)/shard_map/pallas_call | solution.py:615
  90.5 1.2 broadcast_select_fusion.1
  92.4 0.6 dynamic_slice.31.flag_ref
  93.8 1.7 convolution_convert_fusion.12.value_ref
  95.5 1.7 convolution_convert_fusion.13.key_ref
  97.2 1.7 convolution_convert_fusion.14.query_ref
  98.8 6.0 %shard_map.340 = (bf16[512,768]{1,0:T(8,128)(2,1)}, bf16[512,768]{1,0:T(8,128)(2,1)}) custom-call(s32[8]{0:T(128)} %dynamic_slice.31.flag_ref, bf16[512,768]{1,0:T(8,128)(2,1)} %convolution_convert_fusion.14.query_ref, bf16[512,768]{1,0:T(8,128)(2,1)} %convolution_convert_fusion.13.key_ref, bf16[512,768]{1,0:T(8,128)(2,1)} %convolution_convert_fusion.12.value_ref), custom_call_target="tpu_custom_call" | custom-call | flops 402653184 | bytes 1572864 | tf_op jit(solution)/shard_map/pallas_call | solution.py:146
  104.8 2.4 fusion.36
  107.6 0.9 copy-done.3
  108.5 11.0 %convolution_convert_fusion.value_ref = bf16[4608,768]{1,0:T(8,128)(2,1)} fusion(bf16[4608,768]{1,0:T(8,128)(2,1)} %bitcast.192, bf16[768,768]{1,0:T(8,128)(2,1)S(1)} %bitcast.174), kind=kOutput, calls=%fused_computation.2 | convolution fusion | flops 5439356928 | bytes 15335424 | tf_op jit(solution)/shard_map/dot_general | solution.py:26
  119.5 8.3 %convolution_convert_fusion.1.key_ref = bf16[4608,768]{1,0:T(8,128)(2,1)} fusion(bf16[4608,768]{1,0:T(8,128)(2,1)S(1)} %bitcast.196, bf16[768,768]{1,0:T(8,128)(2,1)S(1)} %bitcast.170), kind=kOutput, calls=%fused_computation.3 | convolution fusion | flops 5439356928 | bytes 15335424 | tf_op jit(solution)/shard_map/dot_general | solution.py:26
  127.8 1.9 convolution_convert_fusion.11.query_ref
  129.7 13.3 %shard_map.341 = (bf16[512,768]{1,0:T(8,128)(2,1)}, bf16[4608,768]{1,0:T(8,128)(2,1)}) custom-call(s32[8]{0:T(128)} %dynamic_slice.31.flag_ref, bf16[512,768]{1,0:T(8,128)(2,1)} %convolution_convert_fusion.11.query_ref, bf16[4608,768]{1,0:T(8,128)(2,1)} %convolution_convert_fusion.1.key_ref, bf16[4608,768]{1,0:T(8,128)(2,1)} %convolution_convert_fusion.value_ref), custom_call_target="tpu_custom_call" | custom-call | flops 3623878656 | bytes 14155776 | tf_op jit(solution)/shard_map/pallas_call | solution.py:146
  143.0 2.4 fusion.37
  146.1 4.9 %fusion.34 = f32[512,3072]{1,0:T(8,128)S(1)} fusion(bf16[768,3072]{1,0:T(8,128)(2,1)} %bitcast.197, f32[512,768]{1,0:T(8,128)S(1)} %get-tuple-element.142, f32[768]{0:T(1024)S(1)} %copy-done.43, f32[768]{0:T(1024)S(1)} %copy-done.33, f32[512]{0:T(512)S(1)} %add_rsqrt_fusion.1, f32[512]{0:T(512)S(1)} %broadcast_multiply_fusion.7), kind=kOutput, calls=%fused_computation.134 | convolution fusion | flops 2417885184 | bytes 12593152 | tf_op jit(solution)/shard_map/dot_general | solution.py:26
  151.0 4.9 %add_convert_fusion = bf16[512,768]{1,0:T(8,128)(2,1)} fusion(f32[512,768]{1,0:T(8,128)S(1)} %get-tuple-element.142, bf16[768,3072]{1,0:T(8,128)(2,1)S(1)} %bitcast.203, f32[512,3072]{1,0:T(8,128)S(1)} %fusion.34), kind=kOutput, calls=%fused_computation.44 | convolution fusion | flops 2430861312 | bytes 13369344 | tf_op jit(solution)/shard_map/dot_general | solution.py:26
  155.9 5.7 %fusion.6 = bf16[512,3072]{1,0:T(8,128)(2,1)S(1)} fusion(f32[512,3072]{1,0:T(8,128)S(1)} %fusion.34, bf16[512,768]{1,0:T(8,128)(2,1)S(1)} %bitcast.179, bf16[768,3072]{1,0:T(8,128)(2,1)S(1)} %bitcast.204), kind=kOutput, calls=%fused_computation.10 | convolution fusion | flops 2445803520 | bytes 14942208 | tf_op jit(solution)/shard_map/dot_general | solution.py:26
  161.6 4.7 %convolution_convert_fusion.3 = bf16[768,3072]{1,0:T(8,128)(2,1)} fusion(bf16[512,768]{1,0:T(8,128)(2,1)S(1)} %bitcast.180, f32[512,3072]{1,0:T(8,128)S(1)} %fusion.34), kind=kOutput, calls=%fused_computation.13 | convolution fusion | flops 2432434176 | bytes 11796480 | tf_op jit(solution)/shard_map/dot_general | solution.py:26
  166.4 3.6 multiply_reduce_fusion
  170.0 4.9 %convolution_convert_fusion.4 = bf16[768,3072]{1,0:T(8,128)(2,1)} fusion(bf16[512,3072]{1,0:T(8,128)(2,1)S(1)} %fusion.6, f32[512,768]{1,0:T(8,128)S(1)} %get-tuple-element.142, f32[768]{0:T(1024)S(1)} %copy-done.43, f32[768]{0:T(1024)S(1)} %copy-done.33, f32[512]{0:T(512)S(1)} %add_rsqrt_fusion.1, f32[512]{0:T(512)S(1)} %broadcast_multiply_fusion.7), kind=kOutput, calls=%fused_computation.14 | convolution fusion | flops 2420244480 | bytes 9447424 | tf_op jit(solution)/shard_map/dot_general | solution.py:26
  174.9 1.8 fusion.35
  176.7 1.8 convolution_convert_fusion.8
  178.6 1.7 convolution_convert_fusion.10.grad_ref
  180.2 18.1 %shard_map.342 = (bf16[512,768]{1,0:T(8,128)(2,1)}, bf16[4608,1536]{1,0:T(8,128)(2,1)}) custom-call(bf16[512,768]{1,0:T(8,128)(2,1)} %convolution_convert_fusion.11.query_ref, bf16[4608,768]{1,0:T(8,128)(2,1)} %convolution_convert_fusion.1.key_ref, bf16[4608,768]{1,0:T(8,128)(2,1)} %convolution_convert_fusion.value_ref, ...), custom_call_target="tpu_custom_call" | custom-call | flops 7247757312 | bytes 28311552 | tf_op jit(solution)/shard_map/pallas_call | solution.py:162
  198.3 17.2 %convolution_convert_fusion.5 = bf16[768,1536]{1,0:T(8,128)(2,1)} fusion(bf16[4608,768]{1,0:T(8,128)(2,1)} %bitcast.193, bf16[4608,1536]{1,0:T(8,128)(2,1)} %get-tuple-element.78), kind=kOutput, calls=%fused_computation.15 | convolution fusion | flops 10872815616 | bytes 23592960 | tf_op jit(solution)/shard_map/dot_general | solution.py:26
  215.5 2.0 convolution_convert_fusion.7
  217.6 0.6 pad_add_fusion.side_ref
  218.2 8.7 %shard_map.343 = bf16[5,288,768]{2,1,0:T(8,128)(2,1)} custom-call(s32[2]{0:T(128)} %pad_add_fusion.side_ref, bf16[8,576,1536]{2,1,0:T(8,128)(2,1)} %bitcast.164, bf16[768,768]{1,0:T(8,128)(2,1)} %bitcast.167, bf16[768,768]{1,0:T(8,128)(2,1)} %bitcast.171), custom_call_target="tpu_custom_call" | custom-call | flops 1048576 | bytes 1365 | tf_op jit(solution)/shard_map/pallas_call | solution.py:204
  226.9 0.5 collective-permute-start
  227.4 0.5 iota_compare_fusion
  227.9 0.7 div.46
  228.5 0.7 rsqrt.31
  229.2 3.2 multiply_reduce_fusion.1
  232.4 1.3 multiply_add_fusion.1
  233.7 1.7 convolution_convert_fusion.9.grad_ref
  235.4 9.6 %shard_map.344 = bf16[512,2304]{1,0:T(8,128)(2,1)} custom-call(bf16[512,768]{1,0:T(8,128)(2,1)} %convolution_convert_fusion.14.query_ref, bf16[512,768]{1,0:T(8,128)(2,1)} %convolution_convert_fusion.13.key_ref, bf16[512,768]{1,0:T(8,128)(2,1)} %convolution_convert_fusion.12.value_ref, bf16[512,768]{1,0:T(8,128)(2,1)} %get-tuple-element.73.prob_ref, ...), custom_call_target="tpu_custom_call" | custom-call | flops 1048576 | bytes 1048576 | tf_op jit(solution)/shard_map/pallas_call | solution.py:162
  245.0 3.2 fusion.27
  248.3 3.2 fusion.29
  251.6 0.6 broadcast_in_dim.101.rest_4_
  252.2 0.6 broadcast_in_dim.102.rest_5_
  252.8 0.6 broadcast_in_dim.99.rest_2_
  253.4 0.6 broadcast_in_dim.100.rest_3_
  254.0 4.8 %fusion.21 = (f32[512]{0:T(512)S(1)}, f32[768]{0:T(1024)S(1)}, f32[512]{0:T(512)S(1)}, f32[768]{0:T(1024)S(1)}, f32[512,768]{1,0:T(8,128)}) fusion(f32[768]{0:T(1024)S(1)} %copy-done.25, f32[512]{0:T(512)S(1)} %copy-done.27, f32[512]{0:T(512)S(1)} %copy-done.26, bf16[8,32,768]{2,1,0:T(8,128)(2,1)S(1)} %copy-done.1, ...), kind=kOutput, calls=%fused_computation.34 | convolution fusion | flops 609875456 | bytes 7488512 | tf_op jit(solution)/shard_map/dot_general | solution.py:26
  258.7 0.6 broadcast_in_dim.97.rest_0_
  259.3 0.6 broadcast_in_dim.98.rest_1_
  259.9 6.8 %shard_map.345.rest_6_ = bf16[3,288,768]{2,1,0:T(8,128)(2,1)} custom-call(s32[2]{0:T(128)} %pad_add_fusion.side_ref, bf16[8,576,1536]{2,1,0:T(8,128)(2,1)} %bitcast.165, bf16[768,768]{1,0:T(8,128)(2,1)} %bitcast.168, bf16[768,768]{1,0:T(8,128)(2,1)} %bitcast.172), custom_call_target="tpu_custom_call" | custom-call | flops 1048576 | bytes 1365 | tf_op jit(solution)/shard_map/pallas_call | solution.py:204
  266.8 0.8 constant_dynamic-slice_fusion.3
  267.6 0.7 copy-done.6
  268.3 0.7 fusion.25
  269.0 0.8 constant_dynamic-slice_fusion
  270.3 1.8 convolution_convert_fusion.6
  272.1 3.9 convolution_convert_fusion.2
  276.0 1.5 collective-permute-done.rest_7_
  277.6 109.9 %shard_map.346 = (f32[16,48,384]{2,1,0:T(8,128)}, f32[8,768]{1,0:T(8,128)}, bf16[16,288,768]{2,1,0:T(8,128)(2,1)}, bf16[8,32,768]{2,1,0:T(8,128)(2,1)}, bf16[8,32,768]{2,1,0:T(8,128)(2,1)}) custom-call(bf16[4,2,2,48,3072]{4,3,2,1,0:T(8,128)(2,1)} %bitcast.176, bf16[4,2,2,48,3072]{4,3,2,1,0:T(8,128)(2,1)} %bitcast.175, ...), custom_call_target="tpu_custom_call" | custom-call | bytes 1048576 | tf_op jit(solution)/shard_map/pallas_call | solution.py:1008
  387.5 1.6 slice_reduce_fusion
  389.2 2.1 slice_bitcast_fusion.3
  391.3 9.9 %convert_element_type.156 = f32[16,288,768]{2,1,0:T(8,128)} convert(bf16[16,288,768]{2,1,0:T(8,128)(2,1)} %get-tuple-element.88) | non-fusion elementwise | flops 3538944 | bytes 21233664 | tf_op jit(solution)/shard_map/convert_element_type | solution.py:1066
  401.2 0.7 maximum_bitcast_fusion
  401.9 0.7 pad_maximum_fusion.2
  402.6 1.6 fusion.31
  (136 shorter events, 3.3 us)
Async XLA Ops:
  0.7 4.4 %copy-start.16 = (bf16[48,384]{1,0:T(8,128)(2,1)S(1)}, bf16[48,384]{1,0:T(8,128)(2,1)}, u32[]{:S(2)}) copy-start(bf16[48,384]{1,0:T(8,128)(2,1)} %param.24) | copy-start | bytes 110596
  0.7 4.4 %copy-start.17 = (bf16[48,384]{1,0:T(8,128)(2,1)S(1)}, bf16[48,384]{1,0:T(8,128)(2,1)}, u32[]{:S(2)}) copy-start(bf16[48,384]{1,0:T(8,128)(2,1)} %param.25) | copy-start | bytes 110596
  0.7 4.4 %copy-start.18 = (bf16[384,48]{0,1:T(8,128)(2,1)S(1)}, bf16[384,48]{0,1:T(8,128)(2,1)}, u32[]{:S(2)}) copy-start(bf16[384,48]{0,1:T(8,128)(2,1)} %param.26) | copy-start | bytes 110596
  0.7 4.5 %copy-start.19 = (bf16[48,384]{1,0:T(8,128)(2,1)S(1)}, bf16[48,384]{1,0:T(8,128)(2,1)}, u32[]{:S(2)}) copy-start(bf16[48,384]{1,0:T(8,128)(2,1)} %param.27) | copy-start | bytes 110596
  0.7 4.5 %copy-start.20 = (bf16[48,384]{1,0:T(8,128)(2,1)S(1)}, bf16[48,384]{1,0:T(8,128)(2,1)}, u32[]{:S(2)}) copy-start(bf16[48,384]{1,0:T(8,128)(2,1)} %param.28) | copy-start | bytes 110596
  0.7 4.5 %copy-start.21 = (bf16[48,384]{1,0:T(8,128)(2,1)S(1)}, bf16[48,384]{1,0:T(8,128)(2,1)}, u32[]{:S(2)}) copy-start(bf16[48,384]{1,0:T(8,128)(2,1)} %param.29) | copy-start | bytes 110596
  0.7 4.5 %copy-start.22 = (bf16[384,48]{0,1:T(8,128)(2,1)S(1)}, bf16[384,48]{0,1:T(8,128)(2,1)}, u32[]{:S(2)}) copy-start(bf16[384,48]{0,1:T(8,128)(2,1)} %param.30) | copy-start | bytes 110596
  5.3 0.7 copy-start.15
  6.0 84.5 %copy-start.11 = (bf16[16,32,768]{2,1,0:T(8,128)(2,1)S(1)}, bf16[16,32,768]{2,1,0:T(8,128)(2,1)}, u32[]{:S(2)}) copy-start(bf16[16,32,768]{2,1,0:T(8,128)(2,1)} %param.20) | copy-start | bytes 2359300
  6.0 84.5 %copy-start.12 = (bf16[16,32,768]{2,1,0:T(8,128)(2,1)S(1)}, bf16[16,32,768]{2,1,0:T(8,128)(2,1)}, u32[]{:S(2)}) copy-start(bf16[16,32,768]{2,1,0:T(8,128)(2,1)} %param.39) | copy-start | bytes 2359300
  91.8 1.6 copy-start
  91.8 0.7 copy-start.45
  91.8 1.6 copy-start.23
  91.8 1.6 copy-start.24
  92.4 1.3 copy-start.36
  93.8 1.7 copy-start.39
  95.5 1.7 copy-start.37
  107.2 1.3 copy-start.3
  107.2 12.2 %slice-start = ((s8[7077888]{0:T(1024)(128)(4,1)}), s8[4194304]{0:T(1024)(128)(4,1)S(1)}, s32[]{:S(2)}) async-start(s8[7077888]{0:T(1024)(128)(4,1)} %bitcast.194), calls=%async_computation | async-start | bytes 8388608
  107.5 121.7 %copy-start.28 = (f32[512]{0:T(512)}, f32[512]{0:T(512)S(1)}, u32[]{:S(2)}) copy-start(f32[512]{0:T(512)S(1)} %add_rsqrt_fusion.2) | copy-start | bytes 6148
  108.5 11.0 %copy-start.2 = (bf16[16,48,768]{2,1,0:T(8,128)(2,1)S(1)}, bf16[16,48,768]{2,1,0:T(8,128)(2,1)}, u32[]{:S(2)}) copy-start(bf16[16,48,768]{2,1,0:T(8,128)(2,1)} %get-tuple-element.64) | copy-start | bytes 3538948
  108.5 11.0 %slice-start.1 = ((s8[7077888]{0:T(1024)(128)(4,1)}), s8[2883584]{0:T(1024)(128)(4,1)S(1)}, s32[]{:S(2)}) async-start(s8[7077888]{0:T(1024)(128)(4,1)} %bitcast.194), calls=%async_computation.1 | async-start | bytes 5767168
  119.5 8.3 %copy-start.34 = (f32[768]{0:T(1024)S(1)}, f32[768]{0:T(1024)}, u32[]{:S(2)}) copy-start(f32[768]{0:T(1024)} %param.35) | copy-start | bytes 9220
  119.5 8.3 %copy-start.42 = (bf16[16,48,768]{2,1,0:T(8,128)(2,1)S(1)}, bf16[16,48,768]{2,1,0:T(8,128)(2,1)}, u32[]{:S(2)}) copy-start(bf16[16,48,768]{2,1,0:T(8,128)(2,1)} %get-tuple-element.62) | copy-start | bytes 3538948
  119.5 8.3 %copy-start.44 = (f32[768]{0:T(1024)S(1)}, f32[768]{0:T(1024)}, u32[]{:S(2)}) copy-start(f32[768]{0:T(1024)} %param.36) | copy-start | bytes 9220
  145.4 0.7 copy-start.33
  145.4 0.7 copy-start.43
  145.7 5.3 %slice-start.4 = ((s8[4718592]{0:T(1024)(128)(4,1)}), s8[4194304]{0:T(1024)(128)(4,1)S(1)}, s32[]{:S(2)}) async-start(s8[4718592]{0:T(1024)(128)(4,1)} %bitcast.201), calls=%async_computation.4 | async-start | bytes 8388608
  146.1 4.9 %slice-start.5 = ((s8[4718592]{0:T(1024)(128)(4,1)}), s8[524288]{0:T(1024)(128)(4,1)S(1)}, s32[]{:S(2)}) async-start(s8[4718592]{0:T(1024)(128)(4,1)} %bitcast.201), calls=%async_computation.5 | async-start | bytes 1048576
  151.0 15.4 %slice-start.2 = ((s8[4718592]{0:T(1024)(128)(4,1)}), s8[4194304]{0:T(1024)(128)(4,1)S(1)}, s32[]{:S(2)}) async-start(s8[4718592]{0:T(1024)(128)(4,1)} %bitcast.198), calls=%async_computation.2 | async-start | bytes 8388608
  155.9 10.5 %slice-start.3 = ((s8[4718592]{0:T(1024)(128)(4,1)}), s8[524288]{0:T(1024)(128)(4,1)S(1)}, s32[]{:S(2)}) async-start(s8[4718592]{0:T(1024)(128)(4,1)} %bitcast.198), calls=%async_computation.3 | async-start | bytes 1048576
  174.9 1.8 copy-start.9
  176.7 1.8 copy-start.7
  198.3 17.2 %copy-start.47 = (bf16[512,768]{1,0:T(8,128)(2,1)S(1)}, bf16[512,768]{1,0:T(8,128)(2,1)}, u32[]{:S(2)}) copy-start(bf16[512,768]{1,0:T(8,128)(2,1)} %get-tuple-element.79) | copy-start | bytes 2359300
  226.9 50.7 %collective-permute-start = (bf16[5,288,768]{2,1,0:T(8,128)(2,1)}, bf16[5,288,768]{2,1,0:T(8,128)(2,1)}, u32[]{:S(2)}, u32[]{:S(2)}) collective-permute-start(bf16[5,288,768]{2,1,0:T(8,128)(2,1)} %shard_map.343), channel_id=1, source_target_pairs={{0,1},{1,0},{2,3},{3,2},{4,5},{5,4},{6,7},{7,6},{8,9},{9,8},{10,11... | collective-permute-start | bytes 6635528 | tf_op jit(solution)/shard_map/ppermute | solution.py:179
  229.2 3.2 copy-start.4
  229.2 3.2 copy-start.35
  232.4 1.3 copy-start.41
  235.4 9.6 %copy-start.40 = (bf16[16,48,768]{2,1,0:T(8,128)(2,1)S(1)}, bf16[16,48,768]{2,1,0:T(8,128)(2,1)}, u32[]{:S(2)}) copy-start(bf16[16,48,768]{2,1,0:T(8,128)(2,1)} %get-tuple-element.58) | copy-start | bytes 3538948
  245.0 3.2 copy-start.38
  248.2 3.2 copy-start.46
  248.2 3.4 copy-start.30
  248.2 4.0 copy-start.29
  248.2 4.6 %copy-start.32 = (f32[768]{0:T(1024)S(1)}, f32[768]{0:T(1024)}, u32[]{:S(2)}) copy-start(f32[768]{0:T(1024)} %get-tuple-element.93) | copy-start | bytes 9220
  248.3 5.1 %copy-start.31 = (f32[768]{0:T(1024)S(1)}, f32[768]{0:T(1024)}, u32[]{:S(2)}) copy-start(f32[768]{0:T(1024)} %get-tuple-element.102) | copy-start | bytes 9220
  248.3 5.7 %copy-start.1 = (bf16[8,32,768]{2,1,0:T(8,128)(2,1)S(1)}, bf16[8,32,768]{2,1,0:T(8,128)(2,1)}, u32[]{:S(2)}) copy-start(bf16[8,32,768]{2,1,0:T(8,128)(2,1)} %copy-done) | copy-start | bytes 1179652
  248.3 5.7 %copy-start.25 = (f32[768]{0:T(1024)S(1)}, f32[768]{0:T(1024)}, u32[]{:S(2)}) copy-start(f32[768]{0:T(1024)} %param.33) | copy-start | bytes 9220
  248.3 5.7 %copy-start.26 = (f32[512]{0:T(512)S(1)}, f32[512]{0:T(512)}, u32[]{:S(2)}) copy-start(f32[512]{0:T(512)} %div.46) | copy-start | bytes 6148
  248.3 5.7 %copy-start.27 = (f32[512]{0:T(512)S(1)}, f32[512]{0:T(512)}, u32[]{:S(2)}) copy-start(f32[512]{0:T(512)} %rsqrt.31) | copy-start | bytes 6148
  259.9 6.9 %copy-start.10 = (bf16[512,768]{1,0:T(8,128)(2,1)S(1)}, bf16[512,768]{1,0:T(8,128)(2,1)}, u32[]{:S(2)}) copy-start(bf16[512,768]{1,0:T(8,128)(2,1)} %add_convert_fusion) | copy-start | bytes 2359300
  266.7 1.6 copy-start.6
  269.0 1.3 copy-start.8
  270.3 1.8 copy-start.5
  391.3 11.3 %copy-start.13 = (bf16[8,32,768]{2,1,0:T(8,128)(2,1)S(1)}, bf16[8,32,768]{2,1,0:T(8,128)(2,1)}, u32[]{:S(2)}) copy-start(bf16[8,32,768]{2,1,0:T(8,128)(2,1)} %get-tuple-element.87) | copy-start | bytes 1179652
  391.3 11.3 %copy-start.14 = (bf16[8,32,768]{2,1,0:T(8,128)(2,1)S(1)}, bf16[8,32,768]{2,1,0:T(8,128)(2,1)}, u32[]{:S(2)}) copy-start(bf16[8,32,768]{2,1,0:T(8,128)(2,1)} %get-tuple-element.86) | copy-start | bytes 1179652

commit v8 on v7

--- a/solution.py
+++ b/solution.py
@@ -289,12 +289,10 @@
     grad_query_cross = weight_grad(normed_two, grad_queries).astype(bf16)
     grad_patch = weight_grad(patches, grad_sources).astype(bf16)
     grad_patch, grad_sources, grad_query_cross = lax.optimization_barrier((grad_patch, grad_sources, grad_query_cross))
-    first = count * 5 // 8
-    near, far = (0, first), (first, count)
-    early = patch_product(grad_sources, key_cross, value_cross, *near, 1 - side, 0 * side, first, bf16)
+    first = count // 2
+    early = patch_product(grad_sources, key_cross, value_cross, 0, first, 1 - side, 0 * side, first, bf16)
     early, grad_queries = lax.optimization_barrier((early, grad_queries))
     early = swap(early)
-    late = patch_product(grad_sources, key_cross, value_cross, *far, 1 - side, 0 * side, count - first, bf16)
     grad_normed = matmul_t(grad_queries, query_cross)
     grad_input, gain_two, shift_two = norm_back(normal_two, inverse_two, second_gain, grad_normed)
     grad_stream = grad_stream + grad_input
@@ -313,7 +311,7 @@
     layer_mine, layer_away = split_positions(layer_out.reshape(count, LEN, D), side)
     text_mine, text_away = split_positions(text_grad.reshape(count, LEN, D), side)
     weight_grads, norm_sums, patch_grad, text_back, layer_back = scatter_grads(
-        grads, norm_grads, grad_sources, early, late, key_cross, value_cross, text_away, layer_away
+        grads, norm_grads, grad_sources, early, key_cross, value_cross, text_away, layer_away
     )
     layer_out = join_positions(layer_mine, layer_back, side)
     text_grad = join_positions(text_mine, text_back, side).astype(f32)
@@ -662,6 +660,7 @@
 
 
 PIECES = 16
+PERIOD = 4
 SCATTER_COST = 2**20
 SIDE_LAG = 1
 NORM_STEP = 2
@@ -673,7 +672,7 @@
     scatter_body(exp, con, own, mix_own, ask, source, mix, norms, *rest)
 
 
-def scatter_body(exp, con, own, mix_own, ask, source, mix, norms, away, early, kept, key_w, value_w, text, result, out, norm_out, whole, text_back, result_back, acc, other, side, low, high, last, total, norm_buf, norm_line, back, early_buf, kept_buf, weight_buf, wide, *sems):
+def scatter_body(exp, con, own, mix_own, ask, source, mix, norms, early, kept, key_w, value_w, text, result, out, norm_out, whole, text_back, result_back, acc, other, side, low, high, last, total, norm_buf, norm_line, back, sent, sent_in, early_buf, kept_buf, weight_buf, wide, *sems):
     local_sem, mate_send, mate_recv, side_send, side_recv, line_send, low_recv, high_recv, last_send, last_recv, norm_send, norm_recv, away_send, back_recv, load_sem, wide_sem, trade_send, trade_recv = sems
     z, x, c, y = place()
     half = out.shape[2]
@@ -688,20 +687,24 @@
     pieces += [(own, half, 0), (own, half, 2 * half), (own, half, 4 * half), (mix_own, half, 0), (ask, half, 0)]
     pieces += [(source, half, 0), (source, half, 2 * half), (mix, half, 0)]
 
-    over_x, over_y = pieces[: PIECES * 2 // 3 + 1], pieces[PIECES * 2 // 3 + 1 :]
+    over_x, over_y = pieces[: PIECES - PIECES // PERIOD], pieces[PIECES - PIECES // PERIOD :]
     for p in range(PIECES):
-        ref, stride, offset = over_y[p // 3] if p % 3 == 2 else over_x[p // 3 * 2 + p % 3]
+        odd = p % PERIOD == PERIOD - 1
+        ref, stride, offset = over_y[p // PERIOD] if odd else over_x[p // PERIOD * (PERIOD - 1) + p % PERIOD]
         for k in range(2):
             columns = pl.ds(k * stride + offset, half)
-            spot = (p, slice(None), k) if p % 3 == 2 else (p, slice(None), slice(None), k)
+            spot = (p, slice(None), k) if odd else (p, slice(None), slice(None), k)
             copy(ref.at[:, :, 1 - c, :, columns], other.at[spot], mate_send.at[p, k], mate_recv.at[p, k], mate).start()
             pltpu.make_async_copy(ref.at[:, :, c, :, columns], acc.at[spot], local_sem.at[p, k]).start()
 
-    count, given = kept.shape[0], away.shape[0]
+    count, given = kept.shape[0], back.shape[0]
 
     def load(n):
         return pltpu.make_async_copy(kept.at[n, y], kept_buf.at[n], load_sem.at[n])
 
+    def load_sent(n):
+        return pltpu.make_async_copy(kept.at[count - given + n, 1 - y], sent_in.at[n], load_sem.at[count + 3 + n])
+
     def load_early():
         return pltpu.make_async_copy(early, early_buf, load_sem.at[count])
 
@@ -710,6 +713,8 @@
 
     for k in range(2):
         load_weight(k).start()
+    for n in range(given):
+        load_sent(n).start()
     for n in range(count):
         load(n).start()
     load_early().start()
@@ -723,17 +728,25 @@
         def _():
             put(item - 2).wait()
 
-    def keep(item):
-        @pl.when(item == 0)
+    def product(rows):
+        width = weight_buf.shape[1]
+        return (dot(rows[:, :width], weight_buf[0], 1, 1) + dot(rows[:, width:], weight_buf[1], 1, 1)).astype(bf16)
+
+    def give(n):
+        @pl.when(n == 0)
         def _():
             for k in range(2):
                 load_weight(k).wait()
 
+        load_sent(n).wait()
+        sent[n] = product(sent_in.at[n])
+        for k in range(2):
+            part(2 * n + k).start()
+
+    def keep(item):
         load(item).wait()
         room(item)
-        rows, width = kept_buf.at[item], weight_buf.shape[1]
-        product = dot(rows[:, :width], weight_buf[0], 1, 1) + dot(rows[:, width:], weight_buf[1], 1, 1)
-        wide[item % 2] = product.astype(bf16)
+        wide[item % 2] = product(kept_buf.at[item])
         put(item).start()
 
     def widen_early(item):
@@ -758,12 +771,12 @@
         return copy(src, dst, trade_send.at[k], trade_recv.at[k], (mine, 1 - y))
 
     def part(j):
-        rows = away.shape[1] // 2
+        rows = sent.shape[1] // 2
         spot = (j // 2, pl.ds(pl.multiple_of(j % 2 * rows, 16), rows))
-        return copy(away.at[spot], back.at[spot], away_send.at[j], back_recv.at[j], (mine, 1 - y))
+        return copy(sent.at[spot], back.at[spot], away_send.at[j], back_recv.at[j], (mine, 1 - y))
 
     def kind(p):
-        odd = jnp.where(p % 3 == 2, 1, 0)
+        odd = jnp.where(p % PERIOD == PERIOD - 1, 1, 0)
         u = x * (1 - odd) + y * odd
         w = y * (1 - odd) + x * odd
         over_x = (z * 4 + (1 - x) * 2 + c, y)
@@ -918,11 +931,9 @@
     def step(t, _):
         at(2 * t, open_piece)
         at(2 * t + 1, open_piece)
-        for j in range(2 * away.shape[0]):
-
-            @pl.when(t == 1 + PIECES * j // (2 * away.shape[0]))
-            def _():
-                part(j).start()
+        @pl.when((t % 3 == 1) & (t < 3 * given))
+        def _():
+            give(t // 3)
 
         for k in range(2):
 
@@ -998,16 +1009,17 @@
             norm_down(unit).wait_send()
 
 
-def scatter_near(exp, con, own, mix_own, ask, source, mix, norms, away, early, kept, key_w, value_w, text, result):
+def scatter_near(exp, con, own, mix_own, ask, source, mix, norms, early, kept, key_w, value_w, text, result):
     rows, half = D // (4 * DEPTH), D // 2
     count, height = kept.shape[0], kept.shape[2]
+    given = count - early.shape[0]
     grads = [g.reshape(DEPTH, 2, 2, rows, g.shape[1]) for g in (exp, con, own, mix_own, ask, source, mix)]
     vmem = pl.BlockSpec(memory_space=pltpu.VMEM)
     anywhere = pl.BlockSpec(memory_space=pl.ANY)
     dma = pltpu.SemaphoreType.DMA
     return pl.pallas_call(
         scatter_kernel,
-        in_specs=[anywhere] * 7 + [vmem] * NORMS + [anywhere] * 7,
+        in_specs=[anywhere] * 7 + [vmem] * NORMS + [anywhere] * 6,
         out_specs=[vmem, vmem, anywhere, anywhere, anywhere],
         out_shape=[
             jax.ShapeDtypeStruct((PIECES, rows, half), f32),
@@ -1026,7 +1038,9 @@
             pltpu.VMEM((2, rows, half), f32),
             pltpu.VMEM((6, 8, D), f32),
             pltpu.VMEM((DEPTH, 8, D), f32),
-            pltpu.VMEM(away.shape, bf16),
+            pltpu.VMEM((given, height, D), bf16),
+            pltpu.VMEM((given, height, D), bf16),
+            pltpu.VMEM((given, height, 2 * D), bf16),
             pltpu.VMEM(early.shape, bf16),
             pltpu.VMEM((count, height, 2 * D), bf16),
             pltpu.VMEM((2, D, D), bf16),
@@ -1043,29 +1057,32 @@
             dma((PIECES,)),
             dma((3 + 2 * DEPTH,)),
             dma((3 + DEPTH,)),
-            dma((2 * away.shape[0],)),
-            dma((2 * away.shape[0],)),
-            dma((count + 3,)),
+            dma((2 * given,)),
+            dma((2 * given,)),
+            dma((count + 3 + given,)),
             dma((2,)),
             dma((2,)),
             dma((2,)),
         ],
         cost_estimate=pl.CostEstimate(flops=0, bytes_accessed=SCATTER_COST, transcendentals=0),
         compiler_params=pltpu.CompilerParams(collective_id=1, has_side_effects=True, vmem_limit_bytes=60 * 2**20),
-    )(*grads, *norms, away, early, kept, key_w, value_w, text, result)
-
-
-def scatter_grads(grads, norms, sources, early, late, key_w, value_w, text, result):
+    )(*grads, *norms, early, kept, key_w, value_w, text, result)
+
+
+def scatter_grads(grads, norms, sources, early, key_w, value_w, text, result):
     exp, con, own, mix_own, ask, source, mix = grads
     count = sources.shape[0] // PATCH
     if lax.axis_size("dp") == 4 * DEPTH:
         kept = sources.reshape(count, 2, PATCH // 2, -1)
-        parts, norm_sums, whole, text, result = scatter_near(*grads, norms, late, early, kept, key_w, value_w, text, result)
-        ordered = [parts[p] for p in range(PIECES) if p % 3 != 2] + [parts[p] for p in range(PIECES) if p % 3 == 2]
+        parts, norm_sums, whole, text, result = scatter_near(*grads, norms, early, kept, key_w, value_w, text, result)
+        odd = [p % PERIOD == PERIOD - 1 for p in range(PIECES)]
+        ordered = [parts[p] for p in range(PIECES) if not odd[p]] + [parts[p] for p in range(PIECES) if odd[p]]
         exp, con = (jnp.concatenate(part, axis=1) for part in (ordered[:4], ordered[4:8]))
         return [*ordered[8:], exp, con], norm_sums, whole.astype(f32), text, result
     side = lax.axis_index("mp")
     whole = patch_product(sources, key_w, value_w, 0, count, side, side * count, 2 * count, f32)
+    first = early.shape[0]
+    late = patch_product(sources, key_w, value_w, first, count, 1 - side, 0 * side, count - first, bf16)
     whole = widen(early, swap(late), whole, (1 - side) * count)
     sides = []
     for g in (own, mix_own, ask, source, mix):

time: 411 us -> 407 us (level)
    pallas_call x2 -> x1, Pallas kernels: 15.5 us -> 7.15 us  [patch_product(): pl.pallas_call(patch_kernel, grid_spec=grid_spec, out_shape=jax.ShapeDtyp...]
    pallas_call x1, Pallas kernels: 110 us -> 117 us  [scatter_near(): pl.pallas_call(scatter_kernel, in_specs=[anywhere] * 7 + [vmem] * NORMS +...]
  transfers between devices with their start and end apart: 1 -> 1, of which waited for: 1 -> 0; matrix products, arithmetic and copies ran while one was open for 8% -> 8% of each run, Pallas kernels for 4% -> 2%
where the time goes in v8:
time: 407 us; the launch traced here: 401 us
  Pallas kernels  255 us (63%)
  matrix products  104 us (26%)
  other arithmetic  20.7 us (5%)
  local copies, waits for them, and re-layouts  19.1 us (5%)
    pallas_call x1, Pallas kernels, scatter_near(): pl.pallas_call(scatter_kernel, in_specs=[anywhere] * 7 + [vmem] * NORMS +...  117 us
    dot_general x25, matrix products, dot(): lax.dot_general(left, right, (((left_dim,), (right_dim,)), ((), ())), pre...  104 us
    pallas_call x1, Pallas kernels, gather_near(): pl.pallas_call(gather_kernel, in_specs=[vmem] * 3 + [anywhere] * 3, out_s...  84.5 us
    pallas_call x2, Pallas kernels, attend_back(): pl.pallas_call(functools.partial(attend_back_kernel, batch), grid=(count...  27.7 us
    pallas_call x2, Pallas kernels, attend(): pl.pallas_call(functools.partial(attend_kernel, causal, batch), grid_spec...  19.2 us
    convert_element_type x1, other arithmetic, scatter_grads(): whole.astype(f32)  9.85 us
  transfers between devices with their start and end apart: 1, of which 0 were waited for; matrix products, arithmetic and copies ran while one was open for 8% of the time, Pallas kernels for 2%

profile of v8, /device:TPU:0, one launch (start us, length us, event | category | flops | bytes accessed | tf_op | source)
XLA Modules:
  0.0 401.3 jit_solution(7838976909517019799)
XLA Ops:
  0.7 0.8 bitcast_dynamic-update-slice_fusion.7
  1.6 1.8 constant_dynamic-slice_fusion.5.text_in
  3.3 1.8 constant_dynamic-slice_fusion.4.grad_in
  5.3 0.7 copy-done.15
  6.0 84.5 %shard_map.339 = (bf16[16,48,768]{2,1,0:T(8,128)(2,1)}, bf16[16,48,768]{2,1,0:T(8,128)(2,1)}, bf16[16,48,768]{2,1,0:T(8,128)(2,1)}, bf16[16,48,768]{2,1,0:T(8,12...) custom-call(bf16[8,48,384]{2,1,0:T(8,128)(2,1)} %copy-done.15, ...), custom_call_target="tpu_custom_call" | custom-call | tf_op jit(solution)/shard_map/pallas_call | solution.py:613
  90.5 1.2 broadcast_select_fusion.1
  92.0 0.4 copy-done.45
  92.4 0.6 dynamic_slice.31.flag_ref
  93.8 1.7 convolution_convert_fusion.12.value_ref
  95.5 1.7 convolution_convert_fusion.13.key_ref
  97.2 1.7 convolution_convert_fusion.14.query_ref
  98.9 6.0 %shard_map.340 = (bf16[512,768]{1,0:T(8,128)(2,1)}, bf16[512,768]{1,0:T(8,128)(2,1)}) custom-call(s32[8]{0:T(128)} %dynamic_slice.31.flag_ref, bf16[512,768]{1,0:T(8,128)(2,1)} %convolution_convert_fusion.14.query_ref, bf16[512,768]{1,0:T(8,128)(2,1)} %convolution_convert_fusion.13.key_ref, bf16[512,768]{1,0:T(8,128)(2,1)} %convolution_convert_fusion.12.value_ref), custom_call_target="tpu_custom_call" | custom-call | flops 402653184 | bytes 1572864 | tf_op jit(solution)/shard_map/pallas_call | solution.py:146
  104.8 2.4 fusion.36
  107.6 0.9 copy-done.4
  108.5 11.0 %convolution_convert_fusion.value_ref = bf16[4608,768]{1,0:T(8,128)(2,1)} fusion(bf16[4608,768]{1,0:T(8,128)(2,1)} %bitcast.189, bf16[768,768]{1,0:T(8,128)(2,1)S(1)} %bitcast.174), kind=kOutput, calls=%fused_computation.2 | convolution fusion | flops 5439356928 | bytes 15335424 | tf_op jit(solution)/shard_map/dot_general | solution.py:26
  119.5 8.3 %convolution_convert_fusion.1.key_ref = bf16[4608,768]{1,0:T(8,128)(2,1)} fusion(bf16[4608,768]{1,0:T(8,128)(2,1)S(1)} %bitcast.193, bf16[768,768]{1,0:T(8,128)(2,1)S(1)} %bitcast.171), kind=kOutput, calls=%fused_computation.3 | convolution fusion | flops 5439356928 | bytes 15335424 | tf_op jit(solution)/shard_map/dot_general | solution.py:26
  127.9 1.9 convolution_convert_fusion.11.query_ref
  129.7 13.3 %shard_map.341 = (bf16[512,768]{1,0:T(8,128)(2,1)}, bf16[4608,768]{1,0:T(8,128)(2,1)}) custom-call(s32[8]{0:T(128)} %dynamic_slice.31.flag_ref, bf16[512,768]{1,0:T(8,128)(2,1)} %convolution_convert_fusion.11.query_ref, bf16[4608,768]{1,0:T(8,128)(2,1)} %convolution_convert_fusion.1.key_ref, bf16[4608,768]{1,0:T(8,128)(2,1)} %convolution_convert_fusion.value_ref), custom_call_target="tpu_custom_call" | custom-call | flops 3623878656 | bytes 14155776 | tf_op jit(solution)/shard_map/pallas_call | solution.py:146
  143.0 2.4 fusion.37
  146.1 4.9 %fusion.34 = f32[512,3072]{1,0:T(8,128)S(1)} fusion(bf16[768,3072]{1,0:T(8,128)(2,1)} %bitcast.194, f32[512,768]{1,0:T(8,128)S(1)} %get-tuple-element.142, f32[768]{0:T(1024)S(1)} %copy-done.43, f32[768]{0:T(1024)S(1)} %copy-done.33, f32[512]{0:T(512)S(1)} %add_rsqrt_fusion.1, f32[512]{0:T(512)S(1)} %broadcast_multiply_fusion.7), kind=kOutput, calls=%fused_computation.134 | convolution fusion | flops 2417885184 | bytes 12593152 | tf_op jit(solution)/shard_map/dot_general | solution.py:26
  151.1 4.8 %add_convert_fusion = bf16[512,768]{1,0:T(8,128)(2,1)} fusion(f32[512,768]{1,0:T(8,128)S(1)} %get-tuple-element.142, bf16[768,3072]{1,0:T(8,128)(2,1)S(1)} %bitcast.200, f32[512,3072]{1,0:T(8,128)S(1)} %fusion.34), kind=kOutput, calls=%fused_computation.44 | convolution fusion | flops 2430861312 | bytes 13369344 | tf_op jit(solution)/shard_map/dot_general | solution.py:26
  155.9 5.7 %fusion.6 = bf16[512,3072]{1,0:T(8,128)(2,1)S(1)} fusion(f32[512,3072]{1,0:T(8,128)S(1)} %fusion.34, bf16[512,768]{1,0:T(8,128)(2,1)S(1)} %bitcast.176, bf16[768,3072]{1,0:T(8,128)(2,1)S(1)} %bitcast.201), kind=kOutput, calls=%fused_computation.10 | convolution fusion | flops 2445803520 | bytes 14942208 | tf_op jit(solution)/shard_map/dot_general | solution.py:26
  161.6 4.7 %convolution_convert_fusion.3 = bf16[768,3072]{1,0:T(8,128)(2,1)} fusion(bf16[512,768]{1,0:T(8,128)(2,1)S(1)} %bitcast.177, f32[512,3072]{1,0:T(8,128)S(1)} %fusion.34), kind=kOutput, calls=%fused_computation.13 | convolution fusion | flops 2432434176 | bytes 11796480 | tf_op jit(solution)/shard_map/dot_general | solution.py:26
  166.4 3.6 multiply_reduce_fusion
  170.0 4.9 %convolution_convert_fusion.4 = bf16[768,3072]{1,0:T(8,128)(2,1)} fusion(bf16[512,3072]{1,0:T(8,128)(2,1)S(1)} %fusion.6, f32[512,768]{1,0:T(8,128)S(1)} %get-tuple-element.142, f32[768]{0:T(1024)S(1)} %copy-done.43, f32[768]{0:T(1024)S(1)} %copy-done.33, f32[512]{0:T(512)S(1)} %add_rsqrt_fusion.1, f32[512]{0:T(512)S(1)} %broadcast_multiply_fusion.7), kind=kOutput, calls=%fused_computation.14 | convolution fusion | flops 2420244480 | bytes 9447424 | tf_op jit(solution)/shard_map/dot_general | solution.py:26
  174.9 1.8 fusion.35
  176.7 1.8 convolution_convert_fusion.8
  178.5 1.7 convolution_convert_fusion.10.grad_ref
  180.2 18.1 %shard_map.342 = (bf16[512,768]{1,0:T(8,128)(2,1)}, bf16[4608,1536]{1,0:T(8,128)(2,1)}) custom-call(bf16[512,768]{1,0:T(8,128)(2,1)} %convolution_convert_fusion.11.query_ref, bf16[4608,768]{1,0:T(8,128)(2,1)} %convolution_convert_fusion.1.key_ref, bf16[4608,768]{1,0:T(8,128)(2,1)} %convolution_convert_fusion.value_ref, ...), custom_call_target="tpu_custom_call" | custom-call | flops 7247757312 | bytes 28311552 | tf_op jit(solution)/shard_map/pallas_call | solution.py:162
  198.2 17.0 %convolution_convert_fusion.5 = bf16[768,1536]{1,0:T(8,128)(2,1)} fusion(bf16[4608,768]{1,0:T(8,128)(2,1)} %bitcast.190, bf16[4608,1536]{1,0:T(8,128)(2,1)} %get-tuple-element.78), kind=kOutput, calls=%fused_computation.15 | convolution fusion | flops 10872815616 | bytes 23592960 | tf_op jit(solution)/shard_map/dot_general | solution.py:26
  215.2 2.0 convolution_convert_fusion.7
  217.3 0.6 pad_add_fusion.side_ref
  217.9 7.1 %shard_map.343 = bf16[4,288,768]{2,1,0:T(8,128)(2,1)} custom-call(s32[2]{0:T(128)} %pad_add_fusion.side_ref, bf16[8,576,1536]{2,1,0:T(8,128)(2,1)} %bitcast.164, bf16[768,768]{1,0:T(8,128)(2,1)} %bitcast.169, bf16[768,768]{1,0:T(8,128)(2,1)} %bitcast.172), custom_call_target="tpu_custom_call" | custom-call | flops 1048576 | bytes 1365 | tf_op jit(solution)/shard_map/pallas_call | solution.py:204
  225.0 0.6 collective-permute-start
  225.6 0.5 iota_compare_fusion
  226.1 0.7 div.46
  226.8 0.7 rsqrt.31
  227.4 3.2 multiply_reduce_fusion.1
  230.6 1.3 multiply_add_fusion.1
  231.9 1.7 convolution_convert_fusion.9.grad_ref
  233.6 9.6 %shard_map.344 = bf16[512,2304]{1,0:T(8,128)(2,1)} custom-call(bf16[512,768]{1,0:T(8,128)(2,1)} %convolution_convert_fusion.14.query_ref, bf16[512,768]{1,0:T(8,128)(2,1)} %convolution_convert_fusion.13.key_ref, bf16[512,768]{1,0:T(8,128)(2,1)} %convolution_convert_fusion.12.value_ref, bf16[512,768]{1,0:T(8,128)(2,1)} %get-tuple-element.73.prob_ref, ...), custom_call_target="tpu_custom_call" | custom-call | flops 1048576 | bytes 1048576 | tf_op jit(solution)/shard_map/pallas_call | solution.py:162
  243.3 3.2 fusion.27
  246.6 3.2 fusion.29
  249.9 0.6 broadcast_in_dim.101.rest_4_
  250.5 0.6 broadcast_in_dim.102.rest_5_
  251.1 0.6 broadcast_in_dim.99.rest_2_
  251.7 0.6 broadcast_in_dim.100.rest_3_
  252.3 4.8 %fusion.21 = (f32[512]{0:T(512)S(1)}, f32[768]{0:T(1024)S(1)}, f32[512]{0:T(512)S(1)}, f32[768]{0:T(1024)S(1)}, f32[512,768]{1,0:T(8,128)}) fusion(f32[768]{0:T(1024)S(1)} %copy-done.25, f32[512]{0:T(512)S(1)} %copy-done.27, f32[512]{0:T(512)S(1)} %copy-done.26, bf16[8,32,768]{2,1,0:T(8,128)(2,1)S(1)} %copy-done.1, ...), kind=kOutput, calls=%fused_computation.34 | convolution fusion | flops 609875456 | bytes 7488512 | tf_op jit(solution)/shard_map/dot_general | solution.py:26
  257.1 0.6 broadcast_in_dim.97.rest_0_
  257.6 0.6 broadcast_in_dim.98.rest_1_
  258.2 0.8 constant_dynamic-slice_fusion.3
  259.0 0.7 copy-done.6
  259.8 0.7 fusion.25
  260.5 0.8 constant_dynamic-slice_fusion
  261.3 0.5 copy-done.8
  261.8 1.8 convolution_convert_fusion.6
  263.6 3.9 convolution_convert_fusion.2
  267.5 116.6 %shard_map.345 = (f32[16,48,384]{2,1,0:T(8,128)}, f32[8,768]{1,0:T(8,128)}, bf16[16,288,768]{2,1,0:T(8,128)(2,1)}, bf16[8,32,768]{2,1,0:T(8,128)(2,1)}, bf16[8,32,768]{2,1,0:T(8,128)(2,1)}) custom-call(bf16[4,2,2,48,3072]{4,3,2,1,0:T(8,128)(2,1)} %bitcast.167, bf16[4,2,2,48,3072]{4,3,2,1,0:T(8,128)(2,1)} %bitcast.166, ...), custom_call_target="tpu_custom_call" | custom-call | bytes 1048576 | tf_op jit(solution)/shard_map/pallas_call | solution.py:1020
  384.1 1.6 slice_reduce_fusion
  385.7 2.1 slice_bitcast_fusion.3
  387.9 9.9 %convert_element_type.156 = f32[16,288,768]{2,1,0:T(8,128)} convert(bf16[16,288,768]{2,1,0:T(8,128)(2,1)} %get-tuple-element.88) | non-fusion elementwise | flops 3538944 | bytes 21233664 | tf_op jit(solution)/shard_map/convert_element_type | solution.py:1081
  397.8 0.7 maximum_bitcast_fusion
  398.5 0.7 pad_maximum_fusion.2
  399.2 1.6 fusion.31
  (135 shorter events, 2.4 us)
Async XLA Ops:
  0.7 4.4 %copy-start.16 = (bf16[48,384]{1,0:T(8,128)(2,1)S(1)}, bf16[48,384]{1,0:T(8,128)(2,1)}, u32[]{:S(2)}) copy-start(bf16[48,384]{1,0:T(8,128)(2,1)} %param.24) | copy-start | bytes 110596
  0.7 4.4 %copy-start.17 = (bf16[48,384]{1,0:T(8,128)(2,1)S(1)}, bf16[48,384]{1,0:T(8,128)(2,1)}, u32[]{:S(2)}) copy-start(bf16[48,384]{1,0:T(8,128)(2,1)} %param.25) | copy-start | bytes 110596
  0.7 4.4 %copy-start.18 = (bf16[384,48]{0,1:T(8,128)(2,1)S(1)}, bf16[384,48]{0,1:T(8,128)(2,1)}, u32[]{:S(2)}) copy-start(bf16[384,48]{0,1:T(8,128)(2,1)} %param.26) | copy-start | bytes 110596
  0.7 4.5 %copy-start.19 = (bf16[48,384]{1,0:T(8,128)(2,1)S(1)}, bf16[48,384]{1,0:T(8,128)(2,1)}, u32[]{:S(2)}) copy-start(bf16[48,384]{1,0:T(8,128)(2,1)} %param.27) | copy-start | bytes 110596
  0.7 4.5 %copy-start.20 = (bf16[48,384]{1,0:T(8,128)(2,1)S(1)}, bf16[48,384]{1,0:T(8,128)(2,1)}, u32[]{:S(2)}) copy-start(bf16[48,384]{1,0:T(8,128)(2,1)} %param.28) | copy-start | bytes 110596
  0.7 4.5 %copy-start.21 = (bf16[48,384]{1,0:T(8,128)(2,1)S(1)}, bf16[48,384]{1,0:T(8,128)(2,1)}, u32[]{:S(2)}) copy-start(bf16[48,384]{1,0:T(8,128)(2,1)} %param.29) | copy-start | bytes 110596
  0.7 4.5 %copy-start.22 = (bf16[384,48]{0,1:T(8,128)(2,1)S(1)}, bf16[384,48]{0,1:T(8,128)(2,1)}, u32[]{:S(2)}) copy-start(bf16[384,48]{0,1:T(8,128)(2,1)} %param.30) | copy-start | bytes 110596
  5.3 0.7 copy-start.15
  6.0 84.5 %copy-start.11 = (bf16[16,32,768]{2,1,0:T(8,128)(2,1)S(1)}, bf16[16,32,768]{2,1,0:T(8,128)(2,1)}, u32[]{:S(2)}) copy-start(bf16[16,32,768]{2,1,0:T(8,128)(2,1)} %param.20) | copy-start | bytes 2359300
  6.0 84.5 %copy-start.12 = (bf16[16,32,768]{2,1,0:T(8,128)(2,1)S(1)}, bf16[16,32,768]{2,1,0:T(8,128)(2,1)}, u32[]{:S(2)}) copy-start(bf16[16,32,768]{2,1,0:T(8,128)(2,1)} %param.39) | copy-start | bytes 2359300
  91.8 1.7 copy-start
  91.8 0.7 copy-start.45
  91.8 1.6 copy-start.23
  91.8 1.6 copy-start.24
  92.4 1.4 copy-start.36
  93.8 1.7 copy-start.39
  95.5 1.7 copy-start.37
  107.2 1.3 copy-start.4
  107.3 12.2 %slice-start = ((s8[7077888]{0:T(1024)(128)(4,1)}), s8[4194304]{0:T(1024)(128)(4,1)S(1)}, s32[]{:S(2)}) async-start(s8[7077888]{0:T(1024)(128)(4,1)} %bitcast.191), calls=%async_computation | async-start | bytes 8388608
  107.6 119.9 %copy-start.28 = (f32[512]{0:T(512)}, f32[512]{0:T(512)S(1)}, u32[]{:S(2)}) copy-start(f32[512]{0:T(512)S(1)} %add_rsqrt_fusion.2) | copy-start | bytes 6148
  108.5 11.0 %copy-start.3 = (bf16[16,48,768]{2,1,0:T(8,128)(2,1)S(1)}, bf16[16,48,768]{2,1,0:T(8,128)(2,1)}, u32[]{:S(2)}) copy-start(bf16[16,48,768]{2,1,0:T(8,128)(2,1)} %get-tuple-element.64) | copy-start | bytes 3538948
  108.5 11.0 %slice-start.1 = ((s8[7077888]{0:T(1024)(128)(4,1)}), s8[2883584]{0:T(1024)(128)(4,1)S(1)}, s32[]{:S(2)}) async-start(s8[7077888]{0:T(1024)(128)(4,1)} %bitcast.191), calls=%async_computation.1 | async-start | bytes 5767168
  119.5 8.3 %copy-start.34 = (f32[768]{0:T(1024)S(1)}, f32[768]{0:T(1024)}, u32[]{:S(2)}) copy-start(f32[768]{0:T(1024)} %param.35) | copy-start | bytes 9220
  119.5 8.3 %copy-start.42 = (bf16[16,48,768]{2,1,0:T(8,128)(2,1)S(1)}, bf16[16,48,768]{2,1,0:T(8,128)(2,1)}, u32[]{:S(2)}) copy-start(bf16[16,48,768]{2,1,0:T(8,128)(2,1)} %get-tuple-element.62) | copy-start | bytes 3538948
  119.5 8.3 %copy-start.44 = (f32[768]{0:T(1024)S(1)}, f32[768]{0:T(1024)}, u32[]{:S(2)}) copy-start(f32[768]{0:T(1024)} %param.36) | copy-start | bytes 9220
  145.4 0.7 copy-start.33
  145.4 0.7 copy-start.43
  145.7 5.3 %slice-start.4 = ((s8[4718592]{0:T(1024)(128)(4,1)}), s8[4194304]{0:T(1024)(128)(4,1)S(1)}, s32[]{:S(2)}) async-start(s8[4718592]{0:T(1024)(128)(4,1)} %bitcast.198), calls=%async_computation.4 | async-start | bytes 8388608
  146.1 4.9 %slice-start.5 = ((s8[4718592]{0:T(1024)(128)(4,1)}), s8[524288]{0:T(1024)(128)(4,1)S(1)}, s32[]{:S(2)}) async-start(s8[4718592]{0:T(1024)(128)(4,1)} %bitcast.198), calls=%async_computation.5 | async-start | bytes 1048576
  151.1 15.3 %slice-start.2 = ((s8[4718592]{0:T(1024)(128)(4,1)}), s8[4194304]{0:T(1024)(128)(4,1)S(1)}, s32[]{:S(2)}) async-start(s8[4718592]{0:T(1024)(128)(4,1)} %bitcast.195), calls=%async_computation.2 | async-start | bytes 8388608
  155.9 10.5 %slice-start.3 = ((s8[4718592]{0:T(1024)(128)(4,1)}), s8[524288]{0:T(1024)(128)(4,1)S(1)}, s32[]{:S(2)}) async-start(s8[4718592]{0:T(1024)(128)(4,1)} %bitcast.195), calls=%async_computation.3 | async-start | bytes 1048576
  174.9 1.8 copy-start.9
  176.7 1.8 copy-start.7
  198.2 17.0 %copy-start.47 = (bf16[512,768]{1,0:T(8,128)(2,1)S(1)}, bf16[512,768]{1,0:T(8,128)(2,1)}, u32[]{:S(2)}) copy-start(bf16[512,768]{1,0:T(8,128)(2,1)} %get-tuple-element.79) | copy-start | bytes 2359300
  225.0 42.5 %collective-permute-start = (bf16[4,288,768]{2,1,0:T(8,128)(2,1)}, bf16[4,288,768]{2,1,0:T(8,128)(2,1)}, u32[]{:S(2)}, u32[]{:S(2)}) collective-permute-start(bf16[4,288,768]{2,1,0:T(8,128)(2,1)} %shard_map.343), channel_id=1, source_target_pairs={{0,1},{1,0},{2,3},{3,2},{4,5},{5,4},{6,7},{7,6},{8,9},{9,8},{10,11... | collective-permute-start | bytes 5308424 | tf_op jit(solution)/shard_map/ppermute | solution.py:179
  227.4 3.2 copy-start.2
  227.4 3.2 copy-start.35
  230.6 1.3 copy-start.41
  233.6 9.6 %copy-start.40 = (bf16[16,48,768]{2,1,0:T(8,128)(2,1)S(1)}, bf16[16,48,768]{2,1,0:T(8,128)(2,1)}, u32[]{:S(2)}) copy-start(bf16[16,48,768]{2,1,0:T(8,128)(2,1)} %get-tuple-element.58) | copy-start | bytes 3538948
  243.3 3.2 copy-start.38
  246.5 3.2 copy-start.46
  246.5 3.4 copy-start.30
  246.5 4.0 copy-start.29
  246.5 4.6 %copy-start.32 = (f32[768]{0:T(1024)S(1)}, f32[768]{0:T(1024)}, u32[]{:S(2)}) copy-start(f32[768]{0:T(1024)} %get-tuple-element.93) | copy-start | bytes 9220
  246.5 5.1 %copy-start.31 = (f32[768]{0:T(1024)S(1)}, f32[768]{0:T(1024)}, u32[]{:S(2)}) copy-start(f32[768]{0:T(1024)} %get-tuple-element.102) | copy-start | bytes 9220
  246.5 5.7 %copy-start.1 = (bf16[8,32,768]{2,1,0:T(8,128)(2,1)S(1)}, bf16[8,32,768]{2,1,0:T(8,128)(2,1)}, u32[]{:S(2)}) copy-start(bf16[8,32,768]{2,1,0:T(8,128)(2,1)} %copy-done) | copy-start | bytes 1179652
  246.5 5.7 %copy-start.25 = (f32[768]{0:T(1024)S(1)}, f32[768]{0:T(1024)}, u32[]{:S(2)}) copy-start(f32[768]{0:T(1024)} %param.33) | copy-start | bytes 9220
  246.6 5.7 %copy-start.26 = (f32[512]{0:T(512)S(1)}, f32[512]{0:T(512)}, u32[]{:S(2)}) copy-start(f32[512]{0:T(512)} %div.46) | copy-start | bytes 6148
  246.6 5.7 %copy-start.27 = (f32[512]{0:T(512)S(1)}, f32[512]{0:T(512)}, u32[]{:S(2)}) copy-start(f32[512]{0:T(512)} %rsqrt.31) | copy-start | bytes 6148
  252.2 6.0 %copy-start.10 = (bf16[512,768]{1,0:T(8,128)(2,1)S(1)}, bf16[512,768]{1,0:T(8,128)(2,1)}, u32[]{:S(2)}) copy-start(bf16[512,768]{1,0:T(8,128)(2,1)} %add_convert_fusion) | copy-start | bytes 2359300
  258.2 1.5 copy-start.6
  260.5 1.3 copy-start.8
  261.8 1.8 copy-start.5
  387.9 11.3 %copy-start.13 = (bf16[8,32,768]{2,1,0:T(8,128)(2,1)S(1)}, bf16[8,32,768]{2,1,0:T(8,128)(2,1)}, u32[]{:S(2)}) copy-start(bf16[8,32,768]{2,1,0:T(8,128)(2,1)} %get-tuple-element.87) | copy-start | bytes 1179652
  387.9 11.3 %copy-start.14 = (bf16[8,32,768]{2,1,0:T(8,128)(2,1)S(1)}, bf16[8,32,768]{2,1,0:T(8,128)(2,1)}, u32[]{:S(2)}) copy-start(bf16[8,32,768]{2,1,0:T(8,128)(2,1)} %get-tuple-element.86) | copy-start | bytes 1179652

commit v9 on v8

--- a/solution.py
+++ b/solution.py
@@ -181,9 +181,9 @@
 
 def patch_kernel(side_ref, grad_ref, key_ref, value_ref, out_ref):
     width = key_ref.shape[1]
-    for n in range(grad_ref.shape[0]):
-        product = dot(grad_ref[n, :, :width], key_ref[...], 1, 1) + dot(grad_ref[n, :, width:], value_ref[...], 1, 1)
-        out_ref[n] = product.astype(out_ref.dtype)
+    rows = grad_ref[...].reshape(-1, 2 * width)
+    product = dot(rows[:, :width], key_ref[...], 1, 1) + dot(rows[:, width:], value_ref[...], 1, 1)
+    out_ref[...] = product.astype(out_ref.dtype).reshape(out_ref.shape)
 
 
 def patch_product(grads, key_w, value_w, first, last, half, place_at, total, kind):
@@ -308,10 +308,11 @@
     grads = [grad_expand, grad_contract, grad_self, grad_mix_self, grad_query_cross, grad_patch, grad_mix_cross]
     early, norm_grads[0] = lax.optimization_barrier((early, norm_grads[0]))
     grads = [g.astype(bf16) for g in grads]
-    layer_mine, layer_away = split_positions(layer_out.reshape(count, LEN, D), side)
-    text_mine, text_away = split_positions(text_grad.reshape(count, LEN, D), side)
+    layer_out, text_grad = (rows.reshape(count, LEN, D) for rows in (layer_out, text_grad))
+    layer_mine, _ = split_positions(layer_out, side)
+    text_mine, _ = split_positions(text_grad, side)
     weight_grads, norm_sums, patch_grad, text_back, layer_back = scatter_grads(
-        grads, norm_grads, grad_sources, early, key_cross, value_cross, text_away, layer_away
+        grads, norm_grads, grad_sources, early, key_cross, value_cross, text_grad, layer_out
     )
     layer_out = join_positions(layer_mine, layer_back, side)
     text_grad = join_positions(text_mine, text_back, side).astype(f32)
@@ -561,7 +562,7 @@
     def trade(k):
         src, dst = ((text_in, text_out), (grad_in, grad_out))[k]
         return pltpu.make_async_remote_copy(
-            src_ref=src,
+            src_ref=src.at[pl.ds((1 - y) * count, count)],
             dst_ref=dst,
             send_sem=trade_send.at[k],
             recv_sem=trade_recv.at[k],
@@ -618,8 +619,8 @@
         + [
             jax.ShapeDtypeStruct((dp, rows, 2 * wide), bf16),
             jax.ShapeDtypeStruct((dp, rows, 2 * wide), bf16),
-            jax.ShapeDtypeStruct(text.shape, bf16),
-            jax.ShapeDtypeStruct(grad.shape, bf16),
+            jax.ShapeDtypeStruct((count, *text.shape[1:]), bf16),
+            jax.ShapeDtypeStruct((count, *grad.shape[1:]), bf16),
             jax.ShapeDtypeStruct((count, *image.shape[1:]), bf16),
         ],
         scratch_shapes=[
@@ -654,7 +655,7 @@
         att = sides.transpose(0, 2, 1, 3).reshape(count, width, -1)
         sides = lax.all_gather(jnp.stack(narrow), ("mp", "dp"), axis=1, tiled=True).reshape(2, chunks, 2, width, -1)
         exp, con = sides.transpose(0, 3, 2, 1, 4).reshape(2, width, -1)
-        text, grad = swap(text), swap(grad)
+        text, grad = (swap(split_captions(rows, lax.axis_index("mp"))[1]) for rows in (text, grad))
         patches, _ = split_captions(image, lax.axis_index("mp"))
     return [*(att[i] for i in range(8)), exp, con], text, grad, patches
 
@@ -768,7 +769,8 @@
 
     def trade(k):
         src, dst = ((text, text_back), (result, result_back))[k]
-        return copy(src, dst, trade_send.at[k], trade_recv.at[k], (mine, 1 - y))
+        rows = dst.shape[1]
+        return copy(src.at[:, pl.ds(pl.multiple_of((1 - y) * rows, 16), rows)], dst, trade_send.at[k], trade_recv.at[k], (mine, 1 - y))
 
     def part(j):
         rows = sent.shape[1] // 2
@@ -1025,8 +1027,8 @@
             jax.ShapeDtypeStruct((PIECES, rows, half), f32),
             jax.ShapeDtypeStruct((8, D), f32),
             jax.ShapeDtypeStruct((2 * count, height, D), bf16),
-            jax.ShapeDtypeStruct(text.shape, bf16),
-            jax.ShapeDtypeStruct(result.shape, bf16),
+            jax.ShapeDtypeStruct((count, LEN // 2, D), bf16),
+            jax.ShapeDtypeStruct((count, LEN // 2, D), bf16),
         ],
         scratch_shapes=[
             pltpu.VMEM((PIECES, DEPTH, 2, 2, rows, half), bf16),
@@ -1093,7 +1095,7 @@
     parts = lax.psum_scatter(stacked, ("mp", "dp"), scatter_dimension=1, tiled=True).astype(f32)
     chunks = (parts.shape[0] - 8) // 2
     exp, con = (jnp.concatenate(list(parts[start : start + chunks]), axis=1) for start in (8, 8 + chunks))
-    return [*(parts[i] for i in range(8)), exp, con], lax.psum(jnp.concatenate(norms), BOTH), whole, swap(text), swap(result)
+    return [*(parts[i] for i in range(8)), exp, con], lax.psum(jnp.concatenate(norms), BOTH), whole, *(swap(split_positions(rows, side)[1]) for rows in (text, result))
 
 
 def body(text_tokens, image_tokens, resolution, *rest):
@@ -1102,10 +1104,10 @@
     half = text_tokens.shape[0] // 2
     width = text_tokens.shape[2]
     flat = [shard.T if turned else shard for shard, turned in zip(shards, TURNED)]
-    text_mine, text_away = split_captions(text_tokens, side)
-    grad_mine, grad_away = split_captions(cotangent, side)
+    text_mine, _ = split_captions(text_tokens, side)
+    grad_mine, _ = split_captions(cotangent, side)
     weights, text_back, grad_back, patches = gather_weights(
-        jnp.stack(flat[:8]), flat[8], flat[9], text_away, grad_away, image_tokens
+        jnp.stack(flat[:8]), flat[8], flat[9], text_tokens, cotangent, image_tokens
     )
     text = join_captions(text_mine, text_back, side)
     grad_out = join_captions(grad_mine, grad_back, side)

time: 407 us -> 416 us (1.022)
  other arithmetic: 20.7 us -> 26.7 us
    unnamed x115 -> x121, local copies, waits for them, and re-layouts: 4.64 us -> 9.5 us
where the time goes in v9:
time: 416 us; the launch traced here: 410 us
  Pallas kernels  255 us (61%)
  matrix products  106 us (25%)
  other arithmetic  26.7 us (6%)
  local copies, waits for them, and re-layouts  19.8 us (5%)
    pallas_call x1, Pallas kernels, scatter_near(): pl.pallas_call(scatter_kernel, in_specs=[anywhere] * 7 + [vmem] * NORMS +...  117 us
    dot_general x25, matrix products, dot(): lax.dot_general(left, right, (((left_dim,), (right_dim,)), ((), ())), pre...  106 us
    pallas_call x1, Pallas kernels, gather_near(): pl.pallas_call(gather_kernel, in_specs=[vmem] * 3 + [anywhere] * 3, out_s...  84.5 us
    pallas_call x2, Pallas kernels, attend_back(): pl.pallas_call(functools.partial(attend_back_kernel, batch), grid=(count...  27.7 us
    pallas_call x2, Pallas kernels, attend(): pl.pallas_call(functools.partial(attend_kernel, causal, batch), grid_spec...  19.3 us
    convert_element_type x1, other arithmetic, scatter_grads(): whole.astype(f32)  9.85 us
    unnamed x121, local copies, waits for them, and re-layouts  9.5 us
  transfers between devices with their start and end apart: 1, of which 0 were waited for; matrix products, arithmetic and copies ran while one was open for 8% of the time, Pallas kernels for 2%

profile of v9, /device:TPU:0, one launch (start us, length us, event | category | flops | bytes accessed | tf_op | source)
XLA Modules:
  0.0 409.6 jit_solution(16165556435734126043)
XLA Ops:
  0.7 0.8 bitcast_dynamic-update-slice_fusion.7
  1.4 0.8 bitcast_dynamic-update-slice_fusion.6
  2.2 0.8 bitcast_dynamic-update-slice_fusion.5
  3.0 0.8 bitcast_dynamic-update-slice_fusion.1
  3.8 0.8 bitcast_dynamic-update-slice_fusion.4
  4.5 0.8 bitcast_dynamic-update-slice_fusion.3
  5.3 0.8 bitcast_dynamic-update-slice_fusion.2
  6.1 0.8 bitcast_dynamic-update-slice_fusion.att_in
  6.9 0.7 copy-done.18
  7.6 84.5 %shard_map.339 = (bf16[16,48,768]{2,1,0:T(8,128)(2,1)}, bf16[16,48,768]{2,1,0:T(8,128)(2,1)}, bf16[16,48,768]{2,1,0:T(8,128)(2,1)}, bf16[16,48,768]{2,1,0:T(8,12...) custom-call(bf16[8,48,384]{2,1,0:T(8,128)(2,1)} %copy-done.18, ...), custom_call_target="tpu_custom_call" | custom-call | tf_op jit(solution)/shard_map/pallas_call | solution.py:614
  92.1 2.1 broadcast_select_fusion.1
  94.9 0.6 dynamic_slice.17.flag_ref
  96.3 1.7 convolution_convert_fusion.12.value_ref
  98.0 1.7 convolution_convert_fusion.13.key_ref
  99.6 1.7 convolution_convert_fusion.14.query_ref
  101.3 6.0 %shard_map.340 = (bf16[512,768]{1,0:T(8,128)(2,1)}, bf16[512,768]{1,0:T(8,128)(2,1)}) custom-call(s32[8]{0:T(128)} %dynamic_slice.17.flag_ref, bf16[512,768]{1,0:T(8,128)(2,1)} %convolution_convert_fusion.14.query_ref, bf16[512,768]{1,0:T(8,128)(2,1)} %convolution_convert_fusion.13.key_ref, bf16[512,768]{1,0:T(8,128)(2,1)} %convolution_convert_fusion.12.value_ref), custom_call_target="tpu_custom_call" | custom-call | flops 402653184 | bytes 1572864 | tf_op jit(solution)/shard_map/pallas_call | solution.py:146
  107.3 2.4 fusion.36
  110.0 0.9 copy-done.5
  111.0 10.9 %convolution_convert_fusion.value_ref = bf16[4608,768]{1,0:T(8,128)(2,1)} fusion(bf16[4608,768]{1,0:T(8,128)(2,1)} %bitcast.191, bf16[768,768]{1,0:T(8,128)(2,1)S(1)} %bitcast.176), kind=kOutput, calls=%fused_computation.2 | convolution fusion | flops 5439356928 | bytes 15335424 | tf_op jit(solution)/shard_map/dot_general | solution.py:26
  121.9 8.3 %convolution_convert_fusion.1.key_ref = bf16[4608,768]{1,0:T(8,128)(2,1)} fusion(bf16[4608,768]{1,0:T(8,128)(2,1)S(1)} %bitcast.195, bf16[768,768]{1,0:T(8,128)(2,1)S(1)} %bitcast.173), kind=kOutput, calls=%fused_computation.3 | convolution fusion | flops 5439356928 | bytes 15335424 | tf_op jit(solution)/shard_map/dot_general | solution.py:26
  130.3 1.8 convolution_convert_fusion.11.query_ref
  132.1 13.3 %shard_map.341 = (bf16[512,768]{1,0:T(8,128)(2,1)}, bf16[4608,768]{1,0:T(8,128)(2,1)}) custom-call(s32[8]{0:T(128)} %dynamic_slice.17.flag_ref, bf16[512,768]{1,0:T(8,128)(2,1)} %convolution_convert_fusion.11.query_ref, bf16[4608,768]{1,0:T(8,128)(2,1)} %convolution_convert_fusion.1.key_ref, bf16[4608,768]{1,0:T(8,128)(2,1)} %convolution_convert_fusion.value_ref), custom_call_target="tpu_custom_call" | custom-call | flops 3623878656 | bytes 14155776 | tf_op jit(solution)/shard_map/pallas_call | solution.py:146
  145.4 2.4 fusion.37
  148.1 0.6 copy-done.11
  149.0 5.0 %fusion.34 = f32[512,3072]{1,0:T(8,128)S(1)} fusion(bf16[768,3072]{1,0:T(8,128)(2,1)} %bitcast.196, f32[512,768]{1,0:T(8,128)S(1)} %get-tuple-element.138, f32[768]{0:T(1024)S(1)} %copy-done.45, f32[768]{0:T(1024)S(1)} %copy-done.32, f32[512]{0:T(512)S(1)} %add_rsqrt_fusion.1, f32[512]{0:T(512)S(1)} %broadcast_multiply_fusion.7), kind=kOutput, calls=%fused_computation.130 | convolution fusion | flops 2417885184 | bytes 12593152 | tf_op jit(solution)/shard_map/dot_general | solution.py:26
  154.1 4.9 %add_convert_fusion = bf16[512,768]{1,0:T(8,128)(2,1)} fusion(f32[512,768]{1,0:T(8,128)S(1)} %get-tuple-element.138, bf16[768,3072]{1,0:T(8,128)(2,1)S(1)} %bitcast.202, f32[512,3072]{1,0:T(8,128)S(1)} %fusion.34), kind=kOutput, calls=%fused_computation.44 | convolution fusion | flops 2430861312 | bytes 13369344 | tf_op jit(solution)/shard_map/dot_general | solution.py:26
  159.0 5.8 %fusion.6 = bf16[512,3072]{1,0:T(8,128)(2,1)S(1)} fusion(f32[512,3072]{1,0:T(8,128)S(1)} %fusion.34, bf16[512,768]{1,0:T(8,128)(2,1)S(1)} %bitcast.178, bf16[768,3072]{1,0:T(8,128)(2,1)S(1)} %bitcast.203), kind=kOutput, calls=%fused_computation.10 | convolution fusion | flops 2445803520 | bytes 14942208 | tf_op jit(solution)/shard_map/dot_general | solution.py:26
  164.8 4.7 %convolution_convert_fusion.3 = bf16[768,3072]{1,0:T(8,128)(2,1)} fusion(bf16[512,768]{1,0:T(8,128)(2,1)S(1)} %bitcast.179, f32[512,3072]{1,0:T(8,128)S(1)} %fusion.34), kind=kOutput, calls=%fused_computation.13 | convolution fusion | flops 2432434176 | bytes 11796480 | tf_op jit(solution)/shard_map/dot_general | solution.py:26
  169.5 4.6 %multiply_reduce_fusion = (f32[768]{0:T(1024)}, f32[512]{0:T(512)}, f32[512]{0:T(512)}, f32[768]{0:T(1024)}, f32[512,768]{1,0:T(8,128)}) fusion(f32[512,768]{1,0:T(8,128)S(1)} %get-tuple-element.138, f32[512]{0:T(512)S(1)} %add_rsqrt_fusion.1, f32[512]{0:T(512)S(1)} %broadcast_multiply_fusion.7, f32[768]{0:T(1024)S(1)} %copy-done.32, ...), kind=kOutput, calls=%fused_computation.39 | convolution fusion | flops 2419455488 | bytes 11027456 | tf_op jit(solution)/shard_map/dot_general | solution.py:26
  174.2 4.8 %convolution_convert_fusion.4 = bf16[768,3072]{1,0:T(8,128)(2,1)} fusion(bf16[512,3072]{1,0:T(8,128)(2,1)S(1)} %fusion.6, f32[512,768]{1,0:T(8,128)S(1)} %get-tuple-element.138, f32[768]{0:T(1024)S(1)} %copy-done.45, f32[768]{0:T(1024)S(1)} %copy-done.32, f32[512]{0:T(512)S(1)} %add_rsqrt_fusion.1, f32[512]{0:T(512)S(1)} %broadcast_multiply_fusion.7), kind=kOutput, calls=%fused_computation.14 | convolution fusion | flops 2420244480 | bytes 9447424 | tf_op jit(solution)/shard_map/dot_general | solution.py:26
  179.0 0.7 broadcast_multiply_fusion.5
  179.7 0.7 broadcast_multiply_fusion.6
  180.3 3.4 fusion.35
  183.8 1.8 convolution_convert_fusion.8
  185.6 1.7 convolution_convert_fusion.10.grad_ref
  187.3 18.1 %shard_map.342 = (bf16[512,768]{1,0:T(8,128)(2,1)}, bf16[4608,1536]{1,0:T(8,128)(2,1)}) custom-call(bf16[512,768]{1,0:T(8,128)(2,1)} %convolution_convert_fusion.11.query_ref, bf16[4608,768]{1,0:T(8,128)(2,1)} %convolution_convert_fusion.1.key_ref, bf16[4608,768]{1,0:T(8,128)(2,1)} %convolution_convert_fusion.value_ref, ...), custom_call_target="tpu_custom_call" | custom-call | flops 7247757312 | bytes 28311552 | tf_op jit(solution)/shard_map/pallas_call | solution.py:162
  205.4 17.0 %convolution_convert_fusion.5 = bf16[768,1536]{1,0:T(8,128)(2,1)} fusion(bf16[4608,768]{1,0:T(8,128)(2,1)} %bitcast.192, bf16[4608,1536]{1,0:T(8,128)(2,1)} %get-tuple-element.78), kind=kOutput, calls=%fused_computation.15 | convolution fusion | flops 10872815616 | bytes 23592960 | tf_op jit(solution)/shard_map/dot_general | solution.py:26
  222.4 2.1 convolution_convert_fusion.7
  224.5 0.6 pad_add_fusion.side_ref
  225.1 7.3 %shard_map.343 = bf16[4,288,768]{2,1,0:T(8,128)(2,1)} custom-call(s32[2]{0:T(128)} %pad_add_fusion.side_ref, bf16[8,576,1536]{2,1,0:T(8,128)(2,1)} %bitcast.164, bf16[768,768]{1,0:T(8,128)(2,1)} %bitcast.171, bf16[768,768]{1,0:T(8,128)(2,1)} %bitcast.174), custom_call_target="tpu_custom_call" | custom-call | flops 1048576 | bytes 1365 | tf_op jit(solution)/shard_map/pallas_call | solution.py:204
  233.5 0.7 rsqrt.31
  234.2 3.1 multiply_reduce_fusion.1
  237.8 0.7 copy-done.42
  238.6 1.7 convolution_convert_fusion.9.grad_ref
  240.2 9.6 %shard_map.344 = bf16[512,2304]{1,0:T(8,128)(2,1)} custom-call(bf16[512,768]{1,0:T(8,128)(2,1)} %convolution_convert_fusion.14.query_ref, bf16[512,768]{1,0:T(8,128)(2,1)} %convolution_convert_fusion.13.key_ref, bf16[512,768]{1,0:T(8,128)(2,1)} %convolution_convert_fusion.12.value_ref, bf16[512,768]{1,0:T(8,128)(2,1)} %get-tuple-element.73.prob_ref, ...), custom_call_target="tpu_custom_call" | custom-call | flops 1048576 | bytes 1048576 | tf_op jit(solution)/shard_map/pallas_call | solution.py:162
  249.9 3.2 fusion.27
  253.2 3.1 fusion.29
  256.4 0.6 broadcast_in_dim.93
  257.0 0.6 broadcast_in_dim.101.rest_4_
  257.6 0.6 broadcast_in_dim.102.rest_5_
  258.2 0.6 broadcast_in_dim.99.rest_2_
  259.4 5.4 %fusion.21 = (f32[512]{0:T(512)}, f32[768]{0:T(1024)S(1)}, f32[512]{0:T(512)}, f32[768]{0:T(1024)S(1)}, f32[512,768]{1,0:T(8,128)}) fusion(f32[768]{0:T(1024)S(1)} %copy-done.22, f32[512]{0:T(512)S(1)} %copy-done.23, f32[512]{0:T(512)S(1)} %div.46, bf16[8,32,768]{2,1,0:T(8,128)(2,1)S(1)} %copy-done.1, bf16[8,32,768]{2,1,0:T(8,128)(2,1)S(1)} %get-tuple-element.129, ...), kind=kOutput, calls=%fused_computation.34 | convolution fusion | flops 609875456 | bytes 7488512 | tf_op jit(solution)/shard_map/dot_general | solution.py:26
  266.0 0.7 broadcast_multiply_fusion.1
  266.7 0.7 broadcast_multiply_fusion.2
  267.4 2.3 fusion.25
  269.7 1.8 convolution_convert_fusion.6
  271.9 3.9 convolution_convert_fusion.2
  275.8 116.5 %shard_map.345 = (f32[16,48,384]{2,1,0:T(8,128)}, f32[8,768]{1,0:T(8,128)}, bf16[16,288,768]{2,1,0:T(8,128)(2,1)}, bf16[8,32,768]{2,1,0:T(8,128)(2,1)}, bf16[8,32,768]{2,1,0:T(8,128)(2,1)}) custom-call(bf16[4,2,2,48,3072]{4,3,2,1,0:T(8,128)(2,1)} %bitcast.169, bf16[4,2,2,48,3072]{4,3,2,1,0:T(8,128)(2,1)} %bitcast.168, ...), custom_call_target="tpu_custom_call" | custom-call | bytes 1048576 | tf_op jit(solution)/shard_map/pallas_call | solution.py:1022
  392.3 1.8 slice_reduce_fusion
  394.0 2.1 slice_bitcast_fusion.3
  396.2 9.9 %convert_element_type.156 = f32[16,288,768]{2,1,0:T(8,128)} convert(bf16[16,288,768]{2,1,0:T(8,128)(2,1)} %get-tuple-element.88) | non-fusion elementwise | flops 3538944 | bytes 21233664 | tf_op jit(solution)/shard_map/convert_element_type | solution.py:1083
  406.1 0.7 maximum_bitcast_fusion
  406.8 0.7 pad_maximum_fusion.2
  407.5 1.6 fusion.31
  (139 shorter events, 6.3 us)
Async XLA Ops:
  6.9 0.7 copy-start.18
  7.6 84.5 %copy-start.8 = (bf16[16,32,768]{2,1,0:T(8,128)(2,1)S(1)}, bf16[16,32,768]{2,1,0:T(8,128)(2,1)}, u32[]{:S(2)}) copy-start(bf16[16,32,768]{2,1,0:T(8,128)(2,1)} %text_in.1) | copy-start | bytes 2359300
  7.6 84.5 %copy-start.9 = (bf16[16,32,768]{2,1,0:T(8,128)(2,1)S(1)}, bf16[16,32,768]{2,1,0:T(8,128)(2,1)}, u32[]{:S(2)}) copy-start(bf16[16,32,768]{2,1,0:T(8,128)(2,1)} %grad_in.1) | copy-start | bytes 2359300
  94.2 1.6 copy-start
  94.2 0.7 copy-start.48
  94.2 1.6 copy-start.19
  94.2 1.6 copy-start.21
  94.9 1.4 copy-start.37
  96.3 1.7 copy-start.40
  98.0 1.7 copy-start.38
  109.7 1.3 copy-start.5
  109.7 12.2 %slice-start = ((s8[7077888]{0:T(1024)(128)(4,1)}), s8[4194304]{0:T(1024)(128)(4,1)S(1)}, s32[]{:S(2)}) async-start(s8[7077888]{0:T(1024)(128)(4,1)} %bitcast.193), calls=%async_computation | async-start | bytes 8388608
  110.0 20.2 %copy-start.24 = (f32[512]{0:T(512)}, f32[512]{0:T(512)S(1)}, u32[]{:S(2)}) copy-start(f32[512]{0:T(512)S(1)} %add_rsqrt_fusion.2) | copy-start | bytes 6148
  111.0 10.9 %copy-start.4 = (bf16[16,48,768]{2,1,0:T(8,128)(2,1)S(1)}, bf16[16,48,768]{2,1,0:T(8,128)(2,1)}, u32[]{:S(2)}) copy-start(bf16[16,48,768]{2,1,0:T(8,128)(2,1)} %get-tuple-element.64) | copy-start | bytes 3538948
  111.0 10.9 %slice-start.1 = ((s8[7077888]{0:T(1024)(128)(4,1)}), s8[2883584]{0:T(1024)(128)(4,1)S(1)}, s32[]{:S(2)}) async-start(s8[7077888]{0:T(1024)(128)(4,1)} %bitcast.193), calls=%async_computation.1 | async-start | bytes 5767168
  121.9 8.3 %copy-start.33 = (f32[768]{0:T(1024)S(1)}, f32[768]{0:T(1024)}, u32[]{:S(2)}) copy-start(f32[768]{0:T(1024)} %param.35) | copy-start | bytes 9220
  121.9 8.3 %copy-start.43 = (bf16[16,48,768]{2,1,0:T(8,128)(2,1)S(1)}, bf16[16,48,768]{2,1,0:T(8,128)(2,1)}, u32[]{:S(2)}) copy-start(bf16[16,48,768]{2,1,0:T(8,128)(2,1)} %get-tuple-element.62) | copy-start | bytes 3538948
  121.9 8.3 %copy-start.46 = (f32[768]{0:T(1024)S(1)}, f32[768]{0:T(1024)}, u32[]{:S(2)}) copy-start(f32[768]{0:T(1024)} %param.36) | copy-start | bytes 9220
  147.8 1.0 copy-start.11
  147.8 1.1 copy-start.12
  147.8 1.2 copy-start.32
  147.8 1.2 copy-start.45
  148.1 26.1 %copy-start.27 = (f32[512]{0:T(512)}, f32[512]{0:T(512)S(1)}, u32[]{:S(2)}) copy-start(f32[512]{0:T(512)S(1)} %add_rsqrt_fusion.1) | copy-start | bytes 6148
  148.9 5.1 %slice-start.4 = ((s8[4718592]{0:T(1024)(128)(4,1)}), s8[4194304]{0:T(1024)(128)(4,1)S(1)}, s32[]{:S(2)}) async-start(s8[4718592]{0:T(1024)(128)(4,1)} %bitcast.200), calls=%async_computation.4 | async-start | bytes 8388608
  148.9 15.8 %copy-start.6 = (bf16[8,64,768]{2,1,0:T(8,128)(2,1)}, bf16[8,64,768]{2,1,0:T(8,128)(2,1)S(1)}, u32[]{:S(2)}) copy-start(bf16[8,64,768]{2,1,0:T(8,128)(2,1)S(1)} %pad_maximum_fusion) | copy-start | bytes 2359300
  149.0 5.1 %slice-start.5 = ((s8[4718592]{0:T(1024)(128)(4,1)}), s8[524288]{0:T(1024)(128)(4,1)S(1)}, s32[]{:S(2)}) async-start(s8[4718592]{0:T(1024)(128)(4,1)} %bitcast.200), calls=%async_computation.5 | async-start | bytes 1048576
  154.1 15.4 %slice-start.2 = ((s8[4718592]{0:T(1024)(128)(4,1)}), s8[4194304]{0:T(1024)(128)(4,1)S(1)}, s32[]{:S(2)}) async-start(s8[4718592]{0:T(1024)(128)(4,1)} %bitcast.197), calls=%async_computation.2 | async-start | bytes 8388608
  159.0 10.5 %slice-start.3 = ((s8[4718592]{0:T(1024)(128)(4,1)}), s8[524288]{0:T(1024)(128)(4,1)S(1)}, s32[]{:S(2)}) async-start(s8[4718592]{0:T(1024)(128)(4,1)} %bitcast.197), calls=%async_computation.3 | async-start | bytes 1048576
  180.3 3.4 copy-start.15
  183.8 1.8 copy-start.13
  205.4 17.0 %copy-start.25 = (f32[512]{0:T(512)S(1)}, f32[512]{0:T(512)}, u32[]{:S(2)}) copy-start(f32[512]{0:T(512)} %copy-done.24) | copy-start | bytes 6148
  205.4 17.0 %copy-start.34 = (f32[768]{0:T(1024)S(1)}, f32[768]{0:T(1024)}, u32[]{:S(2)}) copy-start(f32[768]{0:T(1024)} %param.35) | copy-start | bytes 9220
  205.4 17.0 %copy-start.47 = (f32[768]{0:T(1024)S(1)}, f32[768]{0:T(1024)}, u32[]{:S(2)}) copy-start(f32[768]{0:T(1024)} %param.36) | copy-start | bytes 9220
  205.4 17.0 %copy-start.50 = (bf16[512,768]{1,0:T(8,128)(2,1)S(1)}, bf16[512,768]{1,0:T(8,128)(2,1)}, u32[]{:S(2)}) copy-start(bf16[512,768]{1,0:T(8,128)(2,1)} %get-tuple-element.79) | copy-start | bytes 2359300
  225.1 9.1 %copy-start.44 = (bf16[16,48,768]{2,1,0:T(8,128)(2,1)S(1)}, bf16[16,48,768]{2,1,0:T(8,128)(2,1)}, u32[]{:S(2)}) copy-start(bf16[16,48,768]{2,1,0:T(8,128)(2,1)} %get-tuple-element.62) | copy-start | bytes 3538948
  232.4 43.4 %collective-permute-start = (bf16[4,288,768]{2,1,0:T(8,128)(2,1)}, bf16[4,288,768]{2,1,0:T(8,128)(2,1)}, u32[]{:S(2)}, u32[]{:S(2)}) collective-permute-start(bf16[4,288,768]{2,1,0:T(8,128)(2,1)} %shard_map.343), channel_id=1, source_target_pairs={{0,1},{1,0},{2,3},{3,2},{4,5},{5,4},{6,7},{7,6},{8,9},{9,8},{10,11... | collective-permute-start | bytes 5308424 | tf_op jit(solution)/shard_map/ppermute | solution.py:179
  234.2 3.1 copy-start.2
  234.2 3.1 copy-start.26
  234.2 3.1 copy-start.35
  237.3 1.3 copy-start.42
  240.2 9.6 %copy-start.41 = (bf16[16,48,768]{2,1,0:T(8,128)(2,1)S(1)}, bf16[16,48,768]{2,1,0:T(8,128)(2,1)}, u32[]{:S(2)}) copy-start(bf16[16,48,768]{2,1,0:T(8,128)(2,1)} %get-tuple-element.58) | copy-start | bytes 3538948
  249.9 3.2 copy-start.39
  253.1 3.2 copy-start.49
  253.1 3.9 copy-start.29
  253.1 4.5 %copy-start.28 = (f32[768]{0:T(1024)S(1)}, f32[768]{0:T(1024)}, u32[]{:S(2)}) copy-start(f32[768]{0:T(1024)} %get-tuple-element.101) | copy-start | bytes 9220
  253.1 5.1 %copy-start.31 = (f32[768]{0:T(1024)S(1)}, f32[768]{0:T(1024)}, u32[]{:S(2)}) copy-start(f32[768]{0:T(1024)} %get-tuple-element.93) | copy-start | bytes 9220
  253.1 5.7 %copy-start.30 = (f32[768]{0:T(1024)S(1)}, f32[768]{0:T(1024)}, u32[]{:S(2)}) copy-start(f32[768]{0:T(1024)} %get-tuple-element.102) | copy-start | bytes 9220
  253.1 6.2 %copy-start.1 = (bf16[8,32,768]{2,1,0:T(8,128)(2,1)S(1)}, bf16[8,32,768]{2,1,0:T(8,128)(2,1)}, u32[]{:S(2)}) copy-start(bf16[8,32,768]{2,1,0:T(8,128)(2,1)} %copy-done) | copy-start | bytes 1179652
  253.1 6.2 %copy-start.22 = (f32[768]{0:T(1024)S(1)}, f32[768]{0:T(1024)}, u32[]{:S(2)}) copy-start(f32[768]{0:T(1024)} %param.33) | copy-start | bytes 9220
  253.1 6.2 %copy-start.23 = (f32[512]{0:T(512)S(1)}, f32[512]{0:T(512)}, u32[]{:S(2)}) copy-start(f32[512]{0:T(512)} %rsqrt.31) | copy-start | bytes 6148
  259.4 6.6 %copy-start.10 = (bf16[512,768]{1,0:T(8,128)(2,1)S(1)}, bf16[512,768]{1,0:T(8,128)(2,1)}, u32[]{:S(2)}) copy-start(bf16[512,768]{1,0:T(8,128)(2,1)} %add_convert_fusion) | copy-start | bytes 2359300
  259.4 8.0 %copy-start.20 = (f32[768]{0:T(1024)S(1)}, f32[768]{0:T(1024)}, u32[]{:S(2)}) copy-start(f32[768]{0:T(1024)} %param.34) | copy-start | bytes 9220
  267.4 2.3 copy-start.14
  269.6 1.9 copy-start.3
  269.7 2.2 copy-start.7
  396.2 11.3 %copy-start.16 = (bf16[8,32,768]{2,1,0:T(8,128)(2,1)S(1)}, bf16[8,32,768]{2,1,0:T(8,128)(2,1)}, u32[]{:S(2)}) copy-start(bf16[8,32,768]{2,1,0:T(8,128)(2,1)} %get-tuple-element.87) | copy-start | bytes 1179652
  396.2 11.3 %copy-start.17 = (bf16[8,32,768]{2,1,0:T(8,128)(2,1)S(1)}, bf16[8,32,768]{2,1,0:T(8,128)(2,1)}, u32[]{:S(2)}) copy-start(bf16[8,32,768]{2,1,0:T(8,128)(2,1)} %get-tuple-element.86) | copy-start | bytes 1179652
  396.2 11.3 %copy-start.36 = (pred[16]{0:T(512)(128)(4,1)S(1)}, pred[16]{0:T(512)(128)(4,1)}, u32[]{:S(2)}) copy-start(pred[16]{0:T(512)(128)(4,1)} %broadcast_in_dim.93) | copy-start | bytes 52
